TPU v7x, 256 devices: a whole 4x4x8 slice. The times are simulated.
256 devices in a mesh: dp: 32 (over y, x, core), mp: 8 (over z).
Axes of the slice: x: 4, y: 4, z: 8, core: 2. Of those that a mesh axis runs over, the one named last changes fastest.
Arguments:
- hidden: bfloat16 [16384, 4096], P('dp', 'mp'), may hold values from -50 to 50
- norm_gain: float32 [4096], replicated, may hold values from 0.1 to 1.9
- w_query: bfloat16 [4096, 4096], P(None, 'mp'), may hold values from -0.09375 to 0.09375
- w_out: bfloat16 [4096, 4096], P('mp'), may hold values from -0.09375 to 0.09375
- nb_keys: bfloat16 [256, 128, 4096], P('dp', None, 'mp'), may hold values from -250 to 250
- nb_values: bfloat16 [256, 128, 4096], P('dp', None, 'mp'), may hold values from -10 to 10
- neighbours: int32 [256, 2], P('dp'), may hold values from 0 to 255, as said below
- valid_spans: int32 [32], P('dp'), may hold values from 6 to 8, as said below
Outputs:
- mixed: float32 [16384, 4096], P('dp', 'mp')
Inputs may be any that keep to these rules, and one draw needn't show every extreme that they name: Block ids; block b is stored by index b // 8 of dp, its owner. The two neighbours of a span have different owners. The spans of one index of dp name one owner at most 2 times, and some owner is named exactly 2 times by the live spans of every index of dp. `valid_spans`: some index of dp has all 8 spans live.
All inputs are finite; a program needn't handle non-finite values.
Results may differ from a plain program's by a relative error of at most 0.0066.
Values may be sent and summed in bfloat16 or wider, within the bound.
No kernel may reach another device: no remote copies, remote signals or barrier semaphores. Data moves between devices by JAX's collectives and lax.ppermute only.
A program may use at most 128 MiB of HBM per device.

v0:
```python
import math

import jax
import jax.numpy as jnp
from jax import lax
from jax.sharding import PartitionSpec as P

HS = 128
SPAN = 64


eps = 1e-05


def shifted(block, axis, distance):
    devices = range(lax.axis_size(axis))
    route = [(i - distance, i) for i in devices if i - distance in devices]
    return lax.ppermute(block, axis, route)


def partial_attention(query_rows, key_rows, value_rows):
    inner_width = key_rows.shape[-1]
    head_count = inner_width // HS
    query_heads = query_rows.reshape(query_rows.shape[:-1] + (head_count, HS))
    key_heads = key_rows.reshape(key_rows.shape[:-1] + (head_count, HS))
    value_heads = value_rows.reshape(value_rows.shape[:-1] + (head_count, HS))
    factor = 1.0 / math.sqrt(HS)
    scores = (
        jnp.einsum(
            "...qhd,...khd->...qhk", query_heads, key_heads, preferred_element_type=jnp.float32
        )
        * factor
    )
    score_top = jnp.max(scores, axis=-1)
    weights = jnp.exp(scores - score_top[..., None])
    weight_sum = jnp.sum(weights, axis=-1)
    summed = jnp.einsum(
        "...qhk,...khd->...qhd",
        weights.astype(jnp.bfloat16),
        value_heads,
        preferred_element_type=jnp.float32,
    )
    part_out = (summed / weight_sum[..., None]).astype(jnp.bfloat16)
    return (part_out.reshape(part_out.shape[:-2] + (inner_width,)), score_top, weight_sum)


def combine(part_out, score_top, weight_sum):
    head_count = score_top.shape[-1]
    best_score = jnp.max(score_top, axis=1, keepdims=True)
    mix_weight = jnp.exp(score_top - best_score) * weight_sum
    widened = part_out.reshape(part_out.shape[:-1] + (head_count, HS)).astype(jnp.float32)
    merged = (
        jnp.sum(widened * mix_weight[..., None], axis=1) / jnp.sum(mix_weight, axis=1)[..., None]
    )
    return merged.reshape(merged.shape[:-2] + (head_count * HS,)).astype(jnp.bfloat16)


def shards(hidden, norm_gain, w_query, w_out, nb_keys, nb_values, neighbours, valid_spans):
    tok_rows = hidden.shape[0]
    span_dev = tok_rows // SPAN
    stored = nb_keys.shape[0]
    inner_width = w_query.shape[1]
    peer_count = lax.axis_size("dp")
    most_slots = max(2, (2 * span_dev + peer_count - 1) // peer_count)
    widened = lax.all_gather(hidden, "mp", axis=1, tiled=True).astype(jnp.float32)
    normed = (
        widened * lax.rsqrt(jnp.mean(widened * widened, axis=1, keepdims=True) + eps) * norm_gain
    ).astype(jnp.bfloat16)
    queries = jnp.dot(normed, w_query, preferred_element_type=jnp.float32).astype(jnp.bfloat16)
    following = shifted(queries[: SPAN - 1], "dp", -1)
    grouped = jnp.concatenate([queries[SPAN - 1 :], following], axis=0).reshape(
        span_dev, SPAN, inner_width
    )
    live_span = jnp.arange(span_dev, dtype=jnp.int32) < valid_spans[0]
    owners = (neighbours // stored).reshape(-1)
    slot_ids = (neighbours % stored).reshape(-1)
    is_live = jnp.repeat(live_span, 2)
    req_order = jnp.arange(owners.shape[0], dtype=jnp.int32)
    earlier = (
        (owners[:, None] == owners[None, :])
        & is_live[None, :]
        & (req_order[None, :] < req_order[:, None])
    )
    slot_rank = jnp.minimum(jnp.sum(earlier.astype(jnp.int32), axis=1), most_slots - 1)
    target = jnp.where(is_live, owners * most_slots + slot_rank, -1)
    slot_match = target[:, None] == jnp.arange(peer_count * most_slots, dtype=jnp.int32)[None, :]
    filled = jnp.any(slot_match, axis=0)
    request_table = jnp.where(
        filled, jnp.sum(jnp.where(slot_match, slot_ids[:, None], 0), axis=0), -1
    )
    request_table = request_table.reshape(peer_count, most_slots)
    source_span = jnp.sum(jnp.where(slot_match, req_order[:, None] // 2, 0), axis=0)
    sent_rows = grouped[source_span].reshape(peer_count, most_slots, SPAN, inner_width)
    wanted = lax.all_to_all(request_table, "dp", split_axis=0, concat_axis=0, tiled=True)
    asked = lax.all_to_all(sent_rows, "dp", split_axis=0, concat_axis=0, tiled=True)
    safe_ids = jnp.maximum(wanted, 0)
    result = partial_attention(asked, nb_keys[safe_ids], nb_values[safe_ids])
    part_back = lax.all_to_all(
        result[0].astype(jnp.float32), "dp", split_axis=0, concat_axis=0, tiled=True
    ).astype(jnp.bfloat16)
    top_back = lax.all_to_all(result[1], "dp", split_axis=0, concat_axis=0, tiled=True)
    sum_back = lax.all_to_all(result[2], "dp", split_axis=0, concat_axis=0, tiled=True)
    part_out = part_back[owners, slot_rank].reshape(span_dev, 2, SPAN, inner_width)
    score_top = top_back[owners, slot_rank].reshape(span_dev, 2, SPAN, -1)
    weight_sum = sum_back[owners, slot_rank].reshape(span_dev, 2, SPAN, -1)
    merged = combine(part_out, score_top, weight_sum)
    merged = jnp.where(live_span[:, None, None], merged, jnp.zeros_like(merged))
    flat_rows = merged.reshape(tok_rows, inner_width)
    previous = shifted(flat_rows[tok_rows - SPAN + 1 :], "dp", 1)
    placed = jnp.concatenate([previous, flat_rows[: tok_rows - SPAN + 1]], axis=0)
    head_terms = jnp.dot(placed, w_out, preferred_element_type=jnp.float32)
    summed = lax.psum_scatter(head_terms, "mp", scatter_dimension=1, tiled=True)
    return hidden.astype(jnp.float32) + summed


def solution(mesh):
    placed = (
        P("dp", "mp"),
        P(),
        P(None, "mp"),
        P("mp", None),
        P("dp", None, "mp"),
        P("dp", None, "mp"),
        P("dp", None),
        P("dp"),
    )
    return jax.shard_map(
        shards, mesh=mesh, in_specs=placed, out_specs=P("dp", "mp"), check_vma=False
    )
```

profile of v0, /device:TPU:28, one launch (start us, length us, event | category | flops | bytes accessed | tf_op | source)
XLA Modules:
  0.0 368.8 jit_solution(1386096142998444938)
XLA Ops:
  6.5 0.7 all-gather.2.cloned.1.call-update
  8.1 0.7 and_select_fusion.1
  9.1 0.2 convert_reduce_fusion
  9.5 0.7 select_n.98
  10.2 7.3 %all-to-all-start = ((s32[32,1,2]{2,1,0:T(1,128)}), s32[32,1,2]{2,1,0:T(1,128)S(1)}, u32[]{:S(2)}, u32[]{:S(2)}) async-start(s32[32,1,2]{2,1,0:T(1,128)} %bitcast.1), calls=%async_computation | async-start | bytes 32768 | tf_op jit(solution)/shard_map/all_to_all | solution.py:94
  17.6 49.0 %all-gather.2.cloned.1.call-done = bf16[512,4096]{1,0:T(8,128)(2,1)} async-done(((bf16[512,512]{1,0:T(8,128)(2,1)}), bf16[512,4096]{1,0:T(8,128)(2,1)}) %all-gather.2.cloned.1.call-update) | async-done | bytes 4194320 | tf_op jit(solution)/shard_map/all_gather | solution.py:65
  66.6 3.1 fusion
  69.7 5.9 %fusion.24 = bf16[512,512]{1,0:T(8,128)(2,1)S(1)} fusion(bf16[4096,512]{1,0:T(8,128)(2,1)} %param.10, bf16[512,4096]{1,0:T(8,128)(2,1)} %all-gather.2.cloned.1.call-done, f32[4096]{0:T(1024)} %param.9, f32[512]{0:T(512)S(1)} %add_rsqrt_fusion), kind=kOutput, calls=%fused_computation.32 | convolution fusion | flops 2156134400 | bytes 8931328 | tf_op jit(solution)/shard_map/dot_general | solution.py:69
  75.5 1.9 collective-permute-start
  77.5 0.1 slice.28
  77.6 1.8 collective-permute-done
  79.4 2.8 gather_fusion.2
  82.2 10.3 %all-to-all-start.1 = ((bf16[32,2,64,512]{3,2,1,0:T(8,128)(2,1)}), bf16[32,2,64,512]{3,2,1,0:T(8,128)(2,1)}, u32[]{:S(2)}, u32[]{:S(2)}) async-start(bf16[32,2,64,512]{3,2,1,0:T(8,128)(2,1)} %bitcast.69), calls=%async_computation.1 | async-start | bytes 8388608 | tf_op jit(solution)/shard_map/all_to_all | solution.py:95
  92.6 0.1 reshape.234
  92.7 5.3 %gather_fusion.1 = bf16[64,128,512]{2,1,0:T(8,128)(2,1)} fusion(bf16[8,128,512]{2,1,0:T(8,128)(2,1)S(1)} %copy-done, s32[1024]{0:T(1024)S(1)} %pad_clamp_fusion.1), kind=kCustom, calls=%fused_computation.1 | custom fusion | bytes 16777472 | tf_op jit(solution)/shard_map/gather | solution.py:97
  98.0 12.6 %reshape.223 = bf16[32,2,128,4,128]{4,3,2,1,0:T(4,128)(2,1)} reshape(bf16[64,128,512]{2,1,0:T(8,128)(2,1)} %gather_fusion.1) | data formatting | bytes 16777216 | tf_op jit(solution)/shard_map/reshape | solution.py:25
  110.6 5.3 %gather_fusion = bf16[64,128,512]{2,1,0:T(8,128)(2,1)} fusion(bf16[8,128,512]{2,1,0:T(8,128)(2,1)S(1)} %copy-done.2, s32[1024]{0:T(1024)S(1)} %pad_clamp_fusion.1), kind=kCustom, calls=%fused_computation | custom fusion | bytes 16777472 | tf_op jit(solution)/shard_map/gather | solution.py:97
  115.9 12.5 %reshape.222 = bf16[32,2,128,4,128]{4,3,2,1,0:T(4,128)(2,1)} reshape(bf16[64,128,512]{2,1,0:T(8,128)(2,1)} %gather_fusion) | data formatting | bytes 16777216 | tf_op jit(solution)/shard_map/reshape | solution.py:26
  128.5 12.7 %all-to-all-done.1 = bf16[32,2,64,512]{3,2,1,0:T(8,128)(2,1)} async-done(((bf16[32,2,64,512]{3,2,1,0:T(8,128)(2,1)}), bf16[32,2,64,512]{3,2,1,0:T(8,128)(2,1)}, u32[]{:S(2)}, u32[]{:S(2)}) %all-to-all-start.1) | async-done | bytes 4194336 | tf_op jit(solution)/shard_map/all_to_all | solution.py:95
  141.2 11.0 %bitcast_reduce_fusion = (f32[32,2,64,4]{2,3,1,0:T(4,128)S(1)}, f32[32,2,4,128,64]{3,4,2,1,0:T(8,128)}) fusion(bf16[32,2,128,4,128]{4,3,2,1,0:T(4,128)(2,1)} %reshape.223, bf16[32,2,64,512]{3,2,1,0:T(8,128)(2,1)} %all-to-all-done.1), kind=kOutput, calls=%fused_computation.15 | convolution fusion | flops 541048832 | bytes 21037056 | tf_op jit(solution)/shard_map/...qhd,...khd->...qhk/dot_general | solution.py:29
  152.2 0.8 reshape.289
  153.0 9.2 %all-to-all-start.3 = ((f32[32,1,512]{2,1,0:T(1,128)}), f32[32,1,512]{2,1,0:T(1,128)S(1)}, u32[]{:S(2)}, u32[]{:S(2)}) async-start(f32[32,1,512]{2,1,0:T(1,128)} %reshape.289), calls=%async_computation.3 | async-start | bytes 131072 | tf_op jit(solution)/shard_map/all_to_all | solution.py:101
  162.2 6.9 %fusion.9 = f32[32,2,64,4]{2,3,1,0:T(4,128)S(1)} fusion(f32[32,2,4,128,64]{3,4,2,1,0:T(8,128)} %get-tuple-element.12, f32[32,2,64,4]{2,3,1,0:T(4,128)S(1)} %get-tuple-element.11), kind=kLoop, calls=%fused_computation.22 | loop fusion | flops 6275072 | bytes 8519680 | tf_op jit(solution)/shard_map/reduce_sum | solution.py:36
  169.1 0.8 reshape.287
  169.8 7.4 %all-to-all-start.4 = ((f32[32,1,512]{2,1,0:T(1,128)}), f32[32,1,512]{2,1,0:T(1,128)S(1)}, u32[]{:S(2)}, u32[]{:S(2)}) async-start(f32[32,1,512]{2,1,0:T(1,128)} %reshape.287), calls=%async_computation.4 | async-start | bytes 131072 | tf_op jit(solution)/shard_map/all_to_all | solution.py:102
  177.2 9.0 %convert_bitcast_fusion = bf16[32,2,4,8,8,128]{5,4,3,2,1,0:T(8,128)(2,1)S(1)} fusion(f32[32,2,64,4]{2,3,1,0:T(4,128)S(1)} %fusion.9, bf16[32,2,128,4,128]{4,3,2,1,0:T(4,128)(2,1)} %reshape.222, f32[32,2,4,128,64]{3,4,2,1,0:T(8,128)} %get-tuple-element.12, f32[32,2,64,4]{2,3,1,0:T(4,128)S(1)} %get-tuple-element.11), kind=kOutput, calls=%fused_computation.21 | convolution fusion | flops 547356672 | bytes 21102592 | tf_op jit(solution)/shard_map/...qhk,...khd->...qhd/dot_general | solution.py:37
  186.2 2.7 copy.62
  189.0 7.4 %all-to-all-start.2 = ((bf16[32,2,64,512]{3,2,1,0:T(8,128)(2,1)}), bf16[32,2,64,512]{3,2,1,0:T(8,128)(2,1)}, u32[]{:S(2)}, u32[]{:S(2)}) async-start(bf16[32,2,64,512]{3,2,1,0:T(8,128)(2,1)} %bitcast.68), calls=%async_computation.2 | async-start | bytes 8388608 | tf_op jit(solution)/shard_map/all_to_all | solution.py:98
  196.7 0.5 broadcast.277
  197.2 0.8 reduce.4
  198.0 0.1 reshape.290
  198.2 0.8 reduce.5
  199.0 0.1 reshape.288
  199.1 0.6 gather_fusion.4
  199.7 0.6 gather_fusion.5
  200.4 1.0 copy.41
  201.4 0.1 copy.42
  201.6 43.5 %all-to-all-done.2 = bf16[32,2,64,512]{3,2,1,0:T(8,128)(2,1)} async-done(((bf16[32,2,64,512]{3,2,1,0:T(8,128)(2,1)}), bf16[32,2,64,512]{3,2,1,0:T(8,128)(2,1)}, u32[]{:S(2)}, u32[]{:S(2)}) %all-to-all-start.2) | async-done | bytes 4194336 | tf_op jit(solution)/shard_map/all_to_all | solution.py:98
  245.1 2.8 gather_fusion.3
  247.9 0.7 reshape.231
  248.6 2.7 multiply_reduce_fusion
  251.3 0.7 divide_convert_fusion
  252.0 0.1 bitcast_select_fusion
  252.2 1.9 collective-permute-start.1
  254.2 3.6 collective-permute-done.1
  257.8 5.6 %fusion.27 = f32[512,4096]{1,0:T(8,128)} fusion(bf16[512,4096]{1,0:T(8,128)(2,1)S(1)} %copy-done.3, bf16[449,512]{1,0:T(8,128)(2,1)S(1)} %slice.31, bf16[63,512]{1,0:T(8,128)(2,1)S(1)} %collective-permute-done.1), kind=kOutput, calls=%fused_computation.37 | convolution fusion | flops 2148532224 | bytes 13107200 | tf_op jit(solution)/shard_map/dot_general | solution.py:111
  263.4 96.2 %reduce-scatter.2.cloned.1.call-done = f32[512,512]{1,0:T(8,128)} async-done(((f32[512,4096]{1,0:T(8,128)}), f32[512,512]{1,0:T(8,128)}) %reduce-scatter.2.cloned.1.call-update) | async-done | bytes 1048592 | tf_op jit(solution)/shard_map/reduce_scatter | solution.py:112
  359.6 2.4 convert_add_fusion
  (42 shorter events, 1.3 us)
Async XLA Ops:
  6.5 86.2 %copy-start = (bf16[8,128,512]{2,1,0:T(8,128)(2,1)S(1)}, bf16[8,128,512]{2,1,0:T(8,128)(2,1)}, u32[]{:S(2)}) copy-start(bf16[8,128,512]{2,1,0:T(8,128)(2,1)} %param.12) | copy-start | bytes 3145732
  6.5 60.0 %all-gather.2.cloned.1.call-start = ((), (), s32[]{:S(2)}) async-start(), calls=%async_computation.6 | async-start | bytes 4718592 | tf_op jit(solution)/shard_map/all_gather | solution.py:65
  10.2 72.0 %all-to-all-start = ((s32[32,1,2]{2,1,0:T(1,128)}), s32[32,1,2]{2,1,0:T(1,128)S(1)}, u32[]{:S(2)}, u32[]{:S(2)}) async-start(s32[32,1,2]{2,1,0:T(1,128)} %bitcast.1), calls=%async_computation | async-start | bytes 32768 | tf_op jit(solution)/shard_map/all_to_all | solution.py:94
  75.5 3.8 %collective-permute-start = (bf16[63,512]{1,0:T(8,128)(2,1)S(1)}, bf16[63,512]{1,0:T(8,128)(2,1)S(1)}, u32[]{:S(2)}, u32[]{:S(2)}) collective-permute-start(bf16[63,512]{1,0:T(8,128)(2,1)S(1)} %slice.29), channel_id=1, source_target_pairs={{8,0},{16,8},{24,16},{32,24},{40,32},{48,40},{56,48},{64,56},{72,6... | collective-permute-start | bytes 193544 | tf_op jit(solution)/shard_map/ppermute | solution.py:18
  82.2 59.0 %all-to-all-start.1 = ((bf16[32,2,64,512]{3,2,1,0:T(8,128)(2,1)}), bf16[32,2,64,512]{3,2,1,0:T(8,128)(2,1)}, u32[]{:S(2)}, u32[]{:S(2)}) async-start(bf16[32,2,64,512]{3,2,1,0:T(8,128)(2,1)} %bitcast.69), calls=%async_computation.1 | async-start | bytes 8388608 | tf_op jit(solution)/shard_map/all_to_all | solution.py:95
  98.0 12.6 %copy-start.2 = (bf16[8,128,512]{2,1,0:T(8,128)(2,1)S(1)}, bf16[8,128,512]{2,1,0:T(8,128)(2,1)}, u32[]{:S(2)}) copy-start(bf16[8,128,512]{2,1,0:T(8,128)(2,1)} %param.13) | copy-start | bytes 3145732
  153.0 16.9 %all-to-all-start.3 = ((f32[32,1,512]{2,1,0:T(1,128)}), f32[32,1,512]{2,1,0:T(1,128)S(1)}, u32[]{:S(2)}, u32[]{:S(2)}) async-start(f32[32,1,512]{2,1,0:T(1,128)} %reshape.289), calls=%async_computation.3 | async-start | bytes 131072 | tf_op jit(solution)/shard_map/all_to_all | solution.py:101
  169.8 19.1 %all-to-all-start.4 = ((f32[32,1,512]{2,1,0:T(1,128)}), f32[32,1,512]{2,1,0:T(1,128)S(1)}, u32[]{:S(2)}, u32[]{:S(2)}) async-start(f32[32,1,512]{2,1,0:T(1,128)} %reshape.287), calls=%async_computation.4 | async-start | bytes 131072 | tf_op jit(solution)/shard_map/all_to_all | solution.py:102
  189.0 56.1 %all-to-all-start.2 = ((bf16[32,2,64,512]{3,2,1,0:T(8,128)(2,1)}), bf16[32,2,64,512]{3,2,1,0:T(8,128)(2,1)}, u32[]{:S(2)}, u32[]{:S(2)}) async-start(bf16[32,2,64,512]{3,2,1,0:T(8,128)(2,1)} %bitcast.68), calls=%async_computation.2 | async-start | bytes 8388608 | tf_op jit(solution)/shard_map/all_to_all | solution.py:98
  196.4 163.2 %reduce-scatter.2.cloned.1.call-start = ((), (), s32[]{:S(2)}) async-start(), calls=%async_computation.7 | async-start | bytes 9437184 | tf_op jit(solution)/shard_map/reduce_scatter | solution.py:112
  248.6 9.2 %copy-start.3 = (bf16[512,4096]{1,0:T(8,128)(2,1)S(1)}, bf16[512,4096]{1,0:T(8,128)(2,1)}, u32[]{:S(2)}) copy-start(bf16[512,4096]{1,0:T(8,128)(2,1)} %param.11) | copy-start | bytes 12582916
  252.2 5.6 %collective-permute-start.1 = (bf16[63,512]{1,0:T(8,128)(2,1)S(1)}, bf16[63,512]{1,0:T(8,128)(2,1)S(1)}, u32[]{:S(2)}, u32[]{:S(2)}) collective-permute-start(bf16[63,512]{1,0:T(8,128)(2,1)S(1)} %slice.30), channel_id=1, source_target_pairs={{0,8},{8,16},{16,24},{24,32},{32,40},{40,48},{48,56},{56,64},{64,7... | collective-permute-start | bytes 193544 | tf_op jit(solution)/shard_map/ppermute | solution.py:18
  254.2 105.5 %copy-start.4 = (bf16[512,512]{1,0:T(8,128)(2,1)S(1)}, bf16[512,512]{1,0:T(8,128)(2,1)}, u32[]{:S(2)}) copy-start(bf16[512,512]{1,0:T(8,128)(2,1)} %param.8) | copy-start | bytes 1572868
  257.8 104.2 %copy-start.1 = (bf16[8,128,512]{2,1,0:T(8,128)(2,1)S(1)}, bf16[8,128,512]{2,1,0:T(8,128)(2,1)}, u32[]{:S(2)}) copy-start(bf16[8,128,512]{2,1,0:T(8,128)(2,1)} %param.12) | copy-start | bytes 3145732
Sparse Core Ops, SparseCore 0:
  9.1 57.3 all-gather.1
  263.5 96.0 reduce-scatter.1
where the time goes:
time: 371 us; the launch traced here: 369 us
  waiting for transfers between devices  208 us (56%)
  local copies, waits for them, and re-layouts  51.2 us (14%)
  starting transfers between devices  45.6 us (12%)
  matrix products  31.5 us (8%)
  other arithmetic  18.7 us (5%)
  between operations  14.3 us (4%)
    reduce_scatter x1, waiting for transfers between devices, shards(): summed = lax.psum_scatter(head_terms, 'mp', scatter_dimension=1, tiled=True)  96.2 us
    all_gather x1, waiting for transfers between devices, shards(): lax.all_gather(hidden, 'mp', axis=1, tiled=True).astype(jnp.float32)  49 us
    all_to_all x1, waiting for transfers between devices, shards(): lax.all_to_all(result[0].astype(jnp.float32), 'dp', split_axis=0, concat_...  43.5 us
    all_to_all x1, waiting for transfers between devices, shards(): lax.all_to_all(sent_rows, 'dp', split_axis=0, concat_axis=0, tiled=True)  12.7 us
    reshape x1, local copies, waits for them, and re-layouts, partial_attention(): key_heads = key_rows.reshape(key_rows.shape[:-1] + (head_count, HS))  12.6 us
    reshape x1, local copies, waits for them, and re-layouts, partial_attention(): value_heads = value_rows.reshape(value_rows.shape[:-1] + (head_count, HS))  12.5 us
    dot_general x1, matrix products, partial_attention(): jnp.einsum('...qhd,...khd->...qhk', query_heads, key_heads, preferred_ele...  11 us
    gather x2, local copies, waits for them, and re-layouts, shards(): result = partial_attention(asked, nb_keys[safe_ids], nb_values[safe_ids])  10.6 us
  transfers between devices with their start and end apart: 9, of which 6 were waited for; matrix products, arithmetic and copies ran while one was open for 20% of the time, Pallas kernels for 0%

commit v1 on v0

v1 whole, which is shorter than its diff:
```python
import math

import jax
import jax.numpy as jnp
from jax import lax
from jax.experimental import pallas as pl
from jax.experimental.pallas import tpu as pltpu
from jax.sharding import PartitionSpec as P

HS = 128
SPAN = 64
SLOTS = 2
STATS = 8

eps = 1e-05
f32 = jnp.float32
bf16 = jnp.bfloat16


def shifted(block, axis, distance):
    devices = range(lax.axis_size(axis))
    route = [(i - distance, i) for i in devices if i - distance in devices]
    return lax.ppermute(block, axis, route)


def attend_kernel(ids_ref, q_ref, k_ref, v_ref, out_ref):
    peers = q_ref.shape[0]
    heads = q_ref.shape[2] // HS
    step = pl.program_id(0)
    factor = 1.0 / math.sqrt(HS)
    lane = lax.broadcasted_iota(jnp.int32, (SPAN, 128), 1)
    row = lax.broadcasted_iota(jnp.int32, (STATS, 128), 0)
    for p in range(peers):
        stats = []
        for j in range(SLOTS):
            block = ids_ref[(step * peers + p) * SLOTS + j]
            rows = pl.ds(j * SPAN, SPAN)
            stat = jnp.zeros((SPAN, 128), f32)
            for h in range(heads):
                cols = pl.ds(h * HS, HS)
                scores = lax.dot_general(
                    q_ref[p, rows, cols], k_ref[block, :, cols],
                    (((1,), (1,)), ((), ())), preferred_element_type=f32,
                ) * factor
                top = jnp.max(scores, axis=-1, keepdims=True)
                weights = jnp.exp(scores - top)
                total = jnp.sum(weights, axis=-1, keepdims=True)
                summed = jnp.dot(
                    weights.astype(bf16), v_ref[block, :, cols], preferred_element_type=f32
                )
                out_ref[p, rows, cols] = (summed / total).astype(bf16)
                stat = jnp.where(lane == h, top + jnp.log(total), stat)
            stats.append(stat)
        turned = jnp.transpose(jnp.concatenate(stats, axis=0))[:STATS]
        high = turned.astype(bf16).astype(f32)
        middle = (turned - high).astype(bf16).astype(f32)
        low = (turned - high - middle).astype(bf16).astype(f32)
        for h in range(heads):
            piece = jnp.where(
                row == 0, high[h:h + 1],
                jnp.where(row == 1, middle[h:h + 1], jnp.where(row == 2, low[h:h + 1], 0.0)),
            )
            out_ref[p, pl.ds(SLOTS * SPAN, STATS), pl.ds(h * HS, HS)] = piece.astype(bf16)


def attend(ids, asked, keys, values):
    peer_count, rows, width = asked.shape
    step = 4
    stored, tokens, _ = keys.shape
    return pl.pallas_call(
        attend_kernel,
        out_shape=jax.ShapeDtypeStruct((peer_count, rows + STATS, width), bf16),
        grid_spec=pltpu.PrefetchScalarGridSpec(
            num_scalar_prefetch=1,
            grid=(peer_count // step,),
            in_specs=[
                pl.BlockSpec((step, rows, width), lambda i, ids: (i, 0, 0)),
                pl.BlockSpec((stored, tokens, width), lambda i, ids: (0, 0, 0)),
                pl.BlockSpec((stored, tokens, width), lambda i, ids: (0, 0, 0)),
            ],
            out_specs=pl.BlockSpec((step, rows + STATS, width), lambda i, ids: (i, 0, 0)),
        ),
        compiler_params=pltpu.CompilerParams(dimension_semantics=("arbitrary",)),
        name="attend",
    )(ids, asked, keys, values)


def combine_kernel(owner_ref, rank_ref, live_ref, first_ref, second_ref, out_ref, stat_ref):
    span = pl.program_id(0)
    width = out_ref.shape[2]
    heads = width // HS
    parts = []
    for n, ref in enumerate((first_ref, second_ref)):
        offset = pl.multiple_of(rank_ref[2 * span + n] * SPAN, SPAN)
        stat = ref[0, pl.ds(SLOTS * SPAN, STATS), :].astype(f32)
        lse = stat[0:1] + stat[1:2] + stat[2:3]
        row = lax.broadcasted_iota(jnp.int32, (128, 128), 0)
        tile = jnp.zeros((128, 128), f32)
        for h in range(heads):
            tile = jnp.where(row == h, lse[:, h * HS:(h + 1) * HS], tile)
        stat_ref[n] = jnp.transpose(tile)
        parts.append((ref[0, pl.ds(offset, SPAN), :].astype(f32), stat_ref[n, pl.ds(offset, SPAN), :]))
    gap = parts[0][1] - parts[1][1]
    mine = 1.0 / (1.0 + jnp.exp(-gap))
    other = 1.0 / (1.0 + jnp.exp(gap))
    alive = span < live_ref[0]
    for h in range(heads):
        cols = slice(h * HS, (h + 1) * HS)
        merged = parts[0][0][:, cols] * mine[:, h:h + 1] + parts[1][0][:, cols] * other[:, h:h + 1]
        out_ref[0, :, cols] = jnp.where(alive, merged, 0.0).astype(bf16)


def combine(owners, ranks, live, back):
    spans = owners.shape[0] // 2
    _, rows, width = back.shape
    return pl.pallas_call(
        combine_kernel,
        out_shape=jax.ShapeDtypeStruct((spans, SPAN, width), bf16),
        grid_spec=pltpu.PrefetchScalarGridSpec(
            num_scalar_prefetch=3,
            grid=(spans,),
            in_specs=[
                pl.BlockSpec((1, rows, width), lambda i, own, rank, live: (own[2 * i], 0, 0)),
                pl.BlockSpec((1, rows, width), lambda i, own, rank, live: (own[2 * i + 1], 0, 0)),
            ],
            out_specs=pl.BlockSpec((1, SPAN, width), lambda i, own, rank, live: (i, 0, 0)),
            scratch_shapes=[pltpu.VMEM((2, 128, 128), f32)],
        ),
        compiler_params=pltpu.CompilerParams(dimension_semantics=("arbitrary",)),
        name="combine",
    )(owners, ranks, live, back, back)


def shards(hidden, norm_gain, w_query, w_out, nb_keys, nb_values, neighbours, valid_spans):
    tok_rows = hidden.shape[0]
    span_dev = tok_rows // SPAN
    stored = nb_keys.shape[0]
    inner_width = w_query.shape[1]
    peer_count = lax.axis_size("dp")
    widened = lax.all_gather(hidden, "mp", axis=1, tiled=True).astype(f32)
    normed = (
        widened * lax.rsqrt(jnp.mean(widened * widened, axis=1, keepdims=True) + eps) * norm_gain
    ).astype(bf16)
    queries = jnp.dot(normed, w_query, preferred_element_type=f32).astype(bf16)
    following = shifted(queries[: SPAN - 1], "dp", -1)
    grouped = jnp.concatenate([queries[SPAN - 1 :], following], axis=0).reshape(
        span_dev, SPAN, inner_width
    )
    live_span = jnp.arange(span_dev, dtype=jnp.int32) < valid_spans[0]
    owners = (neighbours // stored).reshape(-1)
    slot_ids = (neighbours % stored).reshape(-1)
    is_live = jnp.repeat(live_span, 2)
    req_order = jnp.arange(owners.shape[0], dtype=jnp.int32)
    earlier = (
        (owners[:, None] == owners[None, :])
        & is_live[None, :]
        & (req_order[None, :] < req_order[:, None])
    )
    slot_rank = jnp.minimum(jnp.sum(earlier.astype(jnp.int32), axis=1), SLOTS - 1)
    target = jnp.where(is_live, owners * SLOTS + slot_rank, -1)
    slot_match = target[:, None] == jnp.arange(peer_count * SLOTS, dtype=jnp.int32)[None, :]
    request_table = jnp.sum(jnp.where(slot_match, slot_ids[:, None], 0), axis=0)
    request_table = request_table.reshape(peer_count, SLOTS)
    source_span = jnp.sum(jnp.where(slot_match, req_order[:, None] // 2, 0), axis=0)
    sent_rows = grouped[source_span].reshape(peer_count, SLOTS * SPAN, inner_width)
    wanted = lax.all_to_all(request_table, "dp", split_axis=0, concat_axis=0, tiled=True)
    asked = lax.all_to_all(sent_rows, "dp", split_axis=0, concat_axis=0, tiled=True)
    answers = attend(wanted.reshape(-1), asked, nb_keys, nb_values)
    back = lax.all_to_all(answers, "dp", split_axis=0, concat_axis=0, tiled=True)
    merged = combine(owners, slot_rank, valid_spans, back)
    flat_rows = merged.reshape(tok_rows, inner_width)
    previous = shifted(flat_rows[tok_rows - SPAN + 1 :], "dp", 1)
    placed = jnp.concatenate([previous, flat_rows[: tok_rows - SPAN + 1]], axis=0)
    head_terms = jnp.dot(placed, w_out, preferred_element_type=f32).astype(bf16)
    summed = lax.psum_scatter(head_terms, "mp", scatter_dimension=1, tiled=True)
    return hidden.astype(f32) + summed.astype(f32)


def solution(mesh):
    placed = (
        P("dp", "mp"),
        P(),
        P(None, "mp"),
        P("mp", None),
        P("dp", None, "mp"),
        P("dp", None, "mp"),
        P("dp", None),
        P("dp"),
    )
    return jax.shard_map(
        shards, mesh=mesh, in_specs=placed, out_specs=P("dp", "mp"), check_vma=False
    )
```

time: 371 us -> 352 us (0.949)
  Pallas kernels: 0 us -> 72.4 us
  blocking collectives: 0 us -> 60.1 us
  waiting for transfers between devices: 208 us -> 156 us
  local copies, waits for them, and re-layouts: 51.2 us -> 7.35 us
  starting transfers between devices: 45.6 us -> 21.9 us
  matrix products: 31.5 us -> 11 us
  other arithmetic: 18.7 us -> 7.66 us
    pallas_call x0 -> x2, Pallas kernels: none -> 72.4 us  [the longest x1 65.1 us: attend(): pl.pallas_call(attend_kernel, out_shape=jax.ShapeDtypeStruct((peer_count,...]
    all_to_all x0 -> x1, blocking collectives: none -> 60.1 us  [shards(): lax.all_to_all(answers, 'dp', split_axis=0, concat_axis=0, tiled=True)]
    all_to_all x3 -> x0, waiting for transfers between devices: 43.5 us -> none  [the longest x1 43.5 us: shards(): lax.all_to_all(result[0].astype(jnp.float32), 'dp', split_axis=0, concat_...]
    reduce_scatter x1, waiting for transfers between devices: 96.2 us -> 55.6 us  [shards(): summed = lax.psum_scatter(head_terms, 'mp', scatter_dimension=1, tiled=True)]
    all_to_all x1, waiting for transfers between devices: 12.7 us -> 46.8 us  [shards(): lax.all_to_all(sent_rows, 'dp', split_axis=0, concat_axis=0, tiled=True)]
    reshape x3 -> x1, local copies, waits for them, and re-layouts: 25.3 us -> 0.62 us  [shards(): answers = attend(wanted.reshape(-1), asked, nb_keys, nb_values)]
    all_to_all x3 -> x0, starting transfers between devices: 24 us -> none  [the longest x1 9.21 us: shards(): lax.all_to_all(result[1], 'dp', split_axis=0, concat_axis=0, tiled=True)]
    dot_general x4 -> x2, matrix products: 31.5 us -> 11 us  [the longest x1 6.47 us: shards(): head_terms = jnp.dot(placed, w_out, preferred_element_type=f32).astype(bf16)]
  transfers between devices with their start and end apart: 9 -> 6, of which waited for: 6 -> 5; matrix products, arithmetic and copies ran while one was open for 20% -> 4% of each run, Pallas kernels for 0% -> 0%
where the time goes in v1:
time: 352 us; the launch traced here: 350 us
  waiting for transfers between devices  156 us (44%)
  Pallas kernels  72.4 us (21%)
  blocking collectives  60.1 us (17%)
  starting transfers between devices  21.9 us (6%)
  between operations  14.2 us (4%)
  matrix products  11 us (3%)
  other arithmetic  7.66 us (2%)
  local copies, waits for them, and re-layouts  7.35 us (2%)
    pallas_call x1, Pallas kernels, attend(): pl.pallas_call(attend_kernel, out_shape=jax.ShapeDtypeStruct((peer_count,...  65.1 us
    all_to_all x1, blocking collectives, shards(): lax.all_to_all(answers, 'dp', split_axis=0, concat_axis=0, tiled=True)  60.1 us
    reduce_scatter x1, waiting for transfers between devices, shards(): summed = lax.psum_scatter(head_terms, 'mp', scatter_dimension=1, tiled=True)  55.6 us
    all_gather x1, waiting for transfers between devices, shards(): widened = lax.all_gather(hidden, 'mp', axis=1, tiled=True).astype(f32)  48.6 us
    all_to_all x1, waiting for transfers between devices, shards(): lax.all_to_all(sent_rows, 'dp', split_axis=0, concat_axis=0, tiled=True)  46.8 us
    all_to_all x1, starting transfers between devices, shards(): lax.all_to_all(sent_rows, 'dp', split_axis=0, concat_axis=0, tiled=True)  10.3 us
    pallas_call x1, Pallas kernels, combine(): pl.pallas_call(combine_kernel, out_shape=jax.ShapeDtypeStruct((spans, SPA...  7.34 us
    all_to_all x1, starting transfers between devices, shards(): lax.all_to_all(request_table, 'dp', split_axis=0, concat_axis=0, tiled=True)  7.32 us
  transfers between devices with their start and end apart: 6, of which 5 were waited for; matrix products, arithmetic and copies ran while one was open for 4% of the time, Pallas kernels for 0%

profile of v1, /device:TPU:28, one launch (start us, length us, event | category | flops | bytes accessed | tf_op | source)
XLA Modules:
  0.0 350.3 jit_solution(14998169237825321102)
XLA Ops:
  6.5 0.0 copy-start.3
  6.5 0.0 all-gather.2.cloned.1.call-start
  6.5 0.7 all-gather.2.cloned.1.call-update
  7.9 0.1 broadcast_in_dim.35
  8.0 0.1 and.39
  8.1 0.7 and_select_fusion.1
  8.8 0.1 copy.17
  8.9 0.1 broadcast_in_dim.37
  8.9 0.1 copy.16
  9.0 0.1 reshape.98.owner_ref
  9.1 0.0 copy-start.2
  9.1 0.2 convert_reduce_fusion
  9.3 0.5 add_select_fusion
  9.8 0.1 select_reduce_fusion
  9.9 0.7 all_to_all.12
  10.6 7.3 %all-to-all-start = ((s32[32,1,2]{2,1,0:T(1,128)}), s32[32,1,2]{2,1,0:T(1,128)S(1)}, u32[]{:S(2)}, u32[]{:S(2)}) async-start(s32[32,1,2]{2,1,0:T(1,128)} %bitcast.1), calls=%async_computation | async-start | bytes 32768 | tf_op jit(solution)/shard_map/all_to_all | solution.py:166
  18.0 48.6 %all-gather.2.cloned.1.call-done = bf16[512,4096]{1,0:T(8,128)(2,1)} async-done(((bf16[512,512]{1,0:T(8,128)(2,1)}), bf16[512,4096]{1,0:T(8,128)(2,1)}) %all-gather.2.cloned.1.call-update) | async-done | bytes 4194320 | tf_op jit(solution)/shard_map/all_gather | solution.py:140
  66.6 0.0 copy-start
  66.6 3.2 fusion
  69.8 0.0 copy-done.3
  69.8 0.2 copy-done
  70.0 4.6 %fusion.7 = bf16[512,512]{1,0:T(8,128)(2,1)S(1)} fusion(bf16[4096,512]{1,0:T(8,128)(2,1)} %param.10, bf16[512,4096]{1,0:T(8,128)(2,1)S(1)} %copy-done, f32[4096]{0:T(1024)S(1)} %copy-done.3, f32[512]{0:T(512)S(1)} %add_rsqrt_fusion), kind=kOutput, calls=%fused_computation.10 | convolution fusion | flops 2156134400 | bytes 8931328 | tf_op jit(solution)/shard_map/dot_general | solution.py:144
  74.6 0.0 copy-done.2
  74.6 1.9 collective-permute-start
  76.6 0.1 slice.18
  76.7 1.8 collective-permute-done
  78.5 2.8 gather_fusion
  81.2 0.0 all-to-all-done
  81.2 10.3 %all-to-all-start.1 = ((bf16[32,128,512]{2,1,0:T(8,128)(2,1)}), bf16[32,128,512]{2,1,0:T(8,128)(2,1)}, u32[]{:S(2)}, u32[]{:S(2)}) async-start(bf16[32,128,512]{2,1,0:T(8,128)(2,1)} %bitcast.13), calls=%async_computation.1 | async-start | bytes 8388608 | tf_op jit(solution)/shard_map/all_to_all | solution.py:167
  91.6 0.0 reduce-scatter.2.cloned.1.call-start
  91.6 0.5 broadcast.139
  92.2 0.7 reduce.3
  92.8 0.6 reshape.99.ids_ref
  93.5 46.8 %all-to-all-done.1.q_ref = bf16[32,128,512]{2,1,0:T(8,128)(2,1)} async-done(((bf16[32,128,512]{2,1,0:T(8,128)(2,1)}), bf16[32,128,512]{2,1,0:T(8,128)(2,1)}, u32[]{:S(2)}, u32[]{:S(2)}) %all-to-all-start.1) | async-done | bytes 4194336 | tf_op jit(solution)/shard_map/all_to_all | solution.py:167
  140.3 65.1 %attend.1 = bf16[32,136,512]{2,1,0:T(8,128)(2,1)} custom-call(s32[64]{0:T(128)} %reshape.99.ids_ref, bf16[32,128,512]{2,1,0:T(8,128)(2,1)} %all-to-all-done.1.q_ref, bf16[8,128,512]{2,1,0:T(8,128)(2,1)} %k_ref.1, bf16[8,128,512]{2,1,0:T(8,128)(2,1)} %v_ref.1), custom_call_target="tpu_custom_call" | custom-call | tf_op jit(solution)/shard_map/attend/pallas_call | solution.py:70
  205.3 60.1 %all_to_all.19.first_ref.second_ref = bf16[32,136,512]{2,1,0:T(8,128)(2,1)} all-to-all(bf16[32,136,512]{2,1,0:T(8,128)(2,1)} %attend.1), channel_id=1, replica_groups=mesh['dp'=32,'mp'=8] {'dp'}, dimensions={0} | all-to-all | bytes 8912896 | tf_op jit(solution)/shard_map/all_to_all | solution.py:169
  265.4 7.3 %combine.1 = bf16[8,64,512]{2,1,0:T(8,128)(2,1)} custom-call(s32[16]{0:T(128)} %copy-done.2, s32[16]{0:T(128)} %get-tuple-element.10.rank_ref, s32[1]{0:T(128)} %copy.19.live_ref, bf16[32,136,512]{2,1,0:T(8,128)(2,1)} %all_to_all.19.first_ref.second_ref, bf16[32,136,512]{2,1,0:T(8,128)(2,1)} %all_to_all.19.first_ref.second_ref), custom_call_target="tpu_custom_call" | custom-call | tf_op jit(solution)/shard_map/combine/pallas_call | solution.py:116
  272.8 0.9 slice.20
  273.6 2.2 collective-permute-start.1
  275.9 1.1 slice.21
  276.9 2.3 collective-permute-done.1
  279.2 6.5 %convolution_convert_fusion = bf16[512,4096]{1,0:T(8,128)(2,1)} fusion(bf16[512,4096]{1,0:T(8,128)(2,1)} %param.11, bf16[449,512]{1,0:T(8,128)(2,1)S(1)} %slice.21, bf16[63,512]{1,0:T(8,128)(2,1)S(1)} %collective-permute-done.1), kind=kOutput, calls=%fused_computation.6 | convolution fusion | flops 2150629376 | bytes 8912896 | tf_op jit(solution)/shard_map/dot_general | solution.py:174
  285.7 0.0 copy-start.1
  285.7 0.0 reduce-scatter.2.cloned.1.call-update
  285.7 55.6 %reduce-scatter.2.cloned.1.call-done = bf16[512,512]{1,0:T(8,128)(2,1)} async-done(((bf16[512,4096]{1,0:T(8,128)(2,1)}), bf16[512,512]{1,0:T(8,128)(2,1)}) %reduce-scatter.2.cloned.1.call-update) | async-done | bytes 524304 | tf_op jit(solution)/shard_map/reduce_scatter | solution.py:175
  341.3 0.0 copy-done.1
  341.3 2.2 convert_add_fusion
  (6 shorter events, 0.1 us)
Async XLA Ops:
  6.5 63.3 %copy-start.3 = (f32[4096]{0:T(1024)S(1)}, f32[4096]{0:T(1024)}, u32[]{:S(2)}) copy-start(f32[4096]{0:T(1024)} %param.9) | copy-start | bytes 49156
  6.5 60.0 %all-gather.2.cloned.1.call-start = ((), (), s32[]{:S(2)}) async-start(), calls=%async_computation.4 | async-start | bytes 4718592 | tf_op jit(solution)/shard_map/all_gather | solution.py:140
  9.1 65.5 %copy-start.2 = (s32[16]{0:T(128)}, s32[16]{0:T(128)S(1)}, u32[]{:S(2)}) copy-start(s32[16]{0:T(128)S(1)} %reshape.98.owner_ref) | copy-start | bytes 196
  10.6 70.6 %all-to-all-start = ((s32[32,1,2]{2,1,0:T(1,128)}), s32[32,1,2]{2,1,0:T(1,128)S(1)}, u32[]{:S(2)}, u32[]{:S(2)}) async-start(s32[32,1,2]{2,1,0:T(1,128)} %bitcast.1), calls=%async_computation | async-start | bytes 32768 | tf_op jit(solution)/shard_map/all_to_all | solution.py:166
  66.6 3.4 copy-start
  74.6 3.8 %collective-permute-start = (bf16[63,512]{1,0:T(8,128)(2,1)S(1)}, bf16[63,512]{1,0:T(8,128)(2,1)S(1)}, u32[]{:S(2)}, u32[]{:S(2)}) collective-permute-start(bf16[63,512]{1,0:T(8,128)(2,1)S(1)} %slice.19), channel_id=1, source_target_pairs={{8,0},{16,8},{24,16},{32,24},{40,32},{48,40},{56,48},{64,56},{72,6... | collective-permute-start | bytes 193544 | tf_op jit(solution)/shard_map/ppermute | solution.py:23
  81.2 59.0 %all-to-all-start.1 = ((bf16[32,128,512]{2,1,0:T(8,128)(2,1)}), bf16[32,128,512]{2,1,0:T(8,128)(2,1)}, u32[]{:S(2)}, u32[]{:S(2)}) async-start(bf16[32,128,512]{2,1,0:T(8,128)(2,1)} %bitcast.13), calls=%async_computation.1 | async-start | bytes 8388608 | tf_op jit(solution)/shard_map/all_to_all | solution.py:167
  91.6 249.7 %reduce-scatter.2.cloned.1.call-start = ((), (), s32[]{:S(2)}) async-start(), calls=%async_computation.5 | async-start | bytes 4718592 | tf_op jit(solution)/shard_map/reduce_scatter | solution.py:175
  273.6 5.6 %collective-permute-start.1 = (bf16[63,512]{1,0:T(8,128)(2,1)S(1)}, bf16[63,512]{1,0:T(8,128)(2,1)S(1)}, u32[]{:S(2)}, u32[]{:S(2)}) collective-permute-start(bf16[63,512]{1,0:T(8,128)(2,1)S(1)} %slice.20), channel_id=1, source_target_pairs={{0,8},{8,16},{16,24},{24,32},{32,40},{40,48},{48,56},{56,64},{64,7... | collective-permute-start | bytes 193544 | tf_op jit(solution)/shard_map/ppermute | solution.py:23
  285.7 55.6 %copy-start.1 = (bf16[512,512]{1,0:T(8,128)(2,1)S(1)}, bf16[512,512]{1,0:T(8,128)(2,1)}, u32[]{:S(2)}) copy-start(bf16[512,512]{1,0:T(8,128)(2,1)} %param.8) | copy-start | bytes 1572868
Sparse Core Ops, SparseCore 0:
  9.1 57.3 all-gather.1
  285.8 55.4 reduce-scatter.1

commit v2 on v1

v2 whole, which is shorter than its diff:
```python
import math

import jax
import jax.numpy as jnp
from jax import lax
from jax.experimental import pallas as pl
from jax.experimental.pallas import tpu as pltpu
from jax.sharding import PartitionSpec as P

HS = 128
SPAN = 64
SLOTS = 2
STATS = 8
PARTS = 1
LANES = 128

eps = 1e-05
f32 = jnp.float32
bf16 = jnp.bfloat16


def shifted(block, axis, distance):
    devices = range(lax.axis_size(axis))
    route = [(i - distance, i) for i in devices if i - distance in devices]
    return lax.ppermute(block, axis, route)


def attend_kernel(ids_ref, q_ref, k_ref, v_ref, out_ref):
    peers, rows, width = q_ref.shape
    count = rows // SLOTS
    together = LANES // count
    groups = width // HS // together
    step = pl.program_id(0)
    factor = 1.0 / math.sqrt(HS)
    zero = jnp.zeros((count, HS), bf16)
    row = lax.broadcasted_iota(jnp.int32, (STATS, LANES), 0)
    for p in range(peers):
        for j in range(SLOTS):
            block = ids_ref[(step * peers + p) * SLOTS + j]
            tokens = pl.ds(j * count, count)
            for g in range(groups):
                first = g * together
                cols = pl.ds(first * HS, together * HS)
                spread = []
                for h in range(together):
                    line = [zero] * together
                    line[h] = q_ref[p, tokens, pl.ds((first + h) * HS, HS)]
                    spread.append(jnp.concatenate(line, axis=1))
                scores = lax.dot_general(
                    k_ref[block, :, cols], jnp.concatenate(spread, axis=0),
                    (((1,), (1,)), ((), ())), preferred_element_type=f32,
                ) * factor
                top = jnp.max(scores, axis=0, keepdims=True)
                weights = jnp.exp(scores - top)
                total = jnp.sum(weights, axis=0, keepdims=True)
                summed = lax.dot_general(
                    weights.astype(bf16), v_ref[block, :, cols],
                    (((0,), (0,)), ((), ())), preferred_element_type=f32,
                )
                scale = jnp.transpose(jnp.broadcast_to(1.0 / total, (LANES, LANES)))
                for h in range(together):
                    own = slice(h * count, (h + 1) * count)
                    piece = summed[own, h * HS:(h + 1) * HS] * scale[own]
                    out_ref[p, tokens, pl.ds((first + h) * HS, HS)] = piece.astype(bf16)
                lse = top + jnp.log(total)
                high = lse.astype(bf16).astype(f32)
                middle = (lse - high).astype(bf16).astype(f32)
                low = (lse - high - middle).astype(bf16).astype(f32)
                stat = jnp.where(
                    row == 0, high, jnp.where(row == 1, middle, jnp.where(row == 2, low, 0.0))
                )
                place = pl.ds((g * SLOTS + j) * LANES, LANES)
                out_ref[p, pl.ds(rows, STATS), place] = stat.astype(bf16)
        used = groups * SLOTS * LANES
        if used < width:
            rest = jnp.zeros((STATS, width - used), bf16)
            out_ref[p, pl.ds(rows, STATS), pl.ds(used, width - used)] = rest


def attend(ids, asked, keys, values):
    peer_count, rows, width = asked.shape
    step = 8
    stored, tokens, _ = keys.shape
    slots = peer_count * SLOTS
    return pl.pallas_call(
        attend_kernel,
        out_shape=jax.ShapeDtypeStruct((peer_count, rows + STATS, width), bf16),
        grid_spec=pltpu.PrefetchScalarGridSpec(
            num_scalar_prefetch=1,
            grid=(peer_count // step,),
            in_specs=[
                pl.BlockSpec((step, rows, width), lambda i, ids: (i, 0, 0)),
                pl.BlockSpec((stored, tokens, width), lambda i, ids: (0, 0, 0)),
                pl.BlockSpec((stored, tokens, width), lambda i, ids: (0, 0, 0)),
            ],
            out_specs=pl.BlockSpec((step, rows + STATS, width), lambda i, ids: (i, 0, 0)),
        ),
        compiler_params=pltpu.CompilerParams(dimension_semantics=("arbitrary",)),
        cost_estimate=pl.CostEstimate(
            flops=slots * 4 * LANES * LANES * width,
            bytes_accessed=4 * peer_count * rows * width,
            transcendentals=slots * LANES * LANES,
        ),
        name="attend",
    )(ids, asked, keys, values)


def combine_kernel(owner_ref, rank_ref, live_ref, back_ref, out_ref, part_ref, stat_ref, sems):
    spans, count, width = out_ref.shape
    together = LANES // count
    groups = width // HS // together
    rows = SLOTS * count
    copies = []
    for i in range(2 * spans):
        offset = pl.multiple_of(rank_ref[i] * count, count)
        source = back_ref.at[owner_ref[i]]
        copies.append((
            pltpu.make_async_copy(source.at[pl.ds(offset, count)], part_ref.at[i], sems.at[i, 0]),
            pltpu.make_async_copy(source.at[pl.ds(rows, STATS)], stat_ref.at[i], sems.at[i, 1]),
        ))
    for pair in copies:
        for copy in pair:
            copy.start()
    for s in range(spans):
        for n in range(2):
            for copy in copies[2 * s + n]:
                copy.wait()
        alive = s < live_ref[0]
        for g in range(groups):
            lses = []
            for n in range(2):
                start = pl.multiple_of((g * SLOTS + rank_ref[2 * s + n]) * LANES, LANES)
                stat = stat_ref[2 * s + n, :, pl.ds(start, LANES)].astype(f32)
                lses.append(stat[0:1] + stat[1:2] + stat[2:3])
            gap = lses[0] - lses[1]
            mine = jnp.transpose(jnp.broadcast_to(1.0 / (1.0 + jnp.exp(-gap)), (LANES, LANES)))
            other = jnp.transpose(jnp.broadcast_to(1.0 / (1.0 + jnp.exp(gap)), (LANES, LANES)))
            for h in range(together):
                own = slice(h * count, (h + 1) * count)
                cols = pl.ds((g * together + h) * HS, HS)
                merged = (
                    part_ref[2 * s, :, cols].astype(f32) * mine[own]
                    + part_ref[2 * s + 1, :, cols].astype(f32) * other[own]
                )
                out_ref[s, :, cols] = jnp.where(alive, merged, 0.0).astype(bf16)


def combine(owners, ranks, live, back):
    spans = owners.shape[0] // 2
    _, rows, width = back.shape
    count = (rows - STATS) // SLOTS
    smem = pl.BlockSpec(memory_space=pltpu.SMEM)
    return pl.pallas_call(
        combine_kernel,
        out_shape=jax.ShapeDtypeStruct((spans, count, width), bf16),
        in_specs=[smem, smem, smem, pl.BlockSpec(memory_space=pl.ANY)],
        out_specs=pl.BlockSpec(memory_space=pltpu.VMEM),
        scratch_shapes=[
            pltpu.VMEM((2 * spans, count, width), bf16),
            pltpu.VMEM((2 * spans, STATS, width), bf16),
            pltpu.SemaphoreType.DMA((2 * spans, 2)),
        ],
        cost_estimate=pl.CostEstimate(
            flops=8 * spans * count * width,
            bytes_accessed=6 * spans * count * width,
            transcendentals=0,
        ),
        name="combine",
    )(owners, ranks, live, back)


def shards(hidden, norm_gain, w_query, w_out, nb_keys, nb_values, neighbours, valid_spans):
    tok_rows, width = hidden.shape
    span_dev = tok_rows // SPAN
    stored = nb_keys.shape[0]
    inner_width = w_query.shape[1]
    peer_count = lax.axis_size("dp")
    count = SPAN // PARTS
    pieces = [
        hidden.reshape(span_dev, SPAN, width)[:, i * count:(i + 1) * count].reshape(-1, width)
        for i in range(PARTS)
    ]

    live_span = jnp.arange(span_dev, dtype=jnp.int32) < valid_spans[0]
    owners = (neighbours // stored).reshape(-1)
    slot_ids = (neighbours % stored).reshape(-1)
    is_live = jnp.repeat(live_span, 2)
    req_order = jnp.arange(owners.shape[0], dtype=jnp.int32)
    earlier = (
        (owners[:, None] == owners[None, :])
        & is_live[None, :]
        & (req_order[None, :] < req_order[:, None])
    )
    slot_rank = jnp.minimum(jnp.sum(earlier.astype(jnp.int32), axis=1), SLOTS - 1)
    target = jnp.where(is_live, owners * SLOTS + slot_rank, -1)
    slot_match = target[:, None] == jnp.arange(peer_count * SLOTS, dtype=jnp.int32)[None, :]
    request_table = jnp.sum(jnp.where(slot_match, slot_ids[:, None], 0), axis=0)
    request_table = request_table.reshape(peer_count, SLOTS)
    source_span = jnp.sum(jnp.where(slot_match, req_order[:, None] // 2, 0), axis=0)
    wanted = lax.all_to_all(request_table, "dp", split_axis=0, concat_axis=0, tiled=True)
    wanted = wanted.reshape(-1)

    def is_last(i):
        position = i * count + lax.broadcasted_iota(jnp.int32, (1, count, 1), 1)
        return position == SPAN - 1

    def ask(i):
        widened = lax.all_gather(pieces[i], "mp", axis=1, tiled=True).astype(f32)
        normed = (
            widened * lax.rsqrt(jnp.mean(widened * widened, axis=1, keepdims=True) + eps) * norm_gain
        ).astype(bf16)
        queries = jnp.dot(normed, w_query, preferred_element_type=f32).astype(bf16)
        blocks = queries.reshape(span_dev, count, inner_width)
        following = shifted(blocks[:1], "dp", -1)
        grouped = jnp.concatenate([blocks[1:], following], axis=0)
        if (i + 1) * count == SPAN:
            grouped = jnp.where(is_last(i), blocks, grouped)
        sent_rows = grouped[source_span].reshape(peer_count, SLOTS * count, inner_width)
        return lax.all_to_all(sent_rows, "dp", split_axis=0, concat_axis=0, tiled=True)

    def answer(asked):
        answers = attend(wanted, asked, nb_keys, nb_values)
        return lax.all_to_all(answers, "dp", split_axis=0, concat_axis=0, tiled=True)

    def finish(i, back):
        merged = combine(owners, slot_rank, valid_spans, back)
        previous = shifted(merged[span_dev - 1 :], "dp", 1)
        placed = jnp.concatenate([previous, merged[: span_dev - 1]], axis=0)
        if (i + 1) * count == SPAN:
            placed = jnp.where(is_last(i), merged, placed)
        placed = placed.reshape(-1, inner_width)
        head_terms = jnp.dot(placed, w_out, preferred_element_type=f32).astype(bf16)
        summed = lax.psum_scatter(head_terms, "mp", scatter_dimension=1, tiled=True)
        return summed.astype(f32).reshape(span_dev, count, width)

    asked = [ask(i) for i in range(PARTS)]
    back = [answer(one) for one in asked]
    summed = [finish(i, one) for i, one in enumerate(back)]
    summed = jnp.concatenate(summed, axis=1).reshape(tok_rows, width)
    return hidden.astype(f32) + summed


def solution(mesh):
    placed = (
        P("dp", "mp"),
        P(),
        P(None, "mp"),
        P("mp", None),
        P("dp", None, "mp"),
        P("dp", None, "mp"),
        P("dp", None),
        P("dp"),
    )
    return jax.shard_map(
        shards, mesh=mesh, in_specs=placed, out_specs=P("dp", "mp"), check_vma=False
    )
```

time: 352 us -> 295 us (0.84)
  Pallas kernels: 72.4 us -> 14.5 us
    pallas_call x1, Pallas kernels: 65.1 us -> 10.5 us  [attend(): pl.pallas_call(attend_kernel, out_shape=jax.ShapeDtypeStruct((peer_count,...]
  transfers between devices with their start and end apart: 6 -> 6, of which waited for: 5 -> 5; matrix products, arithmetic and copies ran while one was open for 4% -> 5% of each run, Pallas kernels for 0% -> 0%
where the time goes in v2:
time: 295 us; the launch traced here: 293 us
  waiting for transfers between devices  156 us (53%)
  blocking collectives  60.1 us (20%)
  starting transfers between devices  21.7 us (7%)
  Pallas kernels  14.5 us (5%)
  between operations  14.2 us (5%)
  matrix products  11 us (4%)
  other arithmetic  8.92 us (3%)
  local copies, waits for them, and re-layouts  7.26 us (2%)
    all_to_all x1, blocking collectives, answer(): lax.all_to_all(answers, 'dp', split_axis=0, concat_axis=0, tiled=True)  60.1 us
    reduce_scatter x1, waiting for transfers between devices, finish(): summed = lax.psum_scatter(head_terms, 'mp', scatter_dimension=1, tiled=True)  55.4 us
    all_gather x1, waiting for transfers between devices, ask(): widened = lax.all_gather(pieces[i], 'mp', axis=1, tiled=True).astype(f32)  48.6 us
    all_to_all x1, waiting for transfers between devices, ask(): lax.all_to_all(sent_rows, 'dp', split_axis=0, concat_axis=0, tiled=True)  46.8 us
    pallas_call x1, Pallas kernels, attend(): pl.pallas_call(attend_kernel, out_shape=jax.ShapeDtypeStruct((peer_count,...  10.5 us
    all_to_all x1, starting transfers between devices, ask(): lax.all_to_all(sent_rows, 'dp', split_axis=0, concat_axis=0, tiled=True)  10.3 us
    all_to_all x1, starting transfers between devices, shards(): lax.all_to_all(request_table, 'dp', split_axis=0, concat_axis=0, tiled=True)  7.32 us
    dot_general x1, matrix products, finish(): head_terms = jnp.dot(placed, w_out, preferred_element_type=f32).astype(bf16)  6.47 us
  transfers between devices with their start and end apart: 6, of which 5 were waited for; matrix products, arithmetic and copies ran while one was open for 5% of the time, Pallas kernels for 0%

profile of v2, /device:TPU:28, one launch (start us, length us, event | category | flops | bytes accessed | tf_op | source)
XLA Modules:
  0.0 293.4 jit_solution(4964199761037544435)
XLA Ops:
  6.5 0.0 copy-start.3
  6.5 0.0 all-gather.2.cloned.1.call-start
  6.5 0.7 all-gather.2.cloned.1.call-update
  7.9 0.1 broadcast_in_dim.49
  8.0 0.1 and.39
  8.1 0.7 and_select_fusion.1
  8.8 0.1 copy.17
  8.9 0.1 broadcast_in_dim.51
  8.9 0.1 copy.16
  9.0 0.1 reshape.105.owner_ref
  9.1 0.0 copy-start.2
  9.1 0.2 convert_reduce_fusion
  9.3 0.5 add_select_fusion
  9.8 0.1 select_reduce_fusion
  9.9 0.7 all_to_all.12
  10.6 7.3 %all-to-all-start = ((s32[32,1,2]{2,1,0:T(1,128)}), s32[32,1,2]{2,1,0:T(1,128)S(1)}, u32[]{:S(2)}, u32[]{:S(2)}) async-start(s32[32,1,2]{2,1,0:T(1,128)} %bitcast.1), calls=%async_computation | async-start | bytes 32768 | tf_op jit(solution)/shard_map/all_to_all | solution.py:200
  18.0 48.6 %all-gather.2.cloned.1.call-done = bf16[512,4096]{1,0:T(8,128)(2,1)} async-done(((bf16[512,512]{1,0:T(8,128)(2,1)}), bf16[512,4096]{1,0:T(8,128)(2,1)}) %all-gather.2.cloned.1.call-update) | async-done | bytes 4194320 | tf_op jit(solution)/shard_map/all_gather | solution.py:208
  66.6 0.0 copy-start
  66.6 3.2 %fusion = f32[512]{0:T(512)S(1)} fusion(bf16[512,4096]{1,0:T(8,128)(2,1)} %all-gather.2.cloned.1.call-done), kind=kLoop, calls=%fused_computation.3 | loop fusion | flops 6290944 | bytes 4196352 | tf_op jit(solution)/shard_map/reduce_sum | solution.py:210
  69.8 0.0 copy-done.3
  69.8 0.2 copy-done
  70.0 4.6 %fusion.7 = bf16[512,512]{1,0:T(8,128)(2,1)S(1)} fusion(bf16[4096,512]{1,0:T(8,128)(2,1)} %param.10, bf16[512,4096]{1,0:T(8,128)(2,1)S(1)} %copy-done, f32[4096]{0:T(1024)S(1)} %copy-done.3, f32[512]{0:T(512)S(1)} %add_rsqrt_fusion), kind=kOutput, calls=%fused_computation.10 | convolution fusion | flops 2156134400 | bytes 8931328 | tf_op jit(solution)/shard_map/dot_general | solution.py:212
  74.6 0.0 copy-done.2
  74.6 1.9 collective-permute-start
  76.6 1.8 collective-permute-done
  78.4 0.1 maximum_select_fusion
  78.6 2.8 gather_fusion
  81.3 0.0 all-to-all-done
  81.3 10.3 %all-to-all-start.1 = ((bf16[32,128,512]{2,1,0:T(8,128)(2,1)}), bf16[32,128,512]{2,1,0:T(8,128)(2,1)}, u32[]{:S(2)}, u32[]{:S(2)}) async-start(bf16[32,128,512]{2,1,0:T(8,128)(2,1)} %bitcast.16), calls=%async_computation.1 | async-start | bytes 8388608 | tf_op jit(solution)/shard_map/all_to_all | solution.py:219
  91.7 0.0 reduce-scatter.2.cloned.1.call-start
  91.7 0.5 broadcast.149
  92.2 0.7 reduce.3
  92.9 0.6 reshape.106.ids_ref
  93.6 46.8 %all-to-all-done.1.q_ref = bf16[32,128,512]{2,1,0:T(8,128)(2,1)} async-done(((bf16[32,128,512]{2,1,0:T(8,128)(2,1)}), bf16[32,128,512]{2,1,0:T(8,128)(2,1)}, u32[]{:S(2)}, u32[]{:S(2)}) %all-to-all-start.1) | async-done | bytes 4194336 | tf_op jit(solution)/shard_map/all_to_all | solution.py:219
  140.4 10.5 %attend.1 = bf16[32,136,512]{2,1,0:T(8,128)(2,1)} custom-call(s32[64]{0:T(128)} %reshape.106.ids_ref, bf16[32,128,512]{2,1,0:T(8,128)(2,1)} %all-to-all-done.1.q_ref, bf16[8,128,512]{2,1,0:T(8,128)(2,1)} %k_ref.1, bf16[8,128,512]{2,1,0:T(8,128)(2,1)} %v_ref.1), custom_call_target="tpu_custom_call" | custom-call | flops 2147483648 | bytes 8388608 | tf_op jit(solution)/shard_map/attend/pallas_call | solution.py:85
  150.9 60.1 %all_to_all.19.back_ref = bf16[32,136,512]{2,1,0:T(8,128)(2,1)} all-to-all(bf16[32,136,512]{2,1,0:T(8,128)(2,1)} %attend.1), channel_id=1, replica_groups=mesh['dp'=32,'mp'=8] {'dp'}, dimensions={0} | all-to-all | bytes 8912896 | tf_op jit(solution)/shard_map/all_to_all | solution.py:223
  210.9 4.0 %combine.1 = bf16[8,64,512]{2,1,0:T(8,128)(2,1)} custom-call(s32[16]{0:T(128)} %copy-done.2, s32[16]{0:T(128)} %get-tuple-element.10.rank_ref, s32[1]{0:T(128)} %copy.19.live_ref, bf16[32,136,512]{2,1,0:T(8,128)(2,1)} %all_to_all.19.back_ref), custom_call_target="tpu_custom_call" | custom-call | flops 2097152 | bytes 1572864 | tf_op jit(solution)/shard_map/combine/pallas_call | solution.py:153
  214.9 0.8 slice.28
  215.8 2.1 collective-permute-start.1
  217.9 1.1 slice.29
  218.9 2.4 collective-permute-done.1
  221.4 1.2 maximum_select_fusion.1
  222.5 6.5 %convolution_convert_fusion = bf16[512,4096]{1,0:T(8,128)(2,1)} fusion(bf16[512,512]{1,0:T(8,128)(2,1)S(1)} %bitcast.19, bf16[512,4096]{1,0:T(8,128)(2,1)} %param.11), kind=kOutput, calls=%fused_computation.6 | convolution fusion | flops 2149580800 | bytes 8912896 | tf_op jit(solution)/shard_map/dot_general | solution.py:232
  229.0 0.0 copy-start.1
  229.0 0.0 reduce-scatter.2.cloned.1.call-update
  229.0 55.4 %reduce-scatter.2.cloned.1.call-done = bf16[512,512]{1,0:T(8,128)(2,1)} async-done(((bf16[512,4096]{1,0:T(8,128)(2,1)}), bf16[512,512]{1,0:T(8,128)(2,1)}) %reduce-scatter.2.cloned.1.call-update) | async-done | bytes 524304 | tf_op jit(solution)/shard_map/reduce_scatter | solution.py:233
  284.4 0.0 copy-done.1
  284.4 2.2 convert_add_fusion
  (7 shorter events, 0.1 us)
Async XLA Ops:
  6.5 63.3 %copy-start.3 = (f32[4096]{0:T(1024)S(1)}, f32[4096]{0:T(1024)}, u32[]{:S(2)}) copy-start(f32[4096]{0:T(1024)} %param.9) | copy-start | bytes 49156
  6.5 60.0 %all-gather.2.cloned.1.call-start = ((), (), s32[]{:S(2)}) async-start(), calls=%async_computation.4 | async-start | bytes 4718592 | tf_op jit(solution)/shard_map/all_gather | solution.py:208
  9.1 65.5 %copy-start.2 = (s32[16]{0:T(128)}, s32[16]{0:T(128)S(1)}, u32[]{:S(2)}) copy-start(s32[16]{0:T(128)S(1)} %reshape.105.owner_ref) | copy-start | bytes 196
  10.6 70.7 %all-to-all-start = ((s32[32,1,2]{2,1,0:T(1,128)}), s32[32,1,2]{2,1,0:T(1,128)S(1)}, u32[]{:S(2)}, u32[]{:S(2)}) async-start(s32[32,1,2]{2,1,0:T(1,128)} %bitcast.1), calls=%async_computation | async-start | bytes 32768 | tf_op jit(solution)/shard_map/all_to_all | solution.py:200
  66.6 3.4 %copy-start = (bf16[512,4096]{1,0:T(8,128)(2,1)S(1)}, bf16[512,4096]{1,0:T(8,128)(2,1)}, u32[]{:S(2)}) copy-start(bf16[512,4096]{1,0:T(8,128)(2,1)} %all-gather.2.cloned.1.call-done) | copy-start | bytes 12582916
  74.6 3.8 %collective-permute-start = (bf16[1,64,512]{2,1,0:T(8,128)(2,1)S(1)}, bf16[1,64,512]{2,1,0:T(8,128)(2,1)S(1)}, u32[]{:S(2)}, u32[]{:S(2)}) collective-permute-start(bf16[1,64,512]{2,1,0:T(8,128)(2,1)S(1)} %slice_bitcast_fusion), channel_id=1, source_target_pairs={{8,0},{16,8},{24,16},{32,24},{40,32},{48,40},{56,48},{64,56},{72,6... | collective-permute-start | bytes 196616 | tf_op jit(solution)/shard_map/ppermute | solution.py:25
  81.3 59.0 %all-to-all-start.1 = ((bf16[32,128,512]{2,1,0:T(8,128)(2,1)}), bf16[32,128,512]{2,1,0:T(8,128)(2,1)}, u32[]{:S(2)}, u32[]{:S(2)}) async-start(bf16[32,128,512]{2,1,0:T(8,128)(2,1)} %bitcast.16), calls=%async_computation.1 | async-start | bytes 8388608 | tf_op jit(solution)/shard_map/all_to_all | solution.py:219
  91.7 192.8 %reduce-scatter.2.cloned.1.call-start = ((), (), s32[]{:S(2)}) async-start(), calls=%async_computation.5 | async-start | bytes 4718592 | tf_op jit(solution)/shard_map/reduce_scatter | solution.py:233
  215.8 5.6 %collective-permute-start.1 = (bf16[1,64,512]{2,1,0:T(8,128)(2,1)S(1)}, bf16[1,64,512]{2,1,0:T(8,128)(2,1)S(1)}, u32[]{:S(2)}, u32[]{:S(2)}) collective-permute-start(bf16[1,64,512]{2,1,0:T(8,128)(2,1)S(1)} %slice.28), channel_id=1, source_target_pairs={{0,8},{8,16},{16,24},{24,32},{32,40},{40,48},{48,56},{56,64},{64,7... | collective-permute-start | bytes 196616 | tf_op jit(solution)/shard_map/ppermute | solution.py:25
  229.0 55.4 %copy-start.1 = (bf16[512,512]{1,0:T(8,128)(2,1)S(1)}, bf16[512,512]{1,0:T(8,128)(2,1)}, u32[]{:S(2)}) copy-start(bf16[512,512]{1,0:T(8,128)(2,1)} %param.8) | copy-start | bytes 1572868
Sparse Core Ops, SparseCore 0:
  9.1 57.3 all-gather.1
  229.1 55.2 reduce-scatter.1

commit v3 on v2

--- a/solution.py
+++ b/solution.py
@@ -11,7 +11,7 @@
 SPAN = 64
 SLOTS = 2
 STATS = 8
-PARTS = 1
+PARTS = 2
 LANES = 128
 
 eps = 1e-05

time: 295 us -> 299 us (1.014)
  blocking collectives: 60.1 us -> 36.1 us
  starting transfers between devices: 21.7 us -> 43.4 us
  waiting for transfers between devices: 156 us -> 137 us
  Pallas kernels: 14.5 us -> 25.5 us
  matrix products: 11 us -> 17.9 us
  local copies, waits for them, and re-layouts: 7.26 us -> 13 us
    ppermute x2 -> x4, waiting for transfers between devices: 4.25 us -> 37.2 us  [shifted(): return lax.ppermute(block, axis, route)]
    all_to_all x1, blocking collectives: 60.1 us -> 36.1 us  [answer(): lax.all_to_all(answers, 'dp', split_axis=0, concat_axis=0, tiled=True)]
    all_to_all x1 -> x2, waiting for transfers between devices: 46.8 us -> 23 us  [ask(): lax.all_to_all(sent_rows, 'dp', split_axis=0, concat_axis=0, tiled=True)]
    all_gather x1 -> x2, waiting for transfers between devices: 48.6 us -> 32.8 us  [ask(): widened = lax.all_gather(pieces[i], 'mp', axis=1, tiled=True).astype(f32)]
    reduce_scatter x1 -> x2, waiting for transfers between devices: 55.4 us -> 42.6 us  [finish(): summed = lax.psum_scatter(head_terms, 'mp', scatter_dimension=1, tiled=True)]
    all_to_all x0 -> x1, starting transfers between devices: none -> 9.44 us  [answer(): lax.all_to_all(answers, 'dp', split_axis=0, concat_axis=0, tiled=True)]
    all_to_all x1 -> x2, starting transfers between devices: 10.3 us -> 18.2 us  [ask(): lax.all_to_all(sent_rows, 'dp', split_axis=0, concat_axis=0, tiled=True)]
    pallas_call x1 -> x2, Pallas kernels: 10.5 us -> 18.4 us  [attend(): pl.pallas_call(attend_kernel, out_shape=jax.ShapeDtypeStruct((peer_count,...]
  transfers between devices with their start and end apart: 6 -> 12, of which waited for: 5 -> 8; matrix products, arithmetic and copies ran while one was open for 5% -> 12% of each run, Pallas kernels for 0% -> 9%
where the time goes in v3:
time: 299 us; the launch traced here: 297 us
  waiting for transfers between devices  137 us (46%)
  starting transfers between devices  43.4 us (15%)
  blocking collectives  36.1 us (12%)
  Pallas kernels  25.5 us (9%)
  matrix products  17.9 us (6%)
  between operations  14 us (5%)
  local copies, waits for them, and re-layouts  13 us (4%)
  other arithmetic  9.86 us (3%)
    reduce_scatter x2, waiting for transfers between devices, finish(): summed = lax.psum_scatter(head_terms, 'mp', scatter_dimension=1, tiled=True)  42.6 us
    ppermute x4, waiting for transfers between devices, shifted(): return lax.ppermute(block, axis, route)  37.2 us
    all_to_all x1, blocking collectives, answer(): lax.all_to_all(answers, 'dp', split_axis=0, concat_axis=0, tiled=True)  36.1 us
    all_gather x2, waiting for transfers between devices, ask(): widened = lax.all_gather(pieces[i], 'mp', axis=1, tiled=True).astype(f32)  32.8 us
    all_to_all x2, waiting for transfers between devices, ask(): lax.all_to_all(sent_rows, 'dp', split_axis=0, concat_axis=0, tiled=True)  23 us
    pallas_call x2, Pallas kernels, attend(): pl.pallas_call(attend_kernel, out_shape=jax.ShapeDtypeStruct((peer_count,...  18.4 us
    all_to_all x2, starting transfers between devices, ask(): lax.all_to_all(sent_rows, 'dp', split_axis=0, concat_axis=0, tiled=True)  18.2 us
    dot_general x2, matrix products, finish(): head_terms = jnp.dot(placed, w_out, preferred_element_type=f32).astype(bf16)  9.63 us
  transfers between devices with their start and end apart: 12, of which 8 were waited for; matrix products, arithmetic and copies ran while one was open for 12% of the time, Pallas kernels for 9%

profile of v3, /device:TPU:28, one launch (start us, length us, event | category | flops | bytes accessed | tf_op | source)
XLA Modules:
  0.0 296.8 jit_solution(9603779790571421454)
XLA Ops:
  6.5 1.9 fusion.22
  8.4 0.7 and_select_fusion.1
  10.3 0.2 convert_reduce_fusion
  10.5 0.6 add_select_fusion
  11.0 0.1 select_reduce_fusion
  11.1 0.7 all_to_all.18
  11.8 7.3 %all-to-all-start = ((s32[32,1,2]{2,1,0:T(1,128)}), s32[32,1,2]{2,1,0:T(1,128)S(1)}, u32[]{:S(2)}, u32[]{:S(2)}) async-start(s32[32,1,2]{2,1,0:T(1,128)} %bitcast.1), calls=%async_computation | async-start | bytes 32768 | tf_op jit(solution)/shard_map/all_to_all | solution.py:200
  19.2 0.7 all-gather.5.cloned.1.call-update
  19.9 32.7 %all-gather.3.cloned.1.call-done = bf16[256,4096]{1,0:T(8,128)(2,1)} async-done(((bf16[256,512]{1,0:T(8,128)(2,1)}), bf16[256,4096]{1,0:T(8,128)(2,1)}) %all-gather.3.cloned.1.call-update) | async-done | bytes 2097168 | tf_op jit(solution)/shard_map/all_gather | solution.py:208
  52.7 2.1 fusion
  54.8 4.1 %fusion.14 = bf16[256,512]{1,0:T(8,128)(2,1)S(1)} fusion(bf16[4096,512]{1,0:T(8,128)(2,1)} %param.10, bf16[256,4096]{1,0:T(8,128)(2,1)} %all-gather.3.cloned.1.call-done, f32[4096]{0:T(1024)} %param.9, f32[256]{0:T(256)S(1)} %add_rsqrt_fusion.1), kind=kOutput, calls=%fused_computation.20 | convolution fusion | flops 1078067200 | bytes 6571008 | tf_op jit(solution)/shard_map/dot_general | solution.py:212
  58.9 1.9 collective-permute-start
  60.9 1.5 collective-permute-done
  62.5 2.0 gather_fusion
  64.5 8.3 %all-to-all-start.1 = ((bf16[32,64,512]{2,1,0:T(8,128)(2,1)}), bf16[32,64,512]{2,1,0:T(8,128)(2,1)S(1)}, u32[]{:S(2)}, u32[]{:S(2)}) async-start(bf16[32,64,512]{2,1,0:T(8,128)(2,1)} %bitcast.8), calls=%async_computation.1 | async-start | bytes 4194304 | tf_op jit(solution)/shard_map/all_to_all | solution.py:219
  72.8 0.5 broadcast.194
  73.3 0.7 reduce.3
  74.0 0.6 reshape.149.ids_ref
  74.6 23.0 %all-to-all-done.1.q_ref = bf16[32,64,512]{2,1,0:T(8,128)(2,1)S(1)} async-done(((bf16[32,64,512]{2,1,0:T(8,128)(2,1)}), bf16[32,64,512]{2,1,0:T(8,128)(2,1)S(1)}, u32[]{:S(2)}, u32[]{:S(2)}) %all-to-all-start.1) | async-done | bytes 2097184 | tf_op jit(solution)/shard_map/all_to_all | solution.py:219
  97.6 1.3 copy-done.1
  98.9 9.2 %attend.2 = bf16[32,72,512]{2,1,0:T(8,128)(2,1)} custom-call(s32[64]{0:T(128)} %reshape.149.ids_ref, bf16[32,64,512]{2,1,0:T(8,128)(2,1)} %copy-done.1, bf16[8,128,512]{2,1,0:T(8,128)(2,1)} %k_ref.3, bf16[8,128,512]{2,1,0:T(8,128)(2,1)} %v_ref.3), custom_call_target="tpu_custom_call" | custom-call | flops 2147483648 | bytes 4194304 | tf_op jit(solution)/shard_map/attend/pallas_call | solution.py:85
  108.1 9.4 %all-to-all-start.2 = ((bf16[32,72,512]{2,1,0:T(8,128)(2,1)}), bf16[32,72,512]{2,1,0:T(8,128)(2,1)S(1)}, u32[]{:S(2)}, u32[]{:S(2)}) async-start(bf16[32,72,512]{2,1,0:T(8,128)(2,1)} %attend.2), calls=%async_computation.2 | async-start | bytes 4718592 | tf_op jit(solution)/shard_map/all_to_all | solution.py:223
  117.6 2.1 fusion.3
  119.7 4.1 %fusion.17 = bf16[256,512]{1,0:T(8,128)(2,1)S(1)} fusion(bf16[4096,512]{1,0:T(8,128)(2,1)} %param.10, bf16[256,4096]{1,0:T(8,128)(2,1)} %all-gather.5.cloned.1.call-done, f32[256]{0:T(256)S(1)} %add_rsqrt_fusion, f32[4096]{0:T(1024)S(1)} %copy-done.4), kind=kOutput, calls=%fused_computation.21 | convolution fusion | flops 1078067200 | bytes 6571008 | tf_op jit(solution)/shard_map/dot_general | solution.py:212
  123.8 2.2 collective-permute-start.2
  126.1 16.5 %collective-permute-done.2 = bf16[1,32,512]{2,1,0:T(8,128)(2,1)S(1)} collective-permute-done((bf16[1,32,512]{2,1,0:T(8,128)(2,1)S(1)}, bf16[1,32,512]{2,1,0:T(8,128)(2,1)S(1)}, u32[]{:S(2)}, u32[]{:S(2)}) %collective-permute-start.2) | collective-permute-done | bytes 32800 | tf_op jit(solution)/shard_map/ppermute | solution.py:25
  142.5 0.1 maximum_select_fusion
  142.6 2.0 gather_fusion.1
  144.7 0.8 all-to-all-done.2.back_ref
  145.5 9.9 %all-to-all-start.3 = ((bf16[32,64,512]{2,1,0:T(8,128)(2,1)}), bf16[32,64,512]{2,1,0:T(8,128)(2,1)}, u32[]{:S(2)}, u32[]{:S(2)}) async-start(bf16[32,64,512]{2,1,0:T(8,128)(2,1)} %bitcast.32), calls=%async_computation.4 | async-start | bytes 4194304 | tf_op jit(solution)/shard_map/all_to_all | solution.py:219
  155.5 3.5 %combine.2 = bf16[8,32,512]{2,1,0:T(8,128)(2,1)} custom-call(s32[16]{0:T(128)} %copy-done.3, s32[16]{0:T(128)} %get-tuple-element.12.rank_ref, s32[1]{0:T(128)} %copy.19.live_ref, bf16[32,72,512]{2,1,0:T(8,128)(2,1)} %copy-done), custom_call_target="tpu_custom_call" | custom-call | flops 1048576 | bytes 786432 | tf_op jit(solution)/shard_map/combine/pallas_call | solution.py:153
  159.0 0.8 slice.63
  159.8 2.0 collective-permute-start.1
  161.8 1.0 slice.64
  162.8 17.0 %collective-permute-done.1 = bf16[1,32,512]{2,1,0:T(8,128)(2,1)S(1)} collective-permute-done((bf16[1,32,512]{2,1,0:T(8,128)(2,1)S(1)}, bf16[1,32,512]{2,1,0:T(8,128)(2,1)S(1)}, u32[]{:S(2)}, u32[]{:S(2)}) %collective-permute-start.1) | collective-permute-done | bytes 32800 | tf_op jit(solution)/shard_map/ppermute | solution.py:25
  179.8 4.8 %convolution_convert_fusion.1 = bf16[256,4096]{1,0:T(8,128)(2,1)} fusion(bf16[256,512]{1,0:T(8,128)(2,1)S(1)} %bitcast.39, bf16[512,4096]{1,0:T(8,128)(2,1)} %param.11), kind=kOutput, calls=%fused_computation.7 | convolution fusion | flops 1074790400 | bytes 6553600 | tf_op jit(solution)/shard_map/dot_general | solution.py:232
  184.7 9.2 %attend.3 = bf16[32,72,512]{2,1,0:T(8,128)(2,1)} custom-call(s32[64]{0:T(128)} %reshape.149.ids_ref, bf16[32,64,512]{2,1,0:T(8,128)(2,1)} %all-to-all-done.3.q_ref, bf16[8,128,512]{2,1,0:T(8,128)(2,1)} %k_ref.3, bf16[8,128,512]{2,1,0:T(8,128)(2,1)} %v_ref.3), custom_call_target="tpu_custom_call" | custom-call | flops 2147483648 | bytes 4194304 | tf_op jit(solution)/shard_map/attend/pallas_call | solution.py:85
  193.9 36.1 %all_to_all.29.back_ref = bf16[32,72,512]{2,1,0:T(8,128)(2,1)} all-to-all(bf16[32,72,512]{2,1,0:T(8,128)(2,1)} %attend.3), channel_id=1, replica_groups=mesh['dp'=32,'mp'=8] {'dp'}, dimensions={0} | all-to-all | bytes 4718592 | tf_op jit(solution)/shard_map/all_to_all | solution.py:223
  230.0 3.5 %combine.3 = bf16[8,32,512]{2,1,0:T(8,128)(2,1)} custom-call(s32[16]{0:T(128)} %copy-done.3, s32[16]{0:T(128)} %get-tuple-element.12.rank_ref, s32[1]{0:T(128)} %copy.19.live_ref, bf16[32,72,512]{2,1,0:T(8,128)(2,1)} %all_to_all.29.back_ref), custom_call_target="tpu_custom_call" | custom-call | flops 1048576 | bytes 786432 | tf_op jit(solution)/shard_map/combine/pallas_call | solution.py:153
  233.6 0.8 slice.68
  234.3 2.1 collective-permute-start.3
  236.4 1.0 slice.69
  237.4 2.2 collective-permute-done.3
  239.6 1.0 maximum_select_fusion.1
  240.6 4.8 %convolution_convert_fusion = bf16[256,4096]{1,0:T(8,128)(2,1)} fusion(bf16[256,512]{1,0:T(8,128)(2,1)S(1)} %bitcast.42, bf16[512,4096]{1,0:T(8,128)(2,1)} %param.11), kind=kOutput, calls=%fused_computation.6 | convolution fusion | flops 1074790400 | bytes 6553600 | tf_op jit(solution)/shard_map/dot_general | solution.py:232
  245.5 42.5 %reduce-scatter.5.cloned.1.call-done = bf16[256,512]{1,0:T(8,128)(2,1)} async-done(((bf16[256,4096]{1,0:T(8,128)(2,1)}), bf16[256,512]{1,0:T(8,128)(2,1)}) %reduce-scatter.5.cloned.1.call-update) | async-done | bytes 262160 | tf_op jit(solution)/shard_map/reduce_scatter | solution.py:233
  288.1 1.1 pad_maximum_fusion
  289.1 1.2 convert_add_fusion
  (38 shorter events, 0.9 us)
Async XLA Ops:
  6.5 46.1 %all-gather.3.cloned.1.call-start = ((), (), s32[]{:S(2)}) async-start(), calls=%async_computation.7 | async-start | bytes 2359296 | tf_op jit(solution)/shard_map/all_gather | solution.py:208
  9.3 49.6 %copy-start.3 = (s32[16]{0:T(128)}, s32[16]{0:T(128)S(1)}, u32[]{:S(2)}) copy-start(s32[16]{0:T(128)S(1)} %reshape.148.owner_ref) | copy-start | bytes 196
  11.8 52.6 %all-to-all-start = ((s32[32,1,2]{2,1,0:T(1,128)}), s32[32,1,2]{2,1,0:T(1,128)S(1)}, u32[]{:S(2)}, u32[]{:S(2)}) async-start(s32[32,1,2]{2,1,0:T(1,128)} %bitcast.1), calls=%async_computation | async-start | bytes 32768 | tf_op jit(solution)/shard_map/all_to_all | solution.py:200
  19.2 98.4 %all-gather.5.cloned.1.call-start = ((), (), s32[]{:S(2)}) async-start(), calls=%async_computation.9 | async-start | bytes 2359296 | tf_op jit(solution)/shard_map/all_gather | solution.py:208
  58.9 3.5 %collective-permute-start = (bf16[1,32,512]{2,1,0:T(8,128)(2,1)S(1)}, bf16[1,32,512]{2,1,0:T(8,128)(2,1)S(1)}, u32[]{:S(2)}, u32[]{:S(2)}) collective-permute-start(bf16[1,32,512]{2,1,0:T(8,128)(2,1)S(1)} %slice_bitcast_fusion.1), channel_id=1, source_target_pairs={{8,0},{16,8},{24,16},{32,24},{40,32},{48,40},{56,48},{64,56},{72,6... | collective-permute-start | bytes 98312 | tf_op jit(solution)/shard_map/ppermute | solution.py:25
  64.5 33.1 %all-to-all-start.1 = ((bf16[32,64,512]{2,1,0:T(8,128)(2,1)}), bf16[32,64,512]{2,1,0:T(8,128)(2,1)S(1)}, u32[]{:S(2)}, u32[]{:S(2)}) async-start(bf16[32,64,512]{2,1,0:T(8,128)(2,1)} %bitcast.8), calls=%async_computation.1 | async-start | bytes 4194304 | tf_op jit(solution)/shard_map/all_to_all | solution.py:219
  97.6 1.3 copy-start.1
  108.1 11.6 %copy-start.4 = (f32[4096]{0:T(1024)S(1)}, f32[4096]{0:T(1024)}, u32[]{:S(2)}) copy-start(f32[4096]{0:T(1024)} %param.9) | copy-start | bytes 49156
  108.1 37.4 %all-to-all-start.2 = ((bf16[32,72,512]{2,1,0:T(8,128)(2,1)}), bf16[32,72,512]{2,1,0:T(8,128)(2,1)S(1)}, u32[]{:S(2)}, u32[]{:S(2)}) async-start(bf16[32,72,512]{2,1,0:T(8,128)(2,1)} %attend.2), calls=%async_computation.2 | async-start | bytes 4718592 | tf_op jit(solution)/shard_map/all_to_all | solution.py:223
  123.8 18.7 %collective-permute-start.2 = (bf16[1,32,512]{2,1,0:T(8,128)(2,1)S(1)}, bf16[1,32,512]{2,1,0:T(8,128)(2,1)S(1)}, u32[]{:S(2)}, u32[]{:S(2)}) collective-permute-start(bf16[1,32,512]{2,1,0:T(8,128)(2,1)S(1)} %slice_bitcast_fusion), channel_id=1, source_target_pairs={{8,0},{16,8},{24,16},{32,24},{40,32},{48,40},{56,48},{64,56},{72,6... | collective-permute-start | bytes 98312 | tf_op jit(solution)/shard_map/ppermute | solution.py:25
  145.5 10.0 %copy-start = (bf16[32,72,512]{2,1,0:T(8,128)(2,1)}, bf16[32,72,512]{2,1,0:T(8,128)(2,1)S(1)}, u32[]{:S(2)}) copy-start(bf16[32,72,512]{2,1,0:T(8,128)(2,1)S(1)} %all-to-all-done.2.back_ref) | copy-start | bytes 7077892
  145.5 39.2 %all-to-all-start.3 = ((bf16[32,64,512]{2,1,0:T(8,128)(2,1)}), bf16[32,64,512]{2,1,0:T(8,128)(2,1)}, u32[]{:S(2)}, u32[]{:S(2)}) async-start(bf16[32,64,512]{2,1,0:T(8,128)(2,1)} %bitcast.32), calls=%async_computation.4 | async-start | bytes 4194304 | tf_op jit(solution)/shard_map/all_to_all | solution.py:219
  155.4 90.1 %reduce-scatter.3.cloned.1.call-start = ((), (), s32[]{:S(2)}) async-start(), calls=%async_computation.8 | async-start | bytes 2359296 | tf_op jit(solution)/shard_map/reduce_scatter | solution.py:233
  159.8 20.0 %collective-permute-start.1 = (bf16[1,32,512]{2,1,0:T(8,128)(2,1)S(1)}, bf16[1,32,512]{2,1,0:T(8,128)(2,1)S(1)}, u32[]{:S(2)}, u32[]{:S(2)}) collective-permute-start(bf16[1,32,512]{2,1,0:T(8,128)(2,1)S(1)} %slice.63), channel_id=1, source_target_pairs={{0,8},{8,16},{16,24},{24,32},{32,40},{40,48},{48,56},{56,64},{64,7... | collective-permute-start | bytes 98312 | tf_op jit(solution)/shard_map/ppermute | solution.py:25
  184.6 103.4 %reduce-scatter.5.cloned.1.call-start = ((), (), s32[]{:S(2)}) async-start(), calls=%async_computation.10 | async-start | bytes 2359296 | tf_op jit(solution)/shard_map/reduce_scatter | solution.py:233
  234.3 5.2 %collective-permute-start.3 = (bf16[1,32,512]{2,1,0:T(8,128)(2,1)S(1)}, bf16[1,32,512]{2,1,0:T(8,128)(2,1)S(1)}, u32[]{:S(2)}, u32[]{:S(2)}) collective-permute-start(bf16[1,32,512]{2,1,0:T(8,128)(2,1)S(1)} %slice.68), channel_id=1, source_target_pairs={{0,8},{8,16},{16,24},{24,32},{32,40},{40,48},{48,56},{56,64},{64,7... | collective-permute-start | bytes 98312 | tf_op jit(solution)/shard_map/ppermute | solution.py:25
  240.6 48.5 %copy-start.2 = (bf16[512,512]{1,0:T(8,128)(2,1)S(1)}, bf16[512,512]{1,0:T(8,128)(2,1)}, u32[]{:S(2)}) copy-start(bf16[512,512]{1,0:T(8,128)(2,1)} %param.8) | copy-start | bytes 1572868
Sparse Core Ops, SparseCore 0:
  9.1 43.5 all-gather.2
  54.5 39.4 all-gather.4
  184.8 42.4 reduce-scatter.2
  245.6 42.4 reduce-scatter.4

commit v4 on v2

--- a/solution.py
+++ b/solution.py
@@ -23,6 +23,86 @@
     devices = range(lax.axis_size(axis))
     route = [(i - distance, i) for i in devices if i - distance in devices]
     return lax.ppermute(block, axis, route)
+
+
+def turned(block, distance):
+    size = lax.axis_size("mp")
+    return lax.ppermute(block, "mp", [(i, (i + distance) % size) for i in range(size)])
+
+
+def project(hidden, norm_gain, w_query):
+    size = lax.axis_size("mp")
+    me = lax.axis_index("mp")
+    rows, width = hidden.shape
+    half = rows // 2
+    far = size // 2
+
+    def weights(offset):
+        start = (me + offset) % size * width
+        gain = lax.dynamic_slice(norm_gain, (start,), (width,))
+        part = lax.dynamic_slice(w_query, (start, 0), (width, w_query.shape[1]))
+        return (part.astype(f32) * gain[:, None]).astype(bf16)
+
+    def add(sums, h, block, weight):
+        wide = block.astype(f32)
+        squares = jnp.sum(wide * wide, axis=1, keepdims=True)
+        product = jnp.dot(block, weight, preferred_element_type=f32)
+        if sums[h] is None:
+            sums[h] = (squares, product)
+        else:
+            sums[h] = (sums[h][0] + squares, sums[h][1] + product)
+
+    sums = [None, None]
+    up = [hidden[:half], hidden[half:]]
+    down = list(up)
+    own = weights(0)
+    for h in range(2):
+        add(sums, h, up[h], own)
+    for step in range(1, far):
+        behind, ahead = weights(-step), weights(step)
+        for h in range(2):
+            up[h] = turned(up[h], 1)
+            down[1 - h] = turned(down[1 - h], -1)
+        for h in range(2):
+            add(sums, h, up[h], behind)
+            add(sums, 1 - h, down[1 - h], ahead)
+    opposite = weights(far)
+    add(sums, 0, turned(up[0], 1), opposite)
+    add(sums, 1, turned(down[1], -1), opposite)
+    total = size * width
+    return jnp.concatenate(
+        [product * lax.rsqrt(squares / total + eps) for squares, product in sums], axis=0
+    ).astype(bf16)
+
+
+def output(placed, w_out):
+    size = lax.axis_size("mp")
+    me = lax.axis_index("mp")
+    rows = placed.shape[0]
+    width = w_out.shape[1] // size
+    half = rows // 2
+    far = size // 2
+    halves = [placed[:half], placed[half:]]
+
+    def term(h, offset):
+        start = (me + offset) % size * width
+        part = lax.dynamic_slice(w_out, (0, start), (w_out.shape[0], width))
+        return jnp.dot(halves[h], part, preferred_element_type=f32)
+
+    up = [turned(term(0, far).astype(bf16), 1), None]
+    down = [None, turned(term(1, -far).astype(bf16), -1)]
+    for offset in range(far - 1, 0, -1):
+        for h in (1, 0):
+            one, two = term(h, offset), term(1 - h, -offset)
+            if up[h] is not None:
+                one = one + up[h].astype(f32)
+            if down[1 - h] is not None:
+                two = two + down[1 - h].astype(f32)
+            up[h] = turned(one.astype(bf16), 1)
+            down[1 - h] = turned(two.astype(bf16), -1)
+    return jnp.concatenate(
+        [term(h, 0) + up[h].astype(f32) + down[h].astype(f32) for h in range(2)], axis=0
+    )
 
 
 def attend_kernel(ids_ref, q_ref, k_ref, v_ref, out_ref):
@@ -176,11 +256,6 @@
     inner_width = w_query.shape[1]
     peer_count = lax.axis_size("dp")
     count = SPAN // PARTS
-    pieces = [
-        hidden.reshape(span_dev, SPAN, width)[:, i * count:(i + 1) * count].reshape(-1, width)
-        for i in range(PARTS)
-    ]
-
     live_span = jnp.arange(span_dev, dtype=jnp.int32) < valid_spans[0]
     owners = (neighbours // stored).reshape(-1)
     slot_ids = (neighbours % stored).reshape(-1)
@@ -205,11 +280,7 @@
         return position == SPAN - 1
 
     def ask(i):
-        widened = lax.all_gather(pieces[i], "mp", axis=1, tiled=True).astype(f32)
-        normed = (
-            widened * lax.rsqrt(jnp.mean(widened * widened, axis=1, keepdims=True) + eps) * norm_gain
-        ).astype(bf16)
-        queries = jnp.dot(normed, w_query, preferred_element_type=f32).astype(bf16)
+        queries = project(hidden, norm_gain, w_query)
         blocks = queries.reshape(span_dev, count, inner_width)
         following = shifted(blocks[:1], "dp", -1)
         grouped = jnp.concatenate([blocks[1:], following], axis=0)
@@ -229,9 +300,7 @@
         if (i + 1) * count == SPAN:
             placed = jnp.where(is_last(i), merged, placed)
         placed = placed.reshape(-1, inner_width)
-        head_terms = jnp.dot(placed, w_out, preferred_element_type=f32).astype(bf16)
-        summed = lax.psum_scatter(head_terms, "mp", scatter_dimension=1, tiled=True)
-        return summed.astype(f32).reshape(span_dev, count, width)
+        return output(placed, w_out).reshape(span_dev, count, width)
 
     asked = [ask(i) for i in range(PARTS)]
     back = [answer(one) for one in asked]

time: 295 us -> 266 us (0.902)
  waiting for transfers between devices: 156 us -> 87.3 us
  starting transfers between devices: 21.7 us -> 67.3 us
  between operations: 14.2 us -> 1.46 us
  matrix products: 11 us -> 15.9 us
    reduce_scatter x1 -> x0, waiting for transfers between devices: 55.4 us -> none  [finish(): summed = lax.psum_scatter(head_terms, 'mp', scatter_dimension=1, tiled=True)]
    all_gather x1 -> x0, waiting for transfers between devices: 48.6 us -> none  [ask(): widened = lax.all_gather(pieces[i], 'mp', axis=1, tiled=True).astype(f32)]
    ppermute x0 -> x28, starting transfers between devices: none -> 47.5 us  [turned(): lax.ppermute(block, 'mp', [(i, (i + distance) % size) for i in range(size)])]
    ppermute x0 -> x28, waiting for transfers between devices: none -> 36.4 us  [turned(): lax.ppermute(block, 'mp', [(i, (i + distance) % size) for i in range(size)])]
    dot_general x2 -> x32, matrix products: 11 us -> 15.9 us  [the longest x16 9.83 us: add(): product = jnp.dot(block, weight, preferred_element_type=f32)]
  transfers between devices with their start and end apart: 6 -> 32, of which waited for: 5 -> 15; matrix products, arithmetic and copies ran while one was open for 5% -> 10% of each run, Pallas kernels for 0% -> 0%
where the time goes in v4:
time: 266 us; the launch traced here: 263 us
  waiting for transfers between devices  87.3 us (33%)
  starting transfers between devices  67.3 us (25%)
  blocking collectives  60.1 us (23%)
  matrix products  15.9 us (6%)
  Pallas kernels  14.5 us (5%)
  local copies, waits for them, and re-layouts  9.44 us (4%)
  other arithmetic  6.89 us (3%)
    all_to_all x1, blocking collectives, answer(): lax.all_to_all(answers, 'dp', split_axis=0, concat_axis=0, tiled=True)  60.1 us
    ppermute x28, starting transfers between devices, turned(): lax.ppermute(block, 'mp', [(i, (i + distance) % size) for i in range(size)])  47.5 us
    all_to_all x1, waiting for transfers between devices, ask(): lax.all_to_all(sent_rows, 'dp', split_axis=0, concat_axis=0, tiled=True)  46.9 us
    ppermute x28, waiting for transfers between devices, turned(): lax.ppermute(block, 'mp', [(i, (i + distance) % size) for i in range(size)])  36.4 us
    pallas_call x1, Pallas kernels, attend(): pl.pallas_call(attend_kernel, out_shape=jax.ShapeDtypeStruct((peer_count,...  10.5 us
    dot_general x16, matrix products, add(): product = jnp.dot(block, weight, preferred_element_type=f32)  9.83 us
    all_to_all x1, starting transfers between devices, ask(): lax.all_to_all(sent_rows, 'dp', split_axis=0, concat_axis=0, tiled=True)  8.38 us
    all_to_all x1, starting transfers between devices, shards(): lax.all_to_all(request_table, 'dp', split_axis=0, concat_axis=0, tiled=True)  7.32 us
  transfers between devices with their start and end apart: 32, of which 15 were waited for; matrix products, arithmetic and copies ran while one was open for 10% of the time, Pallas kernels for 0%

profile of v4, /device:TPU:28, one launch (start us, length us, event | category | flops | bytes accessed | tf_op | source)
XLA Modules:
  0.0 262.9 jit_solution(2866796680639967248)
XLA Ops:
  0.0 1.1 fusion.99
  1.1 2.0 collective-permute-start
  3.1 4.0 %collective-permute-start.1 = (bf16[256,512]{1,0:T(8,128)(2,1)S(1)}, bf16[256,512]{1,0:T(8,128)(2,1)S(1)}, u32[]{:S(2)}, u32[]{:S(2)}) collective-permute-start(bf16[256,512]{1,0:T(8,128)(2,1)S(1)} %get-tuple-element.11), channel_id=1, source_target_pairs={{0,7},{1,0},{2,1},{3,2},{4,3},{5,4},{6,5},{7,6},{8,15},{9,8},{10,9... | collective-permute-start | bytes 786440 | tf_op jit(solution)/shard_map/ppermute | solution.py:30
  7.2 1.9 collective-permute-start.7
  11.8 0.7 all_to_all.12
  12.5 7.3 %all-to-all-start = ((s32[32,1,2]{2,1,0:T(1,128)}), s32[32,1,2]{2,1,0:T(1,128)S(1)}, u32[]{:S(2)}, u32[]{:S(2)}) async-start(s32[32,1,2]{2,1,0:T(1,128)} %bitcast.1), calls=%async_computation | async-start | bytes 32768 | tf_op jit(solution)/shard_map/all_to_all | solution.py:275
  20.0 1.1 fusion.100
  21.1 1.8 fusion.56
  22.8 1.5 fusion.57
  24.7 3.2 %collective-permute-start.9 = (bf16[256,512]{1,0:T(8,128)(2,1)S(1)}, bf16[256,512]{1,0:T(8,128)(2,1)S(1)}, u32[]{:S(2)}, u32[]{:S(2)}) collective-permute-start(bf16[256,512]{1,0:T(8,128)(2,1)S(1)} %collective-permute-done.7), channel_id=1, source_target_pairs={{0,7},{1,0},{2,1},{3,2},{4,3},{5,4},{6,5},{7,6},{8,15},{9,8},{10,9... | collective-permute-start | bytes 786440 | tf_op jit(solution)/shard_map/ppermute | solution.py:30
  28.1 2.0 collective-permute-start.3
  30.1 1.4 convolution_add_fusion.9
  33.3 1.1 collective-permute-done.2
  34.6 4.8 %collective-permute-done.3 = bf16[256,512]{1,0:T(8,128)(2,1)S(1)} collective-permute-done((bf16[256,512]{1,0:T(8,128)(2,1)S(1)}, bf16[256,512]{1,0:T(8,128)(2,1)S(1)}, u32[]{:S(2)}, u32[]{:S(2)}) %collective-permute-start.3) | collective-permute-done | bytes 262176 | tf_op jit(solution)/shard_map/ppermute | solution.py:30
  39.4 3.7 %collective-permute-start.5 = (bf16[256,512]{1,0:T(8,128)(2,1)S(1)}, bf16[256,512]{1,0:T(8,128)(2,1)S(1)}, u32[]{:S(2)}, u32[]{:S(2)}) collective-permute-start(bf16[256,512]{1,0:T(8,128)(2,1)S(1)} %collective-permute-done.3), channel_id=1, source_target_pairs={{0,7},{1,0},{2,1},{3,2},{4,3},{5,4},{6,5},{7,6},{8,15},{9,8},{10,9... | collective-permute-start | bytes 786440 | tf_op jit(solution)/shard_map/ppermute | solution.py:30
  43.9 1.8 collective-permute-start.12
  47.5 6.2 %collective-permute-done.11 = bf16[256,512]{1,0:T(8,128)(2,1)S(1)} collective-permute-done((bf16[256,512]{1,0:T(8,128)(2,1)S(1)}, bf16[256,512]{1,0:T(8,128)(2,1)S(1)}, u32[]{:S(2)}, u32[]{:S(2)}) %collective-permute-start.11) | collective-permute-done | bytes 262176 | tf_op jit(solution)/shard_map/ppermute | solution.py:30
  53.7 3.7 %collective-permute-start.13 = (bf16[256,512]{1,0:T(8,128)(2,1)S(1)}, bf16[256,512]{1,0:T(8,128)(2,1)S(1)}, u32[]{:S(2)}, u32[]{:S(2)}) collective-permute-start(bf16[256,512]{1,0:T(8,128)(2,1)S(1)} %collective-permute-done.11), channel_id=1, source_target_pairs={{0,7},{1,0},{2,1},{3,2},{4,3},{5,4},{6,5},{7,6},{8,15},{9,8},{10,9... | collective-permute-start | bytes 786440 | tf_op jit(solution)/shard_map/ppermute | solution.py:30
  59.7 1.8 collective-permute-done.13
  62.5 1.9 collective-permute-start.14
  64.5 1.8 collective-permute-done.14
  66.5 2.8 %gather_fusion = bf16[64,64,512]{2,1,0:T(8,128)(2,1)} fusion(bf16[8,64,512]{2,1,0:T(8,128)(2,1)S(1)} %maximum_select_fusion, s32[1024]{0:T(1024)S(1)} %pad_clamp_fusion), kind=kCustom, calls=%fused_computation | custom fusion | bytes 8388864 | tf_op jit(solution)/shard_map/gather | solution.py:289
  69.3 8.4 %all-to-all-start.1 = ((bf16[32,128,512]{2,1,0:T(8,128)(2,1)}), bf16[32,128,512]{2,1,0:T(8,128)(2,1)}, u32[]{:S(2)}, u32[]{:S(2)}) async-start(bf16[32,128,512]{2,1,0:T(8,128)(2,1)} %bitcast.64), calls=%async_computation.1 | async-start | bytes 8388608 | tf_op jit(solution)/shard_map/all_to_all | solution.py:290
  79.5 46.9 %all-to-all-done.1.q_ref = bf16[32,128,512]{2,1,0:T(8,128)(2,1)} async-done(((bf16[32,128,512]{2,1,0:T(8,128)(2,1)}), bf16[32,128,512]{2,1,0:T(8,128)(2,1)}, u32[]{:S(2)}, u32[]{:S(2)}) %all-to-all-start.1) | async-done | bytes 4194336 | tf_op jit(solution)/shard_map/all_to_all | solution.py:290
  126.3 10.5 %attend.1 = bf16[32,136,512]{2,1,0:T(8,128)(2,1)} custom-call(s32[64]{0:T(128)} %reshape.177.ids_ref, bf16[32,128,512]{2,1,0:T(8,128)(2,1)} %all-to-all-done.1.q_ref, bf16[8,128,512]{2,1,0:T(8,128)(2,1)} %k_ref.1, bf16[8,128,512]{2,1,0:T(8,128)(2,1)} %v_ref.1), custom_call_target="tpu_custom_call" | custom-call | flops 2147483648 | bytes 8388608 | tf_op jit(solution)/shard_map/attend/pallas_call | solution.py:165
  136.9 60.1 %all_to_all.19.back_ref = bf16[32,136,512]{2,1,0:T(8,128)(2,1)} all-to-all(bf16[32,136,512]{2,1,0:T(8,128)(2,1)} %attend.1), channel_id=1, replica_groups=mesh['dp'=32,'mp'=8] {'dp'}, dimensions={0} | all-to-all | bytes 8912896 | tf_op jit(solution)/shard_map/all_to_all | solution.py:294
  196.9 4.0 %combine.1 = bf16[8,64,512]{2,1,0:T(8,128)(2,1)} custom-call(s32[16]{0:T(128)} %copy-done.3, s32[16]{0:T(128)} %get-tuple-element.24.rank_ref, s32[1]{0:T(128)} %copy.19.live_ref, bf16[32,136,512]{2,1,0:T(8,128)(2,1)} %all_to_all.19.back_ref), custom_call_target="tpu_custom_call" | custom-call | flops 2097152 | bytes 1572864 | tf_op jit(solution)/shard_map/combine/pallas_call | solution.py:233
  200.9 0.8 slice.52
  201.7 2.1 collective-permute-start.15
  203.9 1.2 slice.53
  205.1 2.2 collective-permute-done.15
  207.3 1.2 maximum_select_fusion.1
  208.5 1.3 convolution_convert_fusion.3
  210.5 3.8 %collective-permute-start.20 = (bf16[256,512]{1,0:T(8,128)(2,1)S(1)}, bf16[256,512]{1,0:T(8,128)(2,1)S(1)}, u32[]{:S(2)}, u32[]{:S(2)}) collective-permute-start(bf16[256,512]{1,0:T(8,128)(2,1)S(1)} %convolution_convert_fusion.2), channel_id=1, source_target_pairs={{0,7},{1,0},{2,1},{3,2},{4,3},{5,4},{6,5},{7,6},{8,15},{9,8},{10,9... | collective-permute-start | bytes 786440 | tf_op jit(solution)/shard_map/ppermute | solution.py:30
  215.7 3.3 %collective-permute-start.26 = (bf16[256,512]{1,0:T(8,128)(2,1)S(1)}, bf16[256,512]{1,0:T(8,128)(2,1)S(1)}, u32[]{:S(2)}, u32[]{:S(2)}) collective-permute-start(bf16[256,512]{1,0:T(8,128)(2,1)S(1)} %convolution_convert_fusion), channel_id=1, source_target_pairs={{0,7},{1,0},{2,1},{3,2},{4,3},{5,4},{6,5},{7,6},{8,15},{9,8},{10,9... | collective-permute-start | bytes 786440 | tf_op jit(solution)/shard_map/ppermute | solution.py:30
  219.0 2.0 collective-permute-done.20
  221.3 3.8 %collective-permute-start.21 = (bf16[256,512]{1,0:T(8,128)(2,1)S(1)}, bf16[256,512]{1,0:T(8,128)(2,1)S(1)}, u32[]{:S(2)}, u32[]{:S(2)}) collective-permute-start(bf16[256,512]{1,0:T(8,128)(2,1)S(1)} %add_convert_fusion.6), channel_id=1, source_target_pairs={{0,7},{1,0},{2,1},{3,2},{4,3},{5,4},{6,5},{7,6},{8,15},{9,8},{10,9... | collective-permute-start | bytes 786440 | tf_op jit(solution)/shard_map/ppermute | solution.py:30
  225.8 5.2 %collective-permute-done.23 = bf16[256,512]{1,0:T(8,128)(2,1)S(1)} collective-permute-done((bf16[256,512]{1,0:T(8,128)(2,1)S(1)}, bf16[256,512]{1,0:T(8,128)(2,1)S(1)}, u32[]{:S(2)}, u32[]{:S(2)}) %collective-permute-start.23) | collective-permute-done | bytes 262176 | tf_op jit(solution)/shard_map/ppermute | solution.py:30
  231.8 3.3 %collective-permute-start.27 = (bf16[256,512]{1,0:T(8,128)(2,1)S(1)}, bf16[256,512]{1,0:T(8,128)(2,1)S(1)}, u32[]{:S(2)}, u32[]{:S(2)}) collective-permute-start(bf16[256,512]{1,0:T(8,128)(2,1)S(1)} %add_convert_fusion.2), channel_id=1, source_target_pairs={{0,7},{1,0},{2,1},{3,2},{4,3},{5,4},{6,5},{7,6},{8,15},{9,8},{10,9... | collective-permute-start | bytes 786440 | tf_op jit(solution)/shard_map/ppermute | solution.py:30
  235.1 1.6 collective-permute-done.17
  237.4 3.3 %collective-permute-start.22 = (bf16[256,512]{1,0:T(8,128)(2,1)S(1)}, bf16[256,512]{1,0:T(8,128)(2,1)S(1)}, u32[]{:S(2)}, u32[]{:S(2)}) collective-permute-start(bf16[256,512]{1,0:T(8,128)(2,1)S(1)} %add_convert_fusion.5), channel_id=1, source_target_pairs={{0,7},{1,0},{2,1},{3,2},{4,3},{5,4},{6,5},{7,6},{8,15},{9,8},{10,9... | collective-permute-start | bytes 786440 | tf_op jit(solution)/shard_map/ppermute | solution.py:30
  241.0 2.2 collective-permute-start.28
  243.2 3.8 %collective-permute-done.18 = bf16[256,512]{1,0:T(8,128)(2,1)S(1)} collective-permute-done((bf16[256,512]{1,0:T(8,128)(2,1)S(1)}, bf16[256,512]{1,0:T(8,128)(2,1)S(1)}, u32[]{:S(2)}, u32[]{:S(2)}) %collective-permute-start.18) | collective-permute-done | bytes 262176 | tf_op jit(solution)/shard_map/ppermute | solution.py:30
  247.8 2.4 collective-permute-done.28
  250.5 3.8 %collective-permute-start.29 = (bf16[256,512]{1,0:T(8,128)(2,1)S(1)}, bf16[256,512]{1,0:T(8,128)(2,1)S(1)}, u32[]{:S(2)}, u32[]{:S(2)}) collective-permute-start(bf16[256,512]{1,0:T(8,128)(2,1)S(1)} %add_convert_fusion), channel_id=1, source_target_pairs={{0,7},{1,0},{2,1},{3,2},{4,3},{5,4},{6,5},{7,6},{8,15},{9,8},{10,9... | collective-permute-start | bytes 786440 | tf_op jit(solution)/shard_map/ppermute | solution.py:30
  254.3 3.5 %collective-permute-done.19 = bf16[256,512]{1,0:T(8,128)(2,1)S(1)} collective-permute-done((bf16[256,512]{1,0:T(8,128)(2,1)S(1)}, bf16[256,512]{1,0:T(8,128)(2,1)S(1)}, u32[]{:S(2)}, u32[]{:S(2)}) %collective-permute-start.19) | collective-permute-done | bytes 262176 | tf_op jit(solution)/shard_map/ppermute | solution.py:30
  257.9 3.7 %collective-permute-done.25 = bf16[256,512]{1,0:T(8,128)(2,1)S(1)} collective-permute-done((bf16[256,512]{1,0:T(8,128)(2,1)S(1)}, bf16[256,512]{1,0:T(8,128)(2,1)S(1)}, u32[]{:S(2)}, u32[]{:S(2)}) %collective-permute-start.25) | collective-permute-done | bytes 262176 | tf_op jit(solution)/shard_map/ppermute | solution.py:30
  261.7 1.1 maximum_add_fusion
  (108 shorter events, 18.4 us)
Async XLA Ops:
  0.0 24.4 %copy-start.2 = (bf16[512,512]{1,0:T(8,128)(2,1)S(1)}, bf16[512,512]{1,0:T(8,128)(2,1)}, u32[]{:S(2)}) copy-start(bf16[512,512]{1,0:T(8,128)(2,1)} %param.8) | copy-start | bytes 1572868
  1.1 23.5 %collective-permute-start = (bf16[256,512]{1,0:T(8,128)(2,1)S(1)}, bf16[256,512]{1,0:T(8,128)(2,1)S(1)}, u32[]{:S(2)}, u32[]{:S(2)}) collective-permute-start(bf16[256,512]{1,0:T(8,128)(2,1)S(1)} %get-tuple-element.11), channel_id=1, source_target_pairs={{0,1},{1,2},{2,3},{3,4},{4,5},{5,6},{6,7},{7,0},{8,9},{9,10},{10,1... | collective-permute-start | bytes 786440 | tf_op jit(solution)/shard_map/ppermute | solution.py:30
  3.1 24.9 %collective-permute-start.1 = (bf16[256,512]{1,0:T(8,128)(2,1)S(1)}, bf16[256,512]{1,0:T(8,128)(2,1)S(1)}, u32[]{:S(2)}, u32[]{:S(2)}) collective-permute-start(bf16[256,512]{1,0:T(8,128)(2,1)S(1)} %get-tuple-element.11), channel_id=1, source_target_pairs={{0,7},{1,0},{2,1},{3,2},{4,3},{5,4},{6,5},{7,6},{8,15},{9,8},{10,9... | collective-permute-start | bytes 786440 | tf_op jit(solution)/shard_map/ppermute | solution.py:30
  7.2 17.5 %collective-permute-start.7 = (bf16[256,512]{1,0:T(8,128)(2,1)S(1)}, bf16[256,512]{1,0:T(8,128)(2,1)S(1)}, u32[]{:S(2)}, u32[]{:S(2)}) collective-permute-start(bf16[256,512]{1,0:T(8,128)(2,1)S(1)} %get-tuple-element.12), channel_id=1, source_target_pairs={{0,7},{1,0},{2,1},{3,2},{4,3},{5,4},{6,5},{7,6},{8,15},{9,8},{10,9... | collective-permute-start | bytes 786440 | tf_op jit(solution)/shard_map/ppermute | solution.py:30
  9.1 23.2 %collective-permute-start.8 = (bf16[256,512]{1,0:T(8,128)(2,1)S(1)}, bf16[256,512]{1,0:T(8,128)(2,1)S(1)}, u32[]{:S(2)}, u32[]{:S(2)}) collective-permute-start(bf16[256,512]{1,0:T(8,128)(2,1)S(1)} %get-tuple-element.12), channel_id=1, source_target_pairs={{0,1},{1,2},{2,3},{3,4},{4,5},{5,6},{6,7},{7,0},{8,9},{9,10},{10,1... | collective-permute-start | bytes 786440 | tf_op jit(solution)/shard_map/ppermute | solution.py:30
  11.0 21.3 %copy-start.3 = (s32[16]{0:T(128)}, s32[16]{0:T(128)S(1)}, u32[]{:S(2)}) copy-start(s32[16]{0:T(128)S(1)} %reshape.176.owner_ref) | copy-start | bytes 196
  12.5 56.7 %all-to-all-start = ((s32[32,1,2]{2,1,0:T(1,128)}), s32[32,1,2]{2,1,0:T(1,128)S(1)}, u32[]{:S(2)}, u32[]{:S(2)}) async-start(s32[32,1,2]{2,1,0:T(1,128)} %bitcast.1), calls=%async_computation | async-start | bytes 32768 | tf_op jit(solution)/shard_map/all_to_all | solution.py:275
  20.0 11.5 %copy-start = (bf16[4096,512]{1,0:T(8,128)(2,1)S(1)}, bf16[4096,512]{1,0:T(8,128)(2,1)}, u32[]{:S(2)}) copy-start(bf16[4096,512]{1,0:T(8,128)(2,1)} %param.10) | copy-start | bytes 12582916
  24.6 9.8 %collective-permute-start.2 = (bf16[256,512]{1,0:T(8,128)(2,1)S(1)}, bf16[256,512]{1,0:T(8,128)(2,1)S(1)}, u32[]{:S(2)}, u32[]{:S(2)}) collective-permute-start(bf16[256,512]{1,0:T(8,128)(2,1)S(1)} %collective-permute-done), channel_id=1, source_target_pairs={{0,1},{1,2},{2,3},{3,4},{4,5},{5,6},{6,7},{7,0},{8,9},{9,10},{10,1... | collective-permute-start | bytes 786440 | tf_op jit(solution)/shard_map/ppermute | solution.py:30
  24.7 18.4 %collective-permute-start.9 = (bf16[256,512]{1,0:T(8,128)(2,1)S(1)}, bf16[256,512]{1,0:T(8,128)(2,1)S(1)}, u32[]{:S(2)}, u32[]{:S(2)}) collective-permute-start(bf16[256,512]{1,0:T(8,128)(2,1)S(1)} %collective-permute-done.7), channel_id=1, source_target_pairs={{0,7},{1,0},{2,1},{3,2},{4,3},{5,4},{6,5},{7,6},{8,15},{9,8},{10,9... | collective-permute-start | bytes 786440 | tf_op jit(solution)/shard_map/ppermute | solution.py:30
  28.1 11.3 %collective-permute-start.3 = (bf16[256,512]{1,0:T(8,128)(2,1)S(1)}, bf16[256,512]{1,0:T(8,128)(2,1)S(1)}, u32[]{:S(2)}, u32[]{:S(2)}) collective-permute-start(bf16[256,512]{1,0:T(8,128)(2,1)S(1)} %collective-permute-done.1), channel_id=1, source_target_pairs={{0,7},{1,0},{2,1},{3,2},{4,3},{5,4},{6,5},{7,6},{8,15},{9,8},{10,9... | collective-permute-start | bytes 786440 | tf_op jit(solution)/shard_map/ppermute | solution.py:30
  32.3 11.5 %collective-permute-start.10 = (bf16[256,512]{1,0:T(8,128)(2,1)S(1)}, bf16[256,512]{1,0:T(8,128)(2,1)S(1)}, u32[]{:S(2)}, u32[]{:S(2)}) collective-permute-start(bf16[256,512]{1,0:T(8,128)(2,1)S(1)} %collective-permute-done.8), channel_id=1, source_target_pairs={{0,1},{1,2},{2,3},{3,4},{4,5},{5,6},{6,7},{7,0},{8,9},{9,10},{10,1... | collective-permute-start | bytes 786440 | tf_op jit(solution)/shard_map/ppermute | solution.py:30
  34.5 12.8 %collective-permute-start.4 = (bf16[256,512]{1,0:T(8,128)(2,1)S(1)}, bf16[256,512]{1,0:T(8,128)(2,1)S(1)}, u32[]{:S(2)}, u32[]{:S(2)}) collective-permute-start(bf16[256,512]{1,0:T(8,128)(2,1)S(1)} %collective-permute-done.2), channel_id=1, source_target_pairs={{0,1},{1,2},{2,3},{3,4},{4,5},{5,6},{6,7},{7,0},{8,9},{9,10},{10,1... | collective-permute-start | bytes 786440 | tf_op jit(solution)/shard_map/ppermute | solution.py:30
  39.4 18.3 %collective-permute-start.5 = (bf16[256,512]{1,0:T(8,128)(2,1)S(1)}, bf16[256,512]{1,0:T(8,128)(2,1)S(1)}, u32[]{:S(2)}, u32[]{:S(2)}) collective-permute-start(bf16[256,512]{1,0:T(8,128)(2,1)S(1)} %collective-permute-done.3), channel_id=1, source_target_pairs={{0,7},{1,0},{2,1},{3,2},{4,3},{5,4},{6,5},{7,6},{8,15},{9,8},{10,9... | collective-permute-start | bytes 786440 | tf_op jit(solution)/shard_map/ppermute | solution.py:30
  43.1 10.6 %collective-permute-start.11 = (bf16[256,512]{1,0:T(8,128)(2,1)S(1)}, bf16[256,512]{1,0:T(8,128)(2,1)S(1)}, u32[]{:S(2)}, u32[]{:S(2)}) collective-permute-start(bf16[256,512]{1,0:T(8,128)(2,1)S(1)} %collective-permute-done.9), channel_id=1, source_target_pairs={{0,7},{1,0},{2,1},{3,2},{4,3},{5,4},{6,5},{7,6},{8,15},{9,8},{10,9... | collective-permute-start | bytes 786440 | tf_op jit(solution)/shard_map/ppermute | solution.py:30
  43.9 14.3 %collective-permute-start.12 = (bf16[256,512]{1,0:T(8,128)(2,1)S(1)}, bf16[256,512]{1,0:T(8,128)(2,1)S(1)}, u32[]{:S(2)}, u32[]{:S(2)}) collective-permute-start(bf16[256,512]{1,0:T(8,128)(2,1)S(1)} %collective-permute-done.10), channel_id=1, source_target_pairs={{0,1},{1,2},{2,3},{3,4},{4,5},{5,6},{6,7},{7,0},{8,9},{9,10},{10,1... | collective-permute-start | bytes 786440 | tf_op jit(solution)/shard_map/ppermute | solution.py:30
  47.4 12.2 %collective-permute-start.6 = (bf16[256,512]{1,0:T(8,128)(2,1)S(1)}, bf16[256,512]{1,0:T(8,128)(2,1)S(1)}, u32[]{:S(2)}, u32[]{:S(2)}) collective-permute-start(bf16[256,512]{1,0:T(8,128)(2,1)S(1)} %collective-permute-done.4), channel_id=1, source_target_pairs={{0,1},{1,2},{2,3},{3,4},{4,5},{5,6},{6,7},{7,0},{8,9},{9,10},{10,1... | collective-permute-start | bytes 786440 | tf_op jit(solution)/shard_map/ppermute | solution.py:30
  53.7 7.8 %collective-permute-start.13 = (bf16[256,512]{1,0:T(8,128)(2,1)S(1)}, bf16[256,512]{1,0:T(8,128)(2,1)S(1)}, u32[]{:S(2)}, u32[]{:S(2)}) collective-permute-start(bf16[256,512]{1,0:T(8,128)(2,1)S(1)} %collective-permute-done.11), channel_id=1, source_target_pairs={{0,7},{1,0},{2,1},{3,2},{4,3},{5,4},{6,5},{7,6},{8,15},{9,8},{10,9... | collective-permute-start | bytes 786440 | tf_op jit(solution)/shard_map/ppermute | solution.py:30
  62.5 3.8 %collective-permute-start.14 = (bf16[1,64,512]{2,1,0:T(8,128)(2,1)S(1)}, bf16[1,64,512]{2,1,0:T(8,128)(2,1)S(1)}, u32[]{:S(2)}, u32[]{:S(2)}) collective-permute-start(bf16[1,64,512]{2,1,0:T(8,128)(2,1)S(1)} %slice_bitcast_fusion), channel_id=1, source_target_pairs={{8,0},{16,8},{24,16},{32,24},{40,32},{48,40},{56,48},{64,56},{72,6... | collective-permute-start | bytes 196616 | tf_op jit(solution)/shard_map/ppermute | solution.py:25
  69.3 57.1 %all-to-all-start.1 = ((bf16[32,128,512]{2,1,0:T(8,128)(2,1)}), bf16[32,128,512]{2,1,0:T(8,128)(2,1)}, u32[]{:S(2)}, u32[]{:S(2)}) async-start(bf16[32,128,512]{2,1,0:T(8,128)(2,1)} %bitcast.64), calls=%async_computation.1 | async-start | bytes 8388608 | tf_op jit(solution)/shard_map/all_to_all | solution.py:290
  201.7 5.6 %collective-permute-start.15 = (bf16[1,64,512]{2,1,0:T(8,128)(2,1)S(1)}, bf16[1,64,512]{2,1,0:T(8,128)(2,1)S(1)}, u32[]{:S(2)}, u32[]{:S(2)}) collective-permute-start(bf16[1,64,512]{2,1,0:T(8,128)(2,1)S(1)} %slice.52), channel_id=1, source_target_pairs={{0,8},{8,16},{16,24},{24,32},{32,40},{40,48},{48,56},{56,64},{64,7... | collective-permute-start | bytes 196616 | tf_op jit(solution)/shard_map/ppermute | solution.py:25
  203.9 6.0 %copy-start.1 = (bf16[512,4096]{1,0:T(8,128)(2,1)S(1)}, bf16[512,4096]{1,0:T(8,128)(2,1)}, u32[]{:S(2)}) copy-start(bf16[512,4096]{1,0:T(8,128)(2,1)} %param.11) | copy-start | bytes 12582916
  210.5 10.5 %collective-permute-start.20 = (bf16[256,512]{1,0:T(8,128)(2,1)S(1)}, bf16[256,512]{1,0:T(8,128)(2,1)S(1)}, u32[]{:S(2)}, u32[]{:S(2)}) collective-permute-start(bf16[256,512]{1,0:T(8,128)(2,1)S(1)} %convolution_convert_fusion.2), channel_id=1, source_target_pairs={{0,7},{1,0},{2,1},{3,2},{4,3},{5,4},{6,5},{7,6},{8,15},{9,8},{10,9... | collective-permute-start | bytes 786440 | tf_op jit(solution)/shard_map/ppermute | solution.py:30
  215.0 10.5 %collective-permute-start.16 = (bf16[256,512]{1,0:T(8,128)(2,1)S(1)}, bf16[256,512]{1,0:T(8,128)(2,1)S(1)}, u32[]{:S(2)}, u32[]{:S(2)}) collective-permute-start(bf16[256,512]{1,0:T(8,128)(2,1)S(1)} %convolution_convert_fusion.3), channel_id=1, source_target_pairs={{0,1},{1,2},{2,3},{3,4},{4,5},{5,6},{6,7},{7,0},{8,9},{9,10},{10,1... | collective-permute-start | bytes 786440 | tf_op jit(solution)/shard_map/ppermute | solution.py:30
  215.4 15.7 %collective-permute-start.23 = (bf16[256,512]{1,0:T(8,128)(2,1)S(1)}, bf16[256,512]{1,0:T(8,128)(2,1)S(1)}, u32[]{:S(2)}, u32[]{:S(2)}) collective-permute-start(bf16[256,512]{1,0:T(8,128)(2,1)S(1)} %convolution_convert_fusion.1), channel_id=1, source_target_pairs={{0,1},{1,2},{2,3},{3,4},{4,5},{5,6},{6,7},{7,0},{8,9},{9,10},{10,1... | collective-permute-start | bytes 786440 | tf_op jit(solution)/shard_map/ppermute | solution.py:30
  215.7 15.8 %collective-permute-start.26 = (bf16[256,512]{1,0:T(8,128)(2,1)S(1)}, bf16[256,512]{1,0:T(8,128)(2,1)S(1)}, u32[]{:S(2)}, u32[]{:S(2)}) collective-permute-start(bf16[256,512]{1,0:T(8,128)(2,1)S(1)} %convolution_convert_fusion), channel_id=1, source_target_pairs={{0,7},{1,0},{2,1},{3,2},{4,3},{5,4},{6,5},{7,6},{8,15},{9,8},{10,9... | collective-permute-start | bytes 786440 | tf_op jit(solution)/shard_map/ppermute | solution.py:30
  221.3 15.8 %collective-permute-start.21 = (bf16[256,512]{1,0:T(8,128)(2,1)S(1)}, bf16[256,512]{1,0:T(8,128)(2,1)S(1)}, u32[]{:S(2)}, u32[]{:S(2)}) collective-permute-start(bf16[256,512]{1,0:T(8,128)(2,1)S(1)} %add_convert_fusion.6), channel_id=1, source_target_pairs={{0,7},{1,0},{2,1},{3,2},{4,3},{5,4},{6,5},{7,6},{8,15},{9,8},{10,9... | collective-permute-start | bytes 786440 | tf_op jit(solution)/shard_map/ppermute | solution.py:30
  225.8 10.9 %collective-permute-start.17 = (bf16[256,512]{1,0:T(8,128)(2,1)S(1)}, bf16[256,512]{1,0:T(8,128)(2,1)S(1)}, u32[]{:S(2)}, u32[]{:S(2)}) collective-permute-start(bf16[256,512]{1,0:T(8,128)(2,1)S(1)} %add_convert_fusion.9), channel_id=1, source_target_pairs={{0,1},{1,2},{2,3},{3,4},{4,5},{5,6},{6,7},{7,0},{8,9},{9,10},{10,1... | collective-permute-start | bytes 786440 | tf_op jit(solution)/shard_map/ppermute | solution.py:30
  231.4 16.0 %collective-permute-start.24 = (bf16[256,512]{1,0:T(8,128)(2,1)S(1)}, bf16[256,512]{1,0:T(8,128)(2,1)S(1)}, u32[]{:S(2)}, u32[]{:S(2)}) collective-permute-start(bf16[256,512]{1,0:T(8,128)(2,1)S(1)} %add_convert_fusion.4), channel_id=1, source_target_pairs={{0,1},{1,2},{2,3},{3,4},{4,5},{5,6},{6,7},{7,0},{8,9},{9,10},{10,1... | collective-permute-start | bytes 786440 | tf_op jit(solution)/shard_map/ppermute | solution.py:30
  231.8 8.9 %collective-permute-start.27 = (bf16[256,512]{1,0:T(8,128)(2,1)S(1)}, bf16[256,512]{1,0:T(8,128)(2,1)S(1)}, u32[]{:S(2)}, u32[]{:S(2)}) collective-permute-start(bf16[256,512]{1,0:T(8,128)(2,1)S(1)} %add_convert_fusion.2), channel_id=1, source_target_pairs={{0,7},{1,0},{2,1},{3,2},{4,3},{5,4},{6,5},{7,6},{8,15},{9,8},{10,9... | collective-permute-start | bytes 786440 | tf_op jit(solution)/shard_map/ppermute | solution.py:30
  237.0 10.0 %collective-permute-start.18 = (bf16[256,512]{1,0:T(8,128)(2,1)S(1)}, bf16[256,512]{1,0:T(8,128)(2,1)S(1)}, u32[]{:S(2)}, u32[]{:S(2)}) collective-permute-start(bf16[256,512]{1,0:T(8,128)(2,1)S(1)} %add_convert_fusion.8), channel_id=1, source_target_pairs={{0,1},{1,2},{2,3},{3,4},{4,5},{5,6},{6,7},{7,0},{8,9},{9,10},{10,1... | collective-permute-start | bytes 786440 | tf_op jit(solution)/shard_map/ppermute | solution.py:30
  237.4 16.9 %collective-permute-start.22 = (bf16[256,512]{1,0:T(8,128)(2,1)S(1)}, bf16[256,512]{1,0:T(8,128)(2,1)S(1)}, u32[]{:S(2)}, u32[]{:S(2)}) collective-permute-start(bf16[256,512]{1,0:T(8,128)(2,1)S(1)} %add_convert_fusion.5), channel_id=1, source_target_pairs={{0,7},{1,0},{2,1},{3,2},{4,3},{5,4},{6,5},{7,6},{8,15},{9,8},{10,9... | collective-permute-start | bytes 786440 | tf_op jit(solution)/shard_map/ppermute | solution.py:30
  241.0 9.2 %collective-permute-start.28 = (bf16[256,512]{1,0:T(8,128)(2,1)S(1)}, bf16[256,512]{1,0:T(8,128)(2,1)S(1)}, u32[]{:S(2)}, u32[]{:S(2)}) collective-permute-start(bf16[256,512]{1,0:T(8,128)(2,1)S(1)} %add_convert_fusion.1), channel_id=1, source_target_pairs={{0,7},{1,0},{2,1},{3,2},{4,3},{5,4},{6,5},{7,6},{8,15},{9,8},{10,9... | collective-permute-start | bytes 786440 | tf_op jit(solution)/shard_map/ppermute | solution.py:30
  247.3 10.5 %collective-permute-start.19 = (bf16[256,512]{1,0:T(8,128)(2,1)S(1)}, bf16[256,512]{1,0:T(8,128)(2,1)S(1)}, u32[]{:S(2)}, u32[]{:S(2)}) collective-permute-start(bf16[256,512]{1,0:T(8,128)(2,1)S(1)} %add_convert_fusion.7), channel_id=1, source_target_pairs={{0,1},{1,2},{2,3},{3,4},{4,5},{5,6},{6,7},{7,0},{8,9},{9,10},{10,1... | collective-permute-start | bytes 786440 | tf_op jit(solution)/shard_map/ppermute | solution.py:30
  247.8 13.9 %collective-permute-start.25 = (bf16[256,512]{1,0:T(8,128)(2,1)S(1)}, bf16[256,512]{1,0:T(8,128)(2,1)S(1)}, u32[]{:S(2)}, u32[]{:S(2)}) collective-permute-start(bf16[256,512]{1,0:T(8,128)(2,1)S(1)} %add_convert_fusion.3), channel_id=1, source_target_pairs={{0,1},{1,2},{2,3},{3,4},{4,5},{5,6},{6,7},{7,0},{8,9},{9,10},{10,1... | collective-permute-start | bytes 786440 | tf_op jit(solution)/shard_map/ppermute | solution.py:30
  250.5 11.1 %collective-permute-start.29 = (bf16[256,512]{1,0:T(8,128)(2,1)S(1)}, bf16[256,512]{1,0:T(8,128)(2,1)S(1)}, u32[]{:S(2)}, u32[]{:S(2)}) collective-permute-start(bf16[256,512]{1,0:T(8,128)(2,1)S(1)} %add_convert_fusion), channel_id=1, source_target_pairs={{0,7},{1,0},{2,1},{3,2},{4,3},{5,4},{6,5},{7,6},{8,15},{9,8},{10,9... | collective-permute-start | bytes 786440 | tf_op jit(solution)/shard_map/ppermute | solution.py:30

commit v5 on v3

--- a/solution.py
+++ b/solution.py
@@ -23,6 +23,69 @@
     devices = range(lax.axis_size(axis))
     route = [(i - distance, i) for i in devices if i - distance in devices]
     return lax.ppermute(block, axis, route)
+
+
+def turned(block, distance):
+    size = lax.axis_size("mp")
+    return lax.ppermute(block, "mp", [(i, (i + distance) % size) for i in range(size)])
+
+
+def project(hidden, norm_gain, w_query):
+    size = lax.axis_size("mp")
+    me = lax.axis_index("mp")
+    rows, width = hidden.shape
+    half = rows // 2
+    far = size // 2
+
+    def weights(offset):
+        start = (me + offset) % size * width
+        gain = lax.dynamic_slice(norm_gain, (start,), (width,))
+        part = lax.dynamic_slice(w_query, (start, 0), (width, w_query.shape[1]))
+        return (part.astype(f32) * gain[:, None]).astype(bf16)
+
+    def terms(block, offset):
+        wide = block.astype(f32)
+        squares = jnp.sum(wide * wide, axis=1, keepdims=True)
+        return squares, jnp.dot(block, weights(offset), preferred_element_type=f32)
+
+    squares, product = terms(hidden, 0)
+    up = down = hidden
+    for step in range(1, far):
+        up, down = turned(up, 1), turned(down, -1)
+        for block, offset in ((up, -step), (down, step)):
+            more = terms(block, offset)
+            squares, product = squares + more[0], product + more[1]
+    nearly = up
+    last = jnp.concatenate([turned(up[:half], 1), turned(down[half:], -1)], axis=0)
+    more = terms(last, far)
+    squares, product = squares + more[0], product + more[1]
+    total = size * width
+    return (product * lax.rsqrt(squares / total + eps)).astype(bf16), nearly
+
+
+def output(placed, w_out):
+    size = lax.axis_size("mp")
+    me = lax.axis_index("mp")
+    rows = placed.shape[0]
+    width = w_out.shape[1] // size
+    half = rows // 2
+    far = size // 2
+
+    def term(block, offset):
+        start = (me + offset) % size * width
+        part = lax.dynamic_slice(w_out, (0, start), (w_out.shape[0], width))
+        return jnp.dot(block, part, preferred_element_type=f32)
+
+    opposite = term(placed, far).astype(bf16)
+    up, down = turned(opposite[:half], 1), turned(opposite[half:], -1)
+    none = jnp.zeros_like(up)
+    up = jnp.concatenate([up, none], axis=0)
+    down = jnp.concatenate([none, down], axis=0)
+    for offset in range(far - 1, 0, -1):
+        one = term(placed, offset) + up.astype(f32)
+        two = term(placed, -offset) + down.astype(f32)
+        up, down = turned(one.astype(bf16), 1), turned(two.astype(bf16), -1)
+    return term(placed, 0) + up.astype(f32) + down.astype(f32)
 
 
 def attend_kernel(ids_ref, q_ref, k_ref, v_ref, out_ref):
@@ -79,7 +142,7 @@
 
 def attend(ids, asked, keys, values):
     peer_count, rows, width = asked.shape
-    step = 8
+    step = 4
     stored, tokens, _ = keys.shape
     slots = peer_count * SLOTS
     return pl.pallas_call(
@@ -204,23 +267,17 @@
         position = i * count + lax.broadcasted_iota(jnp.int32, (1, count, 1), 1)
         return position == SPAN - 1
 
-    def ask(i):
-        widened = lax.all_gather(pieces[i], "mp", axis=1, tiled=True).astype(f32)
-        normed = (
-            widened * lax.rsqrt(jnp.mean(widened * widened, axis=1, keepdims=True) + eps) * norm_gain
-        ).astype(bf16)
-        queries = jnp.dot(normed, w_query, preferred_element_type=f32).astype(bf16)
+    def request(i, piece):
+        queries, nearly = project(piece, norm_gain, w_query)
         blocks = queries.reshape(span_dev, count, inner_width)
         following = shifted(blocks[:1], "dp", -1)
         grouped = jnp.concatenate([blocks[1:], following], axis=0)
         if (i + 1) * count == SPAN:
             grouped = jnp.where(is_last(i), blocks, grouped)
-        sent_rows = grouped[source_span].reshape(peer_count, SLOTS * count, inner_width)
-        return lax.all_to_all(sent_rows, "dp", split_axis=0, concat_axis=0, tiled=True)
-
-    def answer(asked):
-        answers = attend(wanted, asked, nb_keys, nb_values)
-        return lax.all_to_all(answers, "dp", split_axis=0, concat_axis=0, tiled=True)
+        return grouped[source_span].reshape(peer_count, SLOTS * count, inner_width), nearly
+
+    def exchange(rows):
+        return lax.all_to_all(rows, "dp", split_axis=0, concat_axis=0, tiled=True)
 
     def finish(i, back):
         merged = combine(owners, slot_rank, valid_spans, back)
@@ -229,15 +286,21 @@
         if (i + 1) * count == SPAN:
             placed = jnp.where(is_last(i), merged, placed)
         placed = placed.reshape(-1, inner_width)
-        head_terms = jnp.dot(placed, w_out, preferred_element_type=f32).astype(bf16)
-        summed = lax.psum_scatter(head_terms, "mp", scatter_dimension=1, tiled=True)
-        return summed.astype(f32).reshape(span_dev, count, width)
-
-    asked = [ask(i) for i in range(PARTS)]
-    back = [answer(one) for one in asked]
-    summed = [finish(i, one) for i, one in enumerate(back)]
-    summed = jnp.concatenate(summed, axis=1).reshape(tok_rows, width)
-    return hidden.astype(f32) + summed
+        return output(placed, w_out).reshape(span_dev, count, width)
+
+    sent_0, nearly = request(0, pieces[0])
+    piece_1, _, wanted = lax.optimization_barrier((pieces[1], nearly, wanted))
+    asked_0 = exchange(sent_0)
+    sent_1, _ = request(1, piece_1)
+    asked_0, sent_1 = lax.optimization_barrier((asked_0, sent_1))
+    asked_1 = exchange(sent_1)
+    answers_0 = attend(wanted, asked_0, nb_keys, nb_values)
+    back_0 = exchange(answers_0)
+    answers_1 = attend(wanted, asked_1, nb_keys, nb_values)
+    back_0, answers_1 = lax.optimization_barrier((back_0, answers_1))
+    back_1 = exchange(answers_1)
+    summed = jnp.concatenate([finish(0, back_0), finish(1, back_1)], axis=1)
+    return hidden.astype(f32) + summed.reshape(tok_rows, width)
 
 
 def solution(mesh):

time: 299 us -> 302 us (1.010); the launches traced: 297 us -> 296 us
  starting transfers between devices: 43.4 us -> 110 us
  blocking collectives: 36.1 us -> 0 us
  waiting for transfers between devices: 137 us -> 109 us
  between operations: 14 us -> 1.81 us
  matrix products: 17.9 us -> 23.4 us
  Pallas kernels: 25.5 us -> 29.1 us
    ppermute x0 -> x32, starting transfers between devices: none -> 58.7 us  [turned(): lax.ppermute(block, 'mp', [(i, (i + distance) % size) for i in range(size)])]
    ppermute x0 -> x32, waiting for transfers between devices: none -> 55.7 us  [turned(): lax.ppermute(block, 'mp', [(i, (i + distance) % size) for i in range(size)])]
    reduce_scatter x2 -> x0, waiting for transfers between devices: 42.6 us -> none  [finish(): summed = lax.psum_scatter(head_terms, 'mp', scatter_dimension=1, tiled=True)]
    all_to_all x1 -> x0, blocking collectives: 36.1 us -> none  [answer(): lax.all_to_all(answers, 'dp', split_axis=0, concat_axis=0, tiled=True)]
    all_gather x2 -> x0, waiting for transfers between devices: 32.8 us -> none  [ask(): widened = lax.all_gather(pieces[i], 'mp', axis=1, tiled=True).astype(f32)]
    ppermute x4, waiting for transfers between devices: 37.2 us -> 22.8 us  [shifted(): return lax.ppermute(block, axis, route)]
    all_to_all x3 -> x4, starting transfers between devices: 27.7 us -> 36.3 us  [exchange(): return lax.all_to_all(rows, 'dp', split_axis=0, concat_axis=0, tiled=True)]
    all_to_all x3 -> x4, waiting for transfers between devices: 23.8 us -> 30.6 us  [exchange(): return lax.all_to_all(rows, 'dp', split_axis=0, concat_axis=0, tiled=True)]
  transfers between devices with their start and end apart: 12 -> 41, of which waited for: 8 -> 20; matrix products, arithmetic and copies ran while one was open for 12% -> 13% of each run, Pallas kernels for 9% -> 10%
where the time goes in v5:
time: 302 us; the launch traced here: 296 us
  starting transfers between devices  110 us (36%)
  waiting for transfers between devices  109 us (36%)
  Pallas kernels  29.1 us (10%)
  matrix products  23.4 us (8%)
  local copies, waits for them, and re-layouts  15 us (5%)
  other arithmetic  7.7 us (3%)
    ppermute x32, starting transfers between devices, turned(): lax.ppermute(block, 'mp', [(i, (i + distance) % size) for i in range(size)])  58.7 us
    ppermute x32, waiting for transfers between devices, turned(): lax.ppermute(block, 'mp', [(i, (i + distance) % size) for i in range(size)])  55.7 us
    all_to_all x4, starting transfers between devices, exchange(): return lax.all_to_all(rows, 'dp', split_axis=0, concat_axis=0, tiled=True)  36.3 us
    all_to_all x4, waiting for transfers between devices, exchange(): return lax.all_to_all(rows, 'dp', split_axis=0, concat_axis=0, tiled=True)  30.6 us
    ppermute x4, waiting for transfers between devices, shifted(): return lax.ppermute(block, axis, route)  22.8 us
    pallas_call x2, Pallas kernels, attend(): pl.pallas_call(attend_kernel, out_shape=jax.ShapeDtypeStruct((peer_count,...  22 us
    dot_general x16, matrix products, terms(): jnp.dot(block, weights(offset), preferred_element_type=f32)  12.6 us
    dot_general x16, matrix products, term(): return jnp.dot(block, part, preferred_element_type=f32)  10.8 us
  transfers between devices with their start and end apart: 41, of which 20 were waited for; matrix products, arithmetic and copies ran while one was open for 13% of the time, Pallas kernels for 10%

profile of v5, /device:TPU:28, one launch (start us, length us, event | category | flops | bytes accessed | tf_op | source)
XLA Modules:
  0.0 296.3 jit_solution(8305611715754203284)
XLA Ops:
  1.1 5.9 %collective-permute-start.3 = (bf16[256,512]{1,0:T(8,128)(2,1)S(1)}, bf16[256,512]{1,0:T(8,128)(2,1)S(1)}, u32[]{:S(2)}, u32[]{:S(2)}) collective-permute-start(bf16[256,512]{1,0:T(8,128)(2,1)S(1)} %bitcast.90), channel_id=1, source_target_pairs={{0,7},{1,0},{2,1},{3,2},{4,3},{5,4},{6,5},{7,6},{8,15},{9,8},{10,9... | collective-permute-start | bytes 786440 | tf_op jit(solution)/shard_map/ppermute | solution.py:30
  10.4 7.3 %all-to-all-start = ((s32[32,1,2]{2,1,0:T(1,128)}), s32[32,1,2]{2,1,0:T(1,128)S(1)}, u32[]{:S(2)}, u32[]{:S(2)}) async-start(s32[32,1,2]{2,1,0:T(1,128)} %bitcast.4), calls=%async_computation | async-start | bytes 32768 | tf_op jit(solution)/shard_map/all_to_all | solution.py:263
  23.2 3.2 %collective-permute-start.4 = (bf16[256,512]{1,0:T(8,128)(2,1)S(1)}, bf16[256,512]{1,0:T(8,128)(2,1)S(1)}, u32[]{:S(2)}, u32[]{:S(2)}) collective-permute-start(bf16[256,512]{1,0:T(8,128)(2,1)S(1)} %collective-permute-done.3), channel_id=1, source_target_pairs={{0,7},{1,0},{2,1},{3,2},{4,3},{5,4},{6,5},{7,6},{8,15},{9,8},{10,9... | collective-permute-start | bytes 786440 | tf_op jit(solution)/shard_map/ppermute | solution.py:30
  29.6 2.7 collective-permute-done.4
  32.3 3.7 %collective-permute-start.5 = (bf16[256,512]{1,0:T(8,128)(2,1)S(1)}, bf16[256,512]{1,0:T(8,128)(2,1)S(1)}, u32[]{:S(2)}, u32[]{:S(2)}) collective-permute-start(bf16[256,512]{1,0:T(8,128)(2,1)S(1)} %collective-permute-done.4), channel_id=1, source_target_pairs={{0,7},{1,0},{2,1},{3,2},{4,3},{5,4},{6,5},{7,6},{8,15},{9,8},{10,9... | collective-permute-start | bytes 786440 | tf_op jit(solution)/shard_map/ppermute | solution.py:30
  37.2 3.8 %collective-permute-done.5 = bf16[256,512]{1,0:T(8,128)(2,1)S(1)} collective-permute-done((bf16[256,512]{1,0:T(8,128)(2,1)S(1)}, bf16[256,512]{1,0:T(8,128)(2,1)S(1)}, u32[]{:S(2)}, u32[]{:S(2)}) %collective-permute-start.5) | collective-permute-done | bytes 262176 | tf_op jit(solution)/shard_map/ppermute | solution.py:30
  41.0 3.8 %collective-permute-start.7 = (bf16[128,512]{1,0:T(8,128)(2,1)S(1)}, bf16[128,512]{1,0:T(8,128)(2,1)S(1)}, u32[]{:S(2)}, u32[]{:S(2)}) collective-permute-start(bf16[128,512]{1,0:T(8,128)(2,1)S(1)} %slice.95), channel_id=1, source_target_pairs={{0,7},{1,0},{2,1},{3,2},{4,3},{5,4},{6,5},{7,6},{8,15},{9,8},{10,9... | collective-permute-start | bytes 393224 | tf_op jit(solution)/shard_map/ppermute | solution.py:30
  44.9 3.2 %collective-permute-start.10 = (bf16[256,512]{1,0:T(8,128)(2,1)S(1)}, bf16[256,512]{1,0:T(8,128)(2,1)S(1)}, u32[]{:S(2)}, u32[]{:S(2)}) collective-permute-start(bf16[256,512]{1,0:T(8,128)(2,1)S(1)} %bitcast.84), channel_id=1, source_target_pairs={{0,7},{1,0},{2,1},{3,2},{4,3},{5,4},{6,5},{7,6},{8,15},{9,8},{10,9... | collective-permute-start | bytes 786440 | tf_op jit(solution)/shard_map/ppermute | solution.py:30
  48.8 2.3 collective-permute-done.6
  52.1 1.9 collective-permute-start.8
  55.6 2.0 gather_fusion
  57.6 9.2 %all-to-all-start.1 = ((bf16[32,64,512]{2,1,0:T(8,128)(2,1)}), bf16[32,64,512]{2,1,0:T(8,128)(2,1)S(1)}, u32[]{:S(2)}, u32[]{:S(2)}) async-start(bf16[32,64,512]{2,1,0:T(8,128)(2,1)} %bitcast.10), calls=%async_computation.1 | async-start | bytes 4194304 | tf_op jit(solution)/shard_map/all_to_all | solution.py:280
  73.6 1.6 collective-permute-done.12
  75.3 2.5 collective-permute-start.14
  77.9 4.2 %collective-permute-done.11 = bf16[256,512]{1,0:T(8,128)(2,1)S(1)} collective-permute-done((bf16[256,512]{1,0:T(8,128)(2,1)S(1)}, bf16[256,512]{1,0:T(8,128)(2,1)S(1)}, u32[]{:S(2)}, u32[]{:S(2)}) %collective-permute-start.11) | collective-permute-done | bytes 262176 | tf_op jit(solution)/shard_map/ppermute | solution.py:30
  83.1 3.4 %collective-permute-start.16 = (bf16[128,512]{1,0:T(8,128)(2,1)S(1)}, bf16[128,512]{1,0:T(8,128)(2,1)S(1)}, u32[]{:S(2)}, u32[]{:S(2)}) collective-permute-start(bf16[128,512]{1,0:T(8,128)(2,1)S(1)} %slice.99), channel_id=1, source_target_pairs={{0,7},{1,0},{2,1},{3,2},{4,3},{5,4},{6,5},{7,6},{8,15},{9,8},{10,9... | collective-permute-start | bytes 393224 | tf_op jit(solution)/shard_map/ppermute | solution.py:30
  86.5 4.3 %collective-permute-done.13 = bf16[256,512]{1,0:T(8,128)(2,1)S(1)} collective-permute-done((bf16[256,512]{1,0:T(8,128)(2,1)S(1)}, bf16[256,512]{1,0:T(8,128)(2,1)S(1)}, u32[]{:S(2)}, u32[]{:S(2)}) %collective-permute-start.13) | collective-permute-done | bytes 262176 | tf_op jit(solution)/shard_map/ppermute | solution.py:30
  91.6 5.5 %collective-permute-done.15 = bf16[128,512]{1,0:T(8,128)(2,1)S(1)} collective-permute-done((bf16[128,512]{1,0:T(8,128)(2,1)S(1)}, bf16[128,512]{1,0:T(8,128)(2,1)S(1)}, u32[]{:S(2)}, u32[]{:S(2)}) %collective-permute-start.15) | collective-permute-done | bytes 131104 | tf_op jit(solution)/shard_map/ppermute | solution.py:30
  98.1 1.9 collective-permute-start.17
  101.7 2.0 gather_fusion.1
  103.7 8.3 %all-to-all-start.3 = ((bf16[32,64,512]{2,1,0:T(8,128)(2,1)}), bf16[32,64,512]{2,1,0:T(8,128)(2,1)}, u32[]{:S(2)}, u32[]{:S(2)}) async-start(bf16[32,64,512]{2,1,0:T(8,128)(2,1)} %bitcast.14), calls=%async_computation.3 | async-start | bytes 4194304 | tf_op jit(solution)/shard_map/all_to_all | solution.py:280
  112.1 11.0 %attend.2 = bf16[32,72,512]{2,1,0:T(8,128)(2,1)} custom-call(s32[64]{0:T(128)} %reshape.214.ids_ref, bf16[32,64,512]{2,1,0:T(8,128)(2,1)} %copy-done.6, bf16[8,128,512]{2,1,0:T(8,128)(2,1)} %k_ref.3, bf16[8,128,512]{2,1,0:T(8,128)(2,1)} %v_ref.3), custom_call_target="tpu_custom_call" | custom-call | flops 2147483648 | bytes 4194304 | tf_op jit(solution)/shard_map/attend/pallas_call | solution.py:148
  123.1 13.7 %all-to-all-done.3.q_ref = bf16[32,64,512]{2,1,0:T(8,128)(2,1)} async-done(((bf16[32,64,512]{2,1,0:T(8,128)(2,1)}), bf16[32,64,512]{2,1,0:T(8,128)(2,1)}, u32[]{:S(2)}, u32[]{:S(2)}) %all-to-all-start.3) | async-done | bytes 2097184 | tf_op jit(solution)/shard_map/all_to_all | solution.py:280
  136.8 9.4 %all-to-all-start.2 = ((bf16[32,72,512]{2,1,0:T(8,128)(2,1)}), bf16[32,72,512]{2,1,0:T(8,128)(2,1)S(1)}, u32[]{:S(2)}, u32[]{:S(2)}) async-start(bf16[32,72,512]{2,1,0:T(8,128)(2,1)} %attend.2), calls=%async_computation.2 | async-start | bytes 4718592 | tf_op jit(solution)/shard_map/all_to_all | solution.py:280
  146.3 11.0 %attend.3 = bf16[32,72,512]{2,1,0:T(8,128)(2,1)} custom-call(s32[64]{0:T(128)} %reshape.214.ids_ref, bf16[32,64,512]{2,1,0:T(8,128)(2,1)} %all-to-all-done.3.q_ref, bf16[8,128,512]{2,1,0:T(8,128)(2,1)} %k_ref.3, bf16[8,128,512]{2,1,0:T(8,128)(2,1)} %v_ref.3), custom_call_target="tpu_custom_call" | custom-call | flops 2147483648 | bytes 4194304 | tf_op jit(solution)/shard_map/attend/pallas_call | solution.py:148
  157.3 16.9 %all-to-all-done.2.back_ref = bf16[32,72,512]{2,1,0:T(8,128)(2,1)S(1)} async-done(((bf16[32,72,512]{2,1,0:T(8,128)(2,1)}), bf16[32,72,512]{2,1,0:T(8,128)(2,1)S(1)}, u32[]{:S(2)}, u32[]{:S(2)}) %all-to-all-start.2) | async-done | bytes 2359328 | tf_op jit(solution)/shard_map/all_to_all | solution.py:280
  175.6 9.3 %all-to-all-start.4 = ((bf16[32,72,512]{2,1,0:T(8,128)(2,1)}), bf16[32,72,512]{2,1,0:T(8,128)(2,1)S(1)}, u32[]{:S(2)}, u32[]{:S(2)}) async-start(bf16[32,72,512]{2,1,0:T(8,128)(2,1)} %attend.3), calls=%async_computation.4 | async-start | bytes 4718592 | tf_op jit(solution)/shard_map/all_to_all | solution.py:280
  184.9 3.5 %combine.2 = bf16[8,32,512]{2,1,0:T(8,128)(2,1)} custom-call(s32[16]{0:T(128)} %copy-done.7, s32[16]{0:T(128)} %get-tuple-element.36.rank_ref, s32[1]{0:T(128)} %copy.21.live_ref, bf16[32,72,512]{2,1,0:T(8,128)(2,1)} %copy-done.4), custom_call_target="tpu_custom_call" | custom-call | flops 1048576 | bytes 786432 | tf_op jit(solution)/shard_map/combine/pallas_call | solution.py:216
  189.2 2.0 collective-permute-start.18
  192.2 19.9 %collective-permute-done.18 = bf16[1,32,512]{2,1,0:T(8,128)(2,1)S(1)} collective-permute-done((bf16[1,32,512]{2,1,0:T(8,128)(2,1)S(1)}, bf16[1,32,512]{2,1,0:T(8,128)(2,1)S(1)}, u32[]{:S(2)}, u32[]{:S(2)}) %collective-permute-start.18) | collective-permute-done | bytes 32800 | tf_op jit(solution)/shard_map/ppermute | solution.py:25
  213.5 8.8 %collective-permute-start.23 = (bf16[128,512]{1,0:T(8,128)(2,1)S(1)}, bf16[128,512]{1,0:T(8,128)(2,1)S(1)}, u32[]{:S(2)}, u32[]{:S(2)}) collective-permute-start(bf16[128,512]{1,0:T(8,128)(2,1)S(1)} %get-tuple-element.22), channel_id=1, source_target_pairs={{0,7},{1,0},{2,1},{3,2},{4,3},{5,4},{6,5},{7,6},{8,15},{9,8},{10,9... | collective-permute-start | bytes 393224 | tf_op jit(solution)/shard_map/ppermute | solution.py:30
  222.3 2.0 collective-permute-start.19
  224.3 4.2 %collective-permute-done.23 = bf16[128,512]{1,0:T(8,128)(2,1)S(1)} collective-permute-done((bf16[128,512]{1,0:T(8,128)(2,1)S(1)}, bf16[128,512]{1,0:T(8,128)(2,1)S(1)}, u32[]{:S(2)}, u32[]{:S(2)}) %collective-permute-start.23) | collective-permute-done | bytes 131104 | tf_op jit(solution)/shard_map/ppermute | solution.py:30
  228.5 2.1 fusion.17
  235.5 3.5 %combine.3 = bf16[8,32,512]{2,1,0:T(8,128)(2,1)} custom-call(s32[16]{0:T(128)} %copy-done.7, s32[16]{0:T(128)} %get-tuple-element.36.rank_ref, s32[1]{0:T(128)} %copy.21.live_ref, bf16[32,72,512]{2,1,0:T(8,128)(2,1)} %copy-done.3), custom_call_target="tpu_custom_call" | custom-call | flops 1048576 | bytes 786432 | tf_op jit(solution)/shard_map/combine/pallas_call | solution.py:216
  239.9 2.0 collective-permute-start.27
  243.3 2.5 collective-permute-start.25
  251.8 2.4 collective-permute-done.32
  254.5 3.6 %collective-permute-start.33 = (bf16[256,512]{1,0:T(8,128)(2,1)S(1)}, bf16[256,512]{1,0:T(8,128)(2,1)S(1)}, u32[]{:S(2)}, u32[]{:S(2)}) collective-permute-start(bf16[256,512]{1,0:T(8,128)(2,1)S(1)} %fusion.23), channel_id=1, source_target_pairs={{0,7},{1,0},{2,1},{3,2},{4,3},{5,4},{6,5},{7,6},{8,15},{9,8},{10,9... | collective-permute-start | bytes 786440 | tf_op jit(solution)/shard_map/ppermute | solution.py:30
  258.1 4.8 %collective-permute-done.28 = bf16[128,512]{1,0:T(8,128)(2,1)S(1)} collective-permute-done((bf16[128,512]{1,0:T(8,128)(2,1)S(1)}, bf16[128,512]{1,0:T(8,128)(2,1)S(1)}, u32[]{:S(2)}, u32[]{:S(2)}) %collective-permute-start.28) | collective-permute-done | bytes 131104 | tf_op jit(solution)/shard_map/ppermute | solution.py:30
  263.6 3.3 %collective-permute-start.26 = (bf16[256,512]{1,0:T(8,128)(2,1)S(1)}, bf16[256,512]{1,0:T(8,128)(2,1)S(1)}, u32[]{:S(2)}, u32[]{:S(2)}) collective-permute-start(bf16[256,512]{1,0:T(8,128)(2,1)S(1)} %fusion.15), channel_id=1, source_target_pairs={{0,7},{1,0},{2,1},{3,2},{4,3},{5,4},{6,5},{7,6},{8,15},{9,8},{10,9... | collective-permute-start | bytes 786440 | tf_op jit(solution)/shard_map/ppermute | solution.py:30
  267.2 1.6 collective-permute-start.34
  268.8 4.6 %collective-permute-done.29 = bf16[256,512]{1,0:T(8,128)(2,1)S(1)} collective-permute-done((bf16[256,512]{1,0:T(8,128)(2,1)S(1)}, bf16[256,512]{1,0:T(8,128)(2,1)S(1)}, u32[]{:S(2)}, u32[]{:S(2)}) %collective-permute-start.29) | collective-permute-done | bytes 262176 | tf_op jit(solution)/shard_map/ppermute | solution.py:30
  274.5 4.2 %collective-permute-done.34 = bf16[256,512]{1,0:T(8,128)(2,1)S(1)} collective-permute-done((bf16[256,512]{1,0:T(8,128)(2,1)S(1)}, bf16[256,512]{1,0:T(8,128)(2,1)S(1)}, u32[]{:S(2)}, u32[]{:S(2)}) %collective-permute-start.34) | collective-permute-done | bytes 262176 | tf_op jit(solution)/shard_map/ppermute | solution.py:30
  279.0 3.8 %collective-permute-start.35 = (bf16[256,512]{1,0:T(8,128)(2,1)S(1)}, bf16[256,512]{1,0:T(8,128)(2,1)S(1)}, u32[]{:S(2)}, u32[]{:S(2)}) collective-permute-start(bf16[256,512]{1,0:T(8,128)(2,1)S(1)} %fusion.21), channel_id=1, source_target_pairs={{0,7},{1,0},{2,1},{3,2},{4,3},{5,4},{6,5},{7,6},{8,15},{9,8},{10,9... | collective-permute-start | bytes 786440 | tf_op jit(solution)/shard_map/ppermute | solution.py:30
  282.8 1.6 collective-permute-done.30
  284.8 5.2 %collective-permute-done.22 = bf16[256,512]{1,0:T(8,128)(2,1)S(1)} collective-permute-done((bf16[256,512]{1,0:T(8,128)(2,1)S(1)}, bf16[256,512]{1,0:T(8,128)(2,1)S(1)}, u32[]{:S(2)}, u32[]{:S(2)}) %collective-permute-start.22) | collective-permute-done | bytes 262176 | tf_op jit(solution)/shard_map/ppermute | solution.py:30
  290.3 4.1 %collective-permute-done.31 = bf16[256,512]{1,0:T(8,128)(2,1)S(1)} collective-permute-done((bf16[256,512]{1,0:T(8,128)(2,1)S(1)}, bf16[256,512]{1,0:T(8,128)(2,1)S(1)}, u32[]{:S(2)}, u32[]{:S(2)}) %collective-permute-start.31) | collective-permute-done | bytes 262176 | tf_op jit(solution)/shard_map/ppermute | solution.py:30
  (151 shorter events, 50.5 us)
Async XLA Ops:
  1.1 22.2 %collective-permute-start.3 = (bf16[256,512]{1,0:T(8,128)(2,1)S(1)}, bf16[256,512]{1,0:T(8,128)(2,1)S(1)}, u32[]{:S(2)}, u32[]{:S(2)}) collective-permute-start(bf16[256,512]{1,0:T(8,128)(2,1)S(1)} %bitcast.90), channel_id=1, source_target_pairs={{0,7},{1,0},{2,1},{3,2},{4,3},{5,4},{6,5},{7,6},{8,15},{9,8},{10,9... | collective-permute-start | bytes 786440 | tf_op jit(solution)/shard_map/ppermute | solution.py:30
  7.0 19.5 %collective-permute-start = (bf16[256,512]{1,0:T(8,128)(2,1)S(1)}, bf16[256,512]{1,0:T(8,128)(2,1)S(1)}, u32[]{:S(2)}, u32[]{:S(2)}) collective-permute-start(bf16[256,512]{1,0:T(8,128)(2,1)S(1)} %bitcast.91), channel_id=1, source_target_pairs={{0,1},{1,2},{2,3},{3,4},{4,5},{5,6},{6,7},{7,0},{8,9},{9,10},{10,1... | collective-permute-start | bytes 786440 | tf_op jit(solution)/shard_map/ppermute | solution.py:30
  8.9 28.3 %copy-start.7 = (s32[16]{0:T(128)}, s32[16]{0:T(128)S(1)}, u32[]{:S(2)}) copy-start(s32[16]{0:T(128)S(1)} %reshape.210.owner_ref) | copy-start | bytes 196
  10.4 11.0 %all-to-all-start = ((s32[32,1,2]{2,1,0:T(1,128)}), s32[32,1,2]{2,1,0:T(1,128)S(1)}, u32[]{:S(2)}, u32[]{:S(2)}) async-start(s32[32,1,2]{2,1,0:T(1,128)} %bitcast.4), calls=%async_computation | async-start | bytes 32768 | tf_op jit(solution)/shard_map/all_to_all | solution.py:263
  23.2 13.1 %copy-start.1 = (bf16[4096,512]{1,0:T(8,128)(2,1)S(1)}, bf16[4096,512]{1,0:T(8,128)(2,1)}, u32[]{:S(2)}) copy-start(bf16[4096,512]{1,0:T(8,128)(2,1)} %param.10) | copy-start | bytes 12582916
  23.2 9.1 %collective-permute-start.4 = (bf16[256,512]{1,0:T(8,128)(2,1)S(1)}, bf16[256,512]{1,0:T(8,128)(2,1)S(1)}, u32[]{:S(2)}, u32[]{:S(2)}) collective-permute-start(bf16[256,512]{1,0:T(8,128)(2,1)S(1)} %collective-permute-done.3), channel_id=1, source_target_pairs={{0,7},{1,0},{2,1},{3,2},{4,3},{5,4},{6,5},{7,6},{8,15},{9,8},{10,9... | collective-permute-start | bytes 786440 | tf_op jit(solution)/shard_map/ppermute | solution.py:30
  26.5 9.7 %collective-permute-start.1 = (bf16[256,512]{1,0:T(8,128)(2,1)S(1)}, bf16[256,512]{1,0:T(8,128)(2,1)S(1)}, u32[]{:S(2)}, u32[]{:S(2)}) collective-permute-start(bf16[256,512]{1,0:T(8,128)(2,1)S(1)} %collective-permute-done), channel_id=1, source_target_pairs={{0,1},{1,2},{2,3},{3,4},{4,5},{5,6},{6,7},{7,0},{8,9},{9,10},{10,1... | collective-permute-start | bytes 786440 | tf_op jit(solution)/shard_map/ppermute | solution.py:30
  32.3 8.7 %collective-permute-start.5 = (bf16[256,512]{1,0:T(8,128)(2,1)S(1)}, bf16[256,512]{1,0:T(8,128)(2,1)S(1)}, u32[]{:S(2)}, u32[]{:S(2)}) collective-permute-start(bf16[256,512]{1,0:T(8,128)(2,1)S(1)} %collective-permute-done.4), channel_id=1, source_target_pairs={{0,7},{1,0},{2,1},{3,2},{4,3},{5,4},{6,5},{7,6},{8,15},{9,8},{10,9... | collective-permute-start | bytes 786440 | tf_op jit(solution)/shard_map/ppermute | solution.py:30
  36.3 8.5 %collective-permute-start.2 = (bf16[256,512]{1,0:T(8,128)(2,1)S(1)}, bf16[256,512]{1,0:T(8,128)(2,1)S(1)}, u32[]{:S(2)}, u32[]{:S(2)}) collective-permute-start(bf16[256,512]{1,0:T(8,128)(2,1)S(1)} %collective-permute-done.1), channel_id=1, source_target_pairs={{0,1},{1,2},{2,3},{3,4},{4,5},{5,6},{6,7},{7,0},{8,9},{9,10},{10,1... | collective-permute-start | bytes 786440 | tf_op jit(solution)/shard_map/ppermute | solution.py:30
  41.0 10.1 %collective-permute-start.7 = (bf16[128,512]{1,0:T(8,128)(2,1)S(1)}, bf16[128,512]{1,0:T(8,128)(2,1)S(1)}, u32[]{:S(2)}, u32[]{:S(2)}) collective-permute-start(bf16[128,512]{1,0:T(8,128)(2,1)S(1)} %slice.95), channel_id=1, source_target_pairs={{0,7},{1,0},{2,1},{3,2},{4,3},{5,4},{6,5},{7,6},{8,15},{9,8},{10,9... | collective-permute-start | bytes 393224 | tf_op jit(solution)/shard_map/ppermute | solution.py:30
  44.8 6.3 %collective-permute-start.6 = (bf16[128,512]{1,0:T(8,128)(2,1)S(1)}, bf16[128,512]{1,0:T(8,128)(2,1)S(1)}, u32[]{:S(2)}, u32[]{:S(2)}) collective-permute-start(bf16[128,512]{1,0:T(8,128)(2,1)S(1)} %slice.94), channel_id=1, source_target_pairs={{0,1},{1,2},{2,3},{3,4},{4,5},{5,6},{6,7},{7,0},{8,9},{9,10},{10,1... | collective-permute-start | bytes 393224 | tf_op jit(solution)/shard_map/ppermute | solution.py:30
  44.9 21.9 %collective-permute-start.10 = (bf16[256,512]{1,0:T(8,128)(2,1)S(1)}, bf16[256,512]{1,0:T(8,128)(2,1)S(1)}, u32[]{:S(2)}, u32[]{:S(2)}) collective-permute-start(bf16[256,512]{1,0:T(8,128)(2,1)S(1)} %bitcast.84), channel_id=1, source_target_pairs={{0,7},{1,0},{2,1},{3,2},{4,3},{5,4},{6,5},{7,6},{8,15},{9,8},{10,9... | collective-permute-start | bytes 786440 | tf_op jit(solution)/shard_map/ppermute | solution.py:30
  52.1 3.5 %collective-permute-start.8 = (bf16[1,32,512]{2,1,0:T(8,128)(2,1)S(1)}, bf16[1,32,512]{2,1,0:T(8,128)(2,1)S(1)}, u32[]{:S(2)}, u32[]{:S(2)}) collective-permute-start(bf16[1,32,512]{2,1,0:T(8,128)(2,1)S(1)} %slice_bitcast_fusion.1), channel_id=1, source_target_pairs={{8,0},{16,8},{24,16},{32,24},{40,32},{48,40},{56,48},{64,56},{72,6... | collective-permute-start | bytes 98312 | tf_op jit(solution)/shard_map/ppermute | solution.py:25
  54.1 15.5 %collective-permute-start.9 = (bf16[256,512]{1,0:T(8,128)(2,1)S(1)}, bf16[256,512]{1,0:T(8,128)(2,1)S(1)}, u32[]{:S(2)}, u32[]{:S(2)}) collective-permute-start(bf16[256,512]{1,0:T(8,128)(2,1)S(1)} %bitcast.86), channel_id=1, source_target_pairs={{0,1},{1,2},{2,3},{3,4},{4,5},{5,6},{6,7},{7,0},{8,9},{9,10},{10,1... | collective-permute-start | bytes 786440 | tf_op jit(solution)/shard_map/ppermute | solution.py:30
  57.6 46.1 %all-to-all-start.1 = ((bf16[32,64,512]{2,1,0:T(8,128)(2,1)}), bf16[32,64,512]{2,1,0:T(8,128)(2,1)S(1)}, u32[]{:S(2)}, u32[]{:S(2)}) async-start(bf16[32,64,512]{2,1,0:T(8,128)(2,1)} %bitcast.10), calls=%async_computation.1 | async-start | bytes 4194304 | tf_op jit(solution)/shard_map/all_to_all | solution.py:280
  66.8 15.4 %copy-start.2 = (bf16[4096,512]{1,0:T(8,128)(2,1)S(1)}, bf16[4096,512]{1,0:T(8,128)(2,1)}, u32[]{:S(2)}) copy-start(bf16[4096,512]{1,0:T(8,128)(2,1)} %param.10) | copy-start | bytes 12582916
  66.8 8.4 %collective-permute-start.12 = (bf16[256,512]{1,0:T(8,128)(2,1)S(1)}, bf16[256,512]{1,0:T(8,128)(2,1)S(1)}, u32[]{:S(2)}, u32[]{:S(2)}) collective-permute-start(bf16[256,512]{1,0:T(8,128)(2,1)S(1)} %collective-permute-done.10), channel_id=1, source_target_pairs={{0,7},{1,0},{2,1},{3,2},{4,3},{5,4},{6,5},{7,6},{8,15},{9,8},{10,9... | collective-permute-start | bytes 786440 | tf_op jit(solution)/shard_map/ppermute | solution.py:30
  72.5 9.5 %collective-permute-start.11 = (bf16[256,512]{1,0:T(8,128)(2,1)S(1)}, bf16[256,512]{1,0:T(8,128)(2,1)S(1)}, u32[]{:S(2)}, u32[]{:S(2)}) collective-permute-start(bf16[256,512]{1,0:T(8,128)(2,1)S(1)} %collective-permute-done.9), channel_id=1, source_target_pairs={{0,1},{1,2},{2,3},{3,4},{4,5},{5,6},{6,7},{7,0},{8,9},{9,10},{10,1... | collective-permute-start | bytes 786440 | tf_op jit(solution)/shard_map/ppermute | solution.py:30
  75.3 7.8 %collective-permute-start.14 = (bf16[256,512]{1,0:T(8,128)(2,1)S(1)}, bf16[256,512]{1,0:T(8,128)(2,1)S(1)}, u32[]{:S(2)}, u32[]{:S(2)}) collective-permute-start(bf16[256,512]{1,0:T(8,128)(2,1)S(1)} %collective-permute-done.12), channel_id=1, source_target_pairs={{0,7},{1,0},{2,1},{3,2},{4,3},{5,4},{6,5},{7,6},{8,15},{9,8},{10,9... | collective-permute-start | bytes 786440 | tf_op jit(solution)/shard_map/ppermute | solution.py:30
  82.2 8.6 %collective-permute-start.13 = (bf16[256,512]{1,0:T(8,128)(2,1)S(1)}, bf16[256,512]{1,0:T(8,128)(2,1)S(1)}, u32[]{:S(2)}, u32[]{:S(2)}) collective-permute-start(bf16[256,512]{1,0:T(8,128)(2,1)S(1)} %collective-permute-done.11), channel_id=1, source_target_pairs={{0,1},{1,2},{2,3},{3,4},{4,5},{5,6},{6,7},{7,0},{8,9},{9,10},{10,1... | collective-permute-start | bytes 786440 | tf_op jit(solution)/shard_map/ppermute | solution.py:30
  83.1 14.0 %collective-permute-start.16 = (bf16[128,512]{1,0:T(8,128)(2,1)S(1)}, bf16[128,512]{1,0:T(8,128)(2,1)S(1)}, u32[]{:S(2)}, u32[]{:S(2)}) collective-permute-start(bf16[128,512]{1,0:T(8,128)(2,1)S(1)} %slice.99), channel_id=1, source_target_pairs={{0,7},{1,0},{2,1},{3,2},{4,3},{5,4},{6,5},{7,6},{8,15},{9,8},{10,9... | collective-permute-start | bytes 393224 | tf_op jit(solution)/shard_map/ppermute | solution.py:30
  90.8 6.3 %collective-permute-start.15 = (bf16[128,512]{1,0:T(8,128)(2,1)S(1)}, bf16[128,512]{1,0:T(8,128)(2,1)S(1)}, u32[]{:S(2)}, u32[]{:S(2)}) collective-permute-start(bf16[128,512]{1,0:T(8,128)(2,1)S(1)} %slice.98), channel_id=1, source_target_pairs={{0,1},{1,2},{2,3},{3,4},{4,5},{5,6},{6,7},{7,0},{8,9},{9,10},{10,1... | collective-permute-start | bytes 393224 | tf_op jit(solution)/shard_map/ppermute | solution.py:30
  98.1 3.5 %collective-permute-start.17 = (bf16[1,32,512]{2,1,0:T(8,128)(2,1)S(1)}, bf16[1,32,512]{2,1,0:T(8,128)(2,1)S(1)}, u32[]{:S(2)}, u32[]{:S(2)}) collective-permute-start(bf16[1,32,512]{2,1,0:T(8,128)(2,1)S(1)} %slice_bitcast_fusion), channel_id=1, source_target_pairs={{8,0},{16,8},{24,16},{32,24},{40,32},{48,40},{56,48},{64,56},{72,6... | collective-permute-start | bytes 98312 | tf_op jit(solution)/shard_map/ppermute | solution.py:25
  103.7 8.3 %copy-start.6 = (bf16[32,64,512]{2,1,0:T(8,128)(2,1)}, bf16[32,64,512]{2,1,0:T(8,128)(2,1)S(1)}, u32[]{:S(2)}) copy-start(bf16[32,64,512]{2,1,0:T(8,128)(2,1)S(1)} %all-to-all-done.1.q_ref) | copy-start | bytes 6291460
  103.7 33.1 %all-to-all-start.3 = ((bf16[32,64,512]{2,1,0:T(8,128)(2,1)}), bf16[32,64,512]{2,1,0:T(8,128)(2,1)}, u32[]{:S(2)}, u32[]{:S(2)}) async-start(bf16[32,64,512]{2,1,0:T(8,128)(2,1)} %bitcast.14), calls=%async_computation.3 | async-start | bytes 4194304 | tf_op jit(solution)/shard_map/all_to_all | solution.py:280
  136.8 37.3 %all-to-all-start.2 = ((bf16[32,72,512]{2,1,0:T(8,128)(2,1)}), bf16[32,72,512]{2,1,0:T(8,128)(2,1)S(1)}, u32[]{:S(2)}, u32[]{:S(2)}) async-start(bf16[32,72,512]{2,1,0:T(8,128)(2,1)} %attend.2), calls=%async_computation.2 | async-start | bytes 4718592 | tf_op jit(solution)/shard_map/all_to_all | solution.py:280
  175.6 58.5 %all-to-all-start.4 = ((bf16[32,72,512]{2,1,0:T(8,128)(2,1)}), bf16[32,72,512]{2,1,0:T(8,128)(2,1)S(1)}, u32[]{:S(2)}, u32[]{:S(2)}) async-start(bf16[32,72,512]{2,1,0:T(8,128)(2,1)} %attend.3), calls=%async_computation.4 | async-start | bytes 4718592 | tf_op jit(solution)/shard_map/all_to_all | solution.py:280
  189.2 22.9 %collective-permute-start.18 = (bf16[1,32,512]{2,1,0:T(8,128)(2,1)S(1)}, bf16[1,32,512]{2,1,0:T(8,128)(2,1)S(1)}, u32[]{:S(2)}, u32[]{:S(2)}) collective-permute-start(bf16[1,32,512]{2,1,0:T(8,128)(2,1)S(1)} %slice.102), channel_id=1, source_target_pairs={{0,8},{8,16},{16,24},{24,32},{32,40},{40,48},{48,56},{56,64},{64,7... | collective-permute-start | bytes 98312 | tf_op jit(solution)/shard_map/ppermute | solution.py:25
  213.5 15.0 %collective-permute-start.23 = (bf16[128,512]{1,0:T(8,128)(2,1)S(1)}, bf16[128,512]{1,0:T(8,128)(2,1)S(1)}, u32[]{:S(2)}, u32[]{:S(2)}) collective-permute-start(bf16[128,512]{1,0:T(8,128)(2,1)S(1)} %get-tuple-element.22), channel_id=1, source_target_pairs={{0,7},{1,0},{2,1},{3,2},{4,3},{5,4},{6,5},{7,6},{8,15},{9,8},{10,9... | collective-permute-start | bytes 393224 | tf_op jit(solution)/shard_map/ppermute | solution.py:30
  222.3 9.5 %collective-permute-start.19 = (bf16[128,512]{1,0:T(8,128)(2,1)S(1)}, bf16[128,512]{1,0:T(8,128)(2,1)S(1)}, u32[]{:S(2)}, u32[]{:S(2)}) collective-permute-start(bf16[128,512]{1,0:T(8,128)(2,1)S(1)} %get-tuple-element.21), channel_id=1, source_target_pairs={{0,1},{1,2},{2,3},{3,4},{4,5},{5,6},{6,7},{7,0},{8,9},{9,10},{10,1... | collective-permute-start | bytes 393224 | tf_op jit(solution)/shard_map/ppermute | solution.py:30
  230.6 11.4 %collective-permute-start.24 = (bf16[256,512]{1,0:T(8,128)(2,1)}, bf16[256,512]{1,0:T(8,128)(2,1)S(1)}, u32[]{:S(2)}, u32[]{:S(2)}) collective-permute-start(bf16[256,512]{1,0:T(8,128)(2,1)} %fusion.17), channel_id=1, source_target_pairs={{0,7},{1,0},{2,1},{3,2},{4,3},{5,4},{6,5},{7,6},{8,15},{9,8},{10,9... | collective-permute-start | bytes 786440 | tf_op jit(solution)/shard_map/ppermute | solution.py:30
  233.1 17.1 %collective-permute-start.20 = (bf16[256,512]{1,0:T(8,128)(2,1)S(1)}, bf16[256,512]{1,0:T(8,128)(2,1)S(1)}, u32[]{:S(2)}, u32[]{:S(2)}) collective-permute-start(bf16[256,512]{1,0:T(8,128)(2,1)S(1)} %fusion.14), channel_id=1, source_target_pairs={{0,1},{1,2},{2,3},{3,4},{4,5},{5,6},{6,7},{7,0},{8,9},{9,10},{10,1... | collective-permute-start | bytes 786440 | tf_op jit(solution)/shard_map/ppermute | solution.py:30
  234.0 1.4 copy-start.3
  239.0 11.2 %copy-start = (bf16[512,4096]{1,0:T(8,128)(2,1)S(1)}, bf16[512,4096]{1,0:T(8,128)(2,1)}, u32[]{:S(2)}) copy-start(bf16[512,4096]{1,0:T(8,128)(2,1)} %param.11) | copy-start | bytes 12582916
  239.9 6.8 %collective-permute-start.27 = (bf16[1,32,512]{2,1,0:T(8,128)(2,1)S(1)}, bf16[1,32,512]{2,1,0:T(8,128)(2,1)S(1)}, u32[]{:S(2)}, u32[]{:S(2)}) collective-permute-start(bf16[1,32,512]{2,1,0:T(8,128)(2,1)S(1)} %slice.106), channel_id=1, source_target_pairs={{0,8},{8,16},{16,24},{24,32},{32,40},{40,48},{48,56},{56,64},{64,7... | collective-permute-start | bytes 98312 | tf_op jit(solution)/shard_map/ppermute | solution.py:25
  243.3 20.0 %collective-permute-start.25 = (bf16[256,512]{1,0:T(8,128)(2,1)S(1)}, bf16[256,512]{1,0:T(8,128)(2,1)S(1)}, u32[]{:S(2)}, u32[]{:S(2)}) collective-permute-start(bf16[256,512]{1,0:T(8,128)(2,1)S(1)} %fusion.16), channel_id=1, source_target_pairs={{0,7},{1,0},{2,1},{3,2},{4,3},{5,4},{6,5},{7,6},{8,15},{9,8},{10,9... | collective-permute-start | bytes 786440 | tf_op jit(solution)/shard_map/ppermute | solution.py:30
  249.2 5.0 %collective-permute-start.32 = (bf16[128,512]{1,0:T(8,128)(2,1)S(1)}, bf16[128,512]{1,0:T(8,128)(2,1)S(1)}, u32[]{:S(2)}, u32[]{:S(2)}) collective-permute-start(bf16[128,512]{1,0:T(8,128)(2,1)S(1)} %get-tuple-element.24), channel_id=1, source_target_pairs={{0,7},{1,0},{2,1},{3,2},{4,3},{5,4},{6,5},{7,6},{8,15},{9,8},{10,9... | collective-permute-start | bytes 393224 | tf_op jit(solution)/shard_map/ppermute | solution.py:30
  250.5 23.5 %collective-permute-start.21 = (bf16[256,512]{1,0:T(8,128)(2,1)S(1)}, bf16[256,512]{1,0:T(8,128)(2,1)S(1)}, u32[]{:S(2)}, u32[]{:S(2)}) collective-permute-start(bf16[256,512]{1,0:T(8,128)(2,1)S(1)} %fusion.13), channel_id=1, source_target_pairs={{0,1},{1,2},{2,3},{3,4},{4,5},{5,6},{6,7},{7,0},{8,9},{9,10},{10,1... | collective-permute-start | bytes 786440 | tf_op jit(solution)/shard_map/ppermute | solution.py:30
  251.7 11.2 %collective-permute-start.28 = (bf16[128,512]{1,0:T(8,128)(2,1)S(1)}, bf16[128,512]{1,0:T(8,128)(2,1)S(1)}, u32[]{:S(2)}, u32[]{:S(2)}) collective-permute-start(bf16[128,512]{1,0:T(8,128)(2,1)S(1)} %get-tuple-element.23), channel_id=1, source_target_pairs={{0,1},{1,2},{2,3},{3,4},{4,5},{5,6},{6,7},{7,0},{8,9},{9,10},{10,1... | collective-permute-start | bytes 393224 | tf_op jit(solution)/shard_map/ppermute | solution.py:30
  254.5 12.4 %collective-permute-start.33 = (bf16[256,512]{1,0:T(8,128)(2,1)S(1)}, bf16[256,512]{1,0:T(8,128)(2,1)S(1)}, u32[]{:S(2)}, u32[]{:S(2)}) collective-permute-start(bf16[256,512]{1,0:T(8,128)(2,1)S(1)} %fusion.23), channel_id=1, source_target_pairs={{0,7},{1,0},{2,1},{3,2},{4,3},{5,4},{6,5},{7,6},{8,15},{9,8},{10,9... | collective-permute-start | bytes 786440 | tf_op jit(solution)/shard_map/ppermute | solution.py:30
  263.2 10.2 %collective-permute-start.29 = (bf16[256,512]{1,0:T(8,128)(2,1)S(1)}, bf16[256,512]{1,0:T(8,128)(2,1)S(1)}, u32[]{:S(2)}, u32[]{:S(2)}) collective-permute-start(bf16[256,512]{1,0:T(8,128)(2,1)S(1)} %fusion.20), channel_id=1, source_target_pairs={{0,1},{1,2},{2,3},{3,4},{4,5},{5,6},{6,7},{7,0},{8,9},{9,10},{10,1... | collective-permute-start | bytes 786440 | tf_op jit(solution)/shard_map/ppermute | solution.py:30
  263.6 21.2 %collective-permute-start.26 = (bf16[256,512]{1,0:T(8,128)(2,1)S(1)}, bf16[256,512]{1,0:T(8,128)(2,1)S(1)}, u32[]{:S(2)}, u32[]{:S(2)}) collective-permute-start(bf16[256,512]{1,0:T(8,128)(2,1)S(1)} %fusion.15), channel_id=1, source_target_pairs={{0,7},{1,0},{2,1},{3,2},{4,3},{5,4},{6,5},{7,6},{8,15},{9,8},{10,9... | collective-permute-start | bytes 786440 | tf_op jit(solution)/shard_map/ppermute | solution.py:30
  267.2 11.4 %collective-permute-start.34 = (bf16[256,512]{1,0:T(8,128)(2,1)S(1)}, bf16[256,512]{1,0:T(8,128)(2,1)S(1)}, u32[]{:S(2)}, u32[]{:S(2)}) collective-permute-start(bf16[256,512]{1,0:T(8,128)(2,1)S(1)} %fusion.22), channel_id=1, source_target_pairs={{0,7},{1,0},{2,1},{3,2},{4,3},{5,4},{6,5},{7,6},{8,15},{9,8},{10,9... | collective-permute-start | bytes 786440 | tf_op jit(solution)/shard_map/ppermute | solution.py:30
  273.7 10.7 %collective-permute-start.30 = (bf16[256,512]{1,0:T(8,128)(2,1)S(1)}, bf16[256,512]{1,0:T(8,128)(2,1)S(1)}, u32[]{:S(2)}, u32[]{:S(2)}) collective-permute-start(bf16[256,512]{1,0:T(8,128)(2,1)S(1)} %fusion.19), channel_id=1, source_target_pairs={{0,1},{1,2},{2,3},{3,4},{4,5},{5,6},{6,7},{7,0},{8,9},{9,10},{10,1... | collective-permute-start | bytes 786440 | tf_op jit(solution)/shard_map/ppermute | solution.py:30
  274.4 20.5 %copy-start.5 = (bf16[512,512]{1,0:T(8,128)(2,1)S(1)}, bf16[512,512]{1,0:T(8,128)(2,1)}, u32[]{:S(2)}) copy-start(bf16[512,512]{1,0:T(8,128)(2,1)} %param.8) | copy-start | bytes 1572868
  274.4 15.6 %collective-permute-start.22 = (bf16[256,512]{1,0:T(8,128)(2,1)S(1)}, bf16[256,512]{1,0:T(8,128)(2,1)S(1)}, u32[]{:S(2)}, u32[]{:S(2)}) collective-permute-start(bf16[256,512]{1,0:T(8,128)(2,1)S(1)} %fusion.12), channel_id=1, source_target_pairs={{0,1},{1,2},{2,3},{3,4},{4,5},{5,6},{6,7},{7,0},{8,9},{9,10},{10,1... | collective-permute-start | bytes 786440 | tf_op jit(solution)/shard_map/ppermute | solution.py:30
  279.0 11.3 %collective-permute-start.35 = (bf16[256,512]{1,0:T(8,128)(2,1)S(1)}, bf16[256,512]{1,0:T(8,128)(2,1)S(1)}, u32[]{:S(2)}, u32[]{:S(2)}) collective-permute-start(bf16[256,512]{1,0:T(8,128)(2,1)S(1)} %fusion.21), channel_id=1, source_target_pairs={{0,7},{1,0},{2,1},{3,2},{4,3},{5,4},{6,5},{7,6},{8,15},{9,8},{10,9... | collective-permute-start | bytes 786440 | tf_op jit(solution)/shard_map/ppermute | solution.py:30
  284.7 9.8 %collective-permute-start.31 = (bf16[256,512]{1,0:T(8,128)(2,1)S(1)}, bf16[256,512]{1,0:T(8,128)(2,1)S(1)}, u32[]{:S(2)}, u32[]{:S(2)}) collective-permute-start(bf16[256,512]{1,0:T(8,128)(2,1)S(1)} %fusion.18), channel_id=1, source_target_pairs={{0,1},{1,2},{2,3},{3,4},{4,5},{5,6},{6,7},{7,0},{8,9},{9,10},{10,1... | collective-permute-start | bytes 786440 | tf_op jit(solution)/shard_map/ppermute | solution.py:30
  (1 other events, 1.4 us)

commit v6 on v5

--- a/solution.py
+++ b/solution.py
@@ -1,3 +1,4 @@
+import functools
 import math
 
 import jax
@@ -30,37 +31,92 @@
     return lax.ppermute(block, "mp", [(i, (i + distance) % size) for i in range(size)])
 
 
+def near_kernel(starts_ref, gain_ref, w_ref, *refs):
+    blocks, (product_ref, squares_ref) = refs[:-2], refs[-2:]
+    for i, block_ref in enumerate(blocks):
+        width = block_ref.shape[1]
+        start = pl.multiple_of(starts_ref[i], width)
+        wide = block_ref[...].astype(f32)
+        scaled = (wide * gain_ref[:, pl.ds(start, width)]).astype(bf16)
+        squares = wide * wide
+        squares = sum(squares[:, c:c + LANES] for c in range(0, width, LANES))
+        product = jnp.dot(scaled, w_ref[pl.ds(start, width), :], preferred_element_type=f32)
+        if i == 0:
+            product_ref[...] = product
+            squares_ref[...] = squares
+        else:
+            product_ref[...] += product
+            squares_ref[...] += squares
+
+
+def far_kernel(features, place_ref, gain_ref, w_ref, up_ref, down_ref, product_ref, squares_ref, out_ref):
+    half = up_ref.shape[0]
+    for i, block_ref in enumerate((up_ref, down_ref)):
+        rows = pl.ds(i * half, half)
+        wide = block_ref[...].astype(f32)
+        scaled = (wide * gain_ref[...]).astype(bf16)
+        mean = jnp.sum(wide * wide, axis=1, keepdims=True)
+        mean = (mean + jnp.sum(squares_ref[rows, :], axis=1, keepdims=True)) / features
+        product = jnp.dot(scaled, w_ref[...], preferred_element_type=f32)
+        product = (product + product_ref[rows, :]) * lax.rsqrt(mean + eps)
+        out_ref[rows, :] = product.astype(bf16)
+
+
 def project(hidden, norm_gain, w_query):
     size = lax.axis_size("mp")
     me = lax.axis_index("mp")
     rows, width = hidden.shape
     half = rows // 2
     far = size // 2
-
-    def weights(offset):
-        start = (me + offset) % size * width
-        gain = lax.dynamic_slice(norm_gain, (start,), (width,))
-        part = lax.dynamic_slice(w_query, (start, 0), (width, w_query.shape[1]))
-        return (part.astype(f32) * gain[:, None]).astype(bf16)
-
-    def terms(block, offset):
-        wide = block.astype(f32)
-        squares = jnp.sum(wide * wide, axis=1, keepdims=True)
-        return squares, jnp.dot(block, weights(offset), preferred_element_type=f32)
-
-    squares, product = terms(hidden, 0)
+    smem = pl.BlockSpec(memory_space=pltpu.SMEM)
+    vmem = pl.BlockSpec(memory_space=pltpu.VMEM)
+    gain = norm_gain.reshape(1, -1)
+    offsets = [0]
+    near = [hidden]
     up = down = hidden
     for step in range(1, far):
         up, down = turned(up, 1), turned(down, -1)
-        for block, offset in ((up, -step), (down, step)):
-            more = terms(block, offset)
-            squares, product = squares + more[0], product + more[1]
+        near += [up, down]
+        offsets += [-step, step]
     nearly = up
-    last = jnp.concatenate([turned(up[:half], 1), turned(down[half:], -1)], axis=0)
-    more = terms(last, far)
-    squares, product = squares + more[0], product + more[1]
-    total = size * width
-    return (product * lax.rsqrt(squares / total + eps)).astype(bf16), nearly
+    up, down = turned(up[:half], 1), turned(down[half:], -1)
+    order = jnp.asarray(offsets, jnp.int32)
+    product, squares = pl.pallas_call(
+        near_kernel,
+        out_shape=[
+            jax.ShapeDtypeStruct((rows, w_query.shape[1]), f32),
+            jax.ShapeDtypeStruct((rows, LANES), f32),
+        ],
+        in_specs=[smem] + [vmem] * (2 + len(near)),
+        out_specs=[vmem, vmem],
+        cost_estimate=pl.CostEstimate(
+            flops=2 * rows * w_query.size, bytes_accessed=4 * w_query.size, transcendentals=0
+        ),
+        name="near",
+    )((me + order) % size * width, gain, w_query, *near)
+    inner = w_query.shape[1]
+    queries = pl.pallas_call(
+        functools.partial(far_kernel, size * width),
+        out_shape=jax.ShapeDtypeStruct((rows, inner), bf16),
+        grid_spec=pltpu.PrefetchScalarGridSpec(
+            num_scalar_prefetch=1,
+            grid=(1,),
+            in_specs=[
+                pl.BlockSpec((1, width), lambda i, place: (0, place[0])),
+                pl.BlockSpec((width, inner), lambda i, place: (place[0], 0)),
+                pl.BlockSpec((half, width), lambda i, place: (0, 0)),
+                pl.BlockSpec((half, width), lambda i, place: (0, 0)),
+                pl.BlockSpec((rows, inner), lambda i, place: (0, 0)),
+                pl.BlockSpec((rows, LANES), lambda i, place: (0, 0)),
+            ],
+            out_specs=pl.BlockSpec((rows, inner), lambda i, place: (0, 0)),
+        ),
+        cost_estimate=pl.CostEstimate(
+            flops=2 * rows * width * inner, bytes_accessed=4 * width * inner, transcendentals=0
+        ),
+        name="far",
+    )((me + jnp.full((1,), far, jnp.int32)) % size, gain, w_query, up, down, product, squares)
+    return queries, nearly
 
 
 def output(placed, w_out):
@@ -84,12 +140,66 @@
     for offset in range(far - 1, 0, -1):
         one = term(placed, offset) + up.astype(f32)
         two = term(placed, -offset) + down.astype(f32)
-        up, down = turned(one.astype(bf16), 1), turned(two.astype(bf16), -1)
-    return term(placed, 0) + up.astype(f32) + down.astype(f32)
+        late = one.astype(bf16), two.astype(bf16)
+        up, down = turned(late[0], 1), turned(late[1], -1)
+    return term(placed, 0) + up.astype(f32) + down.astype(f32), late
+
+
+def place_kernel(turn, source_ref, ids_ref, blocks_ref, next_ref, out_ref, group_ref):
+    peers, rows, width = out_ref.shape
+    spans, count, _ = blocks_ref.shape
+    step = pl.program_id(0)
+
+    @pl.when(step == 0)
+    def _():
+        for s in range(spans):
+            rest = blocks_ref[s + 1] if s + 1 < spans else next_ref[0]
+            if turn:
+                position = lax.broadcasted_iota(jnp.int32, (count, width), 0)
+                rest = jnp.where(position == count - 1, blocks_ref[s], rest)
+            group_ref[s] = rest
+
+    for p in range(peers):
+        for j in range(SLOTS):
+            slot = (step * peers + p) * SLOTS + j
+            out_ref[p, pl.ds(j * count, count), :] = group_ref[source_ref[slot]]
+        if rows > SLOTS * count:
+            lane = lax.broadcasted_iota(jnp.int32, (STATS, width), 1)
+            slot = (step * peers + p) * SLOTS
+            line = jnp.where(lane == 0, ids_ref[slot], jnp.where(lane == 1, ids_ref[slot + 1], 0))
+            out_ref[p, pl.ds(SLOTS * count, STATS), :] = line.astype(f32).astype(bf16)
+
+
+def place(turn, with_ids, source_span, ids, blocks, following):
+    spans, count, width = blocks.shape
+    slots = source_span.shape[0]
+    peer_count = slots // SLOTS
+    step = 8
+    rows = SLOTS * count + (STATS if with_ids else 0)
+    return pl.pallas_call(
+        functools.partial(place_kernel, turn),
+        out_shape=jax.ShapeDtypeStruct((peer_count, rows, width), bf16),
+        grid_spec=pltpu.PrefetchScalarGridSpec(
+            num_scalar_prefetch=2,
+            grid=(peer_count // step,),
+            in_specs=[
+                pl.BlockSpec((spans, count, width), lambda i, source, ids: (0, 0, 0)),
+                pl.BlockSpec((1, count, width), lambda i, source, ids: (0, 0, 0)),
+            ],
+            out_specs=pl.BlockSpec((step, rows, width), lambda i, source, ids: (i, 0, 0)),
+            scratch_shapes=[pltpu.VMEM((spans, count, width), bf16)],
+        ),
+        compiler_params=pltpu.CompilerParams(dimension_semantics=("arbitrary",)),
+        cost_estimate=pl.CostEstimate(
+            flops=0, bytes_accessed=2 * peer_count * rows * width, transcendentals=0
+        ),
+        name="place",
+    )(source_span, ids, blocks, following)
 
 
 def attend_kernel(ids_ref, q_ref, k_ref, v_ref, out_ref):
-    peers, rows, width = q_ref.shape
+    peers, rows, width = out_ref.shape
+    rows -= STATS
     count = rows // SLOTS
     together = LANES // count
     groups = width // HS // together
@@ -141,7 +251,8 @@
 
 
 def attend(ids, asked, keys, values):
-    peer_count, rows, width = asked.shape
+    peer_count, given, width = asked.shape
+    rows = SLOTS * (SPAN // PARTS)
     step = 4
     stored, tokens, _ = keys.shape
     slots = peer_count * SLOTS
@@ -152,7 +263,7 @@
             num_scalar_prefetch=1,
             grid=(peer_count // step,),
             in_specs=[
-                pl.BlockSpec((step, rows, width), lambda i, ids: (i, 0, 0)),
+                pl.BlockSpec((step, given, width), lambda i, ids: (i, 0, 0)),
                 pl.BlockSpec((stored, tokens, width), lambda i, ids: (0, 0, 0)),
                 pl.BlockSpec((stored, tokens, width), lambda i, ids: (0, 0, 0)),
             ],
@@ -258,11 +369,7 @@
     target = jnp.where(is_live, owners * SLOTS + slot_rank, -1)
     slot_match = target[:, None] == jnp.arange(peer_count * SLOTS, dtype=jnp.int32)[None, :]
     request_table = jnp.sum(jnp.where(slot_match, slot_ids[:, None], 0), axis=0)
-    request_table = request_table.reshape(peer_count, SLOTS)
     source_span = jnp.sum(jnp.where(slot_match, req_order[:, None] // 2, 0), axis=0)
-    wanted = lax.all_to_all(request_table, "dp", split_axis=0, concat_axis=0, tiled=True)
-    wanted = wanted.reshape(-1)
-
     def is_last(i):
         position = i * count + lax.broadcasted_iota(jnp.int32, (1, count, 1), 1)
         return position == SPAN - 1
@@ -271,10 +378,8 @@
         queries, nearly = project(piece, norm_gain, w_query)
         blocks = queries.reshape(span_dev, count, inner_width)
         following = shifted(blocks[:1], "dp", -1)
-        grouped = jnp.concatenate([blocks[1:], following], axis=0)
-        if (i + 1) * count == SPAN:
-            grouped = jnp.where(is_last(i), blocks, grouped)
-        return grouped[source_span].reshape(peer_count, SLOTS * count, inner_width), nearly
+        turn = (i + 1) * count == SPAN
+        return place(turn, i == 0, source_span, request_table, blocks, following), nearly
 
     def exchange(rows):
         return lax.all_to_all(rows, "dp", split_axis=0, concat_axis=0, tiled=True)
@@ -286,20 +391,25 @@
         if (i + 1) * count == SPAN:
             placed = jnp.where(is_last(i), merged, placed)
         placed = placed.reshape(-1, inner_width)
-        return output(placed, w_out).reshape(span_dev, count, width)
+        summed, late = output(placed, w_out)
+        return summed.reshape(span_dev, count, width), late
 
     sent_0, nearly = request(0, pieces[0])
-    piece_1, _, wanted = lax.optimization_barrier((pieces[1], nearly, wanted))
+    piece_1, _ = lax.optimization_barrier((pieces[1], nearly))
     asked_0 = exchange(sent_0)
     sent_1, _ = request(1, piece_1)
     asked_0, sent_1 = lax.optimization_barrier((asked_0, sent_1))
     asked_1 = exchange(sent_1)
+    wanted = asked_0[:, SLOTS * count, :SLOTS].astype(f32).astype(jnp.int32).reshape(-1)
     answers_0 = attend(wanted, asked_0, nb_keys, nb_values)
     back_0 = exchange(answers_0)
     answers_1 = attend(wanted, asked_1, nb_keys, nb_values)
     back_0, answers_1 = lax.optimization_barrier((back_0, answers_1))
     back_1 = exchange(answers_1)
-    summed = jnp.concatenate([finish(0, back_0), finish(1, back_1)], axis=1)
+    summed_0, late = finish(0, back_0)
+    back_1, _ = lax.optimization_barrier((back_1, late))
+    summed_1, _ = finish(1, back_1)
+    summed = jnp.concatenate([summed_0, summed_1], axis=1)
     return hidden.astype(f32) + summed.reshape(tok_rows, width)
 
 

time: 302 us -> 308 us (1.020)
  Pallas kernels: 29.1 us -> 50.2 us
  starting transfers between devices: 110 us -> 104 us
  matrix products: 23.4 us -> 18.9 us
    pallas_call x0 -> x6, Pallas kernels: none -> 21.1 us  [the longest x2 9.27 us: project(): pl.pallas_call(near_kernel, out_shape=[jax.ShapeDtypeStruct((rows, w_quer...]
    dot_general x16 -> x0, matrix products: 12.6 us -> none  [terms(): jnp.dot(block, weights(offset), preferred_element_type=f32)]
    dot_general x16, matrix products: 10.8 us -> 18.9 us  [term(): return jnp.dot(block, part, preferred_element_type=f32)]
    all_to_all x1 -> x0, starting transfers between devices: 7.33 us -> none  [shards(): lax.all_to_all(request_table, 'dp', split_axis=0, concat_axis=0, tiled=True)]
    gather x2 -> x0, local copies, waits for them, and re-layouts: 4 us -> none  [request(): grouped[source_span].reshape(peer_count, SLOTS * count, inner_width)]
  transfers between devices with their start and end apart: 41 -> 40, of which waited for: 20 -> 25; matrix products, arithmetic and copies ran while one was open for 13% -> 8% of each run, Pallas kernels for 10% -> 13%
where the time goes in v6:
time: 308 us; the launch traced here: 303 us
  waiting for transfers between devices  109 us (35%)
  starting transfers between devices  104 us (34%)
  Pallas kernels  50.2 us (16%)
  matrix products  18.9 us (6%)
  local copies, waits for them, and re-layouts  13.6 us (4%)
  other arithmetic  5.71 us (2%)
    ppermute x32, starting transfers between devices, turned(): lax.ppermute(block, 'mp', [(i, (i + distance) % size) for i in range(size)])  60.6 us
    ppermute x32, waiting for transfers between devices, turned(): lax.ppermute(block, 'mp', [(i, (i + distance) % size) for i in range(size)])  54.7 us
    all_to_all x4, starting transfers between devices, exchange(): return lax.all_to_all(rows, 'dp', split_axis=0, concat_axis=0, tiled=True)  35.3 us
    all_to_all x4, waiting for transfers between devices, exchange(): return lax.all_to_all(rows, 'dp', split_axis=0, concat_axis=0, tiled=True)  29.9 us
    ppermute x4, waiting for transfers between devices, shifted(): return lax.ppermute(block, axis, route)  24.7 us
    pallas_call x2, Pallas kernels, attend(): pl.pallas_call(attend_kernel, out_shape=jax.ShapeDtypeStruct((peer_count,...  22.1 us
    dot_general x16, matrix products, term(): return jnp.dot(block, part, preferred_element_type=f32)  18.9 us
    pallas_call x2, Pallas kernels, project(): pl.pallas_call(near_kernel, out_shape=[jax.ShapeDtypeStruct((rows, w_quer...  9.27 us
  transfers between devices with their start and end apart: 40, of which 25 were waited for; matrix products, arithmetic and copies ran while one was open for 8% of the time, Pallas kernels for 13%

profile of v6, /device:TPU:28, one launch (start us, length us, event | category | flops | bytes accessed | tf_op | source)
XLA Modules:
  0.0 302.9 jit_solution(16091955906118303318)
XLA Ops:
  1.1 5.9 %collective-permute-start.4 = (bf16[256,512]{1,0:T(8,128)(2,1)S(1)}, bf16[256,512]{1,0:T(8,128)(2,1)S(1)}, u32[]{:S(2)}, u32[]{:S(2)}) collective-permute-start(bf16[256,512]{1,0:T(8,128)(2,1)S(1)} %bitcast.59), channel_id=1, source_target_pairs={{0,7},{1,0},{2,1},{3,2},{4,3},{5,4},{6,5},{7,6},{8,15},{9,8},{10,9... | collective-permute-start | bytes 786440 | tf_op jit(solution)/shard_map/ppermute | solution.py:31
  7.7 4.9 %collective-permute-done.4.refs_2_ = bf16[256,512]{1,0:T(8,128)(2,1)S(1)} collective-permute-done((bf16[256,512]{1,0:T(8,128)(2,1)S(1)}, bf16[256,512]{1,0:T(8,128)(2,1)S(1)}, u32[]{:S(2)}, u32[]{:S(2)}) %collective-permute-start.4) | collective-permute-done | bytes 262176 | tf_op jit(solution)/shard_map/ppermute | solution.py:31
  12.6 3.7 %collective-permute-start.5 = (bf16[256,512]{1,0:T(8,128)(2,1)S(1)}, bf16[256,512]{1,0:T(8,128)(2,1)S(1)}, u32[]{:S(2)}, u32[]{:S(2)}) collective-permute-start(bf16[256,512]{1,0:T(8,128)(2,1)S(1)} %collective-permute-done.4.refs_2_), channel_id=1, source_target_pairs={{0,7},{1,0},{2,1},{3,2},{4,3},{5,4},{6,5},{7,6},{8,15},{9,8},{10,9... | collective-permute-start | bytes 786440 | tf_op jit(solution)/shard_map/ppermute | solution.py:31
  17.3 3.7 %collective-permute-done.5.refs_4_ = bf16[256,512]{1,0:T(8,128)(2,1)S(1)} collective-permute-done((bf16[256,512]{1,0:T(8,128)(2,1)S(1)}, bf16[256,512]{1,0:T(8,128)(2,1)S(1)}, u32[]{:S(2)}, u32[]{:S(2)}) %collective-permute-start.5) | collective-permute-done | bytes 262176 | tf_op jit(solution)/shard_map/ppermute | solution.py:31
  21.0 3.7 %collective-permute-start.6 = (bf16[256,512]{1,0:T(8,128)(2,1)S(1)}, bf16[256,512]{1,0:T(8,128)(2,1)S(1)}, u32[]{:S(2)}, u32[]{:S(2)}) collective-permute-start(bf16[256,512]{1,0:T(8,128)(2,1)S(1)} %collective-permute-done.5.refs_4_), channel_id=1, source_target_pairs={{0,7},{1,0},{2,1},{3,2},{4,3},{5,4},{6,5},{7,6},{8,15},{9,8},{10,9... | collective-permute-start | bytes 786440 | tf_op jit(solution)/shard_map/ppermute | solution.py:31
  25.5 3.1 %collective-permute-done.6.refs_6_ = bf16[256,512]{1,0:T(8,128)(2,1)S(1)} collective-permute-done((bf16[256,512]{1,0:T(8,128)(2,1)S(1)}, bf16[256,512]{1,0:T(8,128)(2,1)S(1)}, u32[]{:S(2)}, u32[]{:S(2)}) %collective-permute-start.6) | collective-permute-done | bytes 262176 | tf_op jit(solution)/shard_map/ppermute | solution.py:31
  28.6 3.8 %collective-permute-start.7 = (bf16[128,512]{1,0:T(8,128)(2,1)S(1)}, bf16[128,512]{1,0:T(8,128)(2,1)S(1)}, u32[]{:S(2)}, u32[]{:S(2)}) collective-permute-start(bf16[128,512]{1,0:T(8,128)(2,1)S(1)} %slice.78), channel_id=1, source_target_pairs={{0,7},{1,0},{2,1},{3,2},{4,3},{5,4},{6,5},{7,6},{8,15},{9,8},{10,9... | collective-permute-start | bytes 393224 | tf_op jit(solution)/shard_map/ppermute | solution.py:31
  33.9 4.6 %near.2 = (f32[256,512]{1,0:T(8,128)}, f32[256,128]{1,0:T(8,128)}) custom-call(s32[7]{0:T(128)} %fusion.48.starts_ref, f32[1,4096]{1,0:T(1,128)} %bitcast.62, bf16[4096,512]{1,0:T(8,128)(2,1)} %w_ref.7, bf16[256,512]{1,0:T(8,128)(2,1)} %bitcast.61, bf16[256,512]{1,0:T(8,128)(2,1)} %copy-done.12, bf16[256,512]{1,0:T(8,128)(2,1)} %copy-done.11, ...), custom_call_target="tpu_custom_call" | custom-call | flops 1073741824 | bytes 8388608 | tf_op jit(solution)/shard_map/near/pallas_call | solution.py:84
  39.3 2.3 far.2
  46.5 3.6 %place.2 = bf16[32,72,512]{2,1,0:T(8,128)(2,1)} custom-call(s32[64]{0:T(128)} %get-tuple-element.26.source_ref, s32[64]{0:T(128)} %get-tuple-element.25.ids_ref, bf16[8,32,512]{2,1,0:T(8,128)(2,1)} %bitcast.54, bf16[1,32,512]{2,1,0:T(8,128)(2,1)} %copy-done.22), custom_call_target="tpu_custom_call" | custom-call | bytes 2359296 | tf_op jit(solution)/shard_map/place/pallas_call | solution.py:179
  50.1 8.2 %all-to-all-start = ((bf16[32,72,512]{2,1,0:T(8,128)(2,1)}), bf16[32,72,512]{2,1,0:T(8,128)(2,1)S(1)}, u32[]{:S(2)}, u32[]{:S(2)}) async-start(bf16[32,72,512]{2,1,0:T(8,128)(2,1)} %place.2), calls=%async_computation | async-start | bytes 4718592 | tf_op jit(solution)/shard_map/all_to_all | solution.py:385
  58.4 3.3 %collective-permute-start.13 = (bf16[256,512]{1,0:T(8,128)(2,1)S(1)}, bf16[256,512]{1,0:T(8,128)(2,1)S(1)}, u32[]{:S(2)}, u32[]{:S(2)}) collective-permute-start(bf16[256,512]{1,0:T(8,128)(2,1)S(1)} %bitcast.56), channel_id=1, source_target_pairs={{0,7},{1,0},{2,1},{3,2},{4,3},{5,4},{6,5},{7,6},{8,15},{9,8},{10,9... | collective-permute-start | bytes 786440 | tf_op jit(solution)/shard_map/ppermute | solution.py:31
  61.7 5.8 %collective-permute-done.13.refs_2_ = bf16[256,512]{1,0:T(8,128)(2,1)S(1)} collective-permute-done((bf16[256,512]{1,0:T(8,128)(2,1)S(1)}, bf16[256,512]{1,0:T(8,128)(2,1)S(1)}, u32[]{:S(2)}, u32[]{:S(2)}) %collective-permute-start.13) | collective-permute-done | bytes 262176 | tf_op jit(solution)/shard_map/ppermute | solution.py:31
  67.5 3.7 %collective-permute-start.14 = (bf16[256,512]{1,0:T(8,128)(2,1)S(1)}, bf16[256,512]{1,0:T(8,128)(2,1)S(1)}, u32[]{:S(2)}, u32[]{:S(2)}) collective-permute-start(bf16[256,512]{1,0:T(8,128)(2,1)S(1)} %collective-permute-done.13.refs_2_), channel_id=1, source_target_pairs={{0,7},{1,0},{2,1},{3,2},{4,3},{5,4},{6,5},{7,6},{8,15},{9,8},{10,9... | collective-permute-start | bytes 786440 | tf_op jit(solution)/shard_map/ppermute | solution.py:31
  71.2 5.0 %collective-permute-done.14.refs_4_ = bf16[256,512]{1,0:T(8,128)(2,1)S(1)} collective-permute-done((bf16[256,512]{1,0:T(8,128)(2,1)S(1)}, bf16[256,512]{1,0:T(8,128)(2,1)S(1)}, u32[]{:S(2)}, u32[]{:S(2)}) %collective-permute-start.14) | collective-permute-done | bytes 262176 | tf_op jit(solution)/shard_map/ppermute | solution.py:31
  76.2 3.7 %collective-permute-start.15 = (bf16[256,512]{1,0:T(8,128)(2,1)S(1)}, bf16[256,512]{1,0:T(8,128)(2,1)S(1)}, u32[]{:S(2)}, u32[]{:S(2)}) collective-permute-start(bf16[256,512]{1,0:T(8,128)(2,1)S(1)} %collective-permute-done.14.refs_4_), channel_id=1, source_target_pairs={{0,7},{1,0},{2,1},{3,2},{4,3},{5,4},{6,5},{7,6},{8,15},{9,8},{10,9... | collective-permute-start | bytes 786440 | tf_op jit(solution)/shard_map/ppermute | solution.py:31
  80.0 4.0 %collective-permute-done.15.refs_6_ = bf16[256,512]{1,0:T(8,128)(2,1)S(1)} collective-permute-done((bf16[256,512]{1,0:T(8,128)(2,1)S(1)}, bf16[256,512]{1,0:T(8,128)(2,1)S(1)}, u32[]{:S(2)}, u32[]{:S(2)}) %collective-permute-start.15) | collective-permute-done | bytes 262176 | tf_op jit(solution)/shard_map/ppermute | solution.py:31
  84.7 3.7 %collective-permute-start.16 = (bf16[128,512]{1,0:T(8,128)(2,1)}, bf16[128,512]{1,0:T(8,128)(2,1)S(1)}, u32[]{:S(2)}, u32[]{:S(2)}) collective-permute-start(bf16[128,512]{1,0:T(8,128)(2,1)} %slice.82), channel_id=1, source_target_pairs={{0,7},{1,0},{2,1},{3,2},{4,3},{5,4},{6,5},{7,6},{8,15},{9,8},{10,9... | collective-permute-start | bytes 393224 | tf_op jit(solution)/shard_map/ppermute | solution.py:31
  89.2 4.6 %near.3 = (f32[256,512]{1,0:T(8,128)}, f32[256,128]{1,0:T(8,128)}) custom-call(s32[7]{0:T(128)} %fusion.48.starts_ref, f32[1,4096]{1,0:T(1,128)} %bitcast.64, bf16[4096,512]{1,0:T(8,128)(2,1)} %w_ref.7, bf16[256,512]{1,0:T(8,128)(2,1)} %bitcast.58, bf16[256,512]{1,0:T(8,128)(2,1)} %copy-done.16, bf16[256,512]{1,0:T(8,128)(2,1)} %copy-done.15, ...), custom_call_target="tpu_custom_call" | custom-call | flops 1073741824 | bytes 8388608 | tf_op jit(solution)/shard_map/near/pallas_call | solution.py:84
  95.7 2.3 far.3
  102.9 3.5 %place.3 = bf16[32,64,512]{2,1,0:T(8,128)(2,1)} custom-call(s32[64]{0:T(128)} %get-tuple-element.26.source_ref, s32[64]{0:T(128)} %get-tuple-element.25.ids_ref, bf16[8,32,512]{2,1,0:T(8,128)(2,1)} %bitcast.55, bf16[1,32,512]{2,1,0:T(8,128)(2,1)} %copy-done.23), custom_call_target="tpu_custom_call" | custom-call | bytes 2097152 | tf_op jit(solution)/shard_map/place/pallas_call | solution.py:179
  106.4 8.3 %all-to-all-start.2 = ((bf16[32,64,512]{2,1,0:T(8,128)(2,1)}), bf16[32,64,512]{2,1,0:T(8,128)(2,1)}, u32[]{:S(2)}, u32[]{:S(2)}) async-start(bf16[32,64,512]{2,1,0:T(8,128)(2,1)} %place.3), calls=%async_computation.2 | async-start | bytes 4194304 | tf_op jit(solution)/shard_map/all_to_all | solution.py:385
  115.4 11.1 %attend.2 = bf16[32,72,512]{2,1,0:T(8,128)(2,1)} custom-call(s32[64]{0:T(128)} %convert_element_type.112.ids_ref, bf16[32,72,512]{2,1,0:T(8,128)(2,1)} %copy-done.3, bf16[8,128,512]{2,1,0:T(8,128)(2,1)} %k_ref.3, bf16[8,128,512]{2,1,0:T(8,128)(2,1)} %v_ref.3), custom_call_target="tpu_custom_call" | custom-call | flops 2147483648 | bytes 4194304 | tf_op jit(solution)/shard_map/attend/pallas_call | solution.py:259
  126.5 13.0 %all-to-all-done.2.q_ref = bf16[32,64,512]{2,1,0:T(8,128)(2,1)} async-done(((bf16[32,64,512]{2,1,0:T(8,128)(2,1)}), bf16[32,64,512]{2,1,0:T(8,128)(2,1)}, u32[]{:S(2)}, u32[]{:S(2)}) %all-to-all-start.2) | async-done | bytes 2097184 | tf_op jit(solution)/shard_map/all_to_all | solution.py:385
  139.5 9.4 %all-to-all-start.1 = ((bf16[32,72,512]{2,1,0:T(8,128)(2,1)}), bf16[32,72,512]{2,1,0:T(8,128)(2,1)S(1)}, u32[]{:S(2)}, u32[]{:S(2)}) async-start(bf16[32,72,512]{2,1,0:T(8,128)(2,1)} %attend.2), calls=%async_computation.1 | async-start | bytes 4718592 | tf_op jit(solution)/shard_map/all_to_all | solution.py:385
  148.9 11.0 %attend.3 = bf16[32,72,512]{2,1,0:T(8,128)(2,1)} custom-call(s32[64]{0:T(128)} %convert_element_type.112.ids_ref, bf16[32,64,512]{2,1,0:T(8,128)(2,1)} %all-to-all-done.2.q_ref, bf16[8,128,512]{2,1,0:T(8,128)(2,1)} %k_ref.3, bf16[8,128,512]{2,1,0:T(8,128)(2,1)} %v_ref.3), custom_call_target="tpu_custom_call" | custom-call | flops 2147483648 | bytes 4194304 | tf_op jit(solution)/shard_map/attend/pallas_call | solution.py:259
  159.9 16.9 %all-to-all-done.1.back_ref = bf16[32,72,512]{2,1,0:T(8,128)(2,1)S(1)} async-done(((bf16[32,72,512]{2,1,0:T(8,128)(2,1)}), bf16[32,72,512]{2,1,0:T(8,128)(2,1)S(1)}, u32[]{:S(2)}, u32[]{:S(2)}) %all-to-all-start.1) | async-done | bytes 2359328 | tf_op jit(solution)/shard_map/all_to_all | solution.py:385
  178.3 9.3 %all-to-all-start.3 = ((bf16[32,72,512]{2,1,0:T(8,128)(2,1)}), bf16[32,72,512]{2,1,0:T(8,128)(2,1)S(1)}, u32[]{:S(2)}, u32[]{:S(2)}) async-start(bf16[32,72,512]{2,1,0:T(8,128)(2,1)} %attend.3), calls=%async_computation.3 | async-start | bytes 4718592 | tf_op jit(solution)/shard_map/all_to_all | solution.py:385
  187.6 3.6 %combine.2 = bf16[8,32,512]{2,1,0:T(8,128)(2,1)} custom-call(s32[16]{0:T(128)} %copy-done.24, s32[16]{0:T(128)} %get-tuple-element.36.rank_ref, s32[1]{0:T(128)} %copy.17.live_ref, bf16[32,72,512]{2,1,0:T(8,128)(2,1)} %copy-done.2), custom_call_target="tpu_custom_call" | custom-call | flops 1048576 | bytes 786432 | tf_op jit(solution)/shard_map/combine/pallas_call | solution.py:327
  194.9 19.9 %collective-permute-done.18 = bf16[1,32,512]{2,1,0:T(8,128)(2,1)S(1)} collective-permute-done((bf16[1,32,512]{2,1,0:T(8,128)(2,1)S(1)}, bf16[1,32,512]{2,1,0:T(8,128)(2,1)S(1)}, u32[]{:S(2)}, u32[]{:S(2)}) %collective-permute-start.18) | collective-permute-done | bytes 32800 | tf_op jit(solution)/shard_map/ppermute | solution.py:26
  216.3 3.2 %collective-permute-start.23 = (bf16[128,512]{1,0:T(8,128)(2,1)S(1)}, bf16[128,512]{1,0:T(8,128)(2,1)S(1)}, u32[]{:S(2)}, u32[]{:S(2)}) collective-permute-start(bf16[128,512]{1,0:T(8,128)(2,1)S(1)} %get-tuple-element.31), channel_id=1, source_target_pairs={{0,7},{1,0},{2,1},{3,2},{4,3},{5,4},{6,5},{7,6},{8,15},{9,8},{10,9... | collective-permute-start | bytes 393224 | tf_op jit(solution)/shard_map/ppermute | solution.py:31
  219.5 4.2 %collective-permute-done.19 = bf16[128,512]{1,0:T(8,128)(2,1)S(1)} collective-permute-done((bf16[128,512]{1,0:T(8,128)(2,1)S(1)}, bf16[128,512]{1,0:T(8,128)(2,1)S(1)}, u32[]{:S(2)}, u32[]{:S(2)}) %collective-permute-start.19) | collective-permute-done | bytes 131104 | tf_op jit(solution)/shard_map/ppermute | solution.py:31
  227.3 3.2 %collective-permute-start.24 = (bf16[256,512]{1,0:T(8,128)(2,1)}, bf16[256,512]{1,0:T(8,128)(2,1)S(1)}, u32[]{:S(2)}, u32[]{:S(2)}) collective-permute-start(bf16[256,512]{1,0:T(8,128)(2,1)} %fusion.7), channel_id=1, source_target_pairs={{0,7},{1,0},{2,1},{3,2},{4,3},{5,4},{6,5},{7,6},{8,15},{9,8},{10,9... | collective-permute-start | bytes 786440 | tf_op jit(solution)/shard_map/ppermute | solution.py:31
  230.5 4.1 %collective-permute-done.20 = bf16[256,512]{1,0:T(8,128)(2,1)S(1)} collective-permute-done((bf16[256,512]{1,0:T(8,128)(2,1)S(1)}, bf16[256,512]{1,0:T(8,128)(2,1)S(1)}, u32[]{:S(2)}, u32[]{:S(2)}) %collective-permute-start.20) | collective-permute-done | bytes 262176 | tf_op jit(solution)/shard_map/ppermute | solution.py:31
  236.2 2.1 fusion.6
  238.3 3.5 %collective-permute-start.25 = (bf16[256,512]{1,0:T(8,128)(2,1)}, bf16[256,512]{1,0:T(8,128)(2,1)}, u32[]{:S(2)}, u32[]{:S(2)}) collective-permute-start(bf16[256,512]{1,0:T(8,128)(2,1)} %fusion.6), channel_id=1, source_target_pairs={{0,7},{1,0},{2,1},{3,2},{4,3},{5,4},{6,5},{7,6},{8,15},{9,8},{10,9... | collective-permute-start | bytes 786440 | tf_op jit(solution)/shard_map/ppermute | solution.py:31
  241.8 3.0 %collective-permute-done.21 = bf16[256,512]{1,0:T(8,128)(2,1)} collective-permute-done((bf16[256,512]{1,0:T(8,128)(2,1)S(1)}, bf16[256,512]{1,0:T(8,128)(2,1)}, u32[]{:S(2)}, u32[]{:S(2)}) %collective-permute-start.21) | collective-permute-done | bytes 262176 | tf_op jit(solution)/shard_map/ppermute | solution.py:31
  249.6 3.5 %combine.3 = bf16[8,32,512]{2,1,0:T(8,128)(2,1)} custom-call(s32[16]{0:T(128)} %copy-done.24, s32[16]{0:T(128)} %get-tuple-element.36.rank_ref, s32[1]{0:T(128)} %copy.17.live_ref, bf16[32,72,512]{2,1,0:T(8,128)(2,1)} %copy-done.1), custom_call_target="tpu_custom_call" | custom-call | flops 1048576 | bytes 786432 | tf_op jit(solution)/shard_map/combine/pallas_call | solution.py:327
  257.1 2.3 collective-permute-done.27
  261.8 3.8 %collective-permute-start.32 = (bf16[128,512]{1,0:T(8,128)(2,1)S(1)}, bf16[128,512]{1,0:T(8,128)(2,1)S(1)}, u32[]{:S(2)}, u32[]{:S(2)}) collective-permute-start(bf16[128,512]{1,0:T(8,128)(2,1)S(1)} %get-tuple-element.30), channel_id=1, source_target_pairs={{0,7},{1,0},{2,1},{3,2},{4,3},{5,4},{6,5},{7,6},{8,15},{9,8},{10,9... | collective-permute-start | bytes 393224 | tf_op jit(solution)/shard_map/ppermute | solution.py:31
  265.6 2.5 collective-permute-done.32
  269.5 3.7 %collective-permute-start.33 = (bf16[256,512]{1,0:T(8,128)(2,1)S(1)}, bf16[256,512]{1,0:T(8,128)(2,1)S(1)}, u32[]{:S(2)}, u32[]{:S(2)}) collective-permute-start(bf16[256,512]{1,0:T(8,128)(2,1)S(1)} %fusion.13), channel_id=1, source_target_pairs={{0,7},{1,0},{2,1},{3,2},{4,3},{5,4},{6,5},{7,6},{8,15},{9,8},{10,9... | collective-permute-start | bytes 786440 | tf_op jit(solution)/shard_map/ppermute | solution.py:31
  274.6 2.7 collective-permute-done.33
  277.6 3.8 %collective-permute-start.34 = (bf16[256,512]{1,0:T(8,128)(2,1)S(1)}, bf16[256,512]{1,0:T(8,128)(2,1)S(1)}, u32[]{:S(2)}, u32[]{:S(2)}) collective-permute-start(bf16[256,512]{1,0:T(8,128)(2,1)S(1)} %fusion.12), channel_id=1, source_target_pairs={{0,7},{1,0},{2,1},{3,2},{4,3},{5,4},{6,5},{7,6},{8,15},{9,8},{10,9... | collective-permute-start | bytes 786440 | tf_op jit(solution)/shard_map/ppermute | solution.py:31
  283.2 3.2 %collective-permute-start.26 = (bf16[256,512]{1,0:T(8,128)(2,1)S(1)}, bf16[256,512]{1,0:T(8,128)(2,1)S(1)}, u32[]{:S(2)}, u32[]{:S(2)}) collective-permute-start(bf16[256,512]{1,0:T(8,128)(2,1)S(1)} %fusion.5), channel_id=1, source_target_pairs={{0,7},{1,0},{2,1},{3,2},{4,3},{5,4},{6,5},{7,6},{8,15},{9,8},{10,9... | collective-permute-start | bytes 786440 | tf_op jit(solution)/shard_map/ppermute | solution.py:31
  288.4 3.8 %collective-permute-start.35 = (bf16[256,512]{1,0:T(8,128)(2,1)S(1)}, bf16[256,512]{1,0:T(8,128)(2,1)S(1)}, u32[]{:S(2)}, u32[]{:S(2)}) collective-permute-start(bf16[256,512]{1,0:T(8,128)(2,1)S(1)} %fusion.11), channel_id=1, source_target_pairs={{0,7},{1,0},{2,1},{3,2},{4,3},{5,4},{6,5},{7,6},{8,15},{9,8},{10,9... | collective-permute-start | bytes 786440 | tf_op jit(solution)/shard_map/ppermute | solution.py:31
  292.7 3.5 %collective-permute-done.22 = bf16[256,512]{1,0:T(8,128)(2,1)S(1)} collective-permute-done((bf16[256,512]{1,0:T(8,128)(2,1)S(1)}, bf16[256,512]{1,0:T(8,128)(2,1)S(1)}, u32[]{:S(2)}, u32[]{:S(2)}) %collective-permute-start.22) | collective-permute-done | bytes 262176 | tf_op jit(solution)/shard_map/ppermute | solution.py:31
  297.7 2.6 collective-permute-done.31
  (140 shorter events, 52.9 us)
Async XLA Ops:
  1.1 32.8 %copy-start.6 = (bf16[8,32,512]{2,1,0:T(8,128)(2,1)}, bf16[8,32,512]{2,1,0:T(8,128)(2,1)S(1)}, u32[]{:S(2)}) copy-start(bf16[8,32,512]{2,1,0:T(8,128)(2,1)S(1)} %get-tuple-element.28) | copy-start | bytes 786436
  1.1 60.6 %copy-start.5 = (bf16[8,32,512]{2,1,0:T(8,128)(2,1)}, bf16[8,32,512]{2,1,0:T(8,128)(2,1)S(1)}, u32[]{:S(2)}) copy-start(bf16[8,32,512]{2,1,0:T(8,128)(2,1)S(1)} %get-tuple-element.27) | copy-start | bytes 786436
  1.1 11.5 %collective-permute-start.4 = (bf16[256,512]{1,0:T(8,128)(2,1)S(1)}, bf16[256,512]{1,0:T(8,128)(2,1)S(1)}, u32[]{:S(2)}, u32[]{:S(2)}) collective-permute-start(bf16[256,512]{1,0:T(8,128)(2,1)S(1)} %bitcast.59), channel_id=1, source_target_pairs={{0,7},{1,0},{2,1},{3,2},{4,3},{5,4},{6,5},{7,6},{8,15},{9,8},{10,9... | collective-permute-start | bytes 786440 | tf_op jit(solution)/shard_map/ppermute | solution.py:31
  7.0 9.3 %collective-permute-start = (bf16[256,512]{1,0:T(8,128)(2,1)S(1)}, bf16[256,512]{1,0:T(8,128)(2,1)S(1)}, u32[]{:S(2)}, u32[]{:S(2)}) collective-permute-start(bf16[256,512]{1,0:T(8,128)(2,1)S(1)} %bitcast.60), channel_id=1, source_target_pairs={{0,1},{1,2},{2,3},{3,4},{4,5},{5,6},{6,7},{7,0},{8,9},{9,10},{10,1... | collective-permute-start | bytes 786440 | tf_op jit(solution)/shard_map/ppermute | solution.py:31
  12.6 21.3 %copy-start.11 = (bf16[256,512]{1,0:T(8,128)(2,1)}, bf16[256,512]{1,0:T(8,128)(2,1)S(1)}, u32[]{:S(2)}) copy-start(bf16[256,512]{1,0:T(8,128)(2,1)S(1)} %collective-permute-done.4.refs_2_) | copy-start | bytes 786436
  12.6 8.4 %collective-permute-start.5 = (bf16[256,512]{1,0:T(8,128)(2,1)S(1)}, bf16[256,512]{1,0:T(8,128)(2,1)S(1)}, u32[]{:S(2)}, u32[]{:S(2)}) collective-permute-start(bf16[256,512]{1,0:T(8,128)(2,1)S(1)} %collective-permute-done.4.refs_2_), channel_id=1, source_target_pairs={{0,7},{1,0},{2,1},{3,2},{4,3},{5,4},{6,5},{7,6},{8,15},{9,8},{10,9... | collective-permute-start | bytes 786440 | tf_op jit(solution)/shard_map/ppermute | solution.py:31
  16.3 8.4 %collective-permute-start.1 = (bf16[256,512]{1,0:T(8,128)(2,1)S(1)}, bf16[256,512]{1,0:T(8,128)(2,1)S(1)}, u32[]{:S(2)}, u32[]{:S(2)}) collective-permute-start(bf16[256,512]{1,0:T(8,128)(2,1)S(1)} %collective-permute-done.refs_1_), channel_id=1, source_target_pairs={{0,1},{1,2},{2,3},{3,4},{4,5},{5,6},{6,7},{7,0},{8,9},{9,10},{10,1... | collective-permute-start | bytes 786440 | tf_op jit(solution)/shard_map/ppermute | solution.py:31
  17.3 24.3 %copy-start.24 = (s32[16]{0:T(128)}, s32[16]{0:T(128)S(1)}, u32[]{:S(2)}) copy-start(s32[16]{0:T(128)S(1)} %reshape.111.owner_ref) | copy-start | bytes 196
  21.0 7.6 %collective-permute-start.6 = (bf16[256,512]{1,0:T(8,128)(2,1)S(1)}, bf16[256,512]{1,0:T(8,128)(2,1)S(1)}, u32[]{:S(2)}, u32[]{:S(2)}) collective-permute-start(bf16[256,512]{1,0:T(8,128)(2,1)S(1)} %collective-permute-done.5.refs_4_), channel_id=1, source_target_pairs={{0,7},{1,0},{2,1},{3,2},{4,3},{5,4},{6,5},{7,6},{8,15},{9,8},{10,9... | collective-permute-start | bytes 786440 | tf_op jit(solution)/shard_map/ppermute | solution.py:31
  24.7 7.7 %collective-permute-start.2 = (bf16[256,512]{1,0:T(8,128)(2,1)S(1)}, bf16[256,512]{1,0:T(8,128)(2,1)S(1)}, u32[]{:S(2)}, u32[]{:S(2)}) collective-permute-start(bf16[256,512]{1,0:T(8,128)(2,1)S(1)} %collective-permute-done.1.refs_3_), channel_id=1, source_target_pairs={{0,1},{1,2},{2,3},{3,4},{4,5},{5,6},{6,7},{7,0},{8,9},{9,10},{10,1... | collective-permute-start | bytes 786440 | tf_op jit(solution)/shard_map/ppermute | solution.py:31
  28.6 10.0 %collective-permute-start.7 = (bf16[128,512]{1,0:T(8,128)(2,1)S(1)}, bf16[128,512]{1,0:T(8,128)(2,1)S(1)}, u32[]{:S(2)}, u32[]{:S(2)}) collective-permute-start(bf16[128,512]{1,0:T(8,128)(2,1)S(1)} %slice.78), channel_id=1, source_target_pairs={{0,7},{1,0},{2,1},{3,2},{4,3},{5,4},{6,5},{7,6},{8,15},{9,8},{10,9... | collective-permute-start | bytes 393224 | tf_op jit(solution)/shard_map/ppermute | solution.py:31
  32.4 6.3 %collective-permute-start.3 = (bf16[128,512]{1,0:T(8,128)(2,1)S(1)}, bf16[128,512]{1,0:T(8,128)(2,1)S(1)}, u32[]{:S(2)}, u32[]{:S(2)}) collective-permute-start(bf16[128,512]{1,0:T(8,128)(2,1)S(1)} %slice.77), channel_id=1, source_target_pairs={{0,1},{1,2},{2,3},{3,4},{4,5},{5,6},{6,7},{7,0},{8,9},{9,10},{10,1... | collective-permute-start | bytes 393224 | tf_op jit(solution)/shard_map/ppermute | solution.py:31
  42.4 3.5 %collective-permute-start.8 = (bf16[1,32,512]{2,1,0:T(8,128)(2,1)S(1)}, bf16[1,32,512]{2,1,0:T(8,128)(2,1)S(1)}, u32[]{:S(2)}, u32[]{:S(2)}) collective-permute-start(bf16[1,32,512]{2,1,0:T(8,128)(2,1)S(1)} %slice_bitcast_fusion.1), channel_id=1, source_target_pairs={{8,0},{16,8},{24,16},{32,24},{40,32},{48,40},{56,48},{64,56},{72,6... | collective-permute-start | bytes 98312 | tf_op jit(solution)/shard_map/ppermute | solution.py:26
  50.1 56.3 %all-to-all-start = ((bf16[32,72,512]{2,1,0:T(8,128)(2,1)}), bf16[32,72,512]{2,1,0:T(8,128)(2,1)S(1)}, u32[]{:S(2)}, u32[]{:S(2)}) async-start(bf16[32,72,512]{2,1,0:T(8,128)(2,1)} %place.2), calls=%async_computation | async-start | bytes 4718592 | tf_op jit(solution)/shard_map/all_to_all | solution.py:385
  58.4 9.1 %collective-permute-start.13 = (bf16[256,512]{1,0:T(8,128)(2,1)S(1)}, bf16[256,512]{1,0:T(8,128)(2,1)S(1)}, u32[]{:S(2)}, u32[]{:S(2)}) collective-permute-start(bf16[256,512]{1,0:T(8,128)(2,1)S(1)} %bitcast.56), channel_id=1, source_target_pairs={{0,7},{1,0},{2,1},{3,2},{4,3},{5,4},{6,5},{7,6},{8,15},{9,8},{10,9... | collective-permute-start | bytes 786440 | tf_op jit(solution)/shard_map/ppermute | solution.py:31
  61.7 9.5 %collective-permute-start.9 = (bf16[256,512]{1,0:T(8,128)(2,1)S(1)}, bf16[256,512]{1,0:T(8,128)(2,1)S(1)}, u32[]{:S(2)}, u32[]{:S(2)}) collective-permute-start(bf16[256,512]{1,0:T(8,128)(2,1)S(1)} %bitcast.57), channel_id=1, source_target_pairs={{0,1},{1,2},{2,3},{3,4},{4,5},{5,6},{6,7},{7,0},{8,9},{9,10},{10,1... | collective-permute-start | bytes 786440 | tf_op jit(solution)/shard_map/ppermute | solution.py:31
  67.5 21.7 %copy-start.15 = (bf16[256,512]{1,0:T(8,128)(2,1)}, bf16[256,512]{1,0:T(8,128)(2,1)S(1)}, u32[]{:S(2)}) copy-start(bf16[256,512]{1,0:T(8,128)(2,1)S(1)} %collective-permute-done.13.refs_2_) | copy-start | bytes 786436
  67.5 8.7 %collective-permute-start.14 = (bf16[256,512]{1,0:T(8,128)(2,1)S(1)}, bf16[256,512]{1,0:T(8,128)(2,1)S(1)}, u32[]{:S(2)}, u32[]{:S(2)}) collective-permute-start(bf16[256,512]{1,0:T(8,128)(2,1)S(1)} %collective-permute-done.13.refs_2_), channel_id=1, source_target_pairs={{0,7},{1,0},{2,1},{3,2},{4,3},{5,4},{6,5},{7,6},{8,15},{9,8},{10,9... | collective-permute-start | bytes 786440 | tf_op jit(solution)/shard_map/ppermute | solution.py:31
  71.2 18.0 %copy-start.16 = (bf16[256,512]{1,0:T(8,128)(2,1)}, bf16[256,512]{1,0:T(8,128)(2,1)S(1)}, u32[]{:S(2)}) copy-start(bf16[256,512]{1,0:T(8,128)(2,1)S(1)} %collective-permute-done.9.refs_1_) | copy-start | bytes 786436
  71.2 8.7 %collective-permute-start.10 = (bf16[256,512]{1,0:T(8,128)(2,1)S(1)}, bf16[256,512]{1,0:T(8,128)(2,1)S(1)}, u32[]{:S(2)}, u32[]{:S(2)}) collective-permute-start(bf16[256,512]{1,0:T(8,128)(2,1)S(1)} %collective-permute-done.9.refs_1_), channel_id=1, source_target_pairs={{0,1},{1,2},{2,3},{3,4},{4,5},{5,6},{6,7},{7,0},{8,9},{9,10},{10,1... | collective-permute-start | bytes 786440 | tf_op jit(solution)/shard_map/ppermute | solution.py:31
  76.2 7.8 %collective-permute-start.15 = (bf16[256,512]{1,0:T(8,128)(2,1)S(1)}, bf16[256,512]{1,0:T(8,128)(2,1)S(1)}, u32[]{:S(2)}, u32[]{:S(2)}) collective-permute-start(bf16[256,512]{1,0:T(8,128)(2,1)S(1)} %collective-permute-done.14.refs_4_), channel_id=1, source_target_pairs={{0,7},{1,0},{2,1},{3,2},{4,3},{5,4},{6,5},{7,6},{8,15},{9,8},{10,9... | collective-permute-start | bytes 786440 | tf_op jit(solution)/shard_map/ppermute | solution.py:31
  79.9 8.5 %collective-permute-start.11 = (bf16[256,512]{1,0:T(8,128)(2,1)S(1)}, bf16[256,512]{1,0:T(8,128)(2,1)S(1)}, u32[]{:S(2)}, u32[]{:S(2)}) collective-permute-start(bf16[256,512]{1,0:T(8,128)(2,1)S(1)} %collective-permute-done.10.refs_3_), channel_id=1, source_target_pairs={{0,1},{1,2},{2,3},{3,4},{4,5},{5,6},{6,7},{7,0},{8,9},{9,10},{10,1... | collective-permute-start | bytes 786440 | tf_op jit(solution)/shard_map/ppermute | solution.py:31
  84.7 9.1 %collective-permute-start.16 = (bf16[128,512]{1,0:T(8,128)(2,1)}, bf16[128,512]{1,0:T(8,128)(2,1)S(1)}, u32[]{:S(2)}, u32[]{:S(2)}) collective-permute-start(bf16[128,512]{1,0:T(8,128)(2,1)} %slice.82), channel_id=1, source_target_pairs={{0,7},{1,0},{2,1},{3,2},{4,3},{5,4},{6,5},{7,6},{8,15},{9,8},{10,9... | collective-permute-start | bytes 393224 | tf_op jit(solution)/shard_map/ppermute | solution.py:31
  89.2 6.5 %collective-permute-start.12 = (bf16[128,512]{1,0:T(8,128)(2,1)}, bf16[128,512]{1,0:T(8,128)(2,1)}, u32[]{:S(2)}, u32[]{:S(2)}) collective-permute-start(bf16[128,512]{1,0:T(8,128)(2,1)} %slice.81), channel_id=1, source_target_pairs={{0,1},{1,2},{2,3},{3,4},{4,5},{5,6},{6,7},{7,0},{8,9},{9,10},{10,1... | collective-permute-start | bytes 393224 | tf_op jit(solution)/shard_map/ppermute | solution.py:31
  98.8 3.5 %collective-permute-start.17 = (bf16[1,32,512]{2,1,0:T(8,128)(2,1)S(1)}, bf16[1,32,512]{2,1,0:T(8,128)(2,1)S(1)}, u32[]{:S(2)}, u32[]{:S(2)}) collective-permute-start(bf16[1,32,512]{2,1,0:T(8,128)(2,1)S(1)} %slice_bitcast_fusion), channel_id=1, source_target_pairs={{8,0},{16,8},{24,16},{32,24},{40,32},{48,40},{56,48},{64,56},{72,6... | collective-permute-start | bytes 98312 | tf_op jit(solution)/shard_map/ppermute | solution.py:26
  106.4 33.1 %all-to-all-start.2 = ((bf16[32,64,512]{2,1,0:T(8,128)(2,1)}), bf16[32,64,512]{2,1,0:T(8,128)(2,1)}, u32[]{:S(2)}, u32[]{:S(2)}) async-start(bf16[32,64,512]{2,1,0:T(8,128)(2,1)} %place.3), calls=%async_computation.2 | async-start | bytes 4194304 | tf_op jit(solution)/shard_map/all_to_all | solution.py:385
  139.5 37.3 %all-to-all-start.1 = ((bf16[32,72,512]{2,1,0:T(8,128)(2,1)}), bf16[32,72,512]{2,1,0:T(8,128)(2,1)S(1)}, u32[]{:S(2)}, u32[]{:S(2)}) async-start(bf16[32,72,512]{2,1,0:T(8,128)(2,1)} %attend.2), calls=%async_computation.1 | async-start | bytes 4718592 | tf_op jit(solution)/shard_map/all_to_all | solution.py:385
  178.3 69.9 %all-to-all-start.3 = ((bf16[32,72,512]{2,1,0:T(8,128)(2,1)}), bf16[32,72,512]{2,1,0:T(8,128)(2,1)S(1)}, u32[]{:S(2)}, u32[]{:S(2)}) async-start(bf16[32,72,512]{2,1,0:T(8,128)(2,1)} %attend.3), calls=%async_computation.3 | async-start | bytes 4718592 | tf_op jit(solution)/shard_map/all_to_all | solution.py:385
  192.0 22.8 %collective-permute-start.18 = (bf16[1,32,512]{2,1,0:T(8,128)(2,1)S(1)}, bf16[1,32,512]{2,1,0:T(8,128)(2,1)S(1)}, u32[]{:S(2)}, u32[]{:S(2)}) collective-permute-start(bf16[1,32,512]{2,1,0:T(8,128)(2,1)S(1)} %slice.84), channel_id=1, source_target_pairs={{0,8},{8,16},{16,24},{24,32},{32,40},{40,48},{48,56},{56,64},{64,7... | collective-permute-start | bytes 98312 | tf_op jit(solution)/shard_map/ppermute | solution.py:26
  216.2 7.5 %collective-permute-start.19 = (bf16[128,512]{1,0:T(8,128)(2,1)S(1)}, bf16[128,512]{1,0:T(8,128)(2,1)S(1)}, u32[]{:S(2)}, u32[]{:S(2)}) collective-permute-start(bf16[128,512]{1,0:T(8,128)(2,1)S(1)} %get-tuple-element.32), channel_id=1, source_target_pairs={{0,1},{1,2},{2,3},{3,4},{4,5},{5,6},{6,7},{7,0},{8,9},{9,10},{10,1... | collective-permute-start | bytes 393224 | tf_op jit(solution)/shard_map/ppermute | solution.py:31
  216.3 8.9 %collective-permute-start.23 = (bf16[128,512]{1,0:T(8,128)(2,1)S(1)}, bf16[128,512]{1,0:T(8,128)(2,1)S(1)}, u32[]{:S(2)}, u32[]{:S(2)}) collective-permute-start(bf16[128,512]{1,0:T(8,128)(2,1)S(1)} %get-tuple-element.31), channel_id=1, source_target_pairs={{0,7},{1,0},{2,1},{3,2},{4,3},{5,4},{6,5},{7,6},{8,15},{9,8},{10,9... | collective-permute-start | bytes 393224 | tf_op jit(solution)/shard_map/ppermute | solution.py:31
  225.1 9.5 %collective-permute-start.20 = (bf16[256,512]{1,0:T(8,128)(2,1)S(1)}, bf16[256,512]{1,0:T(8,128)(2,1)S(1)}, u32[]{:S(2)}, u32[]{:S(2)}) collective-permute-start(bf16[256,512]{1,0:T(8,128)(2,1)S(1)} %fusion.4), channel_id=1, source_target_pairs={{0,1},{1,2},{2,3},{3,4},{4,5},{5,6},{6,7},{7,0},{8,9},{9,10},{10,1... | collective-permute-start | bytes 786440 | tf_op jit(solution)/shard_map/ppermute | solution.py:31
  227.3 9.0 %collective-permute-start.24 = (bf16[256,512]{1,0:T(8,128)(2,1)}, bf16[256,512]{1,0:T(8,128)(2,1)S(1)}, u32[]{:S(2)}, u32[]{:S(2)}) collective-permute-start(bf16[256,512]{1,0:T(8,128)(2,1)} %fusion.7), channel_id=1, source_target_pairs={{0,7},{1,0},{2,1},{3,2},{4,3},{5,4},{6,5},{7,6},{8,15},{9,8},{10,9... | collective-permute-start | bytes 786440 | tf_op jit(solution)/shard_map/ppermute | solution.py:31
  235.9 9.0 %collective-permute-start.21 = (bf16[256,512]{1,0:T(8,128)(2,1)S(1)}, bf16[256,512]{1,0:T(8,128)(2,1)}, u32[]{:S(2)}, u32[]{:S(2)}) collective-permute-start(bf16[256,512]{1,0:T(8,128)(2,1)S(1)} %fusion.3), channel_id=1, source_target_pairs={{0,1},{1,2},{2,3},{3,4},{4,5},{5,6},{6,7},{7,0},{8,9},{9,10},{10,1... | collective-permute-start | bytes 786440 | tf_op jit(solution)/shard_map/ppermute | solution.py:31
  238.3 8.4 %collective-permute-start.25 = (bf16[256,512]{1,0:T(8,128)(2,1)}, bf16[256,512]{1,0:T(8,128)(2,1)}, u32[]{:S(2)}, u32[]{:S(2)}) collective-permute-start(bf16[256,512]{1,0:T(8,128)(2,1)} %fusion.6), channel_id=1, source_target_pairs={{0,7},{1,0},{2,1},{3,2},{4,3},{5,4},{6,5},{7,6},{8,15},{9,8},{10,9... | collective-permute-start | bytes 786440 | tf_op jit(solution)/shard_map/ppermute | solution.py:31
  253.1 24.2 %copy-start = (bf16[512,4096]{1,0:T(8,128)(2,1)S(1)}, bf16[512,4096]{1,0:T(8,128)(2,1)}, u32[]{:S(2)}) copy-start(bf16[512,4096]{1,0:T(8,128)(2,1)} %param.13) | copy-start | bytes 12582916
  254.0 5.4 %collective-permute-start.27 = (bf16[1,32,512]{2,1,0:T(8,128)(2,1)S(1)}, bf16[1,32,512]{2,1,0:T(8,128)(2,1)S(1)}, u32[]{:S(2)}, u32[]{:S(2)}) collective-permute-start(bf16[1,32,512]{2,1,0:T(8,128)(2,1)S(1)} %slice.88), channel_id=1, source_target_pairs={{0,8},{8,16},{16,24},{24,32},{32,40},{40,48},{48,56},{56,64},{64,7... | collective-permute-start | bytes 98312 | tf_op jit(solution)/shard_map/ppermute | solution.py:26
  261.8 6.3 %collective-permute-start.32 = (bf16[128,512]{1,0:T(8,128)(2,1)S(1)}, bf16[128,512]{1,0:T(8,128)(2,1)S(1)}, u32[]{:S(2)}, u32[]{:S(2)}) collective-permute-start(bf16[128,512]{1,0:T(8,128)(2,1)S(1)} %get-tuple-element.30), channel_id=1, source_target_pairs={{0,7},{1,0},{2,1},{3,2},{4,3},{5,4},{6,5},{7,6},{8,15},{9,8},{10,9... | collective-permute-start | bytes 393224 | tf_op jit(solution)/shard_map/ppermute | solution.py:31
  265.6 7.6 %collective-permute-start.28 = (bf16[128,512]{1,0:T(8,128)(2,1)S(1)}, bf16[128,512]{1,0:T(8,128)(2,1)S(1)}, u32[]{:S(2)}, u32[]{:S(2)}) collective-permute-start(bf16[128,512]{1,0:T(8,128)(2,1)S(1)} %get-tuple-element.29), channel_id=1, source_target_pairs={{0,1},{1,2},{2,3},{3,4},{4,5},{5,6},{6,7},{7,0},{8,9},{9,10},{10,1... | collective-permute-start | bytes 393224 | tf_op jit(solution)/shard_map/ppermute | solution.py:31
  269.5 7.8 %collective-permute-start.33 = (bf16[256,512]{1,0:T(8,128)(2,1)S(1)}, bf16[256,512]{1,0:T(8,128)(2,1)S(1)}, u32[]{:S(2)}, u32[]{:S(2)}) collective-permute-start(bf16[256,512]{1,0:T(8,128)(2,1)S(1)} %fusion.13), channel_id=1, source_target_pairs={{0,7},{1,0},{2,1},{3,2},{4,3},{5,4},{6,5},{7,6},{8,15},{9,8},{10,9... | collective-permute-start | bytes 786440 | tf_op jit(solution)/shard_map/ppermute | solution.py:31
  274.5 8.1 %collective-permute-start.29 = (bf16[256,512]{1,0:T(8,128)(2,1)S(1)}, bf16[256,512]{1,0:T(8,128)(2,1)S(1)}, u32[]{:S(2)}, u32[]{:S(2)}) collective-permute-start(bf16[256,512]{1,0:T(8,128)(2,1)S(1)} %fusion.10), channel_id=1, source_target_pairs={{0,1},{1,2},{2,3},{3,4},{4,5},{5,6},{6,7},{7,0},{8,9},{9,10},{10,1... | collective-permute-start | bytes 786440 | tf_op jit(solution)/shard_map/ppermute | solution.py:31
  277.6 10.5 %collective-permute-start.34 = (bf16[256,512]{1,0:T(8,128)(2,1)S(1)}, bf16[256,512]{1,0:T(8,128)(2,1)S(1)}, u32[]{:S(2)}, u32[]{:S(2)}) collective-permute-start(bf16[256,512]{1,0:T(8,128)(2,1)S(1)} %fusion.12), channel_id=1, source_target_pairs={{0,7},{1,0},{2,1},{3,2},{4,3},{5,4},{6,5},{7,6},{8,15},{9,8},{10,9... | collective-permute-start | bytes 786440 | tf_op jit(solution)/shard_map/ppermute | solution.py:31
  283.0 18.7 %copy-start.4 = (bf16[512,512]{1,0:T(8,128)(2,1)S(1)}, bf16[512,512]{1,0:T(8,128)(2,1)}, u32[]{:S(2)}) copy-start(bf16[512,512]{1,0:T(8,128)(2,1)} %param.10) | copy-start | bytes 1572868
  283.0 9.3 %collective-permute-start.30 = (bf16[256,512]{1,0:T(8,128)(2,1)S(1)}, bf16[256,512]{1,0:T(8,128)(2,1)S(1)}, u32[]{:S(2)}, u32[]{:S(2)}) collective-permute-start(bf16[256,512]{1,0:T(8,128)(2,1)S(1)} %fusion.9), channel_id=1, source_target_pairs={{0,1},{1,2},{2,3},{3,4},{4,5},{5,6},{6,7},{7,0},{8,9},{9,10},{10,1... | collective-permute-start | bytes 786440 | tf_op jit(solution)/shard_map/ppermute | solution.py:31
  283.1 13.2 %collective-permute-start.22 = (bf16[256,512]{1,0:T(8,128)(2,1)S(1)}, bf16[256,512]{1,0:T(8,128)(2,1)S(1)}, u32[]{:S(2)}, u32[]{:S(2)}) collective-permute-start(bf16[256,512]{1,0:T(8,128)(2,1)S(1)} %fusion.2), channel_id=1, source_target_pairs={{0,1},{1,2},{2,3},{3,4},{4,5},{5,6},{6,7},{7,0},{8,9},{9,10},{10,1... | collective-permute-start | bytes 786440 | tf_op jit(solution)/shard_map/ppermute | solution.py:31
  283.2 13.1 %collective-permute-start.26 = (bf16[256,512]{1,0:T(8,128)(2,1)S(1)}, bf16[256,512]{1,0:T(8,128)(2,1)S(1)}, u32[]{:S(2)}, u32[]{:S(2)}) collective-permute-start(bf16[256,512]{1,0:T(8,128)(2,1)S(1)} %fusion.5), channel_id=1, source_target_pairs={{0,7},{1,0},{2,1},{3,2},{4,3},{5,4},{6,5},{7,6},{8,15},{9,8},{10,9... | collective-permute-start | bytes 786440 | tf_op jit(solution)/shard_map/ppermute | solution.py:31
  288.4 9.2 %collective-permute-start.35 = (bf16[256,512]{1,0:T(8,128)(2,1)S(1)}, bf16[256,512]{1,0:T(8,128)(2,1)S(1)}, u32[]{:S(2)}, u32[]{:S(2)}) collective-permute-start(bf16[256,512]{1,0:T(8,128)(2,1)S(1)} %fusion.11), channel_id=1, source_target_pairs={{0,7},{1,0},{2,1},{3,2},{4,3},{5,4},{6,5},{7,6},{8,15},{9,8},{10,9... | collective-permute-start | bytes 786440 | tf_op jit(solution)/shard_map/ppermute | solution.py:31
  292.6 7.7 %collective-permute-start.31 = (bf16[256,512]{1,0:T(8,128)(2,1)S(1)}, bf16[256,512]{1,0:T(8,128)(2,1)S(1)}, u32[]{:S(2)}, u32[]{:S(2)}) collective-permute-start(bf16[256,512]{1,0:T(8,128)(2,1)S(1)} %fusion.8), channel_id=1, source_target_pairs={{0,1},{1,2},{2,3},{3,4},{4,5},{5,6},{6,7},{7,0},{8,9},{9,10},{10,1... | collective-permute-start | bytes 786440 | tf_op jit(solution)/shard_map/ppermute | solution.py:31
  (17 other events, 81.0 us)

commit v7 on v4

--- a/solution.py
+++ b/solution.py
@@ -56,13 +56,16 @@
     up = [hidden[:half], hidden[half:]]
     down = list(up)
     own = weights(0)
-    for h in range(2):
-        add(sums, h, up[h], own)
     for step in range(1, far):
         behind, ahead = weights(-step), weights(step)
         for h in range(2):
             up[h] = turned(up[h], 1)
             down[1 - h] = turned(down[1 - h], -1)
+        if step == 1:
+            for h in range(2):
+                mine = hidden[h * half:(h + 1) * half]
+                mine, up[h] = lax.optimization_barrier((mine, up[h]))
+                add(sums, h, mine, own)
         for h in range(2):
             add(sums, h, up[h], behind)
             add(sums, 1 - h, down[1 - h], ahead)
@@ -75,33 +78,28 @@
     ).astype(bf16)
 
 
-def output(placed, w_out):
+def output(halves, w_out):
     size = lax.axis_size("mp")
     me = lax.axis_index("mp")
-    rows = placed.shape[0]
     width = w_out.shape[1] // size
-    half = rows // 2
     far = size // 2
-    halves = [placed[:half], placed[half:]]
 
     def term(h, offset):
         start = (me + offset) % size * width
         part = lax.dynamic_slice(w_out, (0, start), (w_out.shape[0], width))
         return jnp.dot(halves[h], part, preferred_element_type=f32)
 
-    up = [turned(term(0, far).astype(bf16), 1), None]
-    down = [None, turned(term(1, -far).astype(bf16), -1)]
-    for offset in range(far - 1, 0, -1):
-        for h in (1, 0):
-            one, two = term(h, offset), term(1 - h, -offset)
-            if up[h] is not None:
-                one = one + up[h].astype(f32)
-            if down[1 - h] is not None:
-                two = two + down[1 - h].astype(f32)
-            up[h] = turned(one.astype(bf16), 1)
-            down[1 - h] = turned(two.astype(bf16), -1)
+    arrived = {}
+    for step in range(far):
+        for h, way, offset in ((1, -1, far), (1, 1, far - 1), (0, 1, far), (0, -1, far - 1)):
+            offset -= step
+            if offset > 0:
+                sums = term(h, way * offset)
+                if (h, way) in arrived:
+                    sums = sums + arrived[h, way].astype(f32)
+                arrived[h, way] = turned(sums.astype(bf16), way)
     return jnp.concatenate(
-        [term(h, 0) + up[h].astype(f32) + down[h].astype(f32) for h in range(2)], axis=0
+        [term(h, 0) + arrived[h, 1].astype(f32) + arrived[h, -1].astype(f32) for h in range(2)], axis=0
     )
 
 
@@ -185,8 +183,11 @@
     )(ids, asked, keys, values)
 
 
-def combine_kernel(owner_ref, rank_ref, live_ref, back_ref, out_ref, part_ref, stat_ref, sems):
-    spans, count, width = out_ref.shape
+def combine_kernel(
+    owner_ref, rank_ref, live_ref, back_ref, low_ref, high_ref, tail_ref, part_ref, stat_ref, sems
+):
+    spans, count, width = part_ref.shape
+    spans //= 2
     together = LANES // count
     groups = width // HS // together
     rows = SLOTS * count
@@ -201,11 +202,14 @@
     for pair in copies:
         for copy in pair:
             copy.start()
+    is_last = lax.broadcasted_iota(jnp.int32, (count, HS), 0) == count - 1
+    before = [jnp.zeros((count, HS), f32)] * (width // HS)
     for s in range(spans):
         for n in range(2):
             for copy in copies[2 * s + n]:
                 copy.wait()
         alive = s < live_ref[0]
+        block_ref = low_ref.at[s] if s < spans // 2 else high_ref.at[s - spans // 2]
         for g in range(groups):
             lses = []
             for n in range(2):
@@ -217,12 +221,17 @@
             other = jnp.transpose(jnp.broadcast_to(1.0 / (1.0 + jnp.exp(gap)), (LANES, LANES)))
             for h in range(together):
                 own = slice(h * count, (h + 1) * count)
-                cols = pl.ds((g * together + h) * HS, HS)
+                head = g * together + h
+                cols = pl.ds(head * HS, HS)
                 merged = (
                     part_ref[2 * s, :, cols].astype(f32) * mine[own]
                     + part_ref[2 * s + 1, :, cols].astype(f32) * other[own]
                 )
-                out_ref[s, :, cols] = jnp.where(alive, merged, 0.0).astype(bf16)
+                merged = jnp.where(alive, merged, 0.0)
+                block_ref[:, cols] = jnp.where(is_last, merged, before[head]).astype(bf16)
+                before[head] = merged
+                if s == spans - 1:
+                    tail_ref[:, cols] = merged.astype(bf16)
 
 
 def combine(owners, ranks, live, back):
@@ -230,11 +239,13 @@
     _, rows, width = back.shape
     count = (rows - STATS) // SLOTS
     smem = pl.BlockSpec(memory_space=pltpu.SMEM)
+    vmem = pl.BlockSpec(memory_space=pltpu.VMEM)
+    half = jax.ShapeDtypeStruct((spans // 2, count, width), bf16)
     return pl.pallas_call(
         combine_kernel,
-        out_shape=jax.ShapeDtypeStruct((spans, count, width), bf16),
+        out_shape=[half, half, jax.ShapeDtypeStruct((count, width), bf16)],
         in_specs=[smem, smem, smem, pl.BlockSpec(memory_space=pl.ANY)],
-        out_specs=pl.BlockSpec(memory_space=pltpu.VMEM),
+        out_specs=[vmem, vmem, vmem],
         scratch_shapes=[
             pltpu.VMEM((2 * spans, count, width), bf16),
             pltpu.VMEM((2 * spans, STATS, width), bf16),
@@ -294,13 +305,13 @@
         return lax.all_to_all(answers, "dp", split_axis=0, concat_axis=0, tiled=True)
 
     def finish(i, back):
-        merged = combine(owners, slot_rank, valid_spans, back)
-        previous = shifted(merged[span_dev - 1 :], "dp", 1)
-        placed = jnp.concatenate([previous, merged[: span_dev - 1]], axis=0)
-        if (i + 1) * count == SPAN:
-            placed = jnp.where(is_last(i), merged, placed)
-        placed = placed.reshape(-1, inner_width)
-        return output(placed, w_out).reshape(span_dev, count, width)
+        low, high, tail = combine(owners, slot_rank, valid_spans, back)
+        previous = shifted(tail, "dp", 1)
+        low = low.reshape(-1, inner_width)
+        row = lax.broadcasted_iota(jnp.int32, (low.shape[0], 1), 0)
+        previous = jnp.pad(previous, ((0, low.shape[0] - SPAN), (0, 0)))
+        low = jnp.where(row < SPAN - 1, previous, low)
+        return output([low, high.reshape(-1, inner_width)], w_out).reshape(span_dev, count, width)
 
     asked = [ask(i) for i in range(PARTS)]
     back = [answer(one) for one in asked]

time: 266 us -> 265 us (level)
  blocking collectives: 60.1 us -> 0 us
  waiting for transfers between devices: 87.3 us -> 145 us
  matrix products: 15.9 us -> 19 us
    all_to_all x1 -> x0, blocking collectives: 60.1 us -> none  [answer(): lax.all_to_all(answers, 'dp', split_axis=0, concat_axis=0, tiled=True)]
    all_to_all x0 -> x1, waiting for transfers between devices: none -> 51.6 us  [answer(): lax.all_to_all(answers, 'dp', split_axis=0, concat_axis=0, tiled=True)]
    all_to_all x0 -> x1, starting transfers between devices: none -> 10.1 us  [answer(): lax.all_to_all(answers, 'dp', split_axis=0, concat_axis=0, tiled=True)]
    ppermute x28, starting transfers between devices: 47.5 us -> 38.6 us  [turned(): lax.ppermute(block, 'mp', [(i, (i + distance) % size) for i in range(size)])]
    ppermute x28, waiting for transfers between devices: 36.4 us -> 43.4 us  [turned(): lax.ppermute(block, 'mp', [(i, (i + distance) % size) for i in range(size)])]
    dot_general x16, matrix products: 6.12 us -> 9.56 us  [term(): return jnp.dot(halves[h], part, preferred_element_type=f32)]
  transfers between devices with their start and end apart: 32 -> 33, of which waited for: 15 -> 18; matrix products, arithmetic and copies ran while one was open for 10% -> 9% of each run, Pallas kernels for 0% -> 0%
where the time goes in v7:
time: 265 us; the launch traced here: 261 us
  waiting for transfers between devices  145 us (55%)
  starting transfers between devices  68.2 us (26%)
  matrix products  19 us (7%)
  Pallas kernels  14.4 us (5%)
  local copies, waits for them, and re-layouts  7.31 us (3%)
  other arithmetic  5.87 us (2%)
    all_to_all x1, waiting for transfers between devices, answer(): lax.all_to_all(answers, 'dp', split_axis=0, concat_axis=0, tiled=True)  51.6 us
    all_to_all x1, waiting for transfers between devices, ask(): lax.all_to_all(sent_rows, 'dp', split_axis=0, concat_axis=0, tiled=True)  46.9 us
    ppermute x28, waiting for transfers between devices, turned(): lax.ppermute(block, 'mp', [(i, (i + distance) % size) for i in range(size)])  43.4 us
    ppermute x28, starting transfers between devices, turned(): lax.ppermute(block, 'mp', [(i, (i + distance) % size) for i in range(size)])  38.6 us
    pallas_call x1, Pallas kernels, attend(): pl.pallas_call(attend_kernel, out_shape=jax.ShapeDtypeStruct((peer_count,...  10.5 us
    all_to_all x1, starting transfers between devices, answer(): lax.all_to_all(answers, 'dp', split_axis=0, concat_axis=0, tiled=True)  10.1 us
    dot_general x16, matrix products, term(): return jnp.dot(halves[h], part, preferred_element_type=f32)  9.56 us
    dot_general x16, matrix products, add(): product = jnp.dot(block, weight, preferred_element_type=f32)  9.4 us
  transfers between devices with their start and end apart: 33, of which 18 were waited for; matrix products, arithmetic and copies ran while one was open for 9% of the time, Pallas kernels for 0%

profile of v7, /device:TPU:28, one launch (start us, length us, event | category | flops | bytes accessed | tf_op | source)
XLA Modules:
  0.0 261.2 jit_solution(6827136371748885077)
XLA Ops:
  1.1 2.0 collective-permute-start.7
  3.1 4.0 %collective-permute-start.8 = (bf16[256,512]{1,0:T(8,128)(2,1)S(1)}, bf16[256,512]{1,0:T(8,128)(2,1)S(1)}, u32[]{:S(2)}, u32[]{:S(2)}) collective-permute-start(bf16[256,512]{1,0:T(8,128)(2,1)S(1)} %get-tuple-element.14), channel_id=1, source_target_pairs={{0,7},{1,0},{2,1},{3,2},{4,3},{5,4},{6,5},{7,6},{8,15},{9,8},{10,9... | collective-permute-start | bytes 786440 | tf_op jit(solution)/shard_map/ppermute | solution.py:30
  7.1 3.2 %collective-permute-start.1 = (bf16[256,512]{1,0:T(8,128)(2,1)S(1)}, bf16[256,512]{1,0:T(8,128)(2,1)S(1)}, u32[]{:S(2)}, u32[]{:S(2)}) collective-permute-start(bf16[256,512]{1,0:T(8,128)(2,1)S(1)} %get-tuple-element.12), channel_id=1, source_target_pairs={{0,7},{1,0},{2,1},{3,2},{4,3},{5,4},{6,5},{7,6},{8,15},{9,8},{10,9... | collective-permute-start | bytes 786440 | tf_op jit(solution)/shard_map/ppermute | solution.py:30
  13.7 7.3 %all-to-all-start = ((s32[32,1,2]{2,1,0:T(1,128)}), s32[32,1,2]{2,1,0:T(1,128)S(1)}, u32[]{:S(2)}, u32[]{:S(2)}) async-start(s32[32,1,2]{2,1,0:T(1,128)} %bitcast.1), calls=%async_computation | async-start | bytes 32768 | tf_op jit(solution)/shard_map/all_to_all | solution.py:286
  22.6 1.4 fusion.46
  24.3 1.4 fusion.47
  25.7 3.3 %collective-permute-start.9 = (bf16[256,512]{1,0:T(8,128)(2,1)S(1)}, bf16[256,512]{1,0:T(8,128)(2,1)S(1)}, u32[]{:S(2)}, u32[]{:S(2)}) collective-permute-start(bf16[256,512]{1,0:T(8,128)(2,1)S(1)} %collective-permute-done.8), channel_id=1, source_target_pairs={{0,7},{1,0},{2,1},{3,2},{4,3},{5,4},{6,5},{7,6},{8,15},{9,8},{10,9... | collective-permute-start | bytes 786440 | tf_op jit(solution)/shard_map/ppermute | solution.py:30
  29.1 1.4 convolution_bitcast_fusion.3
  31.0 2.1 collective-permute-start.3
  33.6 3.9 %collective-permute-done.2 = bf16[256,512]{1,0:T(8,128)(2,1)S(1)} collective-permute-done((bf16[256,512]{1,0:T(8,128)(2,1)S(1)}, bf16[256,512]{1,0:T(8,128)(2,1)S(1)}, u32[]{:S(2)}, u32[]{:S(2)}) %collective-permute-start.2) | collective-permute-done | bytes 262176 | tf_op jit(solution)/shard_map/ppermute | solution.py:30
  39.5 1.1 collective-permute-start.4
  41.7 3.3 %collective-permute-start.5 = (bf16[256,512]{1,0:T(8,128)(2,1)S(1)}, bf16[256,512]{1,0:T(8,128)(2,1)S(1)}, u32[]{:S(2)}, u32[]{:S(2)}) collective-permute-start(bf16[256,512]{1,0:T(8,128)(2,1)S(1)} %collective-permute-done.3), channel_id=1, source_target_pairs={{0,7},{1,0},{2,1},{3,2},{4,3},{5,4},{6,5},{7,6},{8,15},{9,8},{10,9... | collective-permute-start | bytes 786440 | tf_op jit(solution)/shard_map/ppermute | solution.py:30
  45.8 1.8 collective-permute-done.11
  47.6 3.1 %collective-permute-start.13 = (bf16[256,512]{1,0:T(8,128)(2,1)S(1)}, bf16[256,512]{1,0:T(8,128)(2,1)S(1)}, u32[]{:S(2)}, u32[]{:S(2)}) collective-permute-start(bf16[256,512]{1,0:T(8,128)(2,1)S(1)} %collective-permute-done.11), channel_id=1, source_target_pairs={{0,7},{1,0},{2,1},{3,2},{4,3},{5,4},{6,5},{7,6},{8,15},{9,8},{10,9... | collective-permute-start | bytes 786440 | tf_op jit(solution)/shard_map/ppermute | solution.py:30
  50.8 2.2 collective-permute-done.12
  55.5 1.6 collective-permute-done.13
  57.4 3.8 %collective-permute-done.6 = bf16[256,512]{1,0:T(8,128)(2,1)S(1)} collective-permute-done((bf16[256,512]{1,0:T(8,128)(2,1)S(1)}, bf16[256,512]{1,0:T(8,128)(2,1)S(1)}, u32[]{:S(2)}, u32[]{:S(2)}) %collective-permute-start.6) | collective-permute-done | bytes 262176 | tf_op jit(solution)/shard_map/ppermute | solution.py:30
  62.6 1.9 collective-permute-start.14
  64.5 1.8 collective-permute-done.14
  66.5 2.8 %gather_fusion = bf16[64,64,512]{2,1,0:T(8,128)(2,1)} fusion(bf16[8,64,512]{2,1,0:T(8,128)(2,1)S(1)} %maximum_select_fusion, s32[1024]{0:T(1024)S(1)} %pad_clamp_fusion), kind=kCustom, calls=%fused_computation | custom fusion | bytes 8388864 | tf_op jit(solution)/shard_map/gather | solution.py:300
  69.3 8.4 %all-to-all-start.1 = ((bf16[32,128,512]{2,1,0:T(8,128)(2,1)}), bf16[32,128,512]{2,1,0:T(8,128)(2,1)}, u32[]{:S(2)}, u32[]{:S(2)}) async-start(bf16[32,128,512]{2,1,0:T(8,128)(2,1)} %bitcast.91), calls=%async_computation.1 | async-start | bytes 8388608 | tf_op jit(solution)/shard_map/all_to_all | solution.py:301
  79.5 46.9 %all-to-all-done.1.q_ref = bf16[32,128,512]{2,1,0:T(8,128)(2,1)} async-done(((bf16[32,128,512]{2,1,0:T(8,128)(2,1)}), bf16[32,128,512]{2,1,0:T(8,128)(2,1)}, u32[]{:S(2)}, u32[]{:S(2)}) %all-to-all-start.1) | async-done | bytes 4194336 | tf_op jit(solution)/shard_map/all_to_all | solution.py:301
  126.3 10.5 %attend.1 = bf16[32,136,512]{2,1,0:T(8,128)(2,1)} custom-call(s32[64]{0:T(128)} %reshape.185.ids_ref, bf16[32,128,512]{2,1,0:T(8,128)(2,1)} %all-to-all-done.1.q_ref, bf16[8,128,512]{2,1,0:T(8,128)(2,1)} %k_ref.1, bf16[8,128,512]{2,1,0:T(8,128)(2,1)} %v_ref.1), custom_call_target="tpu_custom_call" | custom-call | flops 2147483648 | bytes 8388608 | tf_op jit(solution)/shard_map/attend/pallas_call | solution.py:163
  136.9 10.1 %all-to-all-start.2 = ((bf16[32,136,512]{2,1,0:T(8,128)(2,1)}), bf16[32,136,512]{2,1,0:T(8,128)(2,1)}, u32[]{:S(2)}, u32[]{:S(2)}) async-start(bf16[32,136,512]{2,1,0:T(8,128)(2,1)} %attend.1), calls=%async_computation.2 | async-start | bytes 8912896 | tf_op jit(solution)/shard_map/all_to_all | solution.py:305
  147.0 51.6 %all-to-all-done.2.back_ref = bf16[32,136,512]{2,1,0:T(8,128)(2,1)} async-done(((bf16[32,136,512]{2,1,0:T(8,128)(2,1)}), bf16[32,136,512]{2,1,0:T(8,128)(2,1)}, u32[]{:S(2)}, u32[]{:S(2)}) %all-to-all-start.2) | async-done | bytes 4456480 | tf_op jit(solution)/shard_map/all_to_all | solution.py:305
  198.6 3.9 %combine.1 = (bf16[4,64,512]{2,1,0:T(8,128)(2,1)}, bf16[4,64,512]{2,1,0:T(8,128)(2,1)}, bf16[64,512]{1,0:T(8,128)(2,1)}) custom-call(s32[16]{0:T(128)} %copy-done.5, s32[16]{0:T(128)} %get-tuple-element.34.rank_ref, s32[1]{0:T(128)} %copy.19.live_ref, bf16[32,136,512]{2,1,0:T(8,128)(2,1)} %all-to-all-done.2.back_ref), custom_call_target="tpu_custom_call" | custom-call | flops 2097152 | bytes 1572864 | tf_op jit(solution)/shard_map/combine/pallas_call | solution.py:244
  202.6 1.6 fusion.30
  204.2 1.5 fusion.27
  205.7 1.4 fusion.43
  207.1 1.4 fusion.40
  208.9 1.9 collective-permute-start.15
  211.1 1.1 collective-permute-start.26
  213.2 1.2 collective-permute-done.15
  215.2 1.1 collective-permute-start.20
  217.3 3.0 %collective-permute-done.26 = bf16[256,512]{1,0:T(8,128)(2,1)S(1)} collective-permute-done((bf16[256,512]{1,0:T(8,128)(2,1)S(1)}, bf16[256,512]{1,0:T(8,128)(2,1)S(1)}, u32[]{:S(2)}, u32[]{:S(2)}) %collective-permute-start.26) | collective-permute-done | bytes 262176 | tf_op jit(solution)/shard_map/ppermute | solution.py:30
  220.7 2.3 collective-permute-start.27
  223.4 2.6 collective-permute-done.20
  226.3 2.3 collective-permute-start.21
  229.0 2.6 collective-permute-done.27
  231.7 2.3 collective-permute-start.28
  234.2 5.3 %collective-permute-done.17 = bf16[256,512]{1,0:T(8,128)(2,1)S(1)} collective-permute-done((bf16[256,512]{1,0:T(8,128)(2,1)S(1)}, bf16[256,512]{1,0:T(8,128)(2,1)S(1)}, u32[]{:S(2)}, u32[]{:S(2)}) %collective-permute-start.17) | collective-permute-done | bytes 262176 | tf_op jit(solution)/shard_map/ppermute | solution.py:30
  239.8 2.8 %collective-permute-done.28 = bf16[256,512]{1,0:T(8,128)(2,1)S(1)} collective-permute-done((bf16[256,512]{1,0:T(8,128)(2,1)S(1)}, bf16[256,512]{1,0:T(8,128)(2,1)S(1)}, u32[]{:S(2)}, u32[]{:S(2)}) %collective-permute-start.28) | collective-permute-done | bytes 262176 | tf_op jit(solution)/shard_map/ppermute | solution.py:30
  242.8 2.3 collective-permute-start.29
  245.5 4.8 %collective-permute-done.18 = bf16[256,512]{1,0:T(8,128)(2,1)S(1)} collective-permute-done((bf16[256,512]{1,0:T(8,128)(2,1)S(1)}, bf16[256,512]{1,0:T(8,128)(2,1)S(1)}, u32[]{:S(2)}, u32[]{:S(2)}) %collective-permute-start.18) | collective-permute-done | bytes 262176 | tf_op jit(solution)/shard_map/ppermute | solution.py:30
  250.7 1.3 collective-permute-done.29
  252.1 4.5 %collective-permute-done.22 = bf16[256,512]{1,0:T(8,128)(2,1)S(1)} collective-permute-done((bf16[256,512]{1,0:T(8,128)(2,1)S(1)}, bf16[256,512]{1,0:T(8,128)(2,1)S(1)}, u32[]{:S(2)}, u32[]{:S(2)}) %collective-permute-start.22) | collective-permute-done | bytes 262176 | tf_op jit(solution)/shard_map/ppermute | solution.py:30
  256.7 3.1 %collective-permute-done.19 = bf16[256,512]{1,0:T(8,128)(2,1)S(1)} collective-permute-done((bf16[256,512]{1,0:T(8,128)(2,1)S(1)}, bf16[256,512]{1,0:T(8,128)(2,1)S(1)}, u32[]{:S(2)}, u32[]{:S(2)}) %collective-permute-start.19) | collective-permute-done | bytes 262176 | tf_op jit(solution)/shard_map/ppermute | solution.py:30
  260.1 1.1 maximum_add_fusion
  (114 shorter events, 23.2 us)
Async XLA Ops:
  1.1 21.2 %collective-permute-start.7 = (bf16[256,512]{1,0:T(8,128)(2,1)S(1)}, bf16[256,512]{1,0:T(8,128)(2,1)S(1)}, u32[]{:S(2)}, u32[]{:S(2)}) collective-permute-start(bf16[256,512]{1,0:T(8,128)(2,1)S(1)} %get-tuple-element.14), channel_id=1, source_target_pairs={{0,1},{1,2},{2,3},{3,4},{4,5},{5,6},{6,7},{7,0},{8,9},{9,10},{10,1... | collective-permute-start | bytes 786440 | tf_op jit(solution)/shard_map/ppermute | solution.py:30
  3.1 22.7 %collective-permute-start.8 = (bf16[256,512]{1,0:T(8,128)(2,1)S(1)}, bf16[256,512]{1,0:T(8,128)(2,1)S(1)}, u32[]{:S(2)}, u32[]{:S(2)}) collective-permute-start(bf16[256,512]{1,0:T(8,128)(2,1)S(1)} %get-tuple-element.14), channel_id=1, source_target_pairs={{0,7},{1,0},{2,1},{3,2},{4,3},{5,4},{6,5},{7,6},{8,15},{9,8},{10,9... | collective-permute-start | bytes 786440 | tf_op jit(solution)/shard_map/ppermute | solution.py:30
  7.1 15.5 %collective-permute-start = (bf16[256,512]{1,0:T(8,128)(2,1)S(1)}, bf16[256,512]{1,0:T(8,128)(2,1)S(1)}, u32[]{:S(2)}, u32[]{:S(2)}) collective-permute-start(bf16[256,512]{1,0:T(8,128)(2,1)S(1)} %get-tuple-element.12), channel_id=1, source_target_pairs={{0,1},{1,2},{2,3},{3,4},{4,5},{5,6},{6,7},{7,0},{8,9},{9,10},{10,1... | collective-permute-start | bytes 786440 | tf_op jit(solution)/shard_map/ppermute | solution.py:30
  7.1 23.5 %collective-permute-start.1 = (bf16[256,512]{1,0:T(8,128)(2,1)S(1)}, bf16[256,512]{1,0:T(8,128)(2,1)S(1)}, u32[]{:S(2)}, u32[]{:S(2)}) collective-permute-start(bf16[256,512]{1,0:T(8,128)(2,1)S(1)} %get-tuple-element.12), channel_id=1, source_target_pairs={{0,7},{1,0},{2,1},{3,2},{4,3},{5,4},{6,5},{7,6},{8,15},{9,8},{10,9... | collective-permute-start | bytes 786440 | tf_op jit(solution)/shard_map/ppermute | solution.py:30
  11.2 22.4 %copy-start.5 = (s32[16]{0:T(128)}, s32[16]{0:T(128)S(1)}, u32[]{:S(2)}) copy-start(s32[16]{0:T(128)S(1)} %reshape.184.owner_ref) | copy-start | bytes 196
  13.7 55.6 %all-to-all-start = ((s32[32,1,2]{2,1,0:T(1,128)}), s32[32,1,2]{2,1,0:T(1,128)S(1)}, u32[]{:S(2)}, u32[]{:S(2)}) async-start(s32[32,1,2]{2,1,0:T(1,128)} %bitcast.1), calls=%async_computation | async-start | bytes 32768 | tf_op jit(solution)/shard_map/all_to_all | solution.py:286
  21.2 9.4 %copy-start.2 = (bf16[4096,512]{1,0:T(8,128)(2,1)S(1)}, bf16[4096,512]{1,0:T(8,128)(2,1)}, u32[]{:S(2)}) copy-start(bf16[4096,512]{1,0:T(8,128)(2,1)} %param.10) | copy-start | bytes 12582916
  22.3 18.4 %collective-permute-start.10 = (bf16[256,512]{1,0:T(8,128)(2,1)S(1)}, bf16[256,512]{1,0:T(8,128)(2,1)S(1)}, u32[]{:S(2)}, u32[]{:S(2)}) collective-permute-start(bf16[256,512]{1,0:T(8,128)(2,1)S(1)} %collective-permute-done.7), channel_id=1, source_target_pairs={{0,1},{1,2},{2,3},{3,4},{4,5},{5,6},{6,7},{7,0},{8,9},{9,10},{10,1... | collective-permute-start | bytes 786440 | tf_op jit(solution)/shard_map/ppermute | solution.py:30
  22.6 15.0 %collective-permute-start.2 = (bf16[256,512]{1,0:T(8,128)(2,1)S(1)}, bf16[256,512]{1,0:T(8,128)(2,1)S(1)}, u32[]{:S(2)}, u32[]{:S(2)}) collective-permute-start(bf16[256,512]{1,0:T(8,128)(2,1)S(1)} %collective-permute-done), channel_id=1, source_target_pairs={{0,1},{1,2},{2,3},{3,4},{4,5},{5,6},{6,7},{7,0},{8,9},{9,10},{10,1... | collective-permute-start | bytes 786440 | tf_op jit(solution)/shard_map/ppermute | solution.py:30
  25.7 12.6 %collective-permute-start.9 = (bf16[256,512]{1,0:T(8,128)(2,1)S(1)}, bf16[256,512]{1,0:T(8,128)(2,1)S(1)}, u32[]{:S(2)}, u32[]{:S(2)}) collective-permute-start(bf16[256,512]{1,0:T(8,128)(2,1)S(1)} %collective-permute-done.8), channel_id=1, source_target_pairs={{0,7},{1,0},{2,1},{3,2},{4,3},{5,4},{6,5},{7,6},{8,15},{9,8},{10,9... | collective-permute-start | bytes 786440 | tf_op jit(solution)/shard_map/ppermute | solution.py:30
  31.0 10.7 %collective-permute-start.3 = (bf16[256,512]{1,0:T(8,128)(2,1)S(1)}, bf16[256,512]{1,0:T(8,128)(2,1)S(1)}, u32[]{:S(2)}, u32[]{:S(2)}) collective-permute-start(bf16[256,512]{1,0:T(8,128)(2,1)S(1)} %collective-permute-done.1), channel_id=1, source_target_pairs={{0,7},{1,0},{2,1},{3,2},{4,3},{5,4},{6,5},{7,6},{8,15},{9,8},{10,9... | collective-permute-start | bytes 786440 | tf_op jit(solution)/shard_map/ppermute | solution.py:30
  38.3 9.3 %collective-permute-start.11 = (bf16[256,512]{1,0:T(8,128)(2,1)S(1)}, bf16[256,512]{1,0:T(8,128)(2,1)S(1)}, u32[]{:S(2)}, u32[]{:S(2)}) collective-permute-start(bf16[256,512]{1,0:T(8,128)(2,1)S(1)} %collective-permute-done.9), channel_id=1, source_target_pairs={{0,7},{1,0},{2,1},{3,2},{4,3},{5,4},{6,5},{7,6},{8,15},{9,8},{10,9... | collective-permute-start | bytes 786440 | tf_op jit(solution)/shard_map/ppermute | solution.py:30
  39.5 13.9 %collective-permute-start.4 = (bf16[256,512]{1,0:T(8,128)(2,1)S(1)}, bf16[256,512]{1,0:T(8,128)(2,1)S(1)}, u32[]{:S(2)}, u32[]{:S(2)}) collective-permute-start(bf16[256,512]{1,0:T(8,128)(2,1)S(1)} %collective-permute-done.2), channel_id=1, source_target_pairs={{0,1},{1,2},{2,3},{3,4},{4,5},{5,6},{6,7},{7,0},{8,9},{9,10},{10,1... | collective-permute-start | bytes 786440 | tf_op jit(solution)/shard_map/ppermute | solution.py:30
  40.6 12.3 %collective-permute-start.12 = (bf16[256,512]{1,0:T(8,128)(2,1)S(1)}, bf16[256,512]{1,0:T(8,128)(2,1)S(1)}, u32[]{:S(2)}, u32[]{:S(2)}) collective-permute-start(bf16[256,512]{1,0:T(8,128)(2,1)S(1)} %collective-permute-done.10), channel_id=1, source_target_pairs={{0,1},{1,2},{2,3},{3,4},{4,5},{5,6},{6,7},{7,0},{8,9},{9,10},{10,1... | collective-permute-start | bytes 786440 | tf_op jit(solution)/shard_map/ppermute | solution.py:30
  41.7 12.9 %collective-permute-start.5 = (bf16[256,512]{1,0:T(8,128)(2,1)S(1)}, bf16[256,512]{1,0:T(8,128)(2,1)S(1)}, u32[]{:S(2)}, u32[]{:S(2)}) collective-permute-start(bf16[256,512]{1,0:T(8,128)(2,1)S(1)} %collective-permute-done.3), channel_id=1, source_target_pairs={{0,7},{1,0},{2,1},{3,2},{4,3},{5,4},{6,5},{7,6},{8,15},{9,8},{10,9... | collective-permute-start | bytes 786440 | tf_op jit(solution)/shard_map/ppermute | solution.py:30
  47.6 9.6 %collective-permute-start.13 = (bf16[256,512]{1,0:T(8,128)(2,1)S(1)}, bf16[256,512]{1,0:T(8,128)(2,1)S(1)}, u32[]{:S(2)}, u32[]{:S(2)}) collective-permute-start(bf16[256,512]{1,0:T(8,128)(2,1)S(1)} %collective-permute-done.11), channel_id=1, source_target_pairs={{0,7},{1,0},{2,1},{3,2},{4,3},{5,4},{6,5},{7,6},{8,15},{9,8},{10,9... | collective-permute-start | bytes 786440 | tf_op jit(solution)/shard_map/ppermute | solution.py:30
  53.5 7.7 %collective-permute-start.6 = (bf16[256,512]{1,0:T(8,128)(2,1)S(1)}, bf16[256,512]{1,0:T(8,128)(2,1)S(1)}, u32[]{:S(2)}, u32[]{:S(2)}) collective-permute-start(bf16[256,512]{1,0:T(8,128)(2,1)S(1)} %collective-permute-done.4), channel_id=1, source_target_pairs={{0,1},{1,2},{2,3},{3,4},{4,5},{5,6},{6,7},{7,0},{8,9},{9,10},{10,1... | collective-permute-start | bytes 786440 | tf_op jit(solution)/shard_map/ppermute | solution.py:30
  62.6 3.8 %collective-permute-start.14 = (bf16[1,64,512]{2,1,0:T(8,128)(2,1)S(1)}, bf16[1,64,512]{2,1,0:T(8,128)(2,1)S(1)}, u32[]{:S(2)}, u32[]{:S(2)}) collective-permute-start(bf16[1,64,512]{2,1,0:T(8,128)(2,1)S(1)} %slice_bitcast_fusion), channel_id=1, source_target_pairs={{8,0},{16,8},{24,16},{32,24},{40,32},{48,40},{56,48},{64,56},{72,6... | collective-permute-start | bytes 196616 | tf_op jit(solution)/shard_map/ppermute | solution.py:25
  69.3 57.1 %all-to-all-start.1 = ((bf16[32,128,512]{2,1,0:T(8,128)(2,1)}), bf16[32,128,512]{2,1,0:T(8,128)(2,1)}, u32[]{:S(2)}, u32[]{:S(2)}) async-start(bf16[32,128,512]{2,1,0:T(8,128)(2,1)} %bitcast.91), calls=%async_computation.1 | async-start | bytes 8388608 | tf_op jit(solution)/shard_map/all_to_all | solution.py:301
  136.9 61.8 %all-to-all-start.2 = ((bf16[32,136,512]{2,1,0:T(8,128)(2,1)}), bf16[32,136,512]{2,1,0:T(8,128)(2,1)}, u32[]{:S(2)}, u32[]{:S(2)}) async-start(bf16[32,136,512]{2,1,0:T(8,128)(2,1)} %attend.1), calls=%async_computation.2 | async-start | bytes 8912896 | tf_op jit(solution)/shard_map/all_to_all | solution.py:305
  202.6 6.0 %copy-start = (bf16[512,4096]{1,0:T(8,128)(2,1)S(1)}, bf16[512,4096]{1,0:T(8,128)(2,1)}, u32[]{:S(2)}) copy-start(bf16[512,4096]{1,0:T(8,128)(2,1)} %param.11) | copy-start | bytes 12582916
  202.6 6.0 %copy-start.1 = (bf16[4,64,512]{2,1,0:T(8,128)(2,1)S(1)}, bf16[4,64,512]{2,1,0:T(8,128)(2,1)}, u32[]{:S(2)}) copy-start(bf16[4,64,512]{2,1,0:T(8,128)(2,1)} %get-tuple-element.18) | copy-start | bytes 786436
  202.6 6.3 %copy-start.6 = (bf16[64,512]{1,0:T(8,128)(2,1)S(1)}, bf16[64,512]{1,0:T(8,128)(2,1)}, u32[]{:S(2)}) copy-start(bf16[64,512]{1,0:T(8,128)(2,1)} %get-tuple-element.16) | copy-start | bytes 196612
  202.6 11.9 %copy-start.4 = (bf16[4,64,512]{2,1,0:T(8,128)(2,1)S(1)}, bf16[4,64,512]{2,1,0:T(8,128)(2,1)}, u32[]{:S(2)}) copy-start(bf16[4,64,512]{2,1,0:T(8,128)(2,1)} %get-tuple-element.17) | copy-start | bytes 786436
  208.9 5.6 %collective-permute-start.15 = (bf16[64,512]{1,0:T(8,128)(2,1)S(1)}, bf16[64,512]{1,0:T(8,128)(2,1)S(1)}, u32[]{:S(2)}, u32[]{:S(2)}) collective-permute-start(bf16[64,512]{1,0:T(8,128)(2,1)S(1)} %copy-done.6), channel_id=1, source_target_pairs={{0,8},{8,16},{16,24},{24,32},{32,40},{40,48},{48,56},{56,64},{64,7... | collective-permute-start | bytes 196616 | tf_op jit(solution)/shard_map/ppermute | solution.py:25
  211.1 9.3 %collective-permute-start.26 = (bf16[256,512]{1,0:T(8,128)(2,1)S(1)}, bf16[256,512]{1,0:T(8,128)(2,1)S(1)}, u32[]{:S(2)}, u32[]{:S(2)}) collective-permute-start(bf16[256,512]{1,0:T(8,128)(2,1)S(1)} %convolution_convert_fusion), channel_id=1, source_target_pairs={{0,7},{1,0},{2,1},{3,2},{4,3},{5,4},{6,5},{7,6},{8,15},{9,8},{10,9... | collective-permute-start | bytes 786440 | tf_op jit(solution)/shard_map/ppermute | solution.py:30
  212.2 10.8 %collective-permute-start.23 = (bf16[256,512]{1,0:T(8,128)(2,1)S(1)}, bf16[256,512]{1,0:T(8,128)(2,1)S(1)}, u32[]{:S(2)}, u32[]{:S(2)}) collective-permute-start(bf16[256,512]{1,0:T(8,128)(2,1)S(1)} %convolution_convert_fusion.1), channel_id=1, source_target_pairs={{0,1},{1,2},{2,3},{3,4},{4,5},{5,6},{6,7},{7,0},{8,9},{9,10},{10,1... | collective-permute-start | bytes 786440 | tf_op jit(solution)/shard_map/ppermute | solution.py:30
  215.2 10.8 %collective-permute-start.20 = (bf16[256,512]{1,0:T(8,128)(2,1)S(1)}, bf16[256,512]{1,0:T(8,128)(2,1)S(1)}, u32[]{:S(2)}, u32[]{:S(2)}) collective-permute-start(bf16[256,512]{1,0:T(8,128)(2,1)S(1)} %convolution_convert_fusion.2), channel_id=1, source_target_pairs={{0,7},{1,0},{2,1},{3,2},{4,3},{5,4},{6,5},{7,6},{8,15},{9,8},{10,9... | collective-permute-start | bytes 786440 | tf_op jit(solution)/shard_map/ppermute | solution.py:30
  216.3 12.3 %collective-permute-start.16 = (bf16[256,512]{1,0:T(8,128)(2,1)S(1)}, bf16[256,512]{1,0:T(8,128)(2,1)S(1)}, u32[]{:S(2)}, u32[]{:S(2)}) collective-permute-start(bf16[256,512]{1,0:T(8,128)(2,1)S(1)} %convolution_convert_fusion.3), channel_id=1, source_target_pairs={{0,1},{1,2},{2,3},{3,4},{4,5},{5,6},{6,7},{7,0},{8,9},{9,10},{10,1... | collective-permute-start | bytes 786440 | tf_op jit(solution)/shard_map/ppermute | solution.py:30
  220.7 10.9 %collective-permute-start.27 = (bf16[256,512]{1,0:T(8,128)(2,1)S(1)}, bf16[256,512]{1,0:T(8,128)(2,1)S(1)}, u32[]{:S(2)}, u32[]{:S(2)}) collective-permute-start(bf16[256,512]{1,0:T(8,128)(2,1)S(1)} %add_convert_fusion.2), channel_id=1, source_target_pairs={{0,7},{1,0},{2,1},{3,2},{4,3},{5,4},{6,5},{7,6},{8,15},{9,8},{10,9... | collective-permute-start | bytes 786440 | tf_op jit(solution)/shard_map/ppermute | solution.py:30
  223.3 10.7 %collective-permute-start.24 = (bf16[256,512]{1,0:T(8,128)(2,1)S(1)}, bf16[256,512]{1,0:T(8,128)(2,1)S(1)}, u32[]{:S(2)}, u32[]{:S(2)}) collective-permute-start(bf16[256,512]{1,0:T(8,128)(2,1)S(1)} %add_convert_fusion.4), channel_id=1, source_target_pairs={{0,1},{1,2},{2,3},{3,4},{4,5},{5,6},{6,7},{7,0},{8,9},{9,10},{10,1... | collective-permute-start | bytes 786440 | tf_op jit(solution)/shard_map/ppermute | solution.py:30
  226.3 18.8 %collective-permute-start.21 = (bf16[256,512]{1,0:T(8,128)(2,1)S(1)}, bf16[256,512]{1,0:T(8,128)(2,1)S(1)}, u32[]{:S(2)}, u32[]{:S(2)}) collective-permute-start(bf16[256,512]{1,0:T(8,128)(2,1)S(1)} %fusion.19), channel_id=1, source_target_pairs={{0,7},{1,0},{2,1},{3,2},{4,3},{5,4},{6,5},{7,6},{8,15},{9,8},{10,9... | collective-permute-start | bytes 786440 | tf_op jit(solution)/shard_map/ppermute | solution.py:30
  228.9 10.5 %collective-permute-start.17 = (bf16[256,512]{1,0:T(8,128)(2,1)S(1)}, bf16[256,512]{1,0:T(8,128)(2,1)S(1)}, u32[]{:S(2)}, u32[]{:S(2)}) collective-permute-start(bf16[256,512]{1,0:T(8,128)(2,1)S(1)} %fusion.17), channel_id=1, source_target_pairs={{0,1},{1,2},{2,3},{3,4},{4,5},{5,6},{6,7},{7,0},{8,9},{9,10},{10,1... | collective-permute-start | bytes 786440 | tf_op jit(solution)/shard_map/ppermute | solution.py:30
  231.7 11.0 %collective-permute-start.28 = (bf16[256,512]{1,0:T(8,128)(2,1)S(1)}, bf16[256,512]{1,0:T(8,128)(2,1)S(1)}, u32[]{:S(2)}, u32[]{:S(2)}) collective-permute-start(bf16[256,512]{1,0:T(8,128)(2,1)S(1)} %add_convert_fusion.1), channel_id=1, source_target_pairs={{0,7},{1,0},{2,1},{3,2},{4,3},{5,4},{6,5},{7,6},{8,15},{9,8},{10,9... | collective-permute-start | bytes 786440 | tf_op jit(solution)/shard_map/ppermute | solution.py:30
  234.1 26.0 %copy-start.3 = (bf16[512,512]{1,0:T(8,128)(2,1)S(1)}, bf16[512,512]{1,0:T(8,128)(2,1)}, u32[]{:S(2)}) copy-start(bf16[512,512]{1,0:T(8,128)(2,1)} %param.8) | copy-start | bytes 1572868
  234.1 16.6 %collective-permute-start.25 = (bf16[256,512]{1,0:T(8,128)(2,1)S(1)}, bf16[256,512]{1,0:T(8,128)(2,1)S(1)}, u32[]{:S(2)}, u32[]{:S(2)}) collective-permute-start(bf16[256,512]{1,0:T(8,128)(2,1)S(1)} %add_convert_fusion.3), channel_id=1, source_target_pairs={{0,1},{1,2},{2,3},{3,4},{4,5},{5,6},{6,7},{7,0},{8,9},{9,10},{10,1... | collective-permute-start | bytes 786440 | tf_op jit(solution)/shard_map/ppermute | solution.py:30
  239.8 10.5 %collective-permute-start.18 = (bf16[256,512]{1,0:T(8,128)(2,1)S(1)}, bf16[256,512]{1,0:T(8,128)(2,1)S(1)}, u32[]{:S(2)}, u32[]{:S(2)}) collective-permute-start(bf16[256,512]{1,0:T(8,128)(2,1)S(1)} %fusion.16), channel_id=1, source_target_pairs={{0,1},{1,2},{2,3},{3,4},{4,5},{5,6},{6,7},{7,0},{8,9},{9,10},{10,1... | collective-permute-start | bytes 786440 | tf_op jit(solution)/shard_map/ppermute | solution.py:30
  242.8 9.3 %collective-permute-start.29 = (bf16[256,512]{1,0:T(8,128)(2,1)S(1)}, bf16[256,512]{1,0:T(8,128)(2,1)S(1)}, u32[]{:S(2)}, u32[]{:S(2)}) collective-permute-start(bf16[256,512]{1,0:T(8,128)(2,1)S(1)} %add_convert_fusion), channel_id=1, source_target_pairs={{0,7},{1,0},{2,1},{3,2},{4,3},{5,4},{6,5},{7,6},{8,15},{9,8},{10,9... | collective-permute-start | bytes 786440 | tf_op jit(solution)/shard_map/ppermute | solution.py:30
  245.4 11.3 %collective-permute-start.22 = (bf16[256,512]{1,0:T(8,128)(2,1)S(1)}, bf16[256,512]{1,0:T(8,128)(2,1)S(1)}, u32[]{:S(2)}, u32[]{:S(2)}) collective-permute-start(bf16[256,512]{1,0:T(8,128)(2,1)S(1)} %fusion.18), channel_id=1, source_target_pairs={{0,7},{1,0},{2,1},{3,2},{4,3},{5,4},{6,5},{7,6},{8,15},{9,8},{10,9... | collective-permute-start | bytes 786440 | tf_op jit(solution)/shard_map/ppermute | solution.py:30
  250.6 9.2 %collective-permute-start.19 = (bf16[256,512]{1,0:T(8,128)(2,1)S(1)}, bf16[256,512]{1,0:T(8,128)(2,1)S(1)}, u32[]{:S(2)}, u32[]{:S(2)}) collective-permute-start(bf16[256,512]{1,0:T(8,128)(2,1)S(1)} %fusion.15), channel_id=1, source_target_pairs={{0,1},{1,2},{2,3},{3,4},{4,5},{5,6},{6,7},{7,0},{8,9},{9,10},{10,1... | collective-permute-start | bytes 786440 | tf_op jit(solution)/shard_map/ppermute | solution.py:30

commit v8 on v7

--- a/solution.py
+++ b/solution.py
@@ -91,13 +91,21 @@
 
     arrived = {}
     for step in range(far):
+        new = {}
         for h, way, offset in ((1, -1, far), (1, 1, far - 1), (0, 1, far), (0, -1, far - 1)):
             offset -= step
+            new[h, way] = offset > 0
             if offset > 0:
                 sums = term(h, way * offset)
                 if (h, way) in arrived:
                     sums = sums + arrived[h, way].astype(f32)
-                arrived[h, way] = turned(sums.astype(bf16), way)
+                arrived[h, way] = sums.astype(bf16)
+        if step == 0:
+            for h in range(2):
+                arrived[h, 1], arrived[h, -1], halves[h] = lax.optimization_barrier(
+                    (arrived[h, 1], arrived[h, -1], halves[h])
+                )
+        arrived = {(h, way): turned(sums, way) if new[h, way] else sums for (h, way), sums in arrived.items()}
     return jnp.concatenate(
         [term(h, 0) + arrived[h, 1].astype(f32) + arrived[h, -1].astype(f32) for h in range(2)], axis=0
     )
@@ -251,6 +259,7 @@
             pltpu.VMEM((2 * spans, STATS, width), bf16),
             pltpu.SemaphoreType.DMA((2 * spans, 2)),
         ],
+        compiler_params=pltpu.CompilerParams(vmem_limit_bytes=8 << 20),
         cost_estimate=pl.CostEstimate(
             flops=8 * spans * count * width,
             bytes_accessed=6 * spans * count * width,

time: 265 us -> 259 us (0.977)
  matrix products: 19 us -> 14.3 us
    dot_general x16, matrix products: 9.56 us -> 4.9 us  [term(): return jnp.dot(halves[h], part, preferred_element_type=f32)]
where the time goes in v8:
time: 259 us; the launch traced here: 255 us
  waiting for transfers between devices  145 us (56%)
  starting transfers between devices  68.3 us (26%)
  matrix products  14.3 us (6%)
  Pallas kernels  13.9 us (5%)
  local copies, waits for them, and re-layouts  7.29 us (3%)
  other arithmetic  5.48 us (2%)
    all_to_all x1, waiting for transfers between devices, answer(): lax.all_to_all(answers, 'dp', split_axis=0, concat_axis=0, tiled=True)  51.6 us
    all_to_all x1, waiting for transfers between devices, ask(): lax.all_to_all(sent_rows, 'dp', split_axis=0, concat_axis=0, tiled=True)  46.9 us
    ppermute x28, waiting for transfers between devices, turned(): lax.ppermute(block, 'mp', [(i, (i + distance) % size) for i in range(size)])  43 us
    ppermute x28, starting transfers between devices, turned(): lax.ppermute(block, 'mp', [(i, (i + distance) % size) for i in range(size)])  38.7 us
    pallas_call x1, Pallas kernels, attend(): pl.pallas_call(attend_kernel, out_shape=jax.ShapeDtypeStruct((peer_count,...  10.5 us
    all_to_all x1, starting transfers between devices, answer(): lax.all_to_all(answers, 'dp', split_axis=0, concat_axis=0, tiled=True)  10.1 us
    dot_general x16, matrix products, add(): product = jnp.dot(block, weight, preferred_element_type=f32)  9.42 us
    all_to_all x1, starting transfers between devices, ask(): lax.all_to_all(sent_rows, 'dp', split_axis=0, concat_axis=0, tiled=True)  8.37 us
  transfers between devices with their start and end apart: 33, of which 18 were waited for; matrix products, arithmetic and copies ran while one was open for 9% of the time, Pallas kernels for 0%

profile of v8, /device:TPU:28, one launch (start us, length us, event | category | flops | bytes accessed | tf_op | source)
XLA Modules:
  0.0 255.2 jit_solution(6212328148738788352)
XLA Ops:
  0.0 1.1 fusion.97
  1.1 2.0 collective-permute-start.7
  3.1 4.0 %collective-permute-start.8 = (bf16[256,512]{1,0:T(8,128)(2,1)S(1)}, bf16[256,512]{1,0:T(8,128)(2,1)S(1)}, u32[]{:S(2)}, u32[]{:S(2)}) collective-permute-start(bf16[256,512]{1,0:T(8,128)(2,1)S(1)} %get-tuple-element.20), channel_id=1, source_target_pairs={{0,7},{1,0},{2,1},{3,2},{4,3},{5,4},{6,5},{7,6},{8,15},{9,8},{10,9... | collective-permute-start | bytes 786440 | tf_op jit(solution)/shard_map/ppermute | solution.py:30
  7.1 3.2 %collective-permute-start.1 = (bf16[256,512]{1,0:T(8,128)(2,1)S(1)}, bf16[256,512]{1,0:T(8,128)(2,1)S(1)}, u32[]{:S(2)}, u32[]{:S(2)}) collective-permute-start(bf16[256,512]{1,0:T(8,128)(2,1)S(1)} %get-tuple-element.18), channel_id=1, source_target_pairs={{0,7},{1,0},{2,1},{3,2},{4,3},{5,4},{6,5},{7,6},{8,15},{9,8},{10,9... | collective-permute-start | bytes 786440 | tf_op jit(solution)/shard_map/ppermute | solution.py:30
  13.2 7.3 %all-to-all-start = ((s32[32,1,2]{2,1,0:T(1,128)}), s32[32,1,2]{2,1,0:T(1,128)S(1)}, u32[]{:S(2)}, u32[]{:S(2)}) async-start(s32[32,1,2]{2,1,0:T(1,128)} %bitcast.1), calls=%async_computation | async-start | bytes 32768 | tf_op jit(solution)/shard_map/all_to_all | solution.py:295
  20.7 1.1 fusion.98
  22.1 1.4 fusion.50
  23.8 1.4 fusion.51
  25.2 3.3 %collective-permute-start.9 = (bf16[256,512]{1,0:T(8,128)(2,1)S(1)}, bf16[256,512]{1,0:T(8,128)(2,1)S(1)}, u32[]{:S(2)}, u32[]{:S(2)}) collective-permute-start(bf16[256,512]{1,0:T(8,128)(2,1)S(1)} %collective-permute-done.8), channel_id=1, source_target_pairs={{0,7},{1,0},{2,1},{3,2},{4,3},{5,4},{6,5},{7,6},{8,15},{9,8},{10,9... | collective-permute-start | bytes 786440 | tf_op jit(solution)/shard_map/ppermute | solution.py:30
  28.6 1.4 convolution_bitcast_fusion.3
  30.5 2.1 collective-permute-start.3
  33.1 3.9 %collective-permute-done.2 = bf16[256,512]{1,0:T(8,128)(2,1)S(1)} collective-permute-done((bf16[256,512]{1,0:T(8,128)(2,1)S(1)}, bf16[256,512]{1,0:T(8,128)(2,1)S(1)}, u32[]{:S(2)}, u32[]{:S(2)}) %collective-permute-start.2) | collective-permute-done | bytes 262176 | tf_op jit(solution)/shard_map/ppermute | solution.py:30
  37.8 1.1 collective-permute-start.11
  39.0 1.1 collective-permute-start.4
  41.2 3.3 %collective-permute-start.5 = (bf16[256,512]{1,0:T(8,128)(2,1)S(1)}, bf16[256,512]{1,0:T(8,128)(2,1)S(1)}, u32[]{:S(2)}, u32[]{:S(2)}) collective-permute-start(bf16[256,512]{1,0:T(8,128)(2,1)S(1)} %collective-permute-done.3), channel_id=1, source_target_pairs={{0,7},{1,0},{2,1},{3,2},{4,3},{5,4},{6,5},{7,6},{8,15},{9,8},{10,9... | collective-permute-start | bytes 786440 | tf_op jit(solution)/shard_map/ppermute | solution.py:30
  45.3 1.8 collective-permute-done.11
  47.1 3.1 %collective-permute-start.13 = (bf16[256,512]{1,0:T(8,128)(2,1)S(1)}, bf16[256,512]{1,0:T(8,128)(2,1)S(1)}, u32[]{:S(2)}, u32[]{:S(2)}) collective-permute-start(bf16[256,512]{1,0:T(8,128)(2,1)S(1)} %collective-permute-done.11), channel_id=1, source_target_pairs={{0,7},{1,0},{2,1},{3,2},{4,3},{5,4},{6,5},{7,6},{8,15},{9,8},{10,9... | collective-permute-start | bytes 786440 | tf_op jit(solution)/shard_map/ppermute | solution.py:30
  50.3 2.2 collective-permute-done.12
  55.0 1.6 collective-permute-done.13
  56.8 3.8 %collective-permute-done.6 = bf16[256,512]{1,0:T(8,128)(2,1)S(1)} collective-permute-done((bf16[256,512]{1,0:T(8,128)(2,1)S(1)}, bf16[256,512]{1,0:T(8,128)(2,1)S(1)}, u32[]{:S(2)}, u32[]{:S(2)}) %collective-permute-start.6) | collective-permute-done | bytes 262176 | tf_op jit(solution)/shard_map/ppermute | solution.py:30
  62.1 1.9 collective-permute-start.14
  64.0 1.8 collective-permute-done.14
  66.0 2.8 %gather_fusion = bf16[64,64,512]{2,1,0:T(8,128)(2,1)} fusion(bf16[8,64,512]{2,1,0:T(8,128)(2,1)S(1)} %maximum_select_fusion, s32[1024]{0:T(1024)S(1)} %pad_clamp_fusion), kind=kCustom, calls=%fused_computation | custom fusion | bytes 8388864 | tf_op jit(solution)/shard_map/gather | solution.py:309
  68.8 8.4 %all-to-all-start.1 = ((bf16[32,128,512]{2,1,0:T(8,128)(2,1)}), bf16[32,128,512]{2,1,0:T(8,128)(2,1)}, u32[]{:S(2)}, u32[]{:S(2)}) async-start(bf16[32,128,512]{2,1,0:T(8,128)(2,1)} %bitcast.91), calls=%async_computation.1 | async-start | bytes 8388608 | tf_op jit(solution)/shard_map/all_to_all | solution.py:310
  79.0 46.9 %all-to-all-done.1.q_ref = bf16[32,128,512]{2,1,0:T(8,128)(2,1)} async-done(((bf16[32,128,512]{2,1,0:T(8,128)(2,1)}), bf16[32,128,512]{2,1,0:T(8,128)(2,1)}, u32[]{:S(2)}, u32[]{:S(2)}) %all-to-all-start.1) | async-done | bytes 4194336 | tf_op jit(solution)/shard_map/all_to_all | solution.py:310
  125.8 10.5 %attend.1 = bf16[32,136,512]{2,1,0:T(8,128)(2,1)} custom-call(s32[64]{0:T(128)} %reshape.185.ids_ref, bf16[32,128,512]{2,1,0:T(8,128)(2,1)} %all-to-all-done.1.q_ref, bf16[8,128,512]{2,1,0:T(8,128)(2,1)} %k_ref.1, bf16[8,128,512]{2,1,0:T(8,128)(2,1)} %v_ref.1), custom_call_target="tpu_custom_call" | custom-call | flops 2147483648 | bytes 8388608 | tf_op jit(solution)/shard_map/attend/pallas_call | solution.py:171
  136.3 10.1 %all-to-all-start.2 = ((bf16[32,136,512]{2,1,0:T(8,128)(2,1)}), bf16[32,136,512]{2,1,0:T(8,128)(2,1)}, u32[]{:S(2)}, u32[]{:S(2)}) async-start(bf16[32,136,512]{2,1,0:T(8,128)(2,1)} %attend.1), calls=%async_computation.2 | async-start | bytes 8912896 | tf_op jit(solution)/shard_map/all_to_all | solution.py:314
  146.5 51.6 %all-to-all-done.2.back_ref = bf16[32,136,512]{2,1,0:T(8,128)(2,1)} async-done(((bf16[32,136,512]{2,1,0:T(8,128)(2,1)}), bf16[32,136,512]{2,1,0:T(8,128)(2,1)}, u32[]{:S(2)}, u32[]{:S(2)}) %all-to-all-start.2) | async-done | bytes 4456480 | tf_op jit(solution)/shard_map/all_to_all | solution.py:314
  198.1 3.3 %combine.1 = (bf16[4,64,512]{2,1,0:T(8,128)(2,1)S(1)}, bf16[4,64,512]{2,1,0:T(8,128)(2,1)S(1)}, bf16[64,512]{1,0:T(8,128)(2,1)S(1)}) custom-call(s32[16]{0:T(128)S(1)} %reshape.184.owner_ref, s32[16]{0:T(128)S(1)} %get-tuple-element.46.rank_ref, s32[1]{0:T(128)} %copy.19.live_ref, bf16[32,136,512]{2,1,0:T(8,128)(2,1)} %all-to-all-done.2.back_ref), custom_call_target="tpu_custom_call" | custom-call | flops 2097152 | bytes 1572864 | tf_op jit(solution)/shard_map/combine/pallas_call | solution.py:252
  203.1 1.9 collective-permute-start.15
  205.3 1.1 collective-permute-start.26
  207.4 1.2 collective-permute-done.15
  209.4 1.1 collective-permute-start.20
  210.8 1.1 collective-permute-start.16
  211.9 2.7 %collective-permute-done.26 = bf16[256,512]{1,0:T(8,128)(2,1)S(1)} collective-permute-done((bf16[256,512]{1,0:T(8,128)(2,1)S(1)}, bf16[256,512]{1,0:T(8,128)(2,1)S(1)}, u32[]{:S(2)}, u32[]{:S(2)}) %collective-permute-start.26) | collective-permute-done | bytes 262176 | tf_op jit(solution)/shard_map/ppermute | solution.py:30
  214.9 2.3 collective-permute-start.27
  217.6 2.6 %collective-permute-done.20 = bf16[256,512]{1,0:T(8,128)(2,1)S(1)} collective-permute-done((bf16[256,512]{1,0:T(8,128)(2,1)S(1)}, bf16[256,512]{1,0:T(8,128)(2,1)S(1)}, u32[]{:S(2)}, u32[]{:S(2)}) %collective-permute-start.20) | collective-permute-done | bytes 262176 | tf_op jit(solution)/shard_map/ppermute | solution.py:30
  220.5 2.3 collective-permute-start.21
  223.2 2.6 %collective-permute-done.27 = bf16[256,512]{1,0:T(8,128)(2,1)S(1)} collective-permute-done((bf16[256,512]{1,0:T(8,128)(2,1)S(1)}, bf16[256,512]{1,0:T(8,128)(2,1)S(1)}, u32[]{:S(2)}, u32[]{:S(2)}) %collective-permute-start.27) | collective-permute-done | bytes 262176 | tf_op jit(solution)/shard_map/ppermute | solution.py:30
  225.9 2.3 collective-permute-start.28
  228.4 5.3 %collective-permute-done.17 = bf16[256,512]{1,0:T(8,128)(2,1)S(1)} collective-permute-done((bf16[256,512]{1,0:T(8,128)(2,1)S(1)}, bf16[256,512]{1,0:T(8,128)(2,1)S(1)}, u32[]{:S(2)}, u32[]{:S(2)}) %collective-permute-start.17) | collective-permute-done | bytes 262176 | tf_op jit(solution)/shard_map/ppermute | solution.py:30
  234.1 2.8 %collective-permute-done.28 = bf16[256,512]{1,0:T(8,128)(2,1)S(1)} collective-permute-done((bf16[256,512]{1,0:T(8,128)(2,1)S(1)}, bf16[256,512]{1,0:T(8,128)(2,1)S(1)}, u32[]{:S(2)}, u32[]{:S(2)}) %collective-permute-start.28) | collective-permute-done | bytes 262176 | tf_op jit(solution)/shard_map/ppermute | solution.py:30
  237.0 2.3 collective-permute-start.29
  239.7 4.8 %collective-permute-done.18 = bf16[256,512]{1,0:T(8,128)(2,1)S(1)} collective-permute-done((bf16[256,512]{1,0:T(8,128)(2,1)S(1)}, bf16[256,512]{1,0:T(8,128)(2,1)S(1)}, u32[]{:S(2)}, u32[]{:S(2)}) %collective-permute-start.18) | collective-permute-done | bytes 262176 | tf_op jit(solution)/shard_map/ppermute | solution.py:30
  244.9 1.3 collective-permute-done.29
  246.3 4.5 %collective-permute-done.22 = bf16[256,512]{1,0:T(8,128)(2,1)S(1)} collective-permute-done((bf16[256,512]{1,0:T(8,128)(2,1)S(1)}, bf16[256,512]{1,0:T(8,128)(2,1)S(1)}, u32[]{:S(2)}, u32[]{:S(2)}) %collective-permute-start.22) | collective-permute-done | bytes 262176 | tf_op jit(solution)/shard_map/ppermute | solution.py:30
  250.9 3.1 %collective-permute-done.19 = bf16[256,512]{1,0:T(8,128)(2,1)S(1)} collective-permute-done((bf16[256,512]{1,0:T(8,128)(2,1)S(1)}, bf16[256,512]{1,0:T(8,128)(2,1)S(1)}, u32[]{:S(2)}, u32[]{:S(2)}) %collective-permute-start.19) | collective-permute-done | bytes 262176 | tf_op jit(solution)/shard_map/ppermute | solution.py:30
  254.1 1.2 maximum_add_fusion
  (107 shorter events, 19.7 us)
Async XLA Ops:
  1.1 20.7 %collective-permute-start.7 = (bf16[256,512]{1,0:T(8,128)(2,1)S(1)}, bf16[256,512]{1,0:T(8,128)(2,1)S(1)}, u32[]{:S(2)}, u32[]{:S(2)}) collective-permute-start(bf16[256,512]{1,0:T(8,128)(2,1)S(1)} %get-tuple-element.20), channel_id=1, source_target_pairs={{0,1},{1,2},{2,3},{3,4},{4,5},{5,6},{6,7},{7,0},{8,9},{9,10},{10,1... | collective-permute-start | bytes 786440 | tf_op jit(solution)/shard_map/ppermute | solution.py:30
  3.1 22.1 %collective-permute-start.8 = (bf16[256,512]{1,0:T(8,128)(2,1)S(1)}, bf16[256,512]{1,0:T(8,128)(2,1)S(1)}, u32[]{:S(2)}, u32[]{:S(2)}) collective-permute-start(bf16[256,512]{1,0:T(8,128)(2,1)S(1)} %get-tuple-element.20), channel_id=1, source_target_pairs={{0,7},{1,0},{2,1},{3,2},{4,3},{5,4},{6,5},{7,6},{8,15},{9,8},{10,9... | collective-permute-start | bytes 786440 | tf_op jit(solution)/shard_map/ppermute | solution.py:30
  7.1 14.9 %collective-permute-start = (bf16[256,512]{1,0:T(8,128)(2,1)S(1)}, bf16[256,512]{1,0:T(8,128)(2,1)S(1)}, u32[]{:S(2)}, u32[]{:S(2)}) collective-permute-start(bf16[256,512]{1,0:T(8,128)(2,1)S(1)} %get-tuple-element.18), channel_id=1, source_target_pairs={{0,1},{1,2},{2,3},{3,4},{4,5},{5,6},{6,7},{7,0},{8,9},{9,10},{10,1... | collective-permute-start | bytes 786440 | tf_op jit(solution)/shard_map/ppermute | solution.py:30
  7.1 23.0 %collective-permute-start.1 = (bf16[256,512]{1,0:T(8,128)(2,1)S(1)}, bf16[256,512]{1,0:T(8,128)(2,1)S(1)}, u32[]{:S(2)}, u32[]{:S(2)}) collective-permute-start(bf16[256,512]{1,0:T(8,128)(2,1)S(1)} %get-tuple-element.18), channel_id=1, source_target_pairs={{0,7},{1,0},{2,1},{3,2},{4,3},{5,4},{6,5},{7,6},{8,15},{9,8},{10,9... | collective-permute-start | bytes 786440 | tf_op jit(solution)/shard_map/ppermute | solution.py:30
  13.2 55.6 %all-to-all-start = ((s32[32,1,2]{2,1,0:T(1,128)}), s32[32,1,2]{2,1,0:T(1,128)S(1)}, u32[]{:S(2)}, u32[]{:S(2)}) async-start(s32[32,1,2]{2,1,0:T(1,128)} %bitcast.1), calls=%async_computation | async-start | bytes 32768 | tf_op jit(solution)/shard_map/all_to_all | solution.py:295
  20.7 9.4 %copy-start.1 = (bf16[4096,512]{1,0:T(8,128)(2,1)S(1)}, bf16[4096,512]{1,0:T(8,128)(2,1)}, u32[]{:S(2)}) copy-start(bf16[4096,512]{1,0:T(8,128)(2,1)} %param.10) | copy-start | bytes 12582916
  21.8 18.4 %collective-permute-start.10 = (bf16[256,512]{1,0:T(8,128)(2,1)S(1)}, bf16[256,512]{1,0:T(8,128)(2,1)S(1)}, u32[]{:S(2)}, u32[]{:S(2)}) collective-permute-start(bf16[256,512]{1,0:T(8,128)(2,1)S(1)} %collective-permute-done.7), channel_id=1, source_target_pairs={{0,1},{1,2},{2,3},{3,4},{4,5},{5,6},{6,7},{7,0},{8,9},{9,10},{10,1... | collective-permute-start | bytes 786440 | tf_op jit(solution)/shard_map/ppermute | solution.py:30
  22.0 15.0 %collective-permute-start.2 = (bf16[256,512]{1,0:T(8,128)(2,1)S(1)}, bf16[256,512]{1,0:T(8,128)(2,1)S(1)}, u32[]{:S(2)}, u32[]{:S(2)}) collective-permute-start(bf16[256,512]{1,0:T(8,128)(2,1)S(1)} %collective-permute-done), channel_id=1, source_target_pairs={{0,1},{1,2},{2,3},{3,4},{4,5},{5,6},{6,7},{7,0},{8,9},{9,10},{10,1... | collective-permute-start | bytes 786440 | tf_op jit(solution)/shard_map/ppermute | solution.py:30
  25.2 12.6 %collective-permute-start.9 = (bf16[256,512]{1,0:T(8,128)(2,1)S(1)}, bf16[256,512]{1,0:T(8,128)(2,1)S(1)}, u32[]{:S(2)}, u32[]{:S(2)}) collective-permute-start(bf16[256,512]{1,0:T(8,128)(2,1)S(1)} %collective-permute-done.8), channel_id=1, source_target_pairs={{0,7},{1,0},{2,1},{3,2},{4,3},{5,4},{6,5},{7,6},{8,15},{9,8},{10,9... | collective-permute-start | bytes 786440 | tf_op jit(solution)/shard_map/ppermute | solution.py:30
  30.5 10.7 %collective-permute-start.3 = (bf16[256,512]{1,0:T(8,128)(2,1)S(1)}, bf16[256,512]{1,0:T(8,128)(2,1)S(1)}, u32[]{:S(2)}, u32[]{:S(2)}) collective-permute-start(bf16[256,512]{1,0:T(8,128)(2,1)S(1)} %collective-permute-done.1), channel_id=1, source_target_pairs={{0,7},{1,0},{2,1},{3,2},{4,3},{5,4},{6,5},{7,6},{8,15},{9,8},{10,9... | collective-permute-start | bytes 786440 | tf_op jit(solution)/shard_map/ppermute | solution.py:30
  37.8 9.3 %collective-permute-start.11 = (bf16[256,512]{1,0:T(8,128)(2,1)S(1)}, bf16[256,512]{1,0:T(8,128)(2,1)S(1)}, u32[]{:S(2)}, u32[]{:S(2)}) collective-permute-start(bf16[256,512]{1,0:T(8,128)(2,1)S(1)} %collective-permute-done.9), channel_id=1, source_target_pairs={{0,7},{1,0},{2,1},{3,2},{4,3},{5,4},{6,5},{7,6},{8,15},{9,8},{10,9... | collective-permute-start | bytes 786440 | tf_op jit(solution)/shard_map/ppermute | solution.py:30
  39.0 13.9 %collective-permute-start.4 = (bf16[256,512]{1,0:T(8,128)(2,1)S(1)}, bf16[256,512]{1,0:T(8,128)(2,1)S(1)}, u32[]{:S(2)}, u32[]{:S(2)}) collective-permute-start(bf16[256,512]{1,0:T(8,128)(2,1)S(1)} %collective-permute-done.2), channel_id=1, source_target_pairs={{0,1},{1,2},{2,3},{3,4},{4,5},{5,6},{6,7},{7,0},{8,9},{9,10},{10,1... | collective-permute-start | bytes 786440 | tf_op jit(solution)/shard_map/ppermute | solution.py:30
  40.1 12.3 %collective-permute-start.12 = (bf16[256,512]{1,0:T(8,128)(2,1)S(1)}, bf16[256,512]{1,0:T(8,128)(2,1)S(1)}, u32[]{:S(2)}, u32[]{:S(2)}) collective-permute-start(bf16[256,512]{1,0:T(8,128)(2,1)S(1)} %collective-permute-done.10), channel_id=1, source_target_pairs={{0,1},{1,2},{2,3},{3,4},{4,5},{5,6},{6,7},{7,0},{8,9},{9,10},{10,1... | collective-permute-start | bytes 786440 | tf_op jit(solution)/shard_map/ppermute | solution.py:30
  41.2 12.9 %collective-permute-start.5 = (bf16[256,512]{1,0:T(8,128)(2,1)S(1)}, bf16[256,512]{1,0:T(8,128)(2,1)S(1)}, u32[]{:S(2)}, u32[]{:S(2)}) collective-permute-start(bf16[256,512]{1,0:T(8,128)(2,1)S(1)} %collective-permute-done.3), channel_id=1, source_target_pairs={{0,7},{1,0},{2,1},{3,2},{4,3},{5,4},{6,5},{7,6},{8,15},{9,8},{10,9... | collective-permute-start | bytes 786440 | tf_op jit(solution)/shard_map/ppermute | solution.py:30
  47.1 9.6 %collective-permute-start.13 = (bf16[256,512]{1,0:T(8,128)(2,1)S(1)}, bf16[256,512]{1,0:T(8,128)(2,1)S(1)}, u32[]{:S(2)}, u32[]{:S(2)}) collective-permute-start(bf16[256,512]{1,0:T(8,128)(2,1)S(1)} %collective-permute-done.11), channel_id=1, source_target_pairs={{0,7},{1,0},{2,1},{3,2},{4,3},{5,4},{6,5},{7,6},{8,15},{9,8},{10,9... | collective-permute-start | bytes 786440 | tf_op jit(solution)/shard_map/ppermute | solution.py:30
  53.0 7.7 %collective-permute-start.6 = (bf16[256,512]{1,0:T(8,128)(2,1)S(1)}, bf16[256,512]{1,0:T(8,128)(2,1)S(1)}, u32[]{:S(2)}, u32[]{:S(2)}) collective-permute-start(bf16[256,512]{1,0:T(8,128)(2,1)S(1)} %collective-permute-done.4), channel_id=1, source_target_pairs={{0,1},{1,2},{2,3},{3,4},{4,5},{5,6},{6,7},{7,0},{8,9},{9,10},{10,1... | collective-permute-start | bytes 786440 | tf_op jit(solution)/shard_map/ppermute | solution.py:30
  62.1 3.8 %collective-permute-start.14 = (bf16[1,64,512]{2,1,0:T(8,128)(2,1)S(1)}, bf16[1,64,512]{2,1,0:T(8,128)(2,1)S(1)}, u32[]{:S(2)}, u32[]{:S(2)}) collective-permute-start(bf16[1,64,512]{2,1,0:T(8,128)(2,1)S(1)} %slice_bitcast_fusion), channel_id=1, source_target_pairs={{8,0},{16,8},{24,16},{32,24},{40,32},{48,40},{56,48},{64,56},{72,6... | collective-permute-start | bytes 196616 | tf_op jit(solution)/shard_map/ppermute | solution.py:25
  68.8 57.1 %all-to-all-start.1 = ((bf16[32,128,512]{2,1,0:T(8,128)(2,1)}), bf16[32,128,512]{2,1,0:T(8,128)(2,1)}, u32[]{:S(2)}, u32[]{:S(2)}) async-start(bf16[32,128,512]{2,1,0:T(8,128)(2,1)} %bitcast.91), calls=%async_computation.1 | async-start | bytes 8388608 | tf_op jit(solution)/shard_map/all_to_all | solution.py:310
  136.3 61.8 %all-to-all-start.2 = ((bf16[32,136,512]{2,1,0:T(8,128)(2,1)}), bf16[32,136,512]{2,1,0:T(8,128)(2,1)}, u32[]{:S(2)}, u32[]{:S(2)}) async-start(bf16[32,136,512]{2,1,0:T(8,128)(2,1)} %attend.1), calls=%async_computation.2 | async-start | bytes 8912896 | tf_op jit(solution)/shard_map/all_to_all | solution.py:314
  198.1 3.4 %copy-start = (bf16[512,4096]{1,0:T(8,128)(2,1)S(1)}, bf16[512,4096]{1,0:T(8,128)(2,1)}, u32[]{:S(2)}) copy-start(bf16[512,4096]{1,0:T(8,128)(2,1)} %param.11) | copy-start | bytes 12582916
  203.1 5.6 %collective-permute-start.15 = (bf16[64,512]{1,0:T(8,128)(2,1)S(1)}, bf16[64,512]{1,0:T(8,128)(2,1)S(1)}, u32[]{:S(2)}, u32[]{:S(2)}) collective-permute-start(bf16[64,512]{1,0:T(8,128)(2,1)S(1)} %get-tuple-element.22), channel_id=1, source_target_pairs={{0,8},{8,16},{16,24},{24,32},{32,40},{40,48},{48,56},{56,64},{64,7... | collective-permute-start | bytes 196616 | tf_op jit(solution)/shard_map/ppermute | solution.py:25
  205.3 9.3 %collective-permute-start.26 = (bf16[256,512]{1,0:T(8,128)(2,1)S(1)}, bf16[256,512]{1,0:T(8,128)(2,1)S(1)}, u32[]{:S(2)}, u32[]{:S(2)}) collective-permute-start(bf16[256,512]{1,0:T(8,128)(2,1)S(1)} %convolution_convert_fusion), channel_id=1, source_target_pairs={{0,7},{1,0},{2,1},{3,2},{4,3},{5,4},{6,5},{7,6},{8,15},{9,8},{10,9... | collective-permute-start | bytes 786440 | tf_op jit(solution)/shard_map/ppermute | solution.py:30
  206.4 10.8 %collective-permute-start.23 = (bf16[256,512]{1,0:T(8,128)(2,1)S(1)}, bf16[256,512]{1,0:T(8,128)(2,1)S(1)}, u32[]{:S(2)}, u32[]{:S(2)}) collective-permute-start(bf16[256,512]{1,0:T(8,128)(2,1)S(1)} %convolution_convert_fusion.1), channel_id=1, source_target_pairs={{0,1},{1,2},{2,3},{3,4},{4,5},{5,6},{6,7},{7,0},{8,9},{9,10},{10,1... | collective-permute-start | bytes 786440 | tf_op jit(solution)/shard_map/ppermute | solution.py:30
  209.4 10.8 %collective-permute-start.20 = (bf16[256,512]{1,0:T(8,128)(2,1)S(1)}, bf16[256,512]{1,0:T(8,128)(2,1)S(1)}, u32[]{:S(2)}, u32[]{:S(2)}) collective-permute-start(bf16[256,512]{1,0:T(8,128)(2,1)S(1)} %convolution_convert_fusion.2), channel_id=1, source_target_pairs={{0,7},{1,0},{2,1},{3,2},{4,3},{5,4},{6,5},{7,6},{8,15},{9,8},{10,9... | collective-permute-start | bytes 786440 | tf_op jit(solution)/shard_map/ppermute | solution.py:30
  210.8 12.0 %collective-permute-start.16 = (bf16[256,512]{1,0:T(8,128)(2,1)S(1)}, bf16[256,512]{1,0:T(8,128)(2,1)S(1)}, u32[]{:S(2)}, u32[]{:S(2)}) collective-permute-start(bf16[256,512]{1,0:T(8,128)(2,1)S(1)} %convolution_convert_fusion.3), channel_id=1, source_target_pairs={{0,1},{1,2},{2,3},{3,4},{4,5},{5,6},{6,7},{7,0},{8,9},{9,10},{10,1... | collective-permute-start | bytes 786440 | tf_op jit(solution)/shard_map/ppermute | solution.py:30
  214.9 10.9 %collective-permute-start.27 = (bf16[256,512]{1,0:T(8,128)(2,1)S(1)}, bf16[256,512]{1,0:T(8,128)(2,1)S(1)}, u32[]{:S(2)}, u32[]{:S(2)}) collective-permute-start(bf16[256,512]{1,0:T(8,128)(2,1)S(1)} %add_convert_fusion.2), channel_id=1, source_target_pairs={{0,7},{1,0},{2,1},{3,2},{4,3},{5,4},{6,5},{7,6},{8,15},{9,8},{10,9... | collective-permute-start | bytes 786440 | tf_op jit(solution)/shard_map/ppermute | solution.py:30
  217.5 10.7 %collective-permute-start.24 = (bf16[256,512]{1,0:T(8,128)(2,1)S(1)}, bf16[256,512]{1,0:T(8,128)(2,1)S(1)}, u32[]{:S(2)}, u32[]{:S(2)}) collective-permute-start(bf16[256,512]{1,0:T(8,128)(2,1)S(1)} %add_convert_fusion.4), channel_id=1, source_target_pairs={{0,1},{1,2},{2,3},{3,4},{4,5},{5,6},{6,7},{7,0},{8,9},{9,10},{10,1... | collective-permute-start | bytes 786440 | tf_op jit(solution)/shard_map/ppermute | solution.py:30
  220.5 18.8 %collective-permute-start.21 = (bf16[256,512]{1,0:T(8,128)(2,1)S(1)}, bf16[256,512]{1,0:T(8,128)(2,1)S(1)}, u32[]{:S(2)}, u32[]{:S(2)}) collective-permute-start(bf16[256,512]{1,0:T(8,128)(2,1)S(1)} %add_convert_fusion.6), channel_id=1, source_target_pairs={{0,7},{1,0},{2,1},{3,2},{4,3},{5,4},{6,5},{7,6},{8,15},{9,8},{10,9... | collective-permute-start | bytes 786440 | tf_op jit(solution)/shard_map/ppermute | solution.py:30
  223.1 10.5 %collective-permute-start.17 = (bf16[256,512]{1,0:T(8,128)(2,1)S(1)}, bf16[256,512]{1,0:T(8,128)(2,1)S(1)}, u32[]{:S(2)}, u32[]{:S(2)}) collective-permute-start(bf16[256,512]{1,0:T(8,128)(2,1)S(1)} %add_convert_fusion.9), channel_id=1, source_target_pairs={{0,1},{1,2},{2,3},{3,4},{4,5},{5,6},{6,7},{7,0},{8,9},{9,10},{10,1... | collective-permute-start | bytes 786440 | tf_op jit(solution)/shard_map/ppermute | solution.py:30
  225.9 11.0 %collective-permute-start.28 = (bf16[256,512]{1,0:T(8,128)(2,1)S(1)}, bf16[256,512]{1,0:T(8,128)(2,1)S(1)}, u32[]{:S(2)}, u32[]{:S(2)}) collective-permute-start(bf16[256,512]{1,0:T(8,128)(2,1)S(1)} %add_convert_fusion.1), channel_id=1, source_target_pairs={{0,7},{1,0},{2,1},{3,2},{4,3},{5,4},{6,5},{7,6},{8,15},{9,8},{10,9... | collective-permute-start | bytes 786440 | tf_op jit(solution)/shard_map/ppermute | solution.py:30
  228.3 25.8 %copy-start.2 = (bf16[512,512]{1,0:T(8,128)(2,1)S(1)}, bf16[512,512]{1,0:T(8,128)(2,1)}, u32[]{:S(2)}) copy-start(bf16[512,512]{1,0:T(8,128)(2,1)} %param.8) | copy-start | bytes 1572868
  228.3 16.6 %collective-permute-start.25 = (bf16[256,512]{1,0:T(8,128)(2,1)S(1)}, bf16[256,512]{1,0:T(8,128)(2,1)S(1)}, u32[]{:S(2)}, u32[]{:S(2)}) collective-permute-start(bf16[256,512]{1,0:T(8,128)(2,1)S(1)} %add_convert_fusion.3), channel_id=1, source_target_pairs={{0,1},{1,2},{2,3},{3,4},{4,5},{5,6},{6,7},{7,0},{8,9},{9,10},{10,1... | collective-permute-start | bytes 786440 | tf_op jit(solution)/shard_map/ppermute | solution.py:30
  234.0 10.5 %collective-permute-start.18 = (bf16[256,512]{1,0:T(8,128)(2,1)S(1)}, bf16[256,512]{1,0:T(8,128)(2,1)S(1)}, u32[]{:S(2)}, u32[]{:S(2)}) collective-permute-start(bf16[256,512]{1,0:T(8,128)(2,1)S(1)} %add_convert_fusion.8), channel_id=1, source_target_pairs={{0,1},{1,2},{2,3},{3,4},{4,5},{5,6},{6,7},{7,0},{8,9},{9,10},{10,1... | collective-permute-start | bytes 786440 | tf_op jit(solution)/shard_map/ppermute | solution.py:30
  237.0 9.3 %collective-permute-start.29 = (bf16[256,512]{1,0:T(8,128)(2,1)S(1)}, bf16[256,512]{1,0:T(8,128)(2,1)S(1)}, u32[]{:S(2)}, u32[]{:S(2)}) collective-permute-start(bf16[256,512]{1,0:T(8,128)(2,1)S(1)} %add_convert_fusion), channel_id=1, source_target_pairs={{0,7},{1,0},{2,1},{3,2},{4,3},{5,4},{6,5},{7,6},{8,15},{9,8},{10,9... | collective-permute-start | bytes 786440 | tf_op jit(solution)/shard_map/ppermute | solution.py:30
  239.6 11.2 %collective-permute-start.22 = (bf16[256,512]{1,0:T(8,128)(2,1)S(1)}, bf16[256,512]{1,0:T(8,128)(2,1)S(1)}, u32[]{:S(2)}, u32[]{:S(2)}) collective-permute-start(bf16[256,512]{1,0:T(8,128)(2,1)S(1)} %add_convert_fusion.5), channel_id=1, source_target_pairs={{0,7},{1,0},{2,1},{3,2},{4,3},{5,4},{6,5},{7,6},{8,15},{9,8},{10,9... | collective-permute-start | bytes 786440 | tf_op jit(solution)/shard_map/ppermute | solution.py:30
  244.8 9.2 %collective-permute-start.19 = (bf16[256,512]{1,0:T(8,128)(2,1)S(1)}, bf16[256,512]{1,0:T(8,128)(2,1)S(1)}, u32[]{:S(2)}, u32[]{:S(2)}) collective-permute-start(bf16[256,512]{1,0:T(8,128)(2,1)S(1)} %add_convert_fusion.7), channel_id=1, source_target_pairs={{0,1},{1,2},{2,3},{3,4},{4,5},{5,6},{6,7},{7,0},{8,9},{9,10},{10,1... | collective-permute-start | bytes 786440 | tf_op jit(solution)/shard_map/ppermute | solution.py:30

commit v9 on v8

--- a/solution.py
+++ b/solution.py
@@ -30,7 +30,7 @@
     return lax.ppermute(block, "mp", [(i, (i + distance) % size) for i in range(size)])
 
 
-def project(hidden, norm_gain, w_query):
+def project(hidden, norm_gain, w_query, table):
     size = lax.axis_size("mp")
     me = lax.axis_index("mp")
     rows, width = hidden.shape
@@ -53,29 +53,31 @@
             sums[h] = (sums[h][0] + squares, sums[h][1] + product)
 
     sums = [None, None]
-    up = [hidden[:half], hidden[half:]]
-    down = list(up)
-    own = weights(0)
+    halves = [hidden[:half], hidden[half:]]
+    up, down = list(halves), list(halves)
+    waiting = [(h, halves[h], 0) for h in range(2)]
     for step in range(1, far):
-        behind, ahead = weights(-step), weights(step)
         for h in range(2):
             up[h] = turned(up[h], 1)
             down[1 - h] = turned(down[1 - h], -1)
         if step == 1:
-            for h in range(2):
-                mine = hidden[h * half:(h + 1) * half]
-                mine, up[h] = lax.optimization_barrier((mine, up[h]))
-                add(sums, h, mine, own)
+            up[1], table = lax.optimization_barrier((up[1], table))
+        else:
+            for h, block, offset in waiting:
+                block, up[h] = lax.optimization_barrier((block, up[h]))
+                add(sums, h, block, weights(offset))
+            waiting = []
         for h in range(2):
-            add(sums, h, up[h], behind)
-            add(sums, 1 - h, down[1 - h], ahead)
+            waiting += [(h, up[h], -step), (1 - h, down[1 - h], step)]
+    for h, block, offset in waiting:
+        add(sums, h, block, weights(offset))
     opposite = weights(far)
     add(sums, 0, turned(up[0], 1), opposite)
     add(sums, 1, turned(down[1], -1), opposite)
     total = size * width
     return jnp.concatenate(
         [product * lax.rsqrt(squares / total + eps) for squares, product in sums], axis=0
-    ).astype(bf16)
+    ).astype(bf16), table
 
 
 def output(halves, w_out):
@@ -292,24 +294,23 @@
     request_table = jnp.sum(jnp.where(slot_match, slot_ids[:, None], 0), axis=0)
     request_table = request_table.reshape(peer_count, SLOTS)
     source_span = jnp.sum(jnp.where(slot_match, req_order[:, None] // 2, 0), axis=0)
-    wanted = lax.all_to_all(request_table, "dp", split_axis=0, concat_axis=0, tiled=True)
-    wanted = wanted.reshape(-1)
-
     def is_last(i):
         position = i * count + lax.broadcasted_iota(jnp.int32, (1, count, 1), 1)
         return position == SPAN - 1
 
     def ask(i):
-        queries = project(hidden, norm_gain, w_query)
+        queries, table = project(hidden, norm_gain, w_query, request_table)
         blocks = queries.reshape(span_dev, count, inner_width)
         following = shifted(blocks[:1], "dp", -1)
         grouped = jnp.concatenate([blocks[1:], following], axis=0)
         if (i + 1) * count == SPAN:
             grouped = jnp.where(is_last(i), blocks, grouped)
         sent_rows = grouped[source_span].reshape(peer_count, SLOTS * count, inner_width)
-        return lax.all_to_all(sent_rows, "dp", split_axis=0, concat_axis=0, tiled=True)
-
-    def answer(asked):
+        wanted = lax.all_to_all(table, "dp", split_axis=0, concat_axis=0, tiled=True).reshape(-1)
+        return wanted, lax.all_to_all(sent_rows, "dp", split_axis=0, concat_axis=0, tiled=True)
+
+    def answer(request):
+        wanted, asked = request
         answers = attend(wanted, asked, nb_keys, nb_values)
         return lax.all_to_all(answers, "dp", split_axis=0, concat_axis=0, tiled=True)
 

time: 259 us -> 261 us (level)
  starting transfers between devices: 68.3 us -> 74.9 us
  waiting for transfers between devices: 145 us -> 141 us
    ppermute x28, starting transfers between devices: 38.7 us -> 44.9 us  [turned(): lax.ppermute(block, 'mp', [(i, (i + distance) % size) for i in range(size)])]
    ppermute x2, waiting for transfers between devices: 3.07 us -> 0.01 us  [shifted(): return lax.ppermute(block, axis, route)]
  transfers between devices with their start and end apart: 33 -> 33, of which waited for: 18 -> 19; matrix products, arithmetic and copies ran while one was open for 9% -> 8% of each run, Pallas kernels for 0% -> 0%
where the time goes in v9:
time: 261 us; the launch traced here: 258 us
  waiting for transfers between devices  141 us (54%)
  starting transfers between devices  74.9 us (29%)
  matrix products  14.3 us (5%)
  Pallas kernels  13.9 us (5%)
  local copies, waits for them, and re-layouts  7.29 us (3%)
  other arithmetic  5.48 us (2%)
    all_to_all x1, waiting for transfers between devices, answer(): lax.all_to_all(answers, 'dp', split_axis=0, concat_axis=0, tiled=True)  51.6 us
    all_to_all x1, waiting for transfers between devices, ask(): lax.all_to_all(sent_rows, 'dp', split_axis=0, concat_axis=0, tiled=True)  46.8 us
    ppermute x28, starting transfers between devices, turned(): lax.ppermute(block, 'mp', [(i, (i + distance) % size) for i in range(size)])  44.9 us
    ppermute x28, waiting for transfers between devices, turned(): lax.ppermute(block, 'mp', [(i, (i + distance) % size) for i in range(size)])  41.9 us
    pallas_call x1, Pallas kernels, attend(): pl.pallas_call(attend_kernel, out_shape=jax.ShapeDtypeStruct((peer_count,...  10.5 us
    all_to_all x1, starting transfers between devices, answer(): lax.all_to_all(answers, 'dp', split_axis=0, concat_axis=0, tiled=True)  10.1 us
    dot_general x16, matrix products, add(): product = jnp.dot(block, weight, preferred_element_type=f32)  9.41 us
    all_to_all x1, starting transfers between devices, ask(): lax.all_to_all(sent_rows, 'dp', split_axis=0, concat_axis=0, tiled=True)  8.51 us
  transfers between devices with their start and end apart: 33, of which 19 were waited for; matrix products, arithmetic and copies ran while one was open for 8% of the time, Pallas kernels for 0%

profile of v9, /device:TPU:28, one launch (start us, length us, event | category | flops | bytes accessed | tf_op | source)
XLA Modules:
  0.0 258.1 jit_solution(5920410071337620648)
XLA Ops:
  0.0 1.1 fusion.97
  1.1 2.0 collective-permute-start
  3.1 4.0 %collective-permute-start.9 = (bf16[256,512]{1,0:T(8,128)(2,1)S(1)}, bf16[256,512]{1,0:T(8,128)(2,1)S(1)}, u32[]{:S(2)}, u32[]{:S(2)}) collective-permute-start(bf16[256,512]{1,0:T(8,128)(2,1)S(1)} %get-tuple-element.48), channel_id=1, source_target_pairs={{0,7},{1,0},{2,1},{3,2},{4,3},{5,4},{6,5},{7,6},{8,15},{9,8},{10,9... | collective-permute-start | bytes 786440 | tf_op jit(solution)/shard_map/ppermute | solution.py:30
  7.1 1.9 collective-permute-start.3
  9.1 0.7 and_select_fusion.1
  11.3 0.7 reshape.186
  12.0 2.2 collective-permute-done
  14.2 5.6 %collective-permute-done.1 = bf16[256,512]{1,0:T(8,128)(2,1)S(1)} collective-permute-done((bf16[256,512]{1,0:T(8,128)(2,1)S(1)}, bf16[256,512]{1,0:T(8,128)(2,1)S(1)}, u32[]{:S(2)}, u32[]{:S(2)}) %collective-permute-start.1) | collective-permute-done | bytes 262176 | tf_op jit(solution)/shard_map/ppermute | solution.py:30
  19.9 1.1 fusion.98
  21.0 3.2 %collective-permute-start.10 = (bf16[256,512]{1,0:T(8,128)(2,1)S(1)}, bf16[256,512]{1,0:T(8,128)(2,1)S(1)}, u32[]{:S(2)}, u32[]{:S(2)}) collective-permute-start(bf16[256,512]{1,0:T(8,128)(2,1)S(1)} %collective-permute-done.9), channel_id=1, source_target_pairs={{0,7},{1,0},{2,1},{3,2},{4,3},{5,4},{6,5},{7,6},{8,15},{9,8},{10,9... | collective-permute-start | bytes 786440 | tf_op jit(solution)/shard_map/ppermute | solution.py:30
  24.2 0.8 collective-permute-start.5
  25.4 0.8 collective-permute-start.11
  26.3 4.7 %collective-permute-done.2 = bf16[256,512]{1,0:T(8,128)(2,1)S(1)} collective-permute-done((bf16[256,512]{1,0:T(8,128)(2,1)S(1)}, bf16[256,512]{1,0:T(8,128)(2,1)S(1)}, u32[]{:S(2)}, u32[]{:S(2)}) %collective-permute-start.2) | collective-permute-done | bytes 262176 | tf_op jit(solution)/shard_map/ppermute | solution.py:30
  31.0 1.4 fusion.48
  32.4 1.4 fusion.50
  33.9 1.4 fusion.51
  35.9 3.3 %collective-permute-start.12 = (bf16[256,512]{1,0:T(8,128)(2,1)S(1)}, bf16[256,512]{1,0:T(8,128)(2,1)S(1)}, u32[]{:S(2)}, u32[]{:S(2)}) collective-permute-start(bf16[256,512]{1,0:T(8,128)(2,1)S(1)} %collective-permute-done.10), channel_id=1, source_target_pairs={{0,7},{1,0},{2,1},{3,2},{4,3},{5,4},{6,5},{7,6},{8,15},{9,8},{10,9... | collective-permute-start | bytes 786440 | tf_op jit(solution)/shard_map/ppermute | solution.py:30
  39.6 0.9 collective-permute-start.6
  41.5 1.5 collective-permute-start.7
  45.9 3.7 %collective-permute-start.13 = (bf16[256,512]{1,0:T(8,128)(2,1)S(1)}, bf16[256,512]{1,0:T(8,128)(2,1)S(1)}, u32[]{:S(2)}, u32[]{:S(2)}) collective-permute-start(bf16[256,512]{1,0:T(8,128)(2,1)S(1)} %collective-permute-done.12), channel_id=1, source_target_pairs={{0,7},{1,0},{2,1},{3,2},{4,3},{5,4},{6,5},{7,6},{8,15},{9,8},{10,9... | collective-permute-start | bytes 786440 | tf_op jit(solution)/shard_map/ppermute | solution.py:30
  50.1 0.9 collective-permute-done.6
  51.5 2.8 %collective-permute-done.13 = bf16[256,512]{1,0:T(8,128)(2,1)S(1)} collective-permute-done((bf16[256,512]{1,0:T(8,128)(2,1)S(1)}, bf16[256,512]{1,0:T(8,128)(2,1)S(1)}, u32[]{:S(2)}, u32[]{:S(2)}) %collective-permute-start.13) | collective-permute-done | bytes 262176 | tf_op jit(solution)/shard_map/ppermute | solution.py:30
  55.9 1.9 collective-permute-start.14
  57.8 7.4 %all-to-all-start = ((s32[32,1,2]{2,1,0:T(1,128)}), s32[32,1,2]{2,1,0:T(1,128)S(1)}, u32[]{:S(2)}, u32[]{:S(2)}) async-start(s32[32,1,2]{2,1,0:T(1,128)} %bitcast.13), calls=%async_computation | async-start | bytes 32768 | tf_op jit(solution)/shard_map/all_to_all | solution.py:309
  65.5 2.8 %gather_fusion = bf16[64,64,512]{2,1,0:T(8,128)(2,1)} fusion(bf16[8,64,512]{2,1,0:T(8,128)(2,1)S(1)} %maximum_select_fusion, s32[1024]{0:T(1024)S(1)} %pad_clamp_fusion), kind=kCustom, calls=%fused_computation | custom fusion | bytes 8388864 | tf_op jit(solution)/shard_map/gather | solution.py:308
  68.9 8.5 %all-to-all-start.1 = ((bf16[32,128,512]{2,1,0:T(8,128)(2,1)}), bf16[32,128,512]{2,1,0:T(8,128)(2,1)}, u32[]{:S(2)}, u32[]{:S(2)}) async-start(bf16[32,128,512]{2,1,0:T(8,128)(2,1)} %bitcast.77), calls=%async_computation.1 | async-start | bytes 8388608 | tf_op jit(solution)/shard_map/all_to_all | solution.py:310
  79.2 46.8 %all-to-all-done.1.q_ref = bf16[32,128,512]{2,1,0:T(8,128)(2,1)} async-done(((bf16[32,128,512]{2,1,0:T(8,128)(2,1)}), bf16[32,128,512]{2,1,0:T(8,128)(2,1)}, u32[]{:S(2)}, u32[]{:S(2)}) %all-to-all-start.1) | async-done | bytes 4194336 | tf_op jit(solution)/shard_map/all_to_all | solution.py:310
  126.0 10.5 %attend.1 = bf16[32,136,512]{2,1,0:T(8,128)(2,1)} custom-call(s32[64]{0:T(128)} %reshape.187.ids_ref, bf16[32,128,512]{2,1,0:T(8,128)(2,1)} %all-to-all-done.1.q_ref, bf16[8,128,512]{2,1,0:T(8,128)(2,1)} %k_ref.1, bf16[8,128,512]{2,1,0:T(8,128)(2,1)} %v_ref.1), custom_call_target="tpu_custom_call" | custom-call | flops 2147483648 | bytes 8388608 | tf_op jit(solution)/shard_map/attend/pallas_call | solution.py:173
  136.6 10.1 %all-to-all-start.2 = ((bf16[32,136,512]{2,1,0:T(8,128)(2,1)}), bf16[32,136,512]{2,1,0:T(8,128)(2,1)}, u32[]{:S(2)}, u32[]{:S(2)}) async-start(bf16[32,136,512]{2,1,0:T(8,128)(2,1)} %attend.1), calls=%async_computation.2 | async-start | bytes 8912896 | tf_op jit(solution)/shard_map/all_to_all | solution.py:315
  146.7 51.6 %all-to-all-done.2.back_ref = bf16[32,136,512]{2,1,0:T(8,128)(2,1)} async-done(((bf16[32,136,512]{2,1,0:T(8,128)(2,1)}), bf16[32,136,512]{2,1,0:T(8,128)(2,1)}, u32[]{:S(2)}, u32[]{:S(2)}) %all-to-all-start.2) | async-done | bytes 4456480 | tf_op jit(solution)/shard_map/all_to_all | solution.py:315
  198.3 3.3 %combine.1 = (bf16[4,64,512]{2,1,0:T(8,128)(2,1)S(1)}, bf16[4,64,512]{2,1,0:T(8,128)(2,1)S(1)}, bf16[64,512]{1,0:T(8,128)(2,1)S(1)}) custom-call(s32[16]{0:T(128)S(1)} %reshape.185.owner_ref, s32[16]{0:T(128)S(1)} %get-tuple-element.82.rank_ref, s32[1]{0:T(128)} %copy.27.live_ref, bf16[32,136,512]{2,1,0:T(8,128)(2,1)} %all-to-all-done.2.back_ref), custom_call_target="tpu_custom_call" | custom-call | flops 2097152 | bytes 1572864 | tf_op jit(solution)/shard_map/combine/pallas_call | solution.py:254
  203.3 1.9 collective-permute-start.15
  205.5 3.8 %collective-permute-start.26 = (bf16[256,512]{1,0:T(8,128)(2,1)S(1)}, bf16[256,512]{1,0:T(8,128)(2,1)S(1)}, u32[]{:S(2)}, u32[]{:S(2)}) collective-permute-start(bf16[256,512]{1,0:T(8,128)(2,1)S(1)} %convolution_convert_fusion), channel_id=1, source_target_pairs={{0,7},{1,0},{2,1},{3,2},{4,3},{5,4},{6,5},{7,6},{8,15},{9,8},{10,9... | collective-permute-start | bytes 786440 | tf_op jit(solution)/shard_map/ppermute | solution.py:30
  210.1 3.3 %collective-permute-start.20 = (bf16[256,512]{1,0:T(8,128)(2,1)S(1)}, bf16[256,512]{1,0:T(8,128)(2,1)S(1)}, u32[]{:S(2)}, u32[]{:S(2)}) collective-permute-start(bf16[256,512]{1,0:T(8,128)(2,1)S(1)} %convolution_convert_fusion.2), channel_id=1, source_target_pairs={{0,7},{1,0},{2,1},{3,2},{4,3},{5,4},{6,5},{7,6},{8,15},{9,8},{10,9... | collective-permute-start | bytes 786440 | tf_op jit(solution)/shard_map/ppermute | solution.py:30
  213.8 2.2 collective-permute-done.26
  216.3 3.8 %collective-permute-start.27 = (bf16[256,512]{1,0:T(8,128)(2,1)S(1)}, bf16[256,512]{1,0:T(8,128)(2,1)S(1)}, u32[]{:S(2)}, u32[]{:S(2)}) collective-permute-start(bf16[256,512]{1,0:T(8,128)(2,1)S(1)} %add_convert_fusion.2), channel_id=1, source_target_pairs={{0,7},{1,0},{2,1},{3,2},{4,3},{5,4},{6,5},{7,6},{8,15},{9,8},{10,9... | collective-permute-start | bytes 786440 | tf_op jit(solution)/shard_map/ppermute | solution.py:30
  220.5 1.1 collective-permute-done.20
  221.9 3.8 %collective-permute-start.21 = (bf16[256,512]{1,0:T(8,128)(2,1)S(1)}, bf16[256,512]{1,0:T(8,128)(2,1)S(1)}, u32[]{:S(2)}, u32[]{:S(2)}) collective-permute-start(bf16[256,512]{1,0:T(8,128)(2,1)S(1)} %add_convert_fusion.6), channel_id=1, source_target_pairs={{0,7},{1,0},{2,1},{3,2},{4,3},{5,4},{6,5},{7,6},{8,15},{9,8},{10,9... | collective-permute-start | bytes 786440 | tf_op jit(solution)/shard_map/ppermute | solution.py:30
  226.1 1.1 collective-permute-done.27
  227.3 3.8 %collective-permute-start.28 = (bf16[256,512]{1,0:T(8,128)(2,1)S(1)}, bf16[256,512]{1,0:T(8,128)(2,1)S(1)}, u32[]{:S(2)}, u32[]{:S(2)}) collective-permute-start(bf16[256,512]{1,0:T(8,128)(2,1)S(1)} %add_convert_fusion.1), channel_id=1, source_target_pairs={{0,7},{1,0},{2,1},{3,2},{4,3},{5,4},{6,5},{7,6},{8,15},{9,8},{10,9... | collective-permute-start | bytes 786440 | tf_op jit(solution)/shard_map/ppermute | solution.py:30
  231.3 5.3 %collective-permute-done.17 = bf16[256,512]{1,0:T(8,128)(2,1)S(1)} collective-permute-done((bf16[256,512]{1,0:T(8,128)(2,1)S(1)}, bf16[256,512]{1,0:T(8,128)(2,1)S(1)}, u32[]{:S(2)}, u32[]{:S(2)}) %collective-permute-start.17) | collective-permute-done | bytes 262176 | tf_op jit(solution)/shard_map/ppermute | solution.py:30
  236.9 1.4 collective-permute-done.28
  238.4 3.8 %collective-permute-start.29 = (bf16[256,512]{1,0:T(8,128)(2,1)S(1)}, bf16[256,512]{1,0:T(8,128)(2,1)S(1)}, u32[]{:S(2)}, u32[]{:S(2)}) collective-permute-start(bf16[256,512]{1,0:T(8,128)(2,1)S(1)} %add_convert_fusion), channel_id=1, source_target_pairs={{0,7},{1,0},{2,1},{3,2},{4,3},{5,4},{6,5},{7,6},{8,15},{9,8},{10,9... | collective-permute-start | bytes 786440 | tf_op jit(solution)/shard_map/ppermute | solution.py:30
  242.6 4.8 %collective-permute-done.18 = bf16[256,512]{1,0:T(8,128)(2,1)S(1)} collective-permute-done((bf16[256,512]{1,0:T(8,128)(2,1)S(1)}, bf16[256,512]{1,0:T(8,128)(2,1)S(1)}, u32[]{:S(2)}, u32[]{:S(2)}) %collective-permute-start.18) | collective-permute-done | bytes 262176 | tf_op jit(solution)/shard_map/ppermute | solution.py:30
  247.8 1.1 collective-permute-done.29
  249.0 4.5 %collective-permute-done.22 = bf16[256,512]{1,0:T(8,128)(2,1)S(1)} collective-permute-done((bf16[256,512]{1,0:T(8,128)(2,1)S(1)}, bf16[256,512]{1,0:T(8,128)(2,1)S(1)}, u32[]{:S(2)}, u32[]{:S(2)}) %collective-permute-start.22) | collective-permute-done | bytes 262176 | tf_op jit(solution)/shard_map/ppermute | solution.py:30
  253.5 3.4 %collective-permute-done.19 = bf16[256,512]{1,0:T(8,128)(2,1)S(1)} collective-permute-done((bf16[256,512]{1,0:T(8,128)(2,1)S(1)}, bf16[256,512]{1,0:T(8,128)(2,1)S(1)}, u32[]{:S(2)}, u32[]{:S(2)}) %collective-permute-start.19) | collective-permute-done | bytes 262176 | tf_op jit(solution)/shard_map/ppermute | solution.py:30
  257.0 1.2 maximum_add_fusion
  (107 shorter events, 17.5 us)
Async XLA Ops:
  1.1 13.1 %collective-permute-start = (bf16[256,512]{1,0:T(8,128)(2,1)S(1)}, bf16[256,512]{1,0:T(8,128)(2,1)S(1)}, u32[]{:S(2)}, u32[]{:S(2)}) collective-permute-start(bf16[256,512]{1,0:T(8,128)(2,1)S(1)} %get-tuple-element.48), channel_id=1, source_target_pairs={{0,1},{1,2},{2,3},{3,4},{4,5},{5,6},{6,7},{7,0},{8,9},{9,10},{10,1... | collective-permute-start | bytes 786440 | tf_op jit(solution)/shard_map/ppermute | solution.py:30
  3.1 17.9 %collective-permute-start.9 = (bf16[256,512]{1,0:T(8,128)(2,1)S(1)}, bf16[256,512]{1,0:T(8,128)(2,1)S(1)}, u32[]{:S(2)}, u32[]{:S(2)}) collective-permute-start(bf16[256,512]{1,0:T(8,128)(2,1)S(1)} %get-tuple-element.48), channel_id=1, source_target_pairs={{0,7},{1,0},{2,1},{3,2},{4,3},{5,4},{6,5},{7,6},{8,15},{9,8},{10,9... | collective-permute-start | bytes 786440 | tf_op jit(solution)/shard_map/ppermute | solution.py:30
  7.1 17.1 %collective-permute-start.3 = (bf16[256,512]{1,0:T(8,128)(2,1)S(1)}, bf16[256,512]{1,0:T(8,128)(2,1)S(1)}, u32[]{:S(2)}, u32[]{:S(2)}) collective-permute-start(bf16[256,512]{1,0:T(8,128)(2,1)S(1)} %get-tuple-element.37), channel_id=1, source_target_pairs={{0,7},{1,0},{2,1},{3,2},{4,3},{5,4},{6,5},{7,6},{8,15},{9,8},{10,9... | collective-permute-start | bytes 786440 | tf_op jit(solution)/shard_map/ppermute | solution.py:30
  9.0 10.7 %collective-permute-start.1 = (bf16[256,512]{1,0:T(8,128)(2,1)S(1)}, bf16[256,512]{1,0:T(8,128)(2,1)S(1)}, u32[]{:S(2)}, u32[]{:S(2)}) collective-permute-start(bf16[256,512]{1,0:T(8,128)(2,1)S(1)} %get-tuple-element.37), channel_id=1, source_target_pairs={{0,1},{1,2},{2,3},{3,4},{4,5},{5,6},{6,7},{7,0},{8,9},{9,10},{10,1... | collective-permute-start | bytes 786440 | tf_op jit(solution)/shard_map/ppermute | solution.py:30
  14.2 11.2 %collective-permute-start.8 = (bf16[256,512]{1,0:T(8,128)(2,1)S(1)}, bf16[256,512]{1,0:T(8,128)(2,1)S(1)}, u32[]{:S(2)}, u32[]{:S(2)}) collective-permute-start(bf16[256,512]{1,0:T(8,128)(2,1)S(1)} %collective-permute-done), channel_id=1, source_target_pairs={{0,1},{1,2},{2,3},{3,4},{4,5},{5,6},{6,7},{7,0},{8,9},{9,10},{10,1... | collective-permute-start | bytes 786440 | tf_op jit(solution)/shard_map/ppermute | solution.py:30
  19.8 11.2 %collective-permute-start.2 = (bf16[256,512]{1,0:T(8,128)(2,1)S(1)}, bf16[256,512]{1,0:T(8,128)(2,1)S(1)}, u32[]{:S(2)}, u32[]{:S(2)}) collective-permute-start(bf16[256,512]{1,0:T(8,128)(2,1)S(1)} %collective-permute-done.1), channel_id=1, source_target_pairs={{0,1},{1,2},{2,3},{3,4},{4,5},{5,6},{6,7},{7,0},{8,9},{9,10},{10,1... | collective-permute-start | bytes 786440 | tf_op jit(solution)/shard_map/ppermute | solution.py:30
  19.9 19.3 %copy-start.1 = (bf16[4096,512]{1,0:T(8,128)(2,1)S(1)}, bf16[4096,512]{1,0:T(8,128)(2,1)}, u32[]{:S(2)}) copy-start(bf16[4096,512]{1,0:T(8,128)(2,1)} %param.10) | copy-start | bytes 12582916
  21.0 14.9 %collective-permute-start.10 = (bf16[256,512]{1,0:T(8,128)(2,1)S(1)}, bf16[256,512]{1,0:T(8,128)(2,1)S(1)}, u32[]{:S(2)}, u32[]{:S(2)}) collective-permute-start(bf16[256,512]{1,0:T(8,128)(2,1)S(1)} %collective-permute-done.9), channel_id=1, source_target_pairs={{0,7},{1,0},{2,1},{3,2},{4,3},{5,4},{6,5},{7,6},{8,15},{9,8},{10,9... | collective-permute-start | bytes 786440 | tf_op jit(solution)/shard_map/ppermute | solution.py:30
  24.2 15.5 %collective-permute-start.5 = (bf16[256,512]{1,0:T(8,128)(2,1)S(1)}, bf16[256,512]{1,0:T(8,128)(2,1)S(1)}, u32[]{:S(2)}, u32[]{:S(2)}) collective-permute-start(bf16[256,512]{1,0:T(8,128)(2,1)S(1)} %collective-permute-done.3), channel_id=1, source_target_pairs={{0,7},{1,0},{2,1},{3,2},{4,3},{5,4},{6,5},{7,6},{8,15},{9,8},{10,9... | collective-permute-start | bytes 786440 | tf_op jit(solution)/shard_map/ppermute | solution.py:30
  25.4 15.5 %collective-permute-start.11 = (bf16[256,512]{1,0:T(8,128)(2,1)S(1)}, bf16[256,512]{1,0:T(8,128)(2,1)S(1)}, u32[]{:S(2)}, u32[]{:S(2)}) collective-permute-start(bf16[256,512]{1,0:T(8,128)(2,1)S(1)} %collective-permute-done.8), channel_id=1, source_target_pairs={{0,1},{1,2},{2,3},{3,4},{4,5},{5,6},{6,7},{7,0},{8,9},{9,10},{10,1... | collective-permute-start | bytes 786440 | tf_op jit(solution)/shard_map/ppermute | solution.py:30
  31.0 10.4 %collective-permute-start.4 = (bf16[256,512]{1,0:T(8,128)(2,1)S(1)}, bf16[256,512]{1,0:T(8,128)(2,1)S(1)}, u32[]{:S(2)}, u32[]{:S(2)}) collective-permute-start(bf16[256,512]{1,0:T(8,128)(2,1)S(1)} %collective-permute-done.2), channel_id=1, source_target_pairs={{0,1},{1,2},{2,3},{3,4},{4,5},{5,6},{6,7},{7,0},{8,9},{9,10},{10,1... | collective-permute-start | bytes 786440 | tf_op jit(solution)/shard_map/ppermute | solution.py:30
  35.9 10.0 %collective-permute-start.12 = (bf16[256,512]{1,0:T(8,128)(2,1)S(1)}, bf16[256,512]{1,0:T(8,128)(2,1)S(1)}, u32[]{:S(2)}, u32[]{:S(2)}) collective-permute-start(bf16[256,512]{1,0:T(8,128)(2,1)S(1)} %collective-permute-done.10), channel_id=1, source_target_pairs={{0,7},{1,0},{2,1},{3,2},{4,3},{5,4},{6,5},{7,6},{8,15},{9,8},{10,9... | collective-permute-start | bytes 786440 | tf_op jit(solution)/shard_map/ppermute | solution.py:30
  39.6 11.4 %collective-permute-start.6 = (bf16[256,512]{1,0:T(8,128)(2,1)S(1)}, bf16[256,512]{1,0:T(8,128)(2,1)S(1)}, u32[]{:S(2)}, u32[]{:S(2)}) collective-permute-start(bf16[256,512]{1,0:T(8,128)(2,1)S(1)} %collective-permute-done.5), channel_id=1, source_target_pairs={{0,7},{1,0},{2,1},{3,2},{4,3},{5,4},{6,5},{7,6},{8,15},{9,8},{10,9... | collective-permute-start | bytes 786440 | tf_op jit(solution)/shard_map/ppermute | solution.py:30
  41.5 13.0 %collective-permute-start.7 = (bf16[256,512]{1,0:T(8,128)(2,1)S(1)}, bf16[256,512]{1,0:T(8,128)(2,1)S(1)}, u32[]{:S(2)}, u32[]{:S(2)}) collective-permute-start(bf16[256,512]{1,0:T(8,128)(2,1)S(1)} %collective-permute-done.4), channel_id=1, source_target_pairs={{0,1},{1,2},{2,3},{3,4},{4,5},{5,6},{6,7},{7,0},{8,9},{9,10},{10,1... | collective-permute-start | bytes 786440 | tf_op jit(solution)/shard_map/ppermute | solution.py:30
  45.9 8.4 %collective-permute-start.13 = (bf16[256,512]{1,0:T(8,128)(2,1)S(1)}, bf16[256,512]{1,0:T(8,128)(2,1)S(1)}, u32[]{:S(2)}, u32[]{:S(2)}) collective-permute-start(bf16[256,512]{1,0:T(8,128)(2,1)S(1)} %collective-permute-done.12), channel_id=1, source_target_pairs={{0,7},{1,0},{2,1},{3,2},{4,3},{5,4},{6,5},{7,6},{8,15},{9,8},{10,9... | collective-permute-start | bytes 786440 | tf_op jit(solution)/shard_map/ppermute | solution.py:30
  55.9 9.4 %collective-permute-start.14 = (bf16[1,64,512]{2,1,0:T(8,128)(2,1)S(1)}, bf16[1,64,512]{2,1,0:T(8,128)(2,1)S(1)}, u32[]{:S(2)}, u32[]{:S(2)}) collective-permute-start(bf16[1,64,512]{2,1,0:T(8,128)(2,1)S(1)} %slice_bitcast_fusion), channel_id=1, source_target_pairs={{8,0},{16,8},{24,16},{32,24},{40,32},{48,40},{56,48},{64,56},{72,6... | collective-permute-start | bytes 196616 | tf_op jit(solution)/shard_map/ppermute | solution.py:25
  57.8 11.0 %all-to-all-start = ((s32[32,1,2]{2,1,0:T(1,128)}), s32[32,1,2]{2,1,0:T(1,128)S(1)}, u32[]{:S(2)}, u32[]{:S(2)}) async-start(s32[32,1,2]{2,1,0:T(1,128)} %bitcast.13), calls=%async_computation | async-start | bytes 32768 | tf_op jit(solution)/shard_map/all_to_all | solution.py:309
  68.9 57.2 %all-to-all-start.1 = ((bf16[32,128,512]{2,1,0:T(8,128)(2,1)}), bf16[32,128,512]{2,1,0:T(8,128)(2,1)}, u32[]{:S(2)}, u32[]{:S(2)}) async-start(bf16[32,128,512]{2,1,0:T(8,128)(2,1)} %bitcast.77), calls=%async_computation.1 | async-start | bytes 8388608 | tf_op jit(solution)/shard_map/all_to_all | solution.py:310
  136.6 61.8 %all-to-all-start.2 = ((bf16[32,136,512]{2,1,0:T(8,128)(2,1)}), bf16[32,136,512]{2,1,0:T(8,128)(2,1)}, u32[]{:S(2)}, u32[]{:S(2)}) async-start(bf16[32,136,512]{2,1,0:T(8,128)(2,1)} %attend.1), calls=%async_computation.2 | async-start | bytes 8912896 | tf_op jit(solution)/shard_map/all_to_all | solution.py:315
  198.3 3.4 %copy-start = (bf16[512,4096]{1,0:T(8,128)(2,1)S(1)}, bf16[512,4096]{1,0:T(8,128)(2,1)}, u32[]{:S(2)}) copy-start(bf16[512,4096]{1,0:T(8,128)(2,1)} %param.11) | copy-start | bytes 12582916
  203.3 6.0 %collective-permute-start.15 = (bf16[64,512]{1,0:T(8,128)(2,1)S(1)}, bf16[64,512]{1,0:T(8,128)(2,1)S(1)}, u32[]{:S(2)}, u32[]{:S(2)}) collective-permute-start(bf16[64,512]{1,0:T(8,128)(2,1)S(1)} %get-tuple-element.58), channel_id=1, source_target_pairs={{0,8},{8,16},{16,24},{24,32},{32,40},{40,48},{48,56},{56,64},{64,7... | collective-permute-start | bytes 196616 | tf_op jit(solution)/shard_map/ppermute | solution.py:25
  205.5 10.5 %collective-permute-start.26 = (bf16[256,512]{1,0:T(8,128)(2,1)S(1)}, bf16[256,512]{1,0:T(8,128)(2,1)S(1)}, u32[]{:S(2)}, u32[]{:S(2)}) collective-permute-start(bf16[256,512]{1,0:T(8,128)(2,1)S(1)} %convolution_convert_fusion), channel_id=1, source_target_pairs={{0,7},{1,0},{2,1},{3,2},{4,3},{5,4},{6,5},{7,6},{8,15},{9,8},{10,9... | collective-permute-start | bytes 786440 | tf_op jit(solution)/shard_map/ppermute | solution.py:30
  209.3 10.8 %collective-permute-start.23 = (bf16[256,512]{1,0:T(8,128)(2,1)S(1)}, bf16[256,512]{1,0:T(8,128)(2,1)S(1)}, u32[]{:S(2)}, u32[]{:S(2)}) collective-permute-start(bf16[256,512]{1,0:T(8,128)(2,1)S(1)} %convolution_convert_fusion.1), channel_id=1, source_target_pairs={{0,1},{1,2},{2,3},{3,4},{4,5},{5,6},{6,7},{7,0},{8,9},{9,10},{10,1... | collective-permute-start | bytes 786440 | tf_op jit(solution)/shard_map/ppermute | solution.py:30
  210.1 11.5 %collective-permute-start.20 = (bf16[256,512]{1,0:T(8,128)(2,1)S(1)}, bf16[256,512]{1,0:T(8,128)(2,1)S(1)}, u32[]{:S(2)}, u32[]{:S(2)}) collective-permute-start(bf16[256,512]{1,0:T(8,128)(2,1)S(1)} %convolution_convert_fusion.2), channel_id=1, source_target_pairs={{0,7},{1,0},{2,1},{3,2},{4,3},{5,4},{6,5},{7,6},{8,15},{9,8},{10,9... | collective-permute-start | bytes 786440 | tf_op jit(solution)/shard_map/ppermute | solution.py:30
  213.7 12.0 %collective-permute-start.16 = (bf16[256,512]{1,0:T(8,128)(2,1)S(1)}, bf16[256,512]{1,0:T(8,128)(2,1)S(1)}, u32[]{:S(2)}, u32[]{:S(2)}) collective-permute-start(bf16[256,512]{1,0:T(8,128)(2,1)S(1)} %convolution_convert_fusion.3), channel_id=1, source_target_pairs={{0,1},{1,2},{2,3},{3,4},{4,5},{5,6},{6,7},{7,0},{8,9},{9,10},{10,1... | collective-permute-start | bytes 786440 | tf_op jit(solution)/shard_map/ppermute | solution.py:30
  216.3 10.9 %collective-permute-start.27 = (bf16[256,512]{1,0:T(8,128)(2,1)S(1)}, bf16[256,512]{1,0:T(8,128)(2,1)S(1)}, u32[]{:S(2)}, u32[]{:S(2)}) collective-permute-start(bf16[256,512]{1,0:T(8,128)(2,1)S(1)} %add_convert_fusion.2), channel_id=1, source_target_pairs={{0,7},{1,0},{2,1},{3,2},{4,3},{5,4},{6,5},{7,6},{8,15},{9,8},{10,9... | collective-permute-start | bytes 786440 | tf_op jit(solution)/shard_map/ppermute | solution.py:30
  220.4 10.7 %collective-permute-start.24 = (bf16[256,512]{1,0:T(8,128)(2,1)S(1)}, bf16[256,512]{1,0:T(8,128)(2,1)S(1)}, u32[]{:S(2)}, u32[]{:S(2)}) collective-permute-start(bf16[256,512]{1,0:T(8,128)(2,1)S(1)} %add_convert_fusion.4), channel_id=1, source_target_pairs={{0,1},{1,2},{2,3},{3,4},{4,5},{5,6},{6,7},{7,0},{8,9},{9,10},{10,1... | collective-permute-start | bytes 786440 | tf_op jit(solution)/shard_map/ppermute | solution.py:30
  221.9 20.3 %collective-permute-start.21 = (bf16[256,512]{1,0:T(8,128)(2,1)S(1)}, bf16[256,512]{1,0:T(8,128)(2,1)S(1)}, u32[]{:S(2)}, u32[]{:S(2)}) collective-permute-start(bf16[256,512]{1,0:T(8,128)(2,1)S(1)} %add_convert_fusion.6), channel_id=1, source_target_pairs={{0,7},{1,0},{2,1},{3,2},{4,3},{5,4},{6,5},{7,6},{8,15},{9,8},{10,9... | collective-permute-start | bytes 786440 | tf_op jit(solution)/shard_map/ppermute | solution.py:30
  226.0 10.5 %collective-permute-start.17 = (bf16[256,512]{1,0:T(8,128)(2,1)S(1)}, bf16[256,512]{1,0:T(8,128)(2,1)S(1)}, u32[]{:S(2)}, u32[]{:S(2)}) collective-permute-start(bf16[256,512]{1,0:T(8,128)(2,1)S(1)} %add_convert_fusion.9), channel_id=1, source_target_pairs={{0,1},{1,2},{2,3},{3,4},{4,5},{5,6},{6,7},{7,0},{8,9},{9,10},{10,1... | collective-permute-start | bytes 786440 | tf_op jit(solution)/shard_map/ppermute | solution.py:30
  227.3 11.0 %collective-permute-start.28 = (bf16[256,512]{1,0:T(8,128)(2,1)S(1)}, bf16[256,512]{1,0:T(8,128)(2,1)S(1)}, u32[]{:S(2)}, u32[]{:S(2)}) collective-permute-start(bf16[256,512]{1,0:T(8,128)(2,1)S(1)} %add_convert_fusion.1), channel_id=1, source_target_pairs={{0,7},{1,0},{2,1},{3,2},{4,3},{5,4},{6,5},{7,6},{8,15},{9,8},{10,9... | collective-permute-start | bytes 786440 | tf_op jit(solution)/shard_map/ppermute | solution.py:30
  231.2 25.8 %copy-start.2 = (bf16[512,512]{1,0:T(8,128)(2,1)S(1)}, bf16[512,512]{1,0:T(8,128)(2,1)}, u32[]{:S(2)}) copy-start(bf16[512,512]{1,0:T(8,128)(2,1)} %param.8) | copy-start | bytes 1572868
  231.2 16.6 %collective-permute-start.25 = (bf16[256,512]{1,0:T(8,128)(2,1)S(1)}, bf16[256,512]{1,0:T(8,128)(2,1)S(1)}, u32[]{:S(2)}, u32[]{:S(2)}) collective-permute-start(bf16[256,512]{1,0:T(8,128)(2,1)S(1)} %add_convert_fusion.3), channel_id=1, source_target_pairs={{0,1},{1,2},{2,3},{3,4},{4,5},{5,6},{6,7},{7,0},{8,9},{9,10},{10,1... | collective-permute-start | bytes 786440 | tf_op jit(solution)/shard_map/ppermute | solution.py:30
  236.9 10.5 %collective-permute-start.18 = (bf16[256,512]{1,0:T(8,128)(2,1)S(1)}, bf16[256,512]{1,0:T(8,128)(2,1)S(1)}, u32[]{:S(2)}, u32[]{:S(2)}) collective-permute-start(bf16[256,512]{1,0:T(8,128)(2,1)S(1)} %add_convert_fusion.8), channel_id=1, source_target_pairs={{0,1},{1,2},{2,3},{3,4},{4,5},{5,6},{6,7},{7,0},{8,9},{9,10},{10,1... | collective-permute-start | bytes 786440 | tf_op jit(solution)/shard_map/ppermute | solution.py:30
  238.4 10.5 %collective-permute-start.29 = (bf16[256,512]{1,0:T(8,128)(2,1)S(1)}, bf16[256,512]{1,0:T(8,128)(2,1)S(1)}, u32[]{:S(2)}, u32[]{:S(2)}) collective-permute-start(bf16[256,512]{1,0:T(8,128)(2,1)S(1)} %add_convert_fusion), channel_id=1, source_target_pairs={{0,7},{1,0},{2,1},{3,2},{4,3},{5,4},{6,5},{7,6},{8,15},{9,8},{10,9... | collective-permute-start | bytes 786440 | tf_op jit(solution)/shard_map/ppermute | solution.py:30
  242.5 11.0 %collective-permute-start.22 = (bf16[256,512]{1,0:T(8,128)(2,1)S(1)}, bf16[256,512]{1,0:T(8,128)(2,1)S(1)}, u32[]{:S(2)}, u32[]{:S(2)}) collective-permute-start(bf16[256,512]{1,0:T(8,128)(2,1)S(1)} %add_convert_fusion.5), channel_id=1, source_target_pairs={{0,7},{1,0},{2,1},{3,2},{4,3},{5,4},{6,5},{7,6},{8,15},{9,8},{10,9... | collective-permute-start | bytes 786440 | tf_op jit(solution)/shard_map/ppermute | solution.py:30
  247.7 9.2 %collective-permute-start.19 = (bf16[256,512]{1,0:T(8,128)(2,1)S(1)}, bf16[256,512]{1,0:T(8,128)(2,1)S(1)}, u32[]{:S(2)}, u32[]{:S(2)}) collective-permute-start(bf16[256,512]{1,0:T(8,128)(2,1)S(1)} %add_convert_fusion.7), channel_id=1, source_target_pairs={{0,1},{1,2},{2,3},{3,4},{4,5},{5,6},{6,7},{7,0},{8,9},{9,10},{10,1... | collective-permute-start | bytes 786440 | tf_op jit(solution)/shard_map/ppermute | solution.py:30

commit v10 on v9

--- a/solution.py
+++ b/solution.py
@@ -60,9 +60,7 @@
         for h in range(2):
             up[h] = turned(up[h], 1)
             down[1 - h] = turned(down[1 - h], -1)
-        if step == 1:
-            up[1], table = lax.optimization_barrier((up[1], table))
-        else:
+        if step > 1:
             for h, block, offset in waiting:
                 block, up[h] = lax.optimization_barrier((block, up[h]))
                 add(sums, h, block, weights(offset))

time: 261 us -> 265 us (1.015)
  waiting for transfers between devices: 141 us -> 145 us
  transfers between devices with their start and end apart: 33 -> 33, of which waited for: 19 -> 16; matrix products, arithmetic and copies ran while one was open for 8% -> 9% of each run, Pallas kernels for 0% -> 0%
where the time goes in v10:
time: 265 us; the launch traced here: 262 us
  waiting for transfers between devices  145 us (55%)
  starting transfers between devices  74.8 us (28%)
  matrix products  14.3 us (5%)
  Pallas kernels  13.9 us (5%)
  local copies, waits for them, and re-layouts  7.28 us (3%)
  other arithmetic  5.4 us (2%)
    all_to_all x1, waiting for transfers between devices, answer(): lax.all_to_all(answers, 'dp', split_axis=0, concat_axis=0, tiled=True)  51.6 us
    all_to_all x1, waiting for transfers between devices, ask(): lax.all_to_all(sent_rows, 'dp', split_axis=0, concat_axis=0, tiled=True)  46.9 us
    ppermute x28, starting transfers between devices, turned(): lax.ppermute(block, 'mp', [(i, (i + distance) % size) for i in range(size)])  45.1 us
    ppermute x28, waiting for transfers between devices, turned(): lax.ppermute(block, 'mp', [(i, (i + distance) % size) for i in range(size)])  44.5 us
    pallas_call x1, Pallas kernels, attend(): pl.pallas_call(attend_kernel, out_shape=jax.ShapeDtypeStruct((peer_count,...  10.5 us
    all_to_all x1, starting transfers between devices, answer(): lax.all_to_all(answers, 'dp', split_axis=0, concat_axis=0, tiled=True)  10.1 us
    dot_general x16, matrix products, add(): product = jnp.dot(block, weight, preferred_element_type=f32)  9.42 us
    all_to_all x1, starting transfers between devices, ask(): lax.all_to_all(sent_rows, 'dp', split_axis=0, concat_axis=0, tiled=True)  8.37 us
  transfers between devices with their start and end apart: 33, of which 16 were waited for; matrix products, arithmetic and copies ran while one was open for 9% of the time, Pallas kernels for 0%

profile of v10, /device:TPU:28, one launch (start us, length us, event | category | flops | bytes accessed | tf_op | source)
XLA Modules:
  0.0 261.6 jit_solution(1402968177294755548)
XLA Ops:
  0.0 1.1 fusion.97
  1.1 2.0 collective-permute-start.7
  3.1 4.0 %collective-permute-start.9 = (bf16[256,512]{1,0:T(8,128)(2,1)S(1)}, bf16[256,512]{1,0:T(8,128)(2,1)S(1)}, u32[]{:S(2)}, u32[]{:S(2)}) collective-permute-start(bf16[256,512]{1,0:T(8,128)(2,1)S(1)} %get-tuple-element.44), channel_id=1, source_target_pairs={{0,7},{1,0},{2,1},{3,2},{4,3},{5,4},{6,5},{7,6},{8,15},{9,8},{10,9... | collective-permute-start | bytes 786440 | tf_op jit(solution)/shard_map/ppermute | solution.py:30
  7.1 1.9 collective-permute-start.2
  9.1 0.7 and_select_fusion.1
  11.3 0.7 all_to_all.12
  12.0 7.3 %all-to-all-start = ((s32[32,1,2]{2,1,0:T(1,128)}), s32[32,1,2]{2,1,0:T(1,128)S(1)}, u32[]{:S(2)}, u32[]{:S(2)}) async-start(s32[32,1,2]{2,1,0:T(1,128)} %bitcast.1), calls=%async_computation | async-start | bytes 32768 | tf_op jit(solution)/shard_map/all_to_all | solution.py:307
  19.4 0.9 collective-permute-start.1
  20.3 1.0 fusion.98
  21.4 2.6 collective-permute-start.10
  24.0 1.9 collective-permute-start.4
  25.9 3.9 %collective-permute-done.8 = bf16[256,512]{1,0:T(8,128)(2,1)S(1)} collective-permute-done((bf16[256,512]{1,0:T(8,128)(2,1)S(1)}, bf16[256,512]{1,0:T(8,128)(2,1)S(1)}, u32[]{:S(2)}, u32[]{:S(2)}) %collective-permute-start.8) | collective-permute-done | bytes 262176 | tf_op jit(solution)/shard_map/ppermute | solution.py:30
  29.9 4.8 %collective-permute-done.1 = bf16[256,512]{1,0:T(8,128)(2,1)S(1)} collective-permute-done((bf16[256,512]{1,0:T(8,128)(2,1)S(1)}, bf16[256,512]{1,0:T(8,128)(2,1)S(1)}, u32[]{:S(2)}, u32[]{:S(2)}) %collective-permute-start.1) | collective-permute-done | bytes 262176 | tf_op jit(solution)/shard_map/ppermute | solution.py:30
  34.9 1.4 fusion.48
  36.3 1.4 fusion.51
  37.8 1.4 fusion.50
  40.1 3.0 %collective-permute-start.12 = (bf16[256,512]{1,0:T(8,128)(2,1)S(1)}, bf16[256,512]{1,0:T(8,128)(2,1)S(1)}, u32[]{:S(2)}, u32[]{:S(2)}) collective-permute-start(bf16[256,512]{1,0:T(8,128)(2,1)S(1)} %collective-permute-done.10), channel_id=1, source_target_pairs={{0,7},{1,0},{2,1},{3,2},{4,3},{5,4},{6,5},{7,6},{8,15},{9,8},{10,9... | collective-permute-start | bytes 786440 | tf_op jit(solution)/shard_map/ppermute | solution.py:30
  43.5 2.0 collective-permute-start.5
  45.9 7.8 %collective-permute-done.11 = bf16[256,512]{1,0:T(8,128)(2,1)S(1)} collective-permute-done((bf16[256,512]{1,0:T(8,128)(2,1)S(1)}, bf16[256,512]{1,0:T(8,128)(2,1)S(1)}, u32[]{:S(2)}, u32[]{:S(2)}) %collective-permute-start.11) | collective-permute-done | bytes 262176 | tf_op jit(solution)/shard_map/ppermute | solution.py:30
  56.8 3.3 %collective-permute-start.13 = (bf16[256,512]{1,0:T(8,128)(2,1)S(1)}, bf16[256,512]{1,0:T(8,128)(2,1)S(1)}, u32[]{:S(2)}, u32[]{:S(2)}) collective-permute-start(bf16[256,512]{1,0:T(8,128)(2,1)S(1)} %collective-permute-done.12), channel_id=1, source_target_pairs={{0,7},{1,0},{2,1},{3,2},{4,3},{5,4},{6,5},{7,6},{8,15},{9,8},{10,9... | collective-permute-start | bytes 786440 | tf_op jit(solution)/shard_map/ppermute | solution.py:30
  61.2 3.0 %collective-permute-done.13 = bf16[256,512]{1,0:T(8,128)(2,1)S(1)} collective-permute-done((bf16[256,512]{1,0:T(8,128)(2,1)S(1)}, bf16[256,512]{1,0:T(8,128)(2,1)S(1)}, u32[]{:S(2)}, u32[]{:S(2)}) %collective-permute-start.13) | collective-permute-done | bytes 262176 | tf_op jit(solution)/shard_map/ppermute | solution.py:30
  65.8 1.9 collective-permute-start.14
  67.8 1.8 collective-permute-done.14
  69.7 2.8 %gather_fusion = bf16[64,64,512]{2,1,0:T(8,128)(2,1)} fusion(bf16[8,64,512]{2,1,0:T(8,128)(2,1)S(1)} %maximum_select_fusion, s32[1024]{0:T(1024)S(1)} %pad_clamp_fusion), kind=kCustom, calls=%fused_computation | custom fusion | bytes 8388864 | tf_op jit(solution)/shard_map/gather | solution.py:306
  72.5 8.4 %all-to-all-start.1 = ((bf16[32,128,512]{2,1,0:T(8,128)(2,1)}), bf16[32,128,512]{2,1,0:T(8,128)(2,1)}, u32[]{:S(2)}, u32[]{:S(2)}) async-start(bf16[32,128,512]{2,1,0:T(8,128)(2,1)} %bitcast.75), calls=%async_computation.1 | async-start | bytes 8388608 | tf_op jit(solution)/shard_map/all_to_all | solution.py:308
  81.4 0.7 reduce.3
  82.7 46.9 %all-to-all-done.1.q_ref = bf16[32,128,512]{2,1,0:T(8,128)(2,1)} async-done(((bf16[32,128,512]{2,1,0:T(8,128)(2,1)}), bf16[32,128,512]{2,1,0:T(8,128)(2,1)}, u32[]{:S(2)}, u32[]{:S(2)}) %all-to-all-start.1) | async-done | bytes 4194336 | tf_op jit(solution)/shard_map/all_to_all | solution.py:308
  129.6 10.5 %attend.1 = bf16[32,136,512]{2,1,0:T(8,128)(2,1)} custom-call(s32[64]{0:T(128)} %reshape.185.ids_ref, bf16[32,128,512]{2,1,0:T(8,128)(2,1)} %all-to-all-done.1.q_ref, bf16[8,128,512]{2,1,0:T(8,128)(2,1)} %k_ref.1, bf16[8,128,512]{2,1,0:T(8,128)(2,1)} %v_ref.1), custom_call_target="tpu_custom_call" | custom-call | flops 2147483648 | bytes 8388608 | tf_op jit(solution)/shard_map/attend/pallas_call | solution.py:171
  140.1 10.1 %all-to-all-start.2 = ((bf16[32,136,512]{2,1,0:T(8,128)(2,1)}), bf16[32,136,512]{2,1,0:T(8,128)(2,1)}, u32[]{:S(2)}, u32[]{:S(2)}) async-start(bf16[32,136,512]{2,1,0:T(8,128)(2,1)} %attend.1), calls=%async_computation.2 | async-start | bytes 8912896 | tf_op jit(solution)/shard_map/all_to_all | solution.py:313
  150.3 51.6 %all-to-all-done.2.back_ref = bf16[32,136,512]{2,1,0:T(8,128)(2,1)} async-done(((bf16[32,136,512]{2,1,0:T(8,128)(2,1)}), bf16[32,136,512]{2,1,0:T(8,128)(2,1)}, u32[]{:S(2)}, u32[]{:S(2)}) %all-to-all-start.2) | async-done | bytes 4456480 | tf_op jit(solution)/shard_map/all_to_all | solution.py:313
  201.9 3.3 %combine.1 = (bf16[4,64,512]{2,1,0:T(8,128)(2,1)S(1)}, bf16[4,64,512]{2,1,0:T(8,128)(2,1)S(1)}, bf16[64,512]{1,0:T(8,128)(2,1)S(1)}) custom-call(s32[16]{0:T(128)S(1)} %reshape.184.owner_ref, s32[16]{0:T(128)S(1)} %get-tuple-element.78.rank_ref, s32[1]{0:T(128)} %copy.19.live_ref, bf16[32,136,512]{2,1,0:T(8,128)(2,1)} %all-to-all-done.2.back_ref), custom_call_target="tpu_custom_call" | custom-call | flops 2097152 | bytes 1572864 | tf_op jit(solution)/shard_map/combine/pallas_call | solution.py:252
  206.8 1.9 collective-permute-start.15
  209.0 3.8 %collective-permute-start.26 = (bf16[256,512]{1,0:T(8,128)(2,1)S(1)}, bf16[256,512]{1,0:T(8,128)(2,1)S(1)}, u32[]{:S(2)}, u32[]{:S(2)}) collective-permute-start(bf16[256,512]{1,0:T(8,128)(2,1)S(1)} %convolution_convert_fusion), channel_id=1, source_target_pairs={{0,7},{1,0},{2,1},{3,2},{4,3},{5,4},{6,5},{7,6},{8,15},{9,8},{10,9... | collective-permute-start | bytes 786440 | tf_op jit(solution)/shard_map/ppermute | solution.py:30
  213.6 3.3 %collective-permute-start.20 = (bf16[256,512]{1,0:T(8,128)(2,1)S(1)}, bf16[256,512]{1,0:T(8,128)(2,1)S(1)}, u32[]{:S(2)}, u32[]{:S(2)}) collective-permute-start(bf16[256,512]{1,0:T(8,128)(2,1)S(1)} %convolution_convert_fusion.2), channel_id=1, source_target_pairs={{0,7},{1,0},{2,1},{3,2},{4,3},{5,4},{6,5},{7,6},{8,15},{9,8},{10,9... | collective-permute-start | bytes 786440 | tf_op jit(solution)/shard_map/ppermute | solution.py:30
  217.3 2.2 collective-permute-done.26
  219.8 3.8 %collective-permute-start.27 = (bf16[256,512]{1,0:T(8,128)(2,1)S(1)}, bf16[256,512]{1,0:T(8,128)(2,1)S(1)}, u32[]{:S(2)}, u32[]{:S(2)}) collective-permute-start(bf16[256,512]{1,0:T(8,128)(2,1)S(1)} %add_convert_fusion.2), channel_id=1, source_target_pairs={{0,7},{1,0},{2,1},{3,2},{4,3},{5,4},{6,5},{7,6},{8,15},{9,8},{10,9... | collective-permute-start | bytes 786440 | tf_op jit(solution)/shard_map/ppermute | solution.py:30
  224.0 1.1 collective-permute-done.20
  225.4 3.8 %collective-permute-start.21 = (bf16[256,512]{1,0:T(8,128)(2,1)S(1)}, bf16[256,512]{1,0:T(8,128)(2,1)S(1)}, u32[]{:S(2)}, u32[]{:S(2)}) collective-permute-start(bf16[256,512]{1,0:T(8,128)(2,1)S(1)} %add_convert_fusion.6), channel_id=1, source_target_pairs={{0,7},{1,0},{2,1},{3,2},{4,3},{5,4},{6,5},{7,6},{8,15},{9,8},{10,9... | collective-permute-start | bytes 786440 | tf_op jit(solution)/shard_map/ppermute | solution.py:30
  229.6 1.1 collective-permute-done.27
  230.8 3.8 %collective-permute-start.28 = (bf16[256,512]{1,0:T(8,128)(2,1)S(1)}, bf16[256,512]{1,0:T(8,128)(2,1)S(1)}, u32[]{:S(2)}, u32[]{:S(2)}) collective-permute-start(bf16[256,512]{1,0:T(8,128)(2,1)S(1)} %add_convert_fusion.1), channel_id=1, source_target_pairs={{0,7},{1,0},{2,1},{3,2},{4,3},{5,4},{6,5},{7,6},{8,15},{9,8},{10,9... | collective-permute-start | bytes 786440 | tf_op jit(solution)/shard_map/ppermute | solution.py:30
  234.8 5.3 %collective-permute-done.17 = bf16[256,512]{1,0:T(8,128)(2,1)S(1)} collective-permute-done((bf16[256,512]{1,0:T(8,128)(2,1)S(1)}, bf16[256,512]{1,0:T(8,128)(2,1)S(1)}, u32[]{:S(2)}, u32[]{:S(2)}) %collective-permute-start.17) | collective-permute-done | bytes 262176 | tf_op jit(solution)/shard_map/ppermute | solution.py:30
  240.5 1.4 collective-permute-done.28
  241.9 3.8 %collective-permute-start.29 = (bf16[256,512]{1,0:T(8,128)(2,1)S(1)}, bf16[256,512]{1,0:T(8,128)(2,1)S(1)}, u32[]{:S(2)}, u32[]{:S(2)}) collective-permute-start(bf16[256,512]{1,0:T(8,128)(2,1)S(1)} %add_convert_fusion), channel_id=1, source_target_pairs={{0,7},{1,0},{2,1},{3,2},{4,3},{5,4},{6,5},{7,6},{8,15},{9,8},{10,9... | collective-permute-start | bytes 786440 | tf_op jit(solution)/shard_map/ppermute | solution.py:30
  246.1 4.8 %collective-permute-done.18 = bf16[256,512]{1,0:T(8,128)(2,1)S(1)} collective-permute-done((bf16[256,512]{1,0:T(8,128)(2,1)S(1)}, bf16[256,512]{1,0:T(8,128)(2,1)S(1)}, u32[]{:S(2)}, u32[]{:S(2)}) %collective-permute-start.18) | collective-permute-done | bytes 262176 | tf_op jit(solution)/shard_map/ppermute | solution.py:30
  251.3 1.1 collective-permute-done.29
  252.5 4.5 %collective-permute-done.22 = bf16[256,512]{1,0:T(8,128)(2,1)S(1)} collective-permute-done((bf16[256,512]{1,0:T(8,128)(2,1)S(1)}, bf16[256,512]{1,0:T(8,128)(2,1)S(1)}, u32[]{:S(2)}, u32[]{:S(2)}) %collective-permute-start.22) | collective-permute-done | bytes 262176 | tf_op jit(solution)/shard_map/ppermute | solution.py:30
  257.0 3.4 %collective-permute-done.19 = bf16[256,512]{1,0:T(8,128)(2,1)S(1)} collective-permute-done((bf16[256,512]{1,0:T(8,128)(2,1)S(1)}, bf16[256,512]{1,0:T(8,128)(2,1)S(1)}, u32[]{:S(2)}, u32[]{:S(2)}) %collective-permute-start.19) | collective-permute-done | bytes 262176 | tf_op jit(solution)/shard_map/ppermute | solution.py:30
  260.5 1.2 maximum_add_fusion
  (106 shorter events, 15.8 us)
Async XLA Ops:
  1.1 18.2 %collective-permute-start.7 = (bf16[256,512]{1,0:T(8,128)(2,1)S(1)}, bf16[256,512]{1,0:T(8,128)(2,1)S(1)}, u32[]{:S(2)}, u32[]{:S(2)}) collective-permute-start(bf16[256,512]{1,0:T(8,128)(2,1)S(1)} %get-tuple-element.44), channel_id=1, source_target_pairs={{0,1},{1,2},{2,3},{3,4},{4,5},{5,6},{6,7},{7,0},{8,9},{9,10},{10,1... | collective-permute-start | bytes 786440 | tf_op jit(solution)/shard_map/ppermute | solution.py:30
  3.1 18.3 %collective-permute-start.9 = (bf16[256,512]{1,0:T(8,128)(2,1)S(1)}, bf16[256,512]{1,0:T(8,128)(2,1)S(1)}, u32[]{:S(2)}, u32[]{:S(2)}) collective-permute-start(bf16[256,512]{1,0:T(8,128)(2,1)S(1)} %get-tuple-element.44), channel_id=1, source_target_pairs={{0,7},{1,0},{2,1},{3,2},{4,3},{5,4},{6,5},{7,6},{8,15},{9,8},{10,9... | collective-permute-start | bytes 786440 | tf_op jit(solution)/shard_map/ppermute | solution.py:30
  7.1 16.9 %collective-permute-start.2 = (bf16[256,512]{1,0:T(8,128)(2,1)S(1)}, bf16[256,512]{1,0:T(8,128)(2,1)S(1)}, u32[]{:S(2)}, u32[]{:S(2)}) collective-permute-start(bf16[256,512]{1,0:T(8,128)(2,1)S(1)} %get-tuple-element.34), channel_id=1, source_target_pairs={{0,7},{1,0},{2,1},{3,2},{4,3},{5,4},{6,5},{7,6},{8,15},{9,8},{10,9... | collective-permute-start | bytes 786440 | tf_op jit(solution)/shard_map/ppermute | solution.py:30
  9.0 10.4 %collective-permute-start = (bf16[256,512]{1,0:T(8,128)(2,1)S(1)}, bf16[256,512]{1,0:T(8,128)(2,1)S(1)}, u32[]{:S(2)}, u32[]{:S(2)}) collective-permute-start(bf16[256,512]{1,0:T(8,128)(2,1)S(1)} %get-tuple-element.34), channel_id=1, source_target_pairs={{0,1},{1,2},{2,3},{3,4},{4,5},{5,6},{6,7},{7,0},{8,9},{9,10},{10,1... | collective-permute-start | bytes 786440 | tf_op jit(solution)/shard_map/ppermute | solution.py:30
  12.0 60.5 %all-to-all-start = ((s32[32,1,2]{2,1,0:T(1,128)}), s32[32,1,2]{2,1,0:T(1,128)S(1)}, u32[]{:S(2)}, u32[]{:S(2)}) async-start(s32[32,1,2]{2,1,0:T(1,128)} %bitcast.1), calls=%async_computation | async-start | bytes 32768 | tf_op jit(solution)/shard_map/all_to_all | solution.py:307
  19.3 10.5 %collective-permute-start.8 = (bf16[256,512]{1,0:T(8,128)(2,1)S(1)}, bf16[256,512]{1,0:T(8,128)(2,1)S(1)}, u32[]{:S(2)}, u32[]{:S(2)}) collective-permute-start(bf16[256,512]{1,0:T(8,128)(2,1)S(1)} %collective-permute-done.7), channel_id=1, source_target_pairs={{0,1},{1,2},{2,3},{3,4},{4,5},{5,6},{6,7},{7,0},{8,9},{9,10},{10,1... | collective-permute-start | bytes 786440 | tf_op jit(solution)/shard_map/ppermute | solution.py:30
  19.4 15.3 %collective-permute-start.1 = (bf16[256,512]{1,0:T(8,128)(2,1)S(1)}, bf16[256,512]{1,0:T(8,128)(2,1)S(1)}, u32[]{:S(2)}, u32[]{:S(2)}) collective-permute-start(bf16[256,512]{1,0:T(8,128)(2,1)S(1)} %collective-permute-done), channel_id=1, source_target_pairs={{0,1},{1,2},{2,3},{3,4},{4,5},{5,6},{6,7},{7,0},{8,9},{9,10},{10,1... | collective-permute-start | bytes 786440 | tf_op jit(solution)/shard_map/ppermute | solution.py:30
  20.3 22.8 %copy-start.1 = (bf16[4096,512]{1,0:T(8,128)(2,1)S(1)}, bf16[4096,512]{1,0:T(8,128)(2,1)}, u32[]{:S(2)}) copy-start(bf16[4096,512]{1,0:T(8,128)(2,1)} %param.10) | copy-start | bytes 12582916
  21.4 18.7 %collective-permute-start.10 = (bf16[256,512]{1,0:T(8,128)(2,1)S(1)}, bf16[256,512]{1,0:T(8,128)(2,1)S(1)}, u32[]{:S(2)}, u32[]{:S(2)}) collective-permute-start(bf16[256,512]{1,0:T(8,128)(2,1)S(1)} %collective-permute-done.9), channel_id=1, source_target_pairs={{0,7},{1,0},{2,1},{3,2},{4,3},{5,4},{6,5},{7,6},{8,15},{9,8},{10,9... | collective-permute-start | bytes 786440 | tf_op jit(solution)/shard_map/ppermute | solution.py:30
  24.0 19.6 %collective-permute-start.4 = (bf16[256,512]{1,0:T(8,128)(2,1)S(1)}, bf16[256,512]{1,0:T(8,128)(2,1)S(1)}, u32[]{:S(2)}, u32[]{:S(2)}) collective-permute-start(bf16[256,512]{1,0:T(8,128)(2,1)S(1)} %collective-permute-done.2), channel_id=1, source_target_pairs={{0,7},{1,0},{2,1},{3,2},{4,3},{5,4},{6,5},{7,6},{8,15},{9,8},{10,9... | collective-permute-start | bytes 786440 | tf_op jit(solution)/shard_map/ppermute | solution.py:30
  39.2 14.6 %collective-permute-start.3 = (bf16[256,512]{1,0:T(8,128)(2,1)S(1)}, bf16[256,512]{1,0:T(8,128)(2,1)S(1)}, u32[]{:S(2)}, u32[]{:S(2)}) collective-permute-start(bf16[256,512]{1,0:T(8,128)(2,1)S(1)} %collective-permute-done.1), channel_id=1, source_target_pairs={{0,1},{1,2},{2,3},{3,4},{4,5},{5,6},{6,7},{7,0},{8,9},{9,10},{10,1... | collective-permute-start | bytes 786440 | tf_op jit(solution)/shard_map/ppermute | solution.py:30
  39.7 14.0 %collective-permute-start.11 = (bf16[256,512]{1,0:T(8,128)(2,1)S(1)}, bf16[256,512]{1,0:T(8,128)(2,1)S(1)}, u32[]{:S(2)}, u32[]{:S(2)}) collective-permute-start(bf16[256,512]{1,0:T(8,128)(2,1)S(1)} %collective-permute-done.8), channel_id=1, source_target_pairs={{0,1},{1,2},{2,3},{3,4},{4,5},{5,6},{6,7},{7,0},{8,9},{9,10},{10,1... | collective-permute-start | bytes 786440 | tf_op jit(solution)/shard_map/ppermute | solution.py:30
  40.1 16.7 %collective-permute-start.12 = (bf16[256,512]{1,0:T(8,128)(2,1)S(1)}, bf16[256,512]{1,0:T(8,128)(2,1)S(1)}, u32[]{:S(2)}, u32[]{:S(2)}) collective-permute-start(bf16[256,512]{1,0:T(8,128)(2,1)S(1)} %collective-permute-done.10), channel_id=1, source_target_pairs={{0,7},{1,0},{2,1},{3,2},{4,3},{5,4},{6,5},{7,6},{8,15},{9,8},{10,9... | collective-permute-start | bytes 786440 | tf_op jit(solution)/shard_map/ppermute | solution.py:30
  43.5 17.1 %collective-permute-start.5 = (bf16[256,512]{1,0:T(8,128)(2,1)S(1)}, bf16[256,512]{1,0:T(8,128)(2,1)S(1)}, u32[]{:S(2)}, u32[]{:S(2)}) collective-permute-start(bf16[256,512]{1,0:T(8,128)(2,1)S(1)} %collective-permute-done.4), channel_id=1, source_target_pairs={{0,7},{1,0},{2,1},{3,2},{4,3},{5,4},{6,5},{7,6},{8,15},{9,8},{10,9... | collective-permute-start | bytes 786440 | tf_op jit(solution)/shard_map/ppermute | solution.py:30
  53.8 10.6 %collective-permute-start.6 = (bf16[256,512]{1,0:T(8,128)(2,1)S(1)}, bf16[256,512]{1,0:T(8,128)(2,1)S(1)}, u32[]{:S(2)}, u32[]{:S(2)}) collective-permute-start(bf16[256,512]{1,0:T(8,128)(2,1)S(1)} %collective-permute-done.3), channel_id=1, source_target_pairs={{0,1},{1,2},{2,3},{3,4},{4,5},{5,6},{6,7},{7,0},{8,9},{9,10},{10,1... | collective-permute-start | bytes 786440 | tf_op jit(solution)/shard_map/ppermute | solution.py:30
  56.8 7.4 %collective-permute-start.13 = (bf16[256,512]{1,0:T(8,128)(2,1)S(1)}, bf16[256,512]{1,0:T(8,128)(2,1)S(1)}, u32[]{:S(2)}, u32[]{:S(2)}) collective-permute-start(bf16[256,512]{1,0:T(8,128)(2,1)S(1)} %collective-permute-done.12), channel_id=1, source_target_pairs={{0,7},{1,0},{2,1},{3,2},{4,3},{5,4},{6,5},{7,6},{8,15},{9,8},{10,9... | collective-permute-start | bytes 786440 | tf_op jit(solution)/shard_map/ppermute | solution.py:30
  65.8 3.8 %collective-permute-start.14 = (bf16[1,64,512]{2,1,0:T(8,128)(2,1)S(1)}, bf16[1,64,512]{2,1,0:T(8,128)(2,1)S(1)}, u32[]{:S(2)}, u32[]{:S(2)}) collective-permute-start(bf16[1,64,512]{2,1,0:T(8,128)(2,1)S(1)} %slice_bitcast_fusion), channel_id=1, source_target_pairs={{8,0},{16,8},{24,16},{32,24},{40,32},{48,40},{56,48},{64,56},{72,6... | collective-permute-start | bytes 196616 | tf_op jit(solution)/shard_map/ppermute | solution.py:25
  72.5 57.1 %all-to-all-start.1 = ((bf16[32,128,512]{2,1,0:T(8,128)(2,1)}), bf16[32,128,512]{2,1,0:T(8,128)(2,1)}, u32[]{:S(2)}, u32[]{:S(2)}) async-start(bf16[32,128,512]{2,1,0:T(8,128)(2,1)} %bitcast.75), calls=%async_computation.1 | async-start | bytes 8388608 | tf_op jit(solution)/shard_map/all_to_all | solution.py:308
  140.1 61.8 %all-to-all-start.2 = ((bf16[32,136,512]{2,1,0:T(8,128)(2,1)}), bf16[32,136,512]{2,1,0:T(8,128)(2,1)}, u32[]{:S(2)}, u32[]{:S(2)}) async-start(bf16[32,136,512]{2,1,0:T(8,128)(2,1)} %attend.1), calls=%async_computation.2 | async-start | bytes 8912896 | tf_op jit(solution)/shard_map/all_to_all | solution.py:313
  201.9 3.4 %copy-start = (bf16[512,4096]{1,0:T(8,128)(2,1)S(1)}, bf16[512,4096]{1,0:T(8,128)(2,1)}, u32[]{:S(2)}) copy-start(bf16[512,4096]{1,0:T(8,128)(2,1)} %param.11) | copy-start | bytes 12582916
  206.8 6.0 %collective-permute-start.15 = (bf16[64,512]{1,0:T(8,128)(2,1)S(1)}, bf16[64,512]{1,0:T(8,128)(2,1)S(1)}, u32[]{:S(2)}, u32[]{:S(2)}) collective-permute-start(bf16[64,512]{1,0:T(8,128)(2,1)S(1)} %get-tuple-element.54), channel_id=1, source_target_pairs={{0,8},{8,16},{16,24},{24,32},{32,40},{40,48},{48,56},{56,64},{64,7... | collective-permute-start | bytes 196616 | tf_op jit(solution)/shard_map/ppermute | solution.py:25
  209.0 10.5 %collective-permute-start.26 = (bf16[256,512]{1,0:T(8,128)(2,1)S(1)}, bf16[256,512]{1,0:T(8,128)(2,1)S(1)}, u32[]{:S(2)}, u32[]{:S(2)}) collective-permute-start(bf16[256,512]{1,0:T(8,128)(2,1)S(1)} %convolution_convert_fusion), channel_id=1, source_target_pairs={{0,7},{1,0},{2,1},{3,2},{4,3},{5,4},{6,5},{7,6},{8,15},{9,8},{10,9... | collective-permute-start | bytes 786440 | tf_op jit(solution)/shard_map/ppermute | solution.py:30
  212.8 10.8 %collective-permute-start.23 = (bf16[256,512]{1,0:T(8,128)(2,1)S(1)}, bf16[256,512]{1,0:T(8,128)(2,1)S(1)}, u32[]{:S(2)}, u32[]{:S(2)}) collective-permute-start(bf16[256,512]{1,0:T(8,128)(2,1)S(1)} %convolution_convert_fusion.1), channel_id=1, source_target_pairs={{0,1},{1,2},{2,3},{3,4},{4,5},{5,6},{6,7},{7,0},{8,9},{9,10},{10,1... | collective-permute-start | bytes 786440 | tf_op jit(solution)/shard_map/ppermute | solution.py:30
  213.6 11.5 %collective-permute-start.20 = (bf16[256,512]{1,0:T(8,128)(2,1)S(1)}, bf16[256,512]{1,0:T(8,128)(2,1)S(1)}, u32[]{:S(2)}, u32[]{:S(2)}) collective-permute-start(bf16[256,512]{1,0:T(8,128)(2,1)S(1)} %convolution_convert_fusion.2), channel_id=1, source_target_pairs={{0,7},{1,0},{2,1},{3,2},{4,3},{5,4},{6,5},{7,6},{8,15},{9,8},{10,9... | collective-permute-start | bytes 786440 | tf_op jit(solution)/shard_map/ppermute | solution.py:30
  217.2 12.0 %collective-permute-start.16 = (bf16[256,512]{1,0:T(8,128)(2,1)S(1)}, bf16[256,512]{1,0:T(8,128)(2,1)S(1)}, u32[]{:S(2)}, u32[]{:S(2)}) collective-permute-start(bf16[256,512]{1,0:T(8,128)(2,1)S(1)} %convolution_convert_fusion.3), channel_id=1, source_target_pairs={{0,1},{1,2},{2,3},{3,4},{4,5},{5,6},{6,7},{7,0},{8,9},{9,10},{10,1... | collective-permute-start | bytes 786440 | tf_op jit(solution)/shard_map/ppermute | solution.py:30
  219.8 10.9 %collective-permute-start.27 = (bf16[256,512]{1,0:T(8,128)(2,1)S(1)}, bf16[256,512]{1,0:T(8,128)(2,1)S(1)}, u32[]{:S(2)}, u32[]{:S(2)}) collective-permute-start(bf16[256,512]{1,0:T(8,128)(2,1)S(1)} %add_convert_fusion.2), channel_id=1, source_target_pairs={{0,7},{1,0},{2,1},{3,2},{4,3},{5,4},{6,5},{7,6},{8,15},{9,8},{10,9... | collective-permute-start | bytes 786440 | tf_op jit(solution)/shard_map/ppermute | solution.py:30
  223.9 10.7 %collective-permute-start.24 = (bf16[256,512]{1,0:T(8,128)(2,1)S(1)}, bf16[256,512]{1,0:T(8,128)(2,1)S(1)}, u32[]{:S(2)}, u32[]{:S(2)}) collective-permute-start(bf16[256,512]{1,0:T(8,128)(2,1)S(1)} %add_convert_fusion.4), channel_id=1, source_target_pairs={{0,1},{1,2},{2,3},{3,4},{4,5},{5,6},{6,7},{7,0},{8,9},{9,10},{10,1... | collective-permute-start | bytes 786440 | tf_op jit(solution)/shard_map/ppermute | solution.py:30
  225.4 20.3 %collective-permute-start.21 = (bf16[256,512]{1,0:T(8,128)(2,1)S(1)}, bf16[256,512]{1,0:T(8,128)(2,1)S(1)}, u32[]{:S(2)}, u32[]{:S(2)}) collective-permute-start(bf16[256,512]{1,0:T(8,128)(2,1)S(1)} %add_convert_fusion.6), channel_id=1, source_target_pairs={{0,7},{1,0},{2,1},{3,2},{4,3},{5,4},{6,5},{7,6},{8,15},{9,8},{10,9... | collective-permute-start | bytes 786440 | tf_op jit(solution)/shard_map/ppermute | solution.py:30
  229.5 10.5 %collective-permute-start.17 = (bf16[256,512]{1,0:T(8,128)(2,1)S(1)}, bf16[256,512]{1,0:T(8,128)(2,1)S(1)}, u32[]{:S(2)}, u32[]{:S(2)}) collective-permute-start(bf16[256,512]{1,0:T(8,128)(2,1)S(1)} %add_convert_fusion.9), channel_id=1, source_target_pairs={{0,1},{1,2},{2,3},{3,4},{4,5},{5,6},{6,7},{7,0},{8,9},{9,10},{10,1... | collective-permute-start | bytes 786440 | tf_op jit(solution)/shard_map/ppermute | solution.py:30
  230.8 11.0 %collective-permute-start.28 = (bf16[256,512]{1,0:T(8,128)(2,1)S(1)}, bf16[256,512]{1,0:T(8,128)(2,1)S(1)}, u32[]{:S(2)}, u32[]{:S(2)}) collective-permute-start(bf16[256,512]{1,0:T(8,128)(2,1)S(1)} %add_convert_fusion.1), channel_id=1, source_target_pairs={{0,7},{1,0},{2,1},{3,2},{4,3},{5,4},{6,5},{7,6},{8,15},{9,8},{10,9... | collective-permute-start | bytes 786440 | tf_op jit(solution)/shard_map/ppermute | solution.py:30
  234.7 25.8 %copy-start.2 = (bf16[512,512]{1,0:T(8,128)(2,1)S(1)}, bf16[512,512]{1,0:T(8,128)(2,1)}, u32[]{:S(2)}) copy-start(bf16[512,512]{1,0:T(8,128)(2,1)} %param.8) | copy-start | bytes 1572868
  234.7 16.6 %collective-permute-start.25 = (bf16[256,512]{1,0:T(8,128)(2,1)S(1)}, bf16[256,512]{1,0:T(8,128)(2,1)S(1)}, u32[]{:S(2)}, u32[]{:S(2)}) collective-permute-start(bf16[256,512]{1,0:T(8,128)(2,1)S(1)} %add_convert_fusion.3), channel_id=1, source_target_pairs={{0,1},{1,2},{2,3},{3,4},{4,5},{5,6},{6,7},{7,0},{8,9},{9,10},{10,1... | collective-permute-start | bytes 786440 | tf_op jit(solution)/shard_map/ppermute | solution.py:30
  240.4 10.5 %collective-permute-start.18 = (bf16[256,512]{1,0:T(8,128)(2,1)S(1)}, bf16[256,512]{1,0:T(8,128)(2,1)S(1)}, u32[]{:S(2)}, u32[]{:S(2)}) collective-permute-start(bf16[256,512]{1,0:T(8,128)(2,1)S(1)} %add_convert_fusion.8), channel_id=1, source_target_pairs={{0,1},{1,2},{2,3},{3,4},{4,5},{5,6},{6,7},{7,0},{8,9},{9,10},{10,1... | collective-permute-start | bytes 786440 | tf_op jit(solution)/shard_map/ppermute | solution.py:30
  241.9 10.5 %collective-permute-start.29 = (bf16[256,512]{1,0:T(8,128)(2,1)S(1)}, bf16[256,512]{1,0:T(8,128)(2,1)S(1)}, u32[]{:S(2)}, u32[]{:S(2)}) collective-permute-start(bf16[256,512]{1,0:T(8,128)(2,1)S(1)} %add_convert_fusion), channel_id=1, source_target_pairs={{0,7},{1,0},{2,1},{3,2},{4,3},{5,4},{6,5},{7,6},{8,15},{9,8},{10,9... | collective-permute-start | bytes 786440 | tf_op jit(solution)/shard_map/ppermute | solution.py:30
  246.0 11.0 %collective-permute-start.22 = (bf16[256,512]{1,0:T(8,128)(2,1)S(1)}, bf16[256,512]{1,0:T(8,128)(2,1)S(1)}, u32[]{:S(2)}, u32[]{:S(2)}) collective-permute-start(bf16[256,512]{1,0:T(8,128)(2,1)S(1)} %add_convert_fusion.5), channel_id=1, source_target_pairs={{0,7},{1,0},{2,1},{3,2},{4,3},{5,4},{6,5},{7,6},{8,15},{9,8},{10,9... | collective-permute-start | bytes 786440 | tf_op jit(solution)/shard_map/ppermute | solution.py:30
  251.2 9.2 %collective-permute-start.19 = (bf16[256,512]{1,0:T(8,128)(2,1)S(1)}, bf16[256,512]{1,0:T(8,128)(2,1)S(1)}, u32[]{:S(2)}, u32[]{:S(2)}) collective-permute-start(bf16[256,512]{1,0:T(8,128)(2,1)S(1)} %add_convert_fusion.7), channel_id=1, source_target_pairs={{0,1},{1,2},{2,3},{3,4},{4,5},{5,6},{6,7},{7,0},{8,9},{9,10},{10,1... | collective-permute-start | bytes 786440 | tf_op jit(solution)/shard_map/ppermute | solution.py:30
